TPU v7x, 128 devices: a whole 4x4x4 slice. The times are simulated.
128 devices in a mesh: ctx: 32 (over z, x, core), exp: 4 (over y).
Axes of the slice: x: 4, y: 4, z: 4, core: 2. Of those that a mesh axis runs over, the one named last changes fastest.
Arguments:
- queries: bfloat16 [16384, 6144], P('ctx', 'exp'), may hold values from -0.52734375 to 0.52734375
- key_vectors: bfloat16 [16384, 6144], P('ctx', 'exp'), may hold values from -6 to 6
- values: bfloat16 [16384, 6144], P('ctx', 'exp'), may hold values from -6 to 6
- log_decay: float32 [16384, 48], P('ctx', 'exp'), may hold values from -1 to 0, as said below
- out_gate: bfloat16 [16384, 6144], P(('ctx', 'exp')), may hold values from -6 to 6
- residual: bfloat16 [16384, 6144], P(('ctx', 'exp')), may hold values from -6 to 6
- attn_gain: float32 [6144], replicated, may hold values from 0.1 to 1.9
- moe_gain: float32 [6144], replicated, may hold values from 0.1 to 1.9
- expert_ids: int32 [16384, 2], P(('ctx', 'exp')), may hold values from 0 to 31, as said below
- route_weights: float32 [16384, 2], P(('ctx', 'exp')), may hold values from 0.5 to 1.5
- w_gate: bfloat16 [4, 6144, 9216], P('exp', None, 'ctx'), may hold values from -0.078125 to 0.078125
- w_up: bfloat16 [4, 6144, 9216], P('exp', None, 'ctx'), may hold values from -0.078125 to 0.078125
- w_down: bfloat16 [4, 9216, 6144], P('exp', 'ctx'), may hold values from -0.0625 to 0.0625
Outputs:
- hidden: bfloat16 [16384, 6144], P(('ctx', 'exp'))
- moe_out: bfloat16 [16384, 6144], P(('ctx', 'exp'))
Inputs may be any that keep to these rules, and one draw needn't show every extreme that they name: `expert_ids`: each token names two different experts, at most one of them below 4. The 128 rows of one device name each expert below 4 at most 4 times; in every draw one expert is named exactly 4 times by every device of some index of ctx. `log_decay`: every entry is negative.
All inputs are finite; a program needn't handle non-finite values.
Results may differ from a plain program's by a relative error of at most 0.03.
Values may be sent and summed in bfloat16 or wider, within the bound.
No kernel may reach another device: no remote copies, remote signals or barrier semaphores. Data moves between devices by JAX's collectives and lax.ppermute only.
A program may use at most 128 MiB of HBM per device.

v0:
```python
import jax
import jax.numpy as jnp
from jax import lax
from jax.sharding import PartitionSpec as P

HEAD_DIM = 128
CAP = 4


def entering(shard, axis, combine, identity):
    peers, place = (lax.axis_size(axis), lax.axis_index(axis))
    everything = jax.tree.map(
        lambda part, kind: lax.all_gather(part.astype(kind), axis),
        shard,
        (jnp.bfloat16, jnp.bfloat16),
    )
    start = jax.tree.map(
        lambda part, zero: jnp.broadcast_to(jnp.asarray(zero, part.dtype), part.shape),
        shard,
        identity,
    )

    def turn(k, before):
        reached = k < place
        new = combine(
            before, jax.tree.map(lambda part, own: part[k].astype(own.dtype), everything, shard)
        )
        return jax.tree.map(lambda a, b: jnp.where(reached, a, b), new, before)

    return lax.fori_loop(0, peers, turn, start)


def combine_states(earlier, later):
    return (earlier[0] * later[0], later[0][:, None, None] * earlier[1] + later[1])


def local(
    queries,
    key_vectors,
    values,
    log_decay,
    out_gate,
    residual,
    attn_gain,
    moe_gain,
    expert_ids,
    route_weights,
    w_gate,
    w_up,
    w_down,
):
    highest = lax.Precision.HIGHEST
    row_total = queries.shape[0]
    head_count = log_decay.shape[1]
    query_heads = queries.reshape(row_total, head_count, HEAD_DIM)
    key_heads = key_vectors.reshape(row_total, head_count, HEAD_DIM)
    value_heads = values.reshape(row_total, head_count, HEAD_DIM)
    cumulative = jnp.cumsum(log_decay, axis=0)
    final_cum = cumulative[-1]
    weighted_keys = (
        key_heads.astype(jnp.float32) * jnp.exp(final_cum[None, :] - cumulative)[:, :, None]
    )
    local_state = jnp.einsum(
        "shd,she->hde", weighted_keys, value_heads.astype(jnp.float32), precision=highest
    )
    block_decay = jnp.exp(final_cum)
    prior = entering(
        (block_decay, local_state),
        "ctx",
        combine_states,
        (jnp.ones_like(block_decay), jnp.zeros_like(local_state)),
    )
    carried = prior[1]
    block_size = min(512, row_total)

    def query_part(block_index):
        offset = block_index * block_size
        scores = jnp.einsum(
            "thd,shd->hts", query_heads, key_heads, preferred_element_type=jnp.float32
        )
        log_gap = cumulative.T[:, :, None] - cumulative.T[:, None, :]
        causal = (offset + jnp.arange(block_size))[:, None] >= jnp.arange(row_total)[None, :]
        decay_now = jnp.where(causal[None], jnp.exp(jnp.minimum(log_gap, 0.0)), 0.0)
        weights = (scores * decay_now).astype(jnp.bfloat16)
        inside = jnp.einsum(
            "hts,shd->thd", weights, value_heads, preferred_element_type=jnp.float32
        )
        scaled = query_heads.astype(jnp.float32) * jnp.exp(cumulative)[:, :, None]
        carried_part = jnp.einsum("thd,hde->the", scaled, carried, precision=highest)
        return (inside + carried_part).astype(jnp.bfloat16)

    blocks_out = lax.map(query_part, jnp.arange(row_total // block_size))
    attention = blocks_out.reshape(row_total, head_count * HEAD_DIM)
    token_rows = lax.all_to_all(attention, "exp", split_axis=0, concat_axis=1, tiled=True)
    attn_f32 = token_rows.astype(jnp.float32)
    attn_norm = (
        attn_f32
        * lax.rsqrt(jnp.mean(attn_f32 * attn_f32, axis=-1, keepdims=True) + 1e-05)
        * attn_gain
    )
    hidden = (
        residual.astype(jnp.float32) + attn_norm * jax.nn.sigmoid(out_gate.astype(jnp.float32))
    ).astype(jnp.bfloat16)
    hidden_f32 = hidden.astype(jnp.float32)
    normed = (
        hidden_f32
        * lax.rsqrt(jnp.mean(hidden_f32 * hidden_f32, axis=-1, keepdims=True) + 1e-05)
        * moe_gain
    ).astype(jnp.bfloat16)
    held_count = lax.axis_size("exp")
    expert_index = jnp.arange(held_count, dtype=jnp.int32)
    naming = expert_ids[:, :, None] == expert_index[None, None, :]
    member = jnp.any(naming, axis=1)
    slot_rank = jnp.cumsum(member.astype(jnp.int32), axis=0) - 1
    slot_index = jnp.arange(CAP, dtype=jnp.int32)
    placing = (
        member.T[:, None, :] & (slot_rank.T[:, None, :] == slot_index[None, :, None])
    ).astype(jnp.bfloat16)
    outgoing = jnp.einsum(
        "jct,td->jcd", placing, normed, preferred_element_type=jnp.float32
    ).astype(jnp.bfloat16)
    incoming = lax.all_to_all(outgoing, "exp", split_axis=0, concat_axis=0, tiled=True)
    flat_rows = incoming.reshape(held_count * CAP, incoming.shape[2])
    gate_matrix = w_gate[0]
    up_matrix = w_up[0]
    down_matrix = w_down[0]
    pieces = lax.all_gather(flat_rows, "ctx", axis=0, tiled=True)
    gate_part = jnp.dot(pieces, gate_matrix, preferred_element_type=jnp.float32)
    up_part = jnp.dot(pieces, up_matrix, preferred_element_type=jnp.float32)
    activations = (jax.nn.silu(gate_part) * up_part).astype(jnp.bfloat16)
    summed = lax.psum_scatter(
        jnp.dot(activations, down_matrix, preferred_element_type=jnp.float32).astype(jnp.bfloat16),
        "ctx",
        scatter_dimension=0,
        tiled=True,
    ).astype(jnp.float32)
    leaving = summed.astype(jnp.bfloat16).reshape(held_count, CAP, summed.shape[1])
    returned = lax.all_to_all(leaving, "exp", split_axis=0, concat_axis=0, tiled=True)
    chosen = jnp.sum(jnp.where(expert_ids < held_count, route_weights, 0.0), axis=1)
    gathered_back = jnp.einsum("jct,jcd->td", placing, returned, preferred_element_type=jnp.float32)
    moe_out = (gathered_back * chosen[:, None]).astype(jnp.bfloat16)
    return (hidden, moe_out)


def solution(mesh):
    in_specs = (
        P("ctx", "exp"),
        P("ctx", "exp"),
        P("ctx", "exp"),
        P("ctx", "exp"),
        P(("ctx", "exp"), None),
        P(("ctx", "exp"), None),
        P(),
        P(),
        P(("ctx", "exp"), None),
        P(("ctx", "exp"), None),
        P("exp", None, "ctx"),
        P("exp", None, "ctx"),
        P("exp", "ctx", None),
    )
    out_specs = (P(("ctx", "exp"), None), P(("ctx", "exp"), None))
    return jax.shard_map(local, mesh=mesh, in_specs=in_specs, out_specs=out_specs, check_vma=False)
```

profile of v0, /device:TPU:0, one launch (start us, length us, event | category | flops | bytes accessed | tf_op | source)
XLA Modules:
  0.0 408.7 jit_solution(17558675305011067984)
XLA Ops:
  10.1 3.1 reduce-window.6
  15.9 2.6 copy.101
  18.5 2.6 copy.106
  22.4 4.3 %fusion.35 = bf16[12,128,128]{2,1,0:T(8,128)(2,1)} fusion(bf16[512,12,128]{0,2,1:T(8,128)(2,1)} %bitcast.85, bf16[512,12,128]{0,2,1:T(8,128)(2,1)} %bitcast.83, f32[512,12]{0,1:T(8,128)S(1)} %get-tuple-element.175), kind=kOutput, calls=%fused_computation.42 | convolution fusion | flops 1209729024 | bytes 3563520 | tf_op jit(solution)/shard_map/shd,she->hde/dot_general | solution.py:63
  27.7 22.8 %all-gather.1 = bf16[32,1,12]{2,1,0:T(2,128)(2,1)S(1)} all-gather(bf16[1,1,12]{2,1,0:T(2,128)(2,1)S(1)} %bitcast.98), channel_id=1, replica_groups=mesh['ctx'=32,'exp'=4] {'ctx'}, dimensions={0}, use_global_device_ids=true | all-gather | bytes 792 | tf_op jit(solution)/shard_map/all_gather | solution.py:13
  50.5 2.6 copy.100
  53.9 38.4 %all-gather.7.cloned.1.call-done = bf16[384,128,128]{2,1,0:T(8,128)(2,1)} async-done(((bf16[12,128,128]{2,1,0:T(8,128)(2,1)}), bf16[384,128,128]{2,1,0:T(8,128)(2,1)}) %all-gather.7.cloned.1.call-update) | async-done | bytes 12582928 | tf_op jit(solution)/shard_map/all_gather | solution.py:13
  92.4 72.8 %while.18 = (s32[]{:T(128)}, f32[12,128,128]{2,1,0:T(8,128)}, s32[]{:T(128)}, bf16[32,12]{1,0:T(8,128)(2,1)S(1)}, bf16[32,12,128,128]{3,2,1,0:T(8,128)(2,1)}, /*index=5*/s32[]{:T(128)}, s32[]{:T(128)}) while((s32[]{:T(128)}, f32[12,128,128]{2,1,0:T(8,128)}, s32[]{:T(128)}, bf16[32,12]{1,0:T(8,128)(2,1)S(1)}, ...), condition=%wide.region_3.4_spmd.clone, body=%wide.region_2.3_spmd.clone.sunk | while | flops 983056 | bytes 1966305 | solution.py:30
  165.1 8.3 %fusion.20 = f32[12,128,512]{1,2,0:T(8,128)} fusion(f32[12,128,128]{2,1,0:T(8,128)} %get-tuple-element.117, bf16[512,12,128]{0,2,1:T(8,128)(2,1)} %bitcast.87, f32[512,12]{0,1:T(8,128)} %get-tuple-element.174), kind=kOutput, calls=%fused_computation.30 | convolution fusion | flops 1209532416 | bytes 5529600 | tf_op jit(solution)/shard_map/while/body/eval_jaxpr/thd,hde->the/dot_general | solution.py:89
  173.4 8.8 %fusion.19 = bf16[512,12,128]{2,0,1:T(8,128)(2,1)} fusion(f32[12,128,512]{1,2,0:T(8,128)} %fusion.20, bf16[512,12,128]{0,2,1:T(8,128)(2,1)} %bitcast.86, f32[12,512]{1,0:T(8,128)} %bitcast.93, pred[512,512]{1,0:T(8,128)(4,1)} %iota_compare_fusion, bf16[512,12,128]{0,2,1:T(8,128)(2,1)} %bitcast.88, bf16[512,12,128]{0,2,1:T(8,128)(2,1)} %bitcast.84), kind=kOutput, calls=%fused_computation.28 | convolution fusion | flops 1627914240 | bytes 9723904 | tf_op jit(solution)/shard_map/while/body/eval_jaxpr/hts,shd->thd/dot_general | solution.py:85
  184.8 3.5 all_to_all.16
  188.3 2.8 copy.115
  191.1 4.3 %all-to-all-start = ((bf16[4,128,1536]{1,2,0:T(8,128)(2,1)}), bf16[4,128,1536]{1,2,0:T(8,128)(2,1)}, u32[]{:S(2)}, u32[]{:S(2)}) async-start(bf16[4,128,1536]{1,2,0:T(8,128)(2,1)} %copy.115), calls=%async_computation | async-start | bytes 3145728 | tf_op jit(solution)/shard_map/all_to_all | solution.py:94
  195.7 2.6 copy.116
  205.6 11.3 %all-to-all-done = bf16[4,128,1536]{1,2,0:T(8,128)(2,1)} async-done(((bf16[4,128,1536]{1,2,0:T(8,128)(2,1)}), bf16[4,128,1536]{1,2,0:T(8,128)(2,1)}, u32[]{:S(2)}, u32[]{:S(2)}) %all-to-all-start) | async-done | bytes 1572896 | tf_op jit(solution)/shard_map/all_to_all | solution.py:94
  219.1 3.2 fusion.12
  224.7 9.4 %all_to_all.23 = bf16[4,4,6144]{2,1,0:T(4,128)(2,1)} all-to-all(bf16[4,4,6144]{2,1,0:T(4,128)(2,1)S(1)} %convolution_convert_fusion.1), channel_id=1, replica_groups=mesh['ctx'=32,'exp'=4] {'exp'}, dimensions={0} | all-to-all | bytes 393216 | tf_op jit(solution)/shard_map/all_to_all | solution.py:122
  235.8 47.0 %all-gather.5.cloned.1.call-done = bf16[512,6144]{1,0:T(8,128)(2,1)} async-done(((bf16[16,6144]{1,0:T(8,128)(2,1)}), bf16[512,6144]{1,0:T(8,128)(2,1)}) %all-gather.5.cloned.1.call-update) | async-done | bytes 6291472 | tf_op jit(solution)/shard_map/all_gather | solution.py:127
  282.7 6.7 %fusion.10 = f32[512,288]{0,1:T(8,128)} fusion(bf16[512,6144]{1,0:T(8,128)(2,1)} %all-gather.5.cloned.1.call-done, bf16[1,6144,288]{1,2,0:T(8,128)(2,1)} %param.25), kind=kOutput, calls=%fused_computation.17 | convolution fusion | flops 1811939328 | bytes 10420224 | tf_op jit(solution)/shard_map/dot_general | solution.py:128
  289.4 12.1 %convolution_convert_fusion = bf16[512,6144]{1,0:T(8,128)(2,1)} fusion(bf16[1,288,6144]{2,1,0:T(8,128)(2,1)S(1)} %copy-done, bf16[512,6144]{1,0:T(8,128)(2,1)} %all-gather.5.cloned.1.call-done, bf16[1,6144,288]{1,2,0:T(8,128)(2,1)} %param.26, f32[512,288]{0,1:T(8,128)} %fusion.10), kind=kOutput, calls=%fused_computation.4 | convolution fusion | flops 3627909120 | bytes 20250624 | tf_op jit(solution)/shard_map/dot_general | solution.py:132
  301.5 85.5 %reduce-scatter.2.cloned.1.call-done = bf16[16,6144]{1,0:T(8,128)(2,1)} async-done(((bf16[512,6144]{1,0:T(8,128)(2,1)}), bf16[16,6144]{1,0:T(8,128)(2,1)}) %reduce-scatter.2.cloned.1.call-update) | async-done | bytes 196624 | tf_op jit(solution)/shard_map/reduce_scatter | solution.py:131
  388.6 4.3 %all-to-all-start.2 = ((bf16[4,4,6144]{2,1,0:T(4,128)(2,1)}), bf16[4,4,6144]{2,1,0:T(4,128)(2,1)}, u32[]{:S(2)}, u32[]{:S(2)}) async-start(bf16[4,4,6144]{2,1,0:T(4,128)(2,1)} %reshape.116), calls=%async_computation.3 | async-start | bytes 393216 | tf_op jit(solution)/shard_map/all_to_all | solution.py:138
  395.5 3.8 all-to-all-done.2
  399.3 2.8 fusion.2
  (114 shorter events, 102.0 us)
Async XLA Ops:
  7.2 282.2 %copy-start = (bf16[1,288,6144]{2,1,0:T(8,128)(2,1)S(1)}, bf16[1,288,6144]{2,1,0:T(8,128)(2,1)}, u32[]{:S(2)}) copy-start(bf16[1,288,6144]{2,1,0:T(8,128)(2,1)} %param.27) | copy-start | bytes 10616836
  7.2 85.2 %all-gather.7.cloned.1.call-start = ((), (), s32[]{:S(2)}) async-start(), calls=%async_computation.6 | async-start | bytes 12976128 | tf_op jit(solution)/shard_map/all_gather | solution.py:13
  15.1 0.6 copy-start.2
  191.1 25.8 %all-to-all-start = ((bf16[4,128,1536]{1,2,0:T(8,128)(2,1)}), bf16[4,128,1536]{1,2,0:T(8,128)(2,1)}, u32[]{:S(2)}, u32[]{:S(2)}) async-start(bf16[4,128,1536]{1,2,0:T(8,128)(2,1)} %copy.115), calls=%async_computation | async-start | bytes 3145728 | tf_op jit(solution)/shard_map/all_to_all | solution.py:94
  195.4 5.4 %copy-start.3 = (s32[128,2]{0,1:T(2,128)S(1)}, s32[128,2]{0,1:T(2,128)}, u32[]{:S(2)}) copy-start(s32[128,2]{0,1:T(2,128)} %param.23) | copy-start | bytes 3076
  195.4 87.3 %all-gather.5.cloned.1.call-start = ((), (), s32[]{:S(2)}) async-start(), calls=%async_computation.4 | async-start | bytes 6488064 | tf_op jit(solution)/shard_map/all_gather | solution.py:127
  219.1 4.3 %copy-start.5 = (f32[6144]{0:T(1024)S(1)}, f32[6144]{0:T(1024)}, u32[]{:S(2)}) copy-start(f32[6144]{0:T(1024)} %param.22) | copy-start | bytes 73732
  222.3 1.1 copy-start.1
  235.7 151.2 %reduce-scatter.2.cloned.1.call-start = ((), (), s32[]{:S(2)}) async-start(), calls=%async_computation.5 | async-start | bytes 6488064 | tf_op jit(solution)/shard_map/reduce_scatter | solution.py:131
  301.5 91.4 %copy-start.4 = (f32[128,2]{0,1:T(2,128)S(1)}, f32[128,2]{0,1:T(2,128)}, u32[]{:S(2)}) copy-start(f32[128,2]{0,1:T(2,128)} %param.24) | copy-start | bytes 3076
  388.6 10.7 %all-to-all-start.2 = ((bf16[4,4,6144]{2,1,0:T(4,128)(2,1)}), bf16[4,4,6144]{2,1,0:T(4,128)(2,1)}, u32[]{:S(2)}, u32[]{:S(2)}) async-start(bf16[4,4,6144]{2,1,0:T(4,128)(2,1)} %reshape.116), calls=%async_computation.3 | async-start | bytes 393216 | tf_op jit(solution)/shard_map/all_to_all | solution.py:138
Sparse Core Ops, SparseCore 0:
  26.9 65.4 all-gather.6
  235.8 46.8 all-gather.4
  301.6 85.2 reduce-scatter.1
where the time goes:
time: 411 us; the launch traced here: 409 us
  waiting for transfers between devices  186 us (45%)
  other arithmetic  88.4 us (22%)
  matrix products  44.2 us (11%)
  local copies, waits for them, and re-layouts  35.1 us (9%)
  blocking collectives  32.2 us (8%)
  between operations  13.9 us (3%)
  starting transfers between devices  8.89 us (2%)
    reduce_scatter x1, waiting for transfers between devices, local(): lax.psum_scatter(jnp.dot(activations, down_matrix, preferred_element_type...  85.5 us
    select_n x32, other arithmetic, turn(): return jax.tree.map(lambda a, b: jnp.where(reached, a, b), new, before)  72.5 us
    all_gather x1, waiting for transfers between devices, local(): pieces = lax.all_gather(flat_rows, 'ctx', axis=0, tiled=True)  47 us
    all_gather x1, waiting for transfers between devices, entering(): lax.all_gather(part.astype(kind), axis)  38.4 us
    all_gather x1, blocking collectives, entering(): lax.all_gather(part.astype(kind), axis)  22.8 us
    unnamed x21, local copies, waits for them, and re-layouts  17.3 us
    dot_general x1, matrix products, local(): jnp.dot(activations, down_matrix, preferred_element_type=jnp.float32)  12.1 us
    all_to_all x1, waiting for transfers between devices, local(): lax.all_to_all(attention, 'exp', split_axis=0, concat_axis=1, tiled=True)  11.3 us
  transfers between devices with their start and end apart: 5, of which 5 were waited for; matrix products, arithmetic and copies ran while one was open for 4% of the time, Pallas kernels for 0%

commit v1 on v0

v1 whole, which is shorter than its diff:
```python
import functools

import jax
import jax.numpy as jnp
from jax import lax
from jax.experimental import pallas as pl
from jax.experimental.pallas import tpu as pltpu
from jax.sharding import Mesh, PartitionSpec as P

HEAD_DIM = 128
CAP = 4
EPS = 1e-05
F32 = jnp.float32
BF16 = jnp.bfloat16
HIGHEST = lax.Precision.HIGHEST
CTX = ("z", "x", "core")
VMEM_LIMIT = 48 * 1024 * 1024


def iota(shape, dim):
    return lax.broadcasted_iota(jnp.int32, shape, dim)


def params(**kw):
    return pltpu.CompilerParams(vmem_limit_bytes=VMEM_LIMIT, **kw)


def cost(flops, bytes_accessed):
    return pl.CostEstimate(flops=flops, bytes_accessed=bytes_accessed, transcendentals=0)


def state_kernel(k_ref, v_ref, ld_ref, cum_ref, cumt_ref, msg_ref):
    rows, heads = ld_ref.shape
    per = heads * HEAD_DIM // 32
    ld = ld_ref[...]
    tri = (iota((rows, rows), 0) >= iota((rows, rows), 1)).astype(F32)
    cum = jnp.dot(tri, ld, precision=HIGHEST, preferred_element_type=F32)
    cum_ref[...] = cum
    cumt_ref[...] = lax.dot_general(
        ld, tri, (((0,), (1,)), ((), ())), precision=HIGHEST, preferred_element_type=F32
    )
    final = cum[rows - 1 : rows, :]
    fade = jnp.exp(final - cum)
    decay = jnp.exp(final)
    row16 = iota((16, HEAD_DIM), 0)
    tiles = []
    for h in range(heads):
        cols = slice(h * HEAD_DIM, (h + 1) * HEAD_DIM)
        wk = (k_ref[:, cols].astype(F32) * fade[:, h : h + 1]).astype(BF16)
        state = lax.dot_general(
            wk, v_ref[:, cols], (((0,), (0,)), ((), ())), preferred_element_type=F32
        ).astype(BF16)
        row = h * HEAD_DIM
        while row < (h + 1) * HEAD_DIM:
            part, at = row // per, row % per
            take = min(per - at, (h + 1) * HEAD_DIM - row)
            lo = row - h * HEAD_DIM
            msg_ref[part, at : at + take, :] = state[lo : lo + take, :]
            row += take
        whole = jnp.broadcast_to(decay[:, h : h + 1], (16, HEAD_DIM))
        high = whole.astype(BF16).astype(F32)
        tiles.append((high, whole - high))
    for part in range(32):
        first = per * part // HEAD_DIM
        last = (per * part + per - 1) // HEAD_DIM
        tile = jnp.where(
            row16 == 0,
            tiles[first][0],
            jnp.where(
                row16 == 1, tiles[first][1], jnp.where(row16 == 2, tiles[last][0], tiles[last][1])
            ),
        )
        msg_ref[part, per : per + 16, :] = tile.astype(BF16)


def local_states(k, v, ld):
    rows, width = k.shape
    heads = ld.shape[1]
    per = heads * HEAD_DIM // 32
    return pl.pallas_call(
        state_kernel,
        out_shape=(
            jax.ShapeDtypeStruct((rows, heads), F32),
            jax.ShapeDtypeStruct((heads, rows), F32),
            jax.ShapeDtypeStruct((32, per + 16, HEAD_DIM), BF16),
        ),
        compiler_params=params(),
        cost_estimate=cost(2 * rows * width * HEAD_DIM, 4 * rows * width),
        name="local_states",
    )(k, v, ld)


def scan_kernel(split_ref, in_ref, out_ref):
    parts, per, width = out_ref.shape
    first_rows = iota((per, width), 0) < split_ref[0]
    state = jnp.zeros((per, width), F32)
    for b in range(parts):
        out_ref[b, :, :] = state.astype(BF16)
        if b + 1 < parts:
            tail = in_ref[b, per : per + 16, :].astype(F32)
            d0 = tail[0:1, :] + tail[1:2, :]
            d1 = tail[2:3, :] + tail[3:4, :]
            decay = jnp.where(first_rows, d0, d1)
            state = decay * state + in_ref[b, 0:per, :].astype(F32)


def scan_blocks(msg, part):
    parts, tall, width = msg.shape
    per = tall - 16
    split = (HEAD_DIM - (per * part) % HEAD_DIM).astype(jnp.int32).reshape(1)
    return pl.pallas_call(
        scan_kernel,
        out_shape=jax.ShapeDtypeStruct((parts, per, width), BF16),
        in_specs=[
            pl.BlockSpec(memory_space=pltpu.SMEM),
            pl.BlockSpec(memory_space=pltpu.VMEM),
        ],
        out_specs=pl.BlockSpec(memory_space=pltpu.VMEM),
        compiler_params=params(),
        cost_estimate=cost(1000000, 1000000),
        name="scan_blocks",
    )(split, msg)


def inside_kernel(group, q_ref, k_ref, v_ref, cum_ref, cumt_ref, inside_ref, qs_ref):
    rows, heads = cum_ref.shape
    lane = iota((rows, heads), 1)
    cum = cum_ref[...]
    causal = iota((HEAD_DIM, HEAD_DIM), 0) >= iota((HEAD_DIM, HEAD_DIM), 1)
    for j in range(group):
        h = pl.program_id(0) * group + j
        cols = slice(j * HEAD_DIM, (j + 1) * HEAD_DIM)
        col = jnp.sum(jnp.where(lane == h, cum, 0.0), axis=1, keepdims=True)
        row = cumt_ref[pl.ds(h, 1), :]
        q = q_ref[:, cols]
        k = k_ref[:, cols]
        v = v_ref[:, cols]
        qs_ref[:, cols] = (q.astype(F32) * jnp.exp(col)).astype(BF16)
        for i in range(rows // HEAD_DIM):
            lo, hi = i * HEAD_DIM, (i + 1) * HEAD_DIM
            qi = q[lo:hi]
            ci = col[lo:hi]
            s = lax.dot_general(
                qi, k[lo:hi], (((1,), (1,)), ((), ())), preferred_element_type=F32
            )
            gap = jnp.minimum(ci - row[:, lo:hi], 0.0)
            w = jnp.where(causal, s * jnp.exp(gap), 0.0).astype(BF16)
            total = jnp.dot(w, v[lo:hi], preferred_element_type=F32)
            if i:
                s = lax.dot_general(
                    qi, k[:lo], (((1,), (1,)), ((), ())), preferred_element_type=F32
                )
                w = (s * jnp.exp(jnp.minimum(ci - row[:, :lo], 0.0))).astype(BF16)
                total = total + jnp.dot(w, v[:lo], preferred_element_type=F32)
            inside_ref[lo:hi, cols] = total


def inside_blocks(q, k, v, cum, cumt, group=3):
    rows, width = q.shape
    heads = cum.shape[1]
    block = pl.BlockSpec((rows, group * HEAD_DIM), lambda g: (0, g))
    return pl.pallas_call(
        functools.partial(inside_kernel, group),
        grid=(heads // group,),
        out_shape=(
            jax.ShapeDtypeStruct((rows, width), F32),
            jax.ShapeDtypeStruct((rows, width), BF16),
        ),
        in_specs=[
            block,
            block,
            block,
            pl.BlockSpec((rows, heads), lambda g: (0, 0)),
            pl.BlockSpec((heads, rows), lambda g: (0, 0)),
        ],
        out_specs=(block, block),
        compiler_params=params(),
        cost_estimate=cost(4 * rows * rows * width, 12 * rows * width),
        name="inside_blocks",
    )(q, k, v, cum, cumt)


def carried_kernel(group, inside_ref, qs_ref, state_ref, place_ref, att_ref, sel_ref):
    for j in range(group):
        cols = slice(j * HEAD_DIM, (j + 1) * HEAD_DIM)
        att = (
            inside_ref[:, cols]
            + jnp.dot(qs_ref[:, cols], state_ref[j], preferred_element_type=F32)
        ).astype(BF16)
        att_ref[:, cols] = att
        sel_ref[:, cols] = jnp.dot(
            place_ref[...], att, preferred_element_type=F32
        ).astype(BF16)


def carried_blocks(inside, qs, state, place, group=3):
    rows, width = inside.shape
    heads = width // HEAD_DIM
    chosen = place.shape[0]
    block = pl.BlockSpec((rows, group * HEAD_DIM), lambda g: (0, g))
    return pl.pallas_call(
        functools.partial(carried_kernel, group),
        grid=(heads // group,),
        out_shape=(
            jax.ShapeDtypeStruct((rows, width), BF16),
            jax.ShapeDtypeStruct((chosen, width), BF16),
        ),
        in_specs=[
            block,
            block,
            pl.BlockSpec((group, HEAD_DIM, HEAD_DIM), lambda g: (g, 0, 0)),
            pl.BlockSpec((chosen, rows), lambda g: (0, 0)),
        ],
        out_specs=(block, pl.BlockSpec((chosen, group * HEAD_DIM), lambda g: (0, g))),
        compiler_params=params(),
        cost_estimate=cost(4 * rows * width * HEAD_DIM, 8 * rows * width),
        name="carried_blocks",
    )(inside, qs, state, place)


def members(ids, held):
    return jnp.concatenate(
        [
            ((ids[0:1, :] == e) | (ids[1:2, :] == e)).astype(F32)
            for e in range(held)
        ],
        axis=0,
    )


def place_kernel(ids_ref, place_ref):
    sources, _, tokens = ids_ref.shape
    held = sources
    total = sources * tokens
    ids = jnp.concatenate([ids_ref[j] for j in range(sources)], axis=1)
    m = members(ids, held)
    before = iota((total, total), 0)
    after = iota((total, total), 1)
    upto = ((before <= after) & (before // tokens == after // tokens)).astype(BF16)
    rank = jnp.dot(m.astype(BF16), upto, preferred_element_type=F32) - 1.0
    rows = sources * CAP
    r = iota((rows, total), 0)
    t = iota((rows, total), 1)
    here = (t // tokens == r // CAP).astype(F32)
    slot = (r % CAP).astype(F32)
    for e in range(held):
        hit = jnp.where(rank[e : e + 1, :] == slot, m[e : e + 1, :] * here, 0.0)
        place_ref[e * rows : (e + 1) * rows, :] = hit.astype(BF16)


def place_rows(ids):
    sources, _, tokens = ids.shape
    return pl.pallas_call(
        place_kernel,
        out_shape=jax.ShapeDtypeStruct((sources * sources * CAP, sources * tokens), BF16),
        compiler_params=params(),
        cost_estimate=cost(1000000, 200000),
        name="place_rows",
    )(ids)


def route_kernel(ids_ref, res_ref, gate_ref, out_ref, place_ref):
    held = out_ref.shape[0]
    tokens = ids_ref.shape[1]
    m = members(ids_ref[...], held)
    upto = (iota((tokens, tokens), 0) <= iota((tokens, tokens), 1)).astype(BF16)
    rank = jnp.dot(m.astype(BF16), upto, preferred_element_type=F32) - 1.0
    slot = iota((CAP, tokens), 0).astype(F32)
    for e in range(held):
        hit = jnp.where(rank[e : e + 1, :] == slot, m[e : e + 1, :], 0.0)
        place_ref[e * CAP : (e + 1) * CAP, :] = hit
        chosen = hit.astype(BF16)
        out_ref[e, 0:CAP, :] = jnp.dot(
            chosen, res_ref[...], preferred_element_type=F32
        ).astype(BF16)
        out_ref[e, CAP : 2 * CAP, :] = jnp.dot(
            chosen, gate_ref[...], preferred_element_type=F32
        ).astype(BF16)


def route_rows(ids, residual, out_gate, held):
    tokens, width = residual.shape
    return pl.pallas_call(
        route_kernel,
        out_shape=(
            jax.ShapeDtypeStruct((held, 2 * CAP, width), BF16),
            jax.ShapeDtypeStruct((held * CAP, tokens), F32),
        ),
        compiler_params=params(),
        cost_estimate=cost(64 * tokens * width, 5 * tokens * width),
        name="route_rows",
    )(ids, residual, out_gate)


def gated(att, res, gate, attn_gain):
    norm = att * lax.rsqrt(jnp.mean(att * att, axis=-1, keepdims=True) + EPS) * attn_gain
    return (res + norm * jax.nn.sigmoid(gate)).astype(BF16)


def routed_norm_kernel(att_ref, rg_ref, ag_ref, mg_ref, one_ref, two_ref):
    sources, rows, _ = att_ref.shape
    att = jnp.concatenate([att_ref[s].astype(F32) for s in range(sources)], axis=1)
    rg = [rg_ref[j].astype(F32) for j in range(sources)]
    res = jnp.concatenate([a[0:CAP] for a in rg], axis=0)
    gate = jnp.concatenate([a[CAP : 2 * CAP] for a in rg], axis=0)
    hidden = gated(att, res, gate, ag_ref[...]).astype(F32)
    normed = (
        hidden * lax.rsqrt(jnp.mean(hidden * hidden, axis=-1, keepdims=True) + EPS) * mg_ref[...]
    ).astype(BF16)
    half = normed.shape[1] // 2
    for s in range(one_ref.shape[0]):
        one_ref[s] = normed[:, :half]
        two_ref[s] = normed[:, half:]


def routed_norm(att, rg, attn_gain, moe_gain, copies):
    sources, rows, part = att.shape
    width = sources * part
    return pl.pallas_call(
        routed_norm_kernel,
        out_shape=(
            jax.ShapeDtypeStruct((copies, rows, width // 2), BF16),
            jax.ShapeDtypeStruct((copies, rows, width // 2), BF16),
        ),
        compiler_params=params(),
        cost_estimate=cost(20 * rows * width, 20 * rows * width),
        name="routed_norm",
    )(att, rg, attn_gain, moe_gain)


def hidden_kernel(att_ref, res_ref, gate_ref, ag_ref, out_ref):
    sources = att_ref.shape[0]
    att = jnp.concatenate([att_ref[s].astype(F32) for s in range(sources)], axis=1)
    out_ref[...] = gated(att, res_ref[...].astype(F32), gate_ref[...].astype(F32), ag_ref[...])


def hidden_rows(att, residual, out_gate, attn_gain, tile=32):
    sources, rows, part = att.shape
    width = sources * part
    block = pl.BlockSpec((tile, width), lambda i: (i, 0))
    return pl.pallas_call(
        hidden_kernel,
        grid=(rows // tile,),
        out_shape=jax.ShapeDtypeStruct((rows, width), BF16),
        in_specs=[
            pl.BlockSpec((sources, tile, part), lambda i: (0, i, 0)),
            block,
            block,
            pl.BlockSpec((1, width), lambda i: (0, 0)),
        ],
        out_specs=block,
        compiler_params=params(),
        cost_estimate=cost(20 * rows * width, 8 * rows * width),
        name="hidden_rows",
    )(att, residual, out_gate, attn_gain)


def expert_kernel(
    ksteps, nsteps, one_ref, two_ref, wg_ref, wu_ref, wd_ref, o1_ref, o2_ref, gate_acc, up_acc, act
):
    step = pl.program_id(0)
    nz, nx, rows, _ = one_ref.shape
    depth = one_ref.shape[3]

    def accumulate(lhs, first):
        g = jnp.dot(lhs, wg_ref[0], preferred_element_type=F32)
        u = jnp.dot(lhs, wu_ref[0], preferred_element_type=F32)
        if first:
            gate_acc[...] = g
            up_acc[...] = u
        else:
            gate_acc[...] += g
            up_acc[...] += u

    half = ksteps // 2
    for s in range(ksteps):

        @pl.when(step == s)
        def _():
            if s < half:
                lhs = one_ref[...].reshape(nz * nx * rows, depth)
            else:
                lhs = jnp.concatenate(
                    [two_ref[x, z] for z in range(nz) for x in range(nx)], axis=0
                )
            accumulate(lhs, s == 0)
            if s == ksteps - 1:
                g = gate_acc[...]
                act[...] = (g * jax.nn.sigmoid(g) * up_acc[...]).astype(BF16)

    @pl.when(step >= ksteps)
    def _():
        out = jnp.dot(act[...], wd_ref[0], preferred_element_type=F32).astype(BF16)

        @pl.when(step < ksteps + nsteps // 2)
        def _():
            o1_ref[...] = out.reshape(o1_ref.shape)

        @pl.when(step >= ksteps + nsteps // 2)
        def _():
            for z in range(nz):
                for x in range(nx):
                    at = (z * nx + x) * rows
                    o2_ref[x, z] = out[at : at + rows]


def expert_rows(one, two, w_gate, w_up, w_down, ksteps=4, nsteps=4):
    nz, nx, rows, half = one.shape
    units = w_gate.shape[2]
    depth = 2 * half // ksteps
    wide = 2 * half // nsteps
    kh, nh = ksteps // 2, nsteps // 2
    count = nz * nx * rows

    def k_at(i):
        return jnp.minimum(i, ksteps - 1)

    def n_at(i):
        return jnp.maximum(i - ksteps, 0)

    return pl.pallas_call(
        functools.partial(expert_kernel, ksteps, nsteps),
        grid=(ksteps + nsteps,),
        out_shape=(
            jax.ShapeDtypeStruct((nz, nx, rows, half), BF16),
            jax.ShapeDtypeStruct((nx, nz, rows, half), BF16),
        ),
        in_specs=[
            pl.BlockSpec((nz, nx, rows, depth), lambda i: (0, 0, 0, jnp.minimum(i, kh - 1))),
            pl.BlockSpec(
                (nx, nz, rows, depth), lambda i: (0, 0, 0, jnp.clip(i - kh, 0, kh - 1))
            ),
            pl.BlockSpec((1, depth, units), lambda i: (0, k_at(i), 0)),
            pl.BlockSpec((1, depth, units), lambda i: (0, k_at(i), 0)),
            pl.BlockSpec((1, units, wide), lambda i: (0, 0, n_at(i))),
        ],
        out_specs=(
            pl.BlockSpec((nz, nx, rows, wide), lambda i: (0, 0, 0, jnp.minimum(n_at(i), nh - 1))),
            pl.BlockSpec(
                (nx, nz, rows, wide), lambda i: (0, 0, 0, jnp.clip(n_at(i) - nh, 0, nh - 1))
            ),
        ),
        scratch_shapes=[
            pltpu.VMEM((count, units), F32),
            pltpu.VMEM((count, units), F32),
            pltpu.VMEM((count, units), BF16),
        ],
        compiler_params=params(),
        cost_estimate=cost(12 * count * half * units, 12 * half * units + 8 * count * half),
        name="expert_rows",
    )(one, two, w_gate, w_up, w_down)


def combine_kernel(place_ref, rows_ref, ids_ref, weights_ref, out_ref):
    held = rows_ref.shape[0]
    rows = jnp.concatenate([rows_ref[e].astype(F32) for e in range(held)], axis=0).astype(BF16)
    back = lax.dot_general(
        place_ref[...].astype(BF16), rows, (((0,), (0,)), ((), ())), preferred_element_type=F32
    )
    chosen = jnp.sum(
        jnp.where(ids_ref[...] < held, weights_ref[...], 0.0), axis=1, keepdims=True
    )
    out_ref[...] = (back * chosen).astype(BF16)


def combine_rows(place, rows, ids, weights):
    tokens = ids.shape[0]
    width = rows.shape[2]
    return pl.pallas_call(
        combine_kernel,
        out_shape=jax.ShapeDtypeStruct((tokens, width), BF16),
        compiler_params=params(),
        cost_estimate=cost(32 * tokens * width, 2 * tokens * width),
        name="combine_rows",
    )(place, rows, ids, weights)


def swap(a, axis):
    n = lax.axis_size(axis)
    return lax.ppermute(a, axis, [(i, (i + 1) % n) for i in range(n)])


def exchange(a, axis):
    return lax.all_to_all(a, axis, split_axis=0, concat_axis=0, tiled=True)


def local(
    queries,
    key_vectors,
    values,
    log_decay,
    out_gate,
    residual,
    attn_gain,
    moe_gain,
    expert_ids,
    route_weights,
    w_gate,
    w_up,
    w_down,
):
    held = lax.axis_size("exp")
    nz, nx = lax.axis_size("z"), lax.axis_size("x")
    rows, width = queries.shape
    heads = log_decay.shape[1]
    tokens = residual.shape[0]
    attn_gain = attn_gain.reshape(1, -1)
    moe_gain = moe_gain.reshape(1, -1)
    ids = expert_ids.T

    cum, cumt, msg = local_states(key_vectors, values, log_decay)
    sent = exchange(msg, CTX)
    prior = scan_blocks(sent, lax.axis_index(CTX))
    state = exchange(prior, CTX).reshape(heads, HEAD_DIM, HEAD_DIM)

    all_ids = lax.all_gather(ids, "exp", axis=0)
    place = place_rows(all_ids)
    rg, place_own = route_rows(ids, residual, out_gate, held)
    rg = exchange(rg, "exp")
    inside, qs = inside_blocks(queries, key_vectors, values, cum, cumt)

    attention, routed = carried_blocks(inside, qs, state, place)
    routed = exchange(routed.reshape(held, held * CAP, width), "exp")
    one, two = routed_norm(routed, rg, attn_gain, moe_gain, nx)

    one = exchange(one, "x")
    two = exchange(two, "z")
    one = exchange(jnp.broadcast_to(one[None], (nz,) + one.shape), "z")
    two = exchange(jnp.broadcast_to(two[None], (nx,) + two.shape), "x")
    one_far, two_far = swap(one, "core"), swap(two, "core")

    here1, here2 = expert_rows(one, two, w_gate, w_up, w_down)
    far1, far2 = expert_rows(one_far, two_far, w_gate, w_up, w_down)
    far1, far2 = swap(far1, "core"), swap(far2, "core")

    def total(parts):
        return jnp.sum(parts.astype(F32), axis=0).astype(BF16)

    sum1 = (here1.astype(F32) + far1.astype(F32)).astype(BF16)
    sum2 = (here2.astype(F32) + far2.astype(F32)).astype(BF16)
    sum1 = total(exchange(sum1, "z"))
    sum2 = total(exchange(sum2, "x"))
    sum1 = total(exchange(sum1, "x"))
    sum2 = total(exchange(sum2, "z"))
    back = jnp.concatenate([sum1, sum2], axis=1).reshape(held, CAP, -1)
    back = exchange(back, "exp")
    moe_out = combine_rows(place_own, back, expert_ids, route_weights)

    whole = exchange(attention.reshape(held, tokens, width), "exp")
    hidden = hidden_rows(whole, residual, out_gate, attn_gain)
    return (hidden, moe_out)


def solution(mesh):
    cube = Mesh(mesh.devices.reshape(4, 4, 2, 4), ("z", "x", "core", "exp"))
    both = CTX + ("exp",)
    in_specs = (
        P(CTX, "exp"),
        P(CTX, "exp"),
        P(CTX, "exp"),
        P(CTX, "exp"),
        P(both, None),
        P(both, None),
        P(),
        P(),
        P(both, None),
        P(both, None),
        P("exp", None, CTX),
        P("exp", None, CTX),
        P("exp", CTX, None),
    )
    out_specs = (P(both, None), P(both, None))
    return jax.shard_map(local, mesh=cube, in_specs=in_specs, out_specs=out_specs, check_vma=False)
```

time: 411 us -> 306 us (0.74)
  waiting for transfers between devices: 186 us -> 90.9 us
  other arithmetic: 88.4 us -> 14.1 us
  Pallas kernels: 0 us -> 52.8 us
  matrix products: 44.2 us -> 0 us
  blocking collectives: 32.2 us -> 71 us
  starting transfers between devices: 8.89 us -> 41.6 us
  between operations: 13.9 us -> 0.92 us
    reduce_scatter x1 -> x0, waiting for transfers between devices: 85.5 us -> none  [local(): lax.psum_scatter(jnp.dot(activations, down_matrix, preferred_element_type...]
    all_gather x2 -> x0, waiting for transfers between devices: 85.4 us -> none  [the longest x1 47 us: local(): pieces = lax.all_gather(flat_rows, 'ctx', axis=0, tiled=True)]
    all_to_all x2 -> x9, waiting for transfers between devices: 15.2 us -> 90.9 us  [exchange(): return lax.all_to_all(a, axis, split_axis=0, concat_axis=0, tiled=True)]
    select_n x32 -> x0, other arithmetic: 72.5 us -> none  [turn(): return jax.tree.map(lambda a, b: jnp.where(reached, a, b), new, before)]
    pallas_call x0 -> x11, Pallas kernels: none -> 52.8 us  [the longest x2 23.7 us: expert_rows(): pl.pallas_call(functools.partial(expert_kernel, ksteps, nsteps), grid=(ks...]
    all_to_all x1 -> x5, blocking collectives: 9.38 us -> 60.5 us  [exchange(): return lax.all_to_all(a, axis, split_axis=0, concat_axis=0, tiled=True)]
    dot_general x7 -> x0, matrix products: 44.2 us -> none  [the longest x1 12.1 us: local(): jnp.dot(activations, down_matrix, preferred_element_type=jnp.float32)]
    all_to_all x2 -> x9, starting transfers between devices: 8.59 us -> 41 us  [exchange(): return lax.all_to_all(a, axis, split_axis=0, concat_axis=0, tiled=True)]
  transfers between devices with their start and end apart: 5 -> 13, of which waited for: 5 -> 8; matrix products, arithmetic and copies ran while one was open for 4% -> 9% of each run, Pallas kernels for 0% -> 11%
where the time goes in v1:
time: 306 us; the launch traced here: 303 us
  waiting for transfers between devices  90.9 us (30%)
  blocking collectives  71 us (23%)
  Pallas kernels  52.8 us (17%)
  starting transfers between devices  41.6 us (14%)
  local copies, waits for them, and re-layouts  32 us (10%)
  other arithmetic  14.1 us (5%)
    all_to_all x9, waiting for transfers between devices, exchange(): return lax.all_to_all(a, axis, split_axis=0, concat_axis=0, tiled=True)  90.9 us
    all_to_all x5, blocking collectives, exchange(): return lax.all_to_all(a, axis, split_axis=0, concat_axis=0, tiled=True)  60.5 us
    all_to_all x9, starting transfers between devices, exchange(): return lax.all_to_all(a, axis, split_axis=0, concat_axis=0, tiled=True)  41 us
    unnamed x55, local copies, waits for them, and re-layouts  29.8 us
    pallas_call x2, Pallas kernels, expert_rows(): pl.pallas_call(functools.partial(expert_kernel, ksteps, nsteps), grid=(ks...  23.7 us
    pallas_call x1, Pallas kernels, inside_blocks(): pl.pallas_call(functools.partial(inside_kernel, group), grid=(heads // gr...  11.1 us
    all_gather x1, blocking collectives, local(): all_ids = lax.all_gather(ids, 'exp', axis=0)  10.5 us
    reduce_sum x4, other arithmetic, total(): return jnp.sum(parts.astype(F32), axis=0).astype(BF16)  7.81 us
  transfers between devices with their start and end apart: 13, of which 8 were waited for; matrix products, arithmetic and copies ran while one was open for 9% of the time, Pallas kernels for 11%

profile of v1, /device:TPU:0, one launch (start us, length us, event | category | flops | bytes accessed | tf_op | source)
XLA Modules:
  0.0 303.5 jit_solution(12500791286256495001)
XLA Ops:
  10.0 8.5 %all-to-all-start = ((bf16[32,64,128]{2,1,0:T(8,128)(2,1)}), bf16[32,64,128]{2,1,0:T(8,128)(2,1)}, u32[]{:S(2)}, u32[]{:S(2)}) async-start(bf16[32,64,128]{2,1,0:T(8,128)(2,1)} %copy-done.11), calls=%async_computation | async-start | bytes 1048576 | tf_op jit(solution)/shard_map/all_to_all | solution.py:484
  18.5 11.7 %all-to-all-done.in_ref = bf16[32,64,128]{2,1,0:T(8,128)(2,1)} async-done(((bf16[32,64,128]{2,1,0:T(8,128)(2,1)}), bf16[32,64,128]{2,1,0:T(8,128)(2,1)}, u32[]{:S(2)}, u32[]{:S(2)}) %all-to-all-start) | async-done | bytes 524320 | tf_op jit(solution)/shard_map/all_to_all | solution.py:484
  38.7 7.7 %all-to-all-done.1 = bf16[32,48,128]{2,1,0:T(8,128)(2,1)S(1)} async-done(((bf16[32,48,128]{2,1,0:T(8,128)(2,1)}), bf16[32,48,128]{2,1,0:T(8,128)(2,1)S(1)}, u32[]{:S(2)}, u32[]{:S(2)}) %all-to-all-start.1) | async-done | bytes 393248 | tf_op jit(solution)/shard_map/all_to_all | solution.py:484
  47.1 4.5 %all-to-all-start.4 = ((bf16[4,8,6144]{2,1,0:T(8,128)(2,1)}), bf16[4,8,6144]{2,1,0:T(8,128)(2,1)S(1)}, u32[]{:S(2)}, u32[]{:S(2)}) async-start(bf16[4,8,6144]{2,1,0:T(8,128)(2,1)} %copy-done.12), calls=%async_computation.4 | async-start | bytes 786432 | tf_op jit(solution)/shard_map/all_to_all | solution.py:484
  51.6 10.5 %all-gather.1.ids_ref = s32[4,2,128]{2,1,0:T(2,128)S(1)} all-gather(s32[1,2,128]{2,1,0:T(2,128)S(1)} %bitcast.16), channel_id=2, replica_groups=mesh['z'=4,'x'=4,'core'=2,'exp'=4] {'exp'}, dimensions={0}, use_global_device_ids=true | all-gather | bytes 5120 | tf_op jit(solution)/shard_map/all_gather | solution.py:516
  66.8 11.1 %inside_blocks.1 = (f32[512,1536]{1,0:T(8,128)}, bf16[512,1536]{1,0:T(8,128)(2,1)S(1)}) custom-call(bf16[512,1536]{1,0:T(8,128)(2,1)S(1)} %copy-done.18, bf16[512,1536]{1,0:T(8,128)(2,1)S(1)} %copy-done.8, bf16[512,1536]{1,0:T(8,128)(2,1)} %v_ref.3, f32[512,12]{1,0:T(8,128)S(1)} %copy-done.20, f32[12,512]{1,0:T(8,128)S(1)} %copy-done.22), custom_call_target="tpu_custom_call" | custom-call | flops 1610612736 | bytes 9437184 | tf_op jit(solution)/shard_map/inside_blocks/pallas_call | solution.py:162
  77.9 4.7 %carried_blocks.1 = (bf16[512,1536]{1,0:T(8,128)(2,1)S(1)}, bf16[64,1536]{1,0:T(8,128)(2,1)S(1)}) custom-call(f32[512,1536]{1,0:T(8,128)} %get-tuple-element.19.inside_ref, bf16[512,1536]{1,0:T(8,128)(2,1)S(1)} %get-tuple-element.20.qs_ref, bf16[12,128,128]{2,1,0:T(8,128)(2,1)S(1)} %bitcast.10, bf16[64,512]{1,0:T(8,128)(2,1)S(1)} %place_rows.1.place_ref), custom_call_target="tpu_custom_call" | custom-call | flops 402653184 | bytes 6291456 | tf_op jit(solution)/shard_map/carried_blocks/pallas_call | solution.py:201
  84.4 9.7 %all_to_all.70.att_ref = bf16[4,16,1536]{2,1,0:T(8,128)(2,1)S(1)} all-to-all(bf16[4,16,1536]{2,1,0:T(8,128)(2,1)} %bitcast.11), channel_id=1, replica_groups=mesh['z'=4,'x'=4,'core'=2,'exp'=4] {'exp'}, dimensions={0} | all-to-all | bytes 393216 | tf_op jit(solution)/shard_map/all_to_all | solution.py:484
  96.0 10.0 %all_to_all.71 = bf16[4,16,3072]{2,1,0:T(8,128)(2,1)S(1)} all-to-all(bf16[4,16,3072]{2,1,0:T(8,128)(2,1)S(1)} %get-tuple-element.26), channel_id=1, replica_groups=mesh['z'=4,'x'=4,'core'=2,'exp'=4] {'x'}, dimensions={0} | all-to-all | bytes 786432 | tf_op jit(solution)/shard_map/all_to_all | solution.py:484
  106.0 9.8 %all_to_all.72 = bf16[4,16,3072]{2,1,0:T(8,128)(2,1)S(1)} all-to-all(bf16[4,16,3072]{2,1,0:T(8,128)(2,1)S(1)} %get-tuple-element.27), channel_id=1, replica_groups=mesh['z'=4,'x'=4,'core'=2,'exp'=4] {'z'}, dimensions={0} | all-to-all | bytes 786432 | tf_op jit(solution)/shard_map/all_to_all | solution.py:484
  115.9 19.6 %all_to_all.73.one_ref = bf16[4,4,16,3072]{3,2,1,0:T(8,128)(2,1)} all-to-all(bf16[4,4,16,3072]{3,2,1,0:T(8,128)(2,1)S(1)} %broadcast_in_dim.4), channel_id=1, replica_groups=mesh['z'=4,'x'=4,'core'=2,'exp'=4] {'z'}, dimensions={0} | all-to-all | bytes 3145728 | tf_op jit(solution)/shard_map/all_to_all | solution.py:484
  141.3 15.4 %all-to-all-done.8.two_ref = bf16[4,4,16,3072]{3,2,1,0:T(8,128)(2,1)} async-done(((bf16[4,4,16,3072]{3,2,1,0:T(8,128)(2,1)}), bf16[4,4,16,3072]{3,2,1,0:T(8,128)(2,1)}, u32[]{:S(2)}, u32[]{:S(2)}) %all-to-all-start.8) | async-done | bytes 1572896 | tf_op jit(solution)/shard_map/all_to_all | solution.py:484
  156.7 6.3 %copy.30.wg_ref = bf16[1,6144,288]{2,1,0:T(8,128)(2,1)} copy(bf16[1,6144,288]{1,2,0:T(8,128)(2,1)} %param.23) | data formatting | bytes 7077888 | tf_op args[10]
  162.9 6.3 %copy.31.wu_ref = bf16[1,6144,288]{2,1,0:T(8,128)(2,1)} copy(bf16[1,6144,288]{1,2,0:T(8,128)(2,1)} %param.24) | data formatting | bytes 7077888 | tf_op args[11]
  169.2 12.3 %expert_rows.3 = (bf16[4,4,16,3072]{3,2,1,0:T(8,128)(2,1)}, bf16[4,4,16,3072]{3,2,1,0:T(8,128)(2,1)S(1)}) custom-call(bf16[4,4,16,3072]{3,2,1,0:T(8,128)(2,1)} %collective-permute-done.one_ref, bf16[4,4,16,3072]{3,2,1,0:T(8,128)(2,1)} %collective-permute-done.1.two_ref, bf16[1,6144,288]{2,1,0:T(8,128)(2,1)} %copy.30.wg_ref, ...), custom_call_target="tpu_custom_call" | custom-call | flops 2717908992 | bytes 16908288 | tf_op jit(solution)/shard_map/expert_rows/pallas_call | solution.py:421
  182.1 11.3 %expert_rows.2 = (bf16[4,4,16,3072]{3,2,1,0:T(8,128)(2,1)S(1)}, bf16[4,4,16,3072]{3,2,1,0:T(8,128)(2,1)S(1)}) custom-call(bf16[4,4,16,3072]{3,2,1,0:T(8,128)(2,1)S(1)} %copy-done.2, bf16[4,4,16,3072]{3,2,1,0:T(8,128)(2,1)} %all-to-all-done.8.two_ref, bf16[1,6144,288]{2,1,0:T(8,128)(2,1)} %copy.30.wg_ref, bf16[1,6144,288]{2,1,0:T(8,128)(2,1)} %copy.31.wu_ref, ...), custom_call_target="tpu_custom_call" | custom-call | flops 2717908992 | bytes 16908288 | tf_op jit(solution)/shard_map/expert_rows/pallas_call | solution.py:421
  204.3 18.1 %all-to-all-done.11 = bf16[4,4,16,3072]{3,2,1,0:T(8,128)(2,1)} async-done(((bf16[4,4,16,3072]{3,2,1,0:T(8,128)(2,1)}), bf16[4,4,16,3072]{3,2,1,0:T(8,128)(2,1)}, u32[]{:S(2)}, u32[]{:S(2)}) %all-to-all-start.11) | async-done | bytes 1572896 | tf_op jit(solution)/shard_map/all_to_all | solution.py:484
  222.3 4.3 %all-to-all-start.9 = ((bf16[4,4,16,3072]{3,2,1,0:T(8,128)(2,1)}), bf16[4,4,16,3072]{3,2,1,0:T(8,128)(2,1)}, u32[]{:S(2)}, u32[]{:S(2)}) async-start(bf16[4,4,16,3072]{3,2,1,0:T(8,128)(2,1)} %add_convert_fusion.1), calls=%async_computation.9 | async-start | bytes 3145728 | tf_op jit(solution)/shard_map/all_to_all | solution.py:484
  229.2 18.4 %all-to-all-done.9 = bf16[4,4,16,3072]{3,2,1,0:T(8,128)(2,1)} async-done(((bf16[4,4,16,3072]{3,2,1,0:T(8,128)(2,1)}), bf16[4,4,16,3072]{3,2,1,0:T(8,128)(2,1)}, u32[]{:S(2)}, u32[]{:S(2)}) %all-to-all-start.9) | async-done | bytes 1572896 | tf_op jit(solution)/shard_map/all_to_all | solution.py:484
  253.6 4.8 %all-to-all-done.12 = bf16[4,16,3072]{2,1,0:T(8,128)(2,1)S(1)} async-done(((bf16[4,16,3072]{2,1,0:T(8,128)(2,1)}), bf16[4,16,3072]{2,1,0:T(8,128)(2,1)S(1)}, u32[]{:S(2)}, u32[]{:S(2)}) %all-to-all-start.12) | async-done | bytes 393248 | tf_op jit(solution)/shard_map/all_to_all | solution.py:484
  258.4 11.6 %all_to_all.74 = bf16[4,16,3072]{2,1,0:T(8,128)(2,1)} all-to-all(bf16[4,16,3072]{2,1,0:T(8,128)(2,1)} %reduce_sum.48), channel_id=1, replica_groups=mesh['z'=4,'x'=4,'core'=2,'exp'=4] {'x'}, dimensions={0} | all-to-all | bytes 786432 | tf_op jit(solution)/shard_map/all_to_all | solution.py:484
  270.0 4.3 %all-to-all-start.2 = ((bf16[4,128,1536]{2,1,0:T(8,128)(2,1)}), bf16[4,128,1536]{2,1,0:T(8,128)(2,1)}, u32[]{:S(2)}, u32[]{:S(2)}) async-start(bf16[4,128,1536]{2,1,0:T(8,128)(2,1)} %bitcast.9), calls=%async_computation.2 | async-start | bytes 3145728 | tf_op jit(solution)/shard_map/all_to_all | solution.py:484
  278.8 13.3 %all-to-all-done.2.att_ref = bf16[4,128,1536]{2,1,0:T(8,128)(2,1)} async-done(((bf16[4,128,1536]{2,1,0:T(8,128)(2,1)}), bf16[4,128,1536]{2,1,0:T(8,128)(2,1)}, u32[]{:S(2)}, u32[]{:S(2)}) %all-to-all-start.2) | async-done | bytes 1572896 | tf_op jit(solution)/shard_map/all_to_all | solution.py:484
  295.7 4.5 %hidden_rows.1 = bf16[128,6144]{1,0:T(8,128)(2,1)} custom-call(bf16[4,128,1536]{2,1,0:T(8,128)(2,1)} %all-to-all-done.2.att_ref, bf16[128,6144]{1,0:T(8,128)(2,1)S(1)} %copy-done, bf16[128,6144]{1,0:T(8,128)(2,1)S(1)} %copy-done.1, f32[1,6144]{1,0:T(1,128)S(1)} %bitcast.13), custom_call_target="tpu_custom_call" | custom-call | flops 15728640 | bytes 6291456 | tf_op jit(solution)/shard_map/hidden_rows/pallas_call | solution.py:341
  (84 shorter events, 64.0 us)
Async XLA Ops:
  1.5 1.4 copy-start.7
  4.3 31.7 %copy-start.1 = (bf16[128,6144]{1,0:T(8,128)(2,1)S(1)}, bf16[128,6144]{1,0:T(8,128)(2,1)}, u32[]{:S(2)}) copy-start(bf16[128,6144]{1,0:T(8,128)(2,1)} %gate_ref.3) | copy-start | bytes 4718596
  10.0 26.1 %copy-start = (bf16[128,6144]{1,0:T(8,128)(2,1)S(1)}, bf16[128,6144]{1,0:T(8,128)(2,1)}, u32[]{:S(2)}) copy-start(bf16[128,6144]{1,0:T(8,128)(2,1)} %res_ref.3) | copy-start | bytes 4718596
  10.0 26.1 %copy-start.17 = (s32[128,2]{0,1:T(2,128)S(1)}, s32[128,2]{0,1:T(2,128)}, u32[]{:S(2)}) copy-start(s32[128,2]{0,1:T(2,128)} %param.21) | copy-start | bytes 3076
  10.0 20.3 %all-to-all-start = ((bf16[32,64,128]{2,1,0:T(8,128)(2,1)}), bf16[32,64,128]{2,1,0:T(8,128)(2,1)}, u32[]{:S(2)}, u32[]{:S(2)}) async-start(bf16[32,64,128]{2,1,0:T(8,128)(2,1)} %copy-done.11), calls=%async_computation | async-start | bytes 1048576 | tf_op jit(solution)/shard_map/all_to_all | solution.py:484
  32.2 14.2 %all-to-all-start.1 = ((bf16[32,48,128]{2,1,0:T(8,128)(2,1)}), bf16[32,48,128]{2,1,0:T(8,128)(2,1)S(1)}, u32[]{:S(2)}, u32[]{:S(2)}) async-start(bf16[32,48,128]{2,1,0:T(8,128)(2,1)} %copy-done.6), calls=%async_computation.1 | async-start | bytes 786432 | tf_op jit(solution)/shard_map/all_to_all | solution.py:484
  47.1 37.3 %all-to-all-start.4 = ((bf16[4,8,6144]{2,1,0:T(8,128)(2,1)}), bf16[4,8,6144]{2,1,0:T(8,128)(2,1)S(1)}, u32[]{:S(2)}, u32[]{:S(2)}) async-start(bf16[4,8,6144]{2,1,0:T(8,128)(2,1)} %copy-done.12), calls=%async_computation.4 | async-start | bytes 786432 | tf_op jit(solution)/shard_map/all_to_all | solution.py:484
  62.3 1.4 copy-start.8
  63.7 1.4 copy-start.18
  66.8 11.1 %copy-start.5 = (bf16[32,48,128]{2,1,0:T(8,128)(2,1)S(1)}, bf16[32,48,128]{2,1,0:T(8,128)(2,1)}, u32[]{:S(2)}) copy-start(bf16[32,48,128]{2,1,0:T(8,128)(2,1)} %copy-done.4) | copy-start | bytes 1179652
  136.8 19.9 %all-to-all-start.8 = ((bf16[4,4,16,3072]{3,2,1,0:T(8,128)(2,1)}), bf16[4,4,16,3072]{3,2,1,0:T(8,128)(2,1)}, u32[]{:S(2)}, u32[]{:S(2)}) async-start(bf16[4,4,16,3072]{3,2,1,0:T(8,128)(2,1)} %broadcast_in_dim.5), calls=%async_computation.8 | async-start | bytes 3145728 | tf_op jit(solution)/shard_map/all_to_all | solution.py:484
  141.2 28.0 %collective-permute-start = (bf16[4,4,16,3072]{3,2,1,0:T(8,128)(2,1)}, bf16[4,4,16,3072]{3,2,1,0:T(8,128)(2,1)}, u32[]{:S(2)}, u32[]{:S(2)}) collective-permute-start(bf16[4,4,16,3072]{3,2,1,0:T(8,128)(2,1)} %all_to_all.73.one_ref), channel_id=1, source_target_pairs={{0,4},{4,0},{1,5},{5,1},{2,6},{6,2},{3,7},{7,3},{8,12},{12,8},{9,1... | collective-permute-start | bytes 4718600 | tf_op jit(solution)/shard_map/ppermute | solution.py:480
  156.7 12.5 %collective-permute-start.1 = (bf16[4,4,16,3072]{3,2,1,0:T(8,128)(2,1)}, bf16[4,4,16,3072]{3,2,1,0:T(8,128)(2,1)}, u32[]{:S(2)}, u32[]{:S(2)}) collective-permute-start(bf16[4,4,16,3072]{3,2,1,0:T(8,128)(2,1)} %all-to-all-done.8.two_ref), channel_id=1, source_target_pairs={{0,4},{4,0},{1,5},{5,1},{2,6},{6,2},{3,7},{7,3},{8,12},{12,8},{9,1... | collective-permute-start | bytes 4718600 | tf_op jit(solution)/shard_map/ppermute | solution.py:480
  169.2 12.9 %copy-start.2 = (bf16[4,4,16,3072]{3,2,1,0:T(8,128)(2,1)S(1)}, bf16[4,4,16,3072]{3,2,1,0:T(8,128)(2,1)}, u32[]{:S(2)}) copy-start(bf16[4,4,16,3072]{3,2,1,0:T(8,128)(2,1)} %all_to_all.73.one_ref) | copy-start | bytes 4718596
  181.5 13.0 %collective-permute-start.3 = (bf16[4,4,16,3072]{3,2,1,0:T(8,128)(2,1)S(1)}, bf16[4,4,16,3072]{3,2,1,0:T(8,128)(2,1)S(1)}, u32[]{:S(2)}, u32[]{:S(2)}) collective-permute-start(bf16[4,4,16,3072]{3,2,1,0:T(8,128)(2,1)S(1)} %get-tuple-element.31), channel_id=1, source_target_pairs={{0,4},{4,0},{1,5},{5,1},{2,6},{6,2},{3,7},{7,3},{8,12},{12,8},{9,1... | collective-permute-start | bytes 4718600 | tf_op jit(solution)/shard_map/ppermute | solution.py:480
  182.0 18.6 %collective-permute-start.2 = (bf16[4,4,16,3072]{3,2,1,0:T(8,128)(2,1)}, bf16[4,4,16,3072]{3,2,1,0:T(8,128)(2,1)}, u32[]{:S(2)}, u32[]{:S(2)}) collective-permute-start(bf16[4,4,16,3072]{3,2,1,0:T(8,128)(2,1)} %get-tuple-element.29), channel_id=1, source_target_pairs={{0,4},{4,0},{1,5},{5,1},{2,6},{6,2},{3,7},{7,3},{8,12},{12,8},{9,1... | collective-permute-start | bytes 4718600 | tf_op jit(solution)/shard_map/ppermute | solution.py:480
  196.3 26.0 %all-to-all-start.11 = ((bf16[4,4,16,3072]{3,2,1,0:T(8,128)(2,1)}), bf16[4,4,16,3072]{3,2,1,0:T(8,128)(2,1)}, u32[]{:S(2)}, u32[]{:S(2)}) async-start(bf16[4,4,16,3072]{3,2,1,0:T(8,128)(2,1)} %add_convert_fusion), calls=%async_computation.11 | async-start | bytes 3145728 | tf_op jit(solution)/shard_map/all_to_all | solution.py:484
  222.3 25.3 %all-to-all-start.9 = ((bf16[4,4,16,3072]{3,2,1,0:T(8,128)(2,1)}), bf16[4,4,16,3072]{3,2,1,0:T(8,128)(2,1)}, u32[]{:S(2)}, u32[]{:S(2)}) async-start(bf16[4,4,16,3072]{3,2,1,0:T(8,128)(2,1)} %add_convert_fusion.1), calls=%async_computation.9 | async-start | bytes 3145728 | tf_op jit(solution)/shard_map/all_to_all | solution.py:484
  247.6 10.8 %all-to-all-start.12 = ((bf16[4,16,3072]{2,1,0:T(8,128)(2,1)}), bf16[4,16,3072]{2,1,0:T(8,128)(2,1)S(1)}, u32[]{:S(2)}, u32[]{:S(2)}) async-start(bf16[4,16,3072]{2,1,0:T(8,128)(2,1)} %reduce_sum.50), calls=%async_computation.12 | async-start | bytes 786432 | tf_op jit(solution)/shard_map/all_to_all | solution.py:484
  258.4 11.6 %copy-start.23 = (bf16[4,16,3072]{2,1,0:T(8,128)(2,1)}, bf16[4,16,3072]{2,1,0:T(8,128)(2,1)S(1)}, u32[]{:S(2)}) copy-start(bf16[4,16,3072]{2,1,0:T(8,128)(2,1)S(1)} %all-to-all-done.12) | copy-start | bytes 1179652
  270.0 22.1 %all-to-all-start.2 = ((bf16[4,128,1536]{2,1,0:T(8,128)(2,1)}), bf16[4,128,1536]{2,1,0:T(8,128)(2,1)}, u32[]{:S(2)}, u32[]{:S(2)}) async-start(bf16[4,128,1536]{2,1,0:T(8,128)(2,1)} %bitcast.9), calls=%async_computation.2 | async-start | bytes 3145728 | tf_op jit(solution)/shard_map/all_to_all | solution.py:484
  274.3 21.2 %copy-start.24 = (f32[128,2]{0,1:T(2,128)S(1)}, f32[128,2]{0,1:T(2,128)}, u32[]{:S(2)}) copy-start(f32[128,2]{0,1:T(2,128)} %param.22) | copy-start | bytes 3076
  274.3 21.3 %copy-start.15 = (f32[6144]{0:T(1024)S(1)}, f32[6144]{0:T(1024)}, u32[]{:S(2)}) copy-start(f32[6144]{0:T(1024)} %param.19) | copy-start | bytes 73732
  292.1 9.7 %all-to-all-start.13 = ((bf16[4,4,6144]{2,1,0:T(4,128)(2,1)}), bf16[4,4,6144]{2,1,0:T(4,128)(2,1)S(1)}, u32[]{:S(2)}, u32[]{:S(2)}) async-start(bf16[4,4,6144]{2,1,0:T(4,128)(2,1)} %reshape.33), calls=%async_computation.13 | async-start | bytes 393216 | tf_op jit(solution)/shard_map/all_to_all | solution.py:484
  (14 other events, 11.9 us)

commit v2 on v1

v2 whole, which is shorter than its diff:
```python
import functools

import jax
import jax.numpy as jnp
from jax import lax
from jax.experimental import pallas as pl
from jax.experimental.pallas import tpu as pltpu
from jax.sharding import Mesh, PartitionSpec as P

HEAD_DIM = 128
CAP = 4
EPS = 1e-05
F32 = jnp.float32
BF16 = jnp.bfloat16
HIGHEST = lax.Precision.HIGHEST
CTX = ("z", "x", "core")
VMEM_LIMIT = 60 * 1024 * 1024


def iota(shape, dim):
    return lax.broadcasted_iota(jnp.int32, shape, dim)


def params(**kw):
    return pltpu.CompilerParams(vmem_limit_bytes=VMEM_LIMIT, **kw)


def cost(flops, bytes_accessed):
    return pl.CostEstimate(flops=flops, bytes_accessed=bytes_accessed, transcendentals=0)


def running_sum(ld, axis):
    rows = ld.shape[1]
    a, b = iota((rows, rows), 0), iota((rows, rows), 1)
    ones = (a >= b).astype(BF16)
    total = None
    rest = ld
    for _ in range(3):
        part = rest.astype(BF16)
        rest = rest - part.astype(F32)
        pair = (ones, part) if axis == 0 else (part, ones)
        term = lax.dot_general(*pair, (((1,), (1,)), ((), ())), preferred_element_type=F32)
        total = term if total is None else total + term
    return total


def column(table, h):
    lane = iota(table.shape, 1)
    return jnp.sum(jnp.where(lane == h, table, 0.0), axis=1, keepdims=True)


def state_kernel(group, k_ref, v_ref, ld_ref, cum_ref, msg_ref, fade_ref, decay_ref):
    heads, rows = ld_ref.shape
    per = heads * HEAD_DIM // 32
    parts = group * HEAD_DIM // per
    g = pl.program_id(0)

    @pl.when(g == 0)
    def _():
        cum = running_sum(ld_ref[...], 0)
        cum_ref[...] = cum
        final = cum[rows - 1 : rows, :]
        fade_ref[...] = jnp.exp(final - cum)
        decay_ref[...] = jnp.broadcast_to(jnp.exp(final), decay_ref.shape)

    fade = fade_ref[...]
    decay = decay_ref[...]
    row16 = iota((16, HEAD_DIM), 0)
    tiles = []
    for j in range(group):
        h = g * group + j
        cols = slice(j * HEAD_DIM, (j + 1) * HEAD_DIM)
        wk = (k_ref[:, cols].astype(F32) * column(fade, h)).astype(BF16)
        state = lax.dot_general(
            wk, v_ref[:, cols], (((0,), (0,)), ((), ())), preferred_element_type=F32
        ).astype(BF16)
        row = j * HEAD_DIM
        while row < (j + 1) * HEAD_DIM:
            part, at = row // per, row % per
            take = min(per - at, (j + 1) * HEAD_DIM - row)
            lo = row - j * HEAD_DIM
            msg_ref[part, at : at + take, :] = state[lo : lo + take, :]
            row += take
        whole = jnp.broadcast_to(column(decay, h), (16, HEAD_DIM))
        high = whole.astype(BF16).astype(F32)
        tiles.append((high, whole - high))
    for part in range(parts):
        first = per * part // HEAD_DIM
        last = (per * part + per - 1) // HEAD_DIM
        tile = jnp.where(
            row16 == 0,
            tiles[first][0],
            jnp.where(
                row16 == 1, tiles[first][1], jnp.where(row16 == 2, tiles[last][0], tiles[last][1])
            ),
        )
        msg_ref[part, per : per + 16, :] = tile.astype(BF16)


def local_states(k, v, ld, group=3):
    rows, width = k.shape
    heads = ld.shape[0]
    per = heads * HEAD_DIM // 32
    parts = group * HEAD_DIM // per
    block = pl.BlockSpec((rows, group * HEAD_DIM), lambda g: (0, g))
    return pl.pallas_call(
        functools.partial(state_kernel, group),
        grid=(heads // group,),
        out_shape=(
            jax.ShapeDtypeStruct((rows, heads), F32),
            jax.ShapeDtypeStruct((32, per + 16, HEAD_DIM), BF16),
        ),
        in_specs=[block, block, pl.BlockSpec((heads, rows), lambda g: (0, 0))],
        out_specs=(
            pl.BlockSpec((rows, heads), lambda g: (0, 0)),
            pl.BlockSpec((parts, per + 16, HEAD_DIM), lambda g: (g, 0, 0)),
        ),
        scratch_shapes=[pltpu.VMEM((rows, heads), F32), pltpu.VMEM((16, heads), F32)],
        compiler_params=params(),
        cost_estimate=cost(2 * rows * width * HEAD_DIM, 4 * rows * width),
        name="local_states",
    )(k, v, ld)


def scan_kernel(split_ref, in_ref, out_ref):
    parts, per, width = out_ref.shape
    first_rows = iota((per, width), 0) < split_ref[0]
    state = jnp.zeros((per, width), F32)
    for b in range(parts):
        out_ref[b, :, :] = state.astype(BF16)
        if b + 1 < parts:
            tail = in_ref[b, per : per + 16, :].astype(F32)
            d0 = tail[0:1, :] + tail[1:2, :]
            d1 = tail[2:3, :] + tail[3:4, :]
            decay = jnp.where(first_rows, d0, d1)
            state = decay * state + in_ref[b, 0:per, :].astype(F32)


def scan_blocks(msg, part):
    parts, tall, width = msg.shape
    per = tall - 16
    split = (HEAD_DIM - (per * part) % HEAD_DIM).astype(jnp.int32).reshape(1)
    return pl.pallas_call(
        scan_kernel,
        out_shape=jax.ShapeDtypeStruct((parts, per, width), BF16),
        in_specs=[
            pl.BlockSpec(memory_space=pltpu.SMEM),
            pl.BlockSpec(memory_space=pltpu.VMEM),
        ],
        out_specs=pl.BlockSpec(memory_space=pltpu.VMEM),
        compiler_params=params(),
        cost_estimate=cost(1000000, 1000000),
        name="scan_blocks",
    )(split, msg)


def inside_kernel(group, q_ref, k_ref, v_ref, cum_ref, ld_ref, inside_ref, qs_ref, cumt_ref):
    rows, heads = cum_ref.shape

    @pl.when(pl.program_id(0) == 0)
    def _():
        cumt_ref[...] = running_sum(ld_ref[...], 1)

    cum = cum_ref[...]
    causal = iota((HEAD_DIM, HEAD_DIM), 0) >= iota((HEAD_DIM, HEAD_DIM), 1)
    for j in range(group):
        h = pl.program_id(0) * group + j
        cols = slice(j * HEAD_DIM, (j + 1) * HEAD_DIM)
        col = column(cum, h)
        row = cumt_ref[pl.ds(h, 1), :]
        q = q_ref[:, cols]
        k = k_ref[:, cols]
        v = v_ref[:, cols]
        qs_ref[:, cols] = (q.astype(F32) * jnp.exp(col)).astype(BF16)
        for i in range(rows // HEAD_DIM):
            lo, hi = i * HEAD_DIM, (i + 1) * HEAD_DIM
            qi = q[lo:hi]
            ci = col[lo:hi]
            s = lax.dot_general(
                qi, k[lo:hi], (((1,), (1,)), ((), ())), preferred_element_type=F32
            )
            gap = jnp.minimum(ci - row[:, lo:hi], 0.0)
            w = jnp.where(causal, s * jnp.exp(gap), 0.0).astype(BF16)
            total = jnp.dot(w, v[lo:hi], preferred_element_type=F32)
            if i:
                s = lax.dot_general(
                    qi, k[:lo], (((1,), (1,)), ((), ())), preferred_element_type=F32
                )
                w = (s * jnp.exp(jnp.minimum(ci - row[:, :lo], 0.0))).astype(BF16)
                total = total + jnp.dot(w, v[:lo], preferred_element_type=F32)
            inside_ref[lo:hi, cols] = total


def inside_blocks(q, k, v, cum, ld, group=3):
    rows, width = q.shape
    heads = cum.shape[1]
    block = pl.BlockSpec((rows, group * HEAD_DIM), lambda g: (0, g))
    return pl.pallas_call(
        functools.partial(inside_kernel, group),
        grid=(heads // group,),
        out_shape=(
            jax.ShapeDtypeStruct((rows, width), F32),
            jax.ShapeDtypeStruct((rows, width), BF16),
        ),
        in_specs=[
            block,
            block,
            block,
            pl.BlockSpec((rows, heads), lambda g: (0, 0)),
            pl.BlockSpec((heads, rows), lambda g: (0, 0)),
        ],
        out_specs=(block, block),
        scratch_shapes=[pltpu.VMEM((heads, rows), F32)],
        compiler_params=params(),
        cost_estimate=cost(4 * rows * rows * width, 12 * rows * width),
        name="inside_blocks",
    )(q, k, v, cum, ld)


def carried_kernel(group, inside_ref, qs_ref, state_ref, place_ref, att_ref, sel_ref):
    for j in range(group):
        cols = slice(j * HEAD_DIM, (j + 1) * HEAD_DIM)
        att = (
            inside_ref[:, cols]
            + jnp.dot(qs_ref[:, cols], state_ref[j], preferred_element_type=F32)
        ).astype(BF16)
        att_ref[:, cols] = att
        sel_ref[:, cols] = jnp.dot(
            place_ref[...], att, preferred_element_type=F32
        ).astype(BF16)


def carried_blocks(inside, qs, state, place, group=3):
    rows, width = inside.shape
    heads = width // HEAD_DIM
    chosen = place.shape[0]
    block = pl.BlockSpec((rows, group * HEAD_DIM), lambda g: (0, g))
    return pl.pallas_call(
        functools.partial(carried_kernel, group),
        grid=(heads // group,),
        out_shape=(
            jax.ShapeDtypeStruct((rows, width), BF16),
            jax.ShapeDtypeStruct((chosen, width), BF16),
        ),
        in_specs=[
            block,
            block,
            pl.BlockSpec((group, HEAD_DIM, HEAD_DIM), lambda g: (g, 0, 0)),
            pl.BlockSpec((chosen, rows), lambda g: (0, 0)),
        ],
        out_specs=(block, pl.BlockSpec((chosen, group * HEAD_DIM), lambda g: (0, g))),
        compiler_params=params(),
        cost_estimate=cost(4 * rows * width * HEAD_DIM, 8 * rows * width),
        name="carried_blocks",
    )(inside, qs, state, place)


def route_kernel(me_ref, ids_ref, res_ref, gate_ref, *refs):
    outs, place_ref = refs[:-1], refs[-1]
    held = len(outs)
    tokens, width = res_ref.shape
    me = me_ref[0]
    ids = ids_ref[...]
    hits = [
        ((ids[0:1, :] == e) | (ids[1:2, :] == e)).astype(F32) for e in range(held)
    ]
    m = jnp.concatenate(hits, axis=0)
    upto = (iota((tokens, tokens), 0) <= iota((tokens, tokens), 1)).astype(BF16)
    rank = jnp.dot(m.astype(BF16), upto, preferred_element_type=F32) - 1.0
    slot = iota((CAP, tokens), 0).astype(F32)
    places = [
        jnp.where(rank[e : e + 1, :] == slot, m[e : e + 1, :], 0.0) for e in range(held)
    ]
    place = jnp.concatenate(places, axis=0)
    place_ref[...] = place
    for d in range(held):
        expert = lax.rem(me + d, held)
        mine = places[0]
        for e in range(1, held):
            mine = jnp.where(expert == e, places[e], mine)
        mine = mine.astype(BF16)
        outs[d][0:CAP, 0:width] = jnp.dot(
            mine, res_ref[...], preferred_element_type=F32
        ).astype(BF16)
        outs[d][CAP : 2 * CAP, 0:width] = jnp.dot(
            mine, gate_ref[...], preferred_element_type=F32
        ).astype(BF16)
        for n in range(2):
            outs[d][:, width + n * tokens : width + (n + 1) * tokens] = jnp.broadcast_to(
                ids[n : n + 1, :].astype(F32), (2 * CAP, tokens)
            ).astype(BF16)


def route_rows(me, ids, residual, out_gate, held):
    tokens, width = residual.shape
    whole = pl.BlockSpec(memory_space=pltpu.VMEM)
    piece = jax.ShapeDtypeStruct((2 * CAP, width + 2 * tokens), BF16)
    outs = pl.pallas_call(
        route_kernel,
        out_shape=(piece,) * held + (jax.ShapeDtypeStruct((held * CAP, tokens), F32),),
        in_specs=[pl.BlockSpec(memory_space=pltpu.SMEM), whole, whole, whole],
        out_specs=(whole,) * (held + 1),
        compiler_params=params(),
        cost_estimate=cost(64 * tokens * width, 5 * tokens * width),
        name="route_rows",
    )(me, ids, residual, out_gate)
    return outs[:-1], outs[-1]


def by_source(me, pieces, j):
    count = len(pieces)
    out = pieces[0]
    for d in range(1, count):
        out = jnp.where(lax.rem(me + count - d, count) == j, pieces[d], out)
    return out


def place_kernel(me_ref, *refs):
    pieces, place_ref = refs[:-1], refs[-1]
    held = len(pieces)
    tokens = pieces[0].shape[1] // 2
    total = held * tokens
    me = me_ref[0]
    tables = [p[...].astype(F32) for p in pieces]
    ordered = [by_source(me, tables, j) for j in range(held)]
    first = jnp.concatenate([a[0:1, :tokens] for a in ordered], axis=1)
    second = jnp.concatenate([a[0:1, tokens:] for a in ordered], axis=1)
    m = jnp.concatenate(
        [((first == float(e)) | (second == float(e))).astype(F32) for e in range(held)], axis=0
    )
    before = iota((total, total), 0)
    after = iota((total, total), 1)
    upto = ((before <= after) & (before // tokens == after // tokens)).astype(BF16)
    rank = jnp.dot(m.astype(BF16), upto, preferred_element_type=F32) - 1.0
    rows = held * CAP
    r = iota((rows, total), 0)
    t = iota((rows, total), 1)
    chunk = r // (rows // 2)
    inner = r % (rows // 2)
    source = inner // (CAP // 2)
    slot = (chunk * (CAP // 2) + inner % (CAP // 2)).astype(F32)
    here = (t // tokens == source).astype(F32)
    for e in range(held):
        hit = jnp.where(rank[e : e + 1, :] == slot, m[e : e + 1, :] * here, 0.0)
        place_ref[e * rows : (e + 1) * rows, :] = hit.astype(BF16)


def place_rows(me, pieces, tokens):
    held = len(pieces)
    width = pieces[0].shape[1] - 2 * tokens
    at = width // (2 * tokens)
    return pl.pallas_call(
        place_kernel,
        grid=(1,),
        out_shape=jax.ShapeDtypeStruct((held * held * CAP, held * tokens), BF16),
        in_specs=[pl.BlockSpec(memory_space=pltpu.SMEM)]
        + [pl.BlockSpec((2 * CAP, 2 * tokens), lambda i: (0, at))] * held,
        out_specs=pl.BlockSpec((held * held * CAP, held * tokens), lambda i: (0, 0)),
        compiler_params=params(),
        cost_estimate=cost(1000000, 200000),
        name="place_rows",
    )(me, *pieces)


def gated(att, res, gate, attn_gain):
    norm = att * lax.rsqrt(jnp.mean(att * att, axis=-1, keepdims=True) + EPS) * attn_gain
    return (res + norm * jax.nn.sigmoid(gate)).astype(BF16)


def routed_norm_kernel(me_ref, att_ref, ag_ref, mg_ref, *refs):
    pieces, one_ref, two_ref = refs[:-2], refs[-2], refs[-1]
    sources, rows, part = att_ref.shape
    width = sources * part
    me = me_ref[0]
    att = jnp.concatenate([att_ref[s].astype(F32) for s in range(sources)], axis=1)
    tables = [p[...][:, :width].astype(F32) for p in pieces]
    ordered = [by_source(me, tables, j) for j in range(sources)]
    half = CAP // 2
    res = jnp.concatenate(
        [a[c * half : (c + 1) * half] for c in range(2) for a in ordered], axis=0
    )
    gate = jnp.concatenate(
        [a[CAP + c * half : CAP + (c + 1) * half] for c in range(2) for a in ordered], axis=0
    )
    hidden = gated(att, res, gate, ag_ref[...]).astype(F32)
    normed = (
        hidden * lax.rsqrt(jnp.mean(hidden * hidden, axis=-1, keepdims=True) + EPS) * mg_ref[...]
    )
    one_ref[...] = normed[: rows // 2].astype(BF16)
    two_ref[...] = normed[rows // 2 :].astype(BF16)


def routed_norm(me, att, pieces, attn_gain, moe_gain):
    sources, rows, part = att.shape
    width = sources * part
    whole = pl.BlockSpec(memory_space=pltpu.VMEM)
    shape = jax.ShapeDtypeStruct((rows // 2, width), BF16)
    return pl.pallas_call(
        routed_norm_kernel,
        out_shape=(shape, shape),
        in_specs=[pl.BlockSpec(memory_space=pltpu.SMEM)] + [whole] * (3 + len(pieces)),
        out_specs=(whole, whole),
        compiler_params=params(),
        cost_estimate=cost(20 * rows * width, 20 * rows * width),
        name="routed_norm",
    )(me, att, attn_gain, moe_gain, *pieces)


def hidden_kernel(att_ref, res_ref, gate_ref, ag_ref, out_ref):
    sources = att_ref.shape[0]
    att = jnp.concatenate([att_ref[s].astype(F32) for s in range(sources)], axis=1)
    out_ref[...] = gated(att, res_ref[...].astype(F32), gate_ref[...].astype(F32), ag_ref[...])


def hidden_rows(att, residual, out_gate, attn_gain, tile=32):
    sources, rows, part = att.shape
    width = sources * part
    block = pl.BlockSpec((tile, width), lambda i: (i, 0))
    return pl.pallas_call(
        hidden_kernel,
        grid=(rows // tile,),
        out_shape=jax.ShapeDtypeStruct((rows, width), BF16),
        in_specs=[
            pl.BlockSpec((sources, tile, part), lambda i: (0, i, 0)),
            block,
            block,
            pl.BlockSpec((1, width), lambda i: (0, 0)),
        ],
        out_specs=block,
        compiler_params=params(),
        cost_estimate=cost(20 * rows * width, 8 * rows * width),
        name="hidden_rows",
    )(att, residual, out_gate, attn_gain)


def expert_kernel(
    ksteps, core_ref, x_ref, wg_ref, wu_ref, wd_ref, own_ref, other_ref, gate_acc, up_acc, act
):
    step = pl.program_id(0)
    chips, rows, wide = own_ref.shape
    nt = (((1,), (1,)), ((), ()))

    @pl.when(step < ksteps)
    def _():
        x = x_ref[...]
        g = lax.dot_general(wg_ref[0], x, nt, preferred_element_type=F32)
        u = lax.dot_general(wu_ref[0], x, nt, preferred_element_type=F32)

        @pl.when(step == 0)
        def _():
            gate_acc[...] = g
            up_acc[...] = u

        @pl.when(step > 0)
        def _():
            gate_acc[...] += g
            up_acc[...] += u

    @pl.when(step == ksteps - 1)
    def _():
        g = gate_acc[...]
        act[...] = (g * jax.nn.sigmoid(g) * up_acc[...]).T.astype(BF16)

    @pl.when(step >= ksteps)
    def _():
        out = jnp.dot(act[...], wd_ref[0], preferred_element_type=F32)
        out = out.reshape(chips, 2, rows, wide)
        first = core_ref[0] == 0

        @pl.when(first)
        def _():
            own_ref[...] = out[:, 0].astype(BF16)
            other_ref[...] = out[:, 1].astype(BF16)

        @pl.when(jnp.logical_not(first))
        def _():
            own_ref[...] = out[:, 1].astype(BF16)
            other_ref[...] = out[:, 0].astype(BF16)


def expert_rows(core, x, w_gate, w_up, w_down, ksteps=4, nsteps=4):
    count, width = x.shape
    units = w_gate.shape[1]
    depth, wide = width // ksteps, width // nsteps
    rows = count // 32

    def k_at(i):
        return jnp.minimum(i, ksteps - 1)

    def n_at(i):
        return jnp.maximum(i - ksteps, 0)

    return pl.pallas_call(
        functools.partial(expert_kernel, ksteps),
        grid=(ksteps + nsteps,),
        out_shape=(jax.ShapeDtypeStruct((16, rows, width), BF16),) * 2,
        in_specs=[
            pl.BlockSpec(memory_space=pltpu.SMEM),
            pl.BlockSpec((count, depth), lambda i: (0, k_at(i))),
            pl.BlockSpec((1, units, depth), lambda i: (0, 0, k_at(i))),
            pl.BlockSpec((1, units, depth), lambda i: (0, 0, k_at(i))),
            pl.BlockSpec((1, units, wide), lambda i: (0, 0, n_at(i))),
        ],
        out_specs=(pl.BlockSpec((16, rows, wide), lambda i: (0, 0, n_at(i))),) * 2,
        scratch_shapes=[
            pltpu.VMEM((units, count), F32),
            pltpu.VMEM((units, count), F32),
            pltpu.VMEM((count, units), BF16),
        ],
        compiler_params=params(),
        cost_estimate=cost(6 * count * width * units, 6 * width * units + 4 * count * width),
        name="expert_rows",
    )(core, x, w_gate, w_up, w_down)


def pair_kernel(a_ref, b_ref, out_ref):
    out_ref[...] = (a_ref[...].astype(F32) + b_ref[...].astype(F32)).astype(BF16)


def pair_sum(own, other, steps=4):
    chips, rows, width = own.shape
    wide = width // steps
    block = pl.BlockSpec((chips, rows, wide), lambda i: (0, 0, i))
    return pl.pallas_call(
        pair_kernel,
        grid=(steps,),
        out_shape=jax.ShapeDtypeStruct((chips, rows, width), BF16),
        in_specs=[block, block],
        out_specs=block,
        compiler_params=params(),
        cost_estimate=cost(chips * rows * width, 6 * chips * rows * width),
        name="pair_sum",
    )(own, other)


def chip_sum_kernel(one_ref, two_ref, out_ref):
    def total(ref):
        out = ref[0].astype(F32)
        for i in range(1, ref.shape[0]):
            out = out + ref[i].astype(F32)
        return out

    one, two = total(one_ref), total(two_ref)
    half = CAP // 2
    for j in range(out_ref.shape[0]):
        at = slice(j * half, (j + 1) * half)
        out_ref[j] = jnp.concatenate([one[at], two[at]], axis=0).astype(BF16)


def chip_sum(one, two, held, steps=4):
    chips, rows, width = one.shape
    wide = width // steps
    block = pl.BlockSpec((chips, rows, wide), lambda i: (0, 0, i))
    return pl.pallas_call(
        chip_sum_kernel,
        grid=(steps,),
        out_shape=jax.ShapeDtypeStruct((held, CAP, width), BF16),
        in_specs=[block, block],
        out_specs=pl.BlockSpec((held, CAP, wide), lambda i: (0, 0, i)),
        compiler_params=params(),
        cost_estimate=cost(2 * chips * rows * width, 4 * chips * rows * width),
        name="chip_sum",
    )(one, two)


def combine_kernel(place_ref, rows_ref, ids_ref, weights_ref, out_ref):
    held = rows_ref.shape[0]
    rows = jnp.concatenate([rows_ref[e].astype(F32) for e in range(held)], axis=0).astype(BF16)
    back = lax.dot_general(
        place_ref[...].astype(BF16), rows, (((0,), (0,)), ((), ())), preferred_element_type=F32
    )
    chosen = jnp.sum(
        jnp.where(ids_ref[...] < held, weights_ref[...], 0.0), axis=1, keepdims=True
    )
    out_ref[...] = (back * chosen).astype(BF16)


def combine_rows(place, rows, ids, weights):
    tokens = ids.shape[0]
    width = rows.shape[2]
    return pl.pallas_call(
        combine_kernel,
        out_shape=jax.ShapeDtypeStruct((tokens, width), BF16),
        compiler_params=params(),
        cost_estimate=cost(32 * tokens * width, 2 * tokens * width),
        name="combine_rows",
    )(place, rows, ids, weights)


def exchange(a, axis):
    return lax.all_to_all(a, axis, split_axis=0, concat_axis=0, tiled=True)


def shift(a, axis, by):
    n = lax.axis_size(axis)
    return lax.ppermute(a, axis, [(i, (i + by) % n) for i in range(n)])


def local(
    queries,
    key_vectors,
    values,
    log_decay,
    out_gate,
    residual,
    attn_gain,
    moe_gain,
    expert_ids,
    route_weights,
    w_gate,
    w_up,
    w_down,
):
    held = lax.axis_size("exp")
    rows, width = queries.shape
    heads = log_decay.shape[1]
    tokens = residual.shape[0]
    attn_gain = attn_gain.reshape(1, -1)
    moe_gain = moe_gain.reshape(1, -1)
    w_gate = jnp.swapaxes(w_gate, 1, 2)
    w_up = jnp.swapaxes(w_up, 1, 2)
    ids = expert_ids.T
    ld = log_decay.T
    me = lax.axis_index("exp").reshape(1)
    core = lax.axis_index("core").reshape(1)
    keep = lax.optimization_barrier

    cum, msg = local_states(key_vectors, values, ld)
    sent = exchange(msg, CTX)
    inside, qs = inside_blocks(queries, key_vectors, values, cum, ld)
    pieces, place_own = route_rows(me, ids, residual, out_gate, held)
    sent, inside, qs, pieces = keep((sent, inside, qs, pieces))
    prior = scan_blocks(sent, lax.axis_index(CTX))
    state = exchange(prior, CTX).reshape(heads, HEAD_DIM, HEAD_DIM)
    pieces = [pieces[0]] + [shift(pieces[d], "exp", d) for d in range(1, held)]
    place = place_rows(me, pieces, tokens)

    attention, routed = carried_blocks(inside, qs, state, place)
    routed = exchange(routed.reshape(held, held * CAP, width), "exp")
    one, two = routed_norm(me, routed, pieces, attn_gain, moe_gain)

    def gather(a):
        return lax.all_gather(a, CTX, axis=0).reshape(32 * a.shape[0], a.shape[1])

    attention, one, two = keep((attention, one, two))
    one, two = gather(one), gather(two)
    whole = exchange(attention.reshape(held, tokens, width), "exp")
    hidden = hidden_rows(whole, residual, out_gate, attn_gain)
    one, hidden = keep((one, hidden))

    def expert(a):
        own, other = expert_rows(core, a, w_gate, w_up, w_down)
        return pair_sum(own, shift(other, "core", 1))

    one = expert(one)
    one, two = keep((one, two))
    one = exchange(one, ("z", "x"))
    two = exchange(expert(two), ("z", "x"))
    back = exchange(chip_sum(one, two, held), "exp")
    moe_out = combine_rows(place_own, back, expert_ids, route_weights)
    return (hidden, moe_out)


def solution(mesh):
    cube = Mesh(mesh.devices.reshape(4, 4, 2, 4), ("z", "x", "core", "exp"))
    both = CTX + ("exp",)
    in_specs = (
        P(CTX, "exp"),
        P(CTX, "exp"),
        P(CTX, "exp"),
        P(CTX, "exp"),
        P(both, None),
        P(both, None),
        P(),
        P(),
        P(both, None),
        P(both, None),
        P("exp", None, CTX),
        P("exp", None, CTX),
        P("exp", CTX, None),
    )
    out_specs = (P(both, None), P(both, None))
    return jax.shard_map(local, mesh=cube, in_specs=in_specs, out_specs=out_specs, check_vma=False)
```

time: 306 us -> 265 us (0.87)
  local copies, waits for them, and re-layouts: 32 us -> 7.35 us
  Pallas kernels: 52.8 us -> 74.8 us
  waiting for transfers between devices: 90.9 us -> 74.9 us
  other arithmetic: 14.1 us -> 0 us
  between operations: 0.92 us -> 14.2 us
  starting transfers between devices: 41.6 us -> 31.5 us
  blocking collectives: 71 us -> 61 us
    all_to_all x9 -> x4, waiting for transfers between devices: 90.9 us -> 25.1 us  [exchange(): return lax.all_to_all(a, axis, split_axis=0, concat_axis=0, tiled=True)]
    all_gather x0 -> x2, waiting for transfers between devices: none -> 41.9 us  [gather(): return lax.all_gather(a, CTX, axis=0).reshape(32 * a.shape[0], a.shape[1])]
    unnamed x55 -> x30, local copies, waits for them, and re-layouts: 29.8 us -> 7.35 us
    pallas_call x6 -> x9, Pallas kernels: 29.6 us -> 47.8 us  [the longest x2 22.2 us: expert_rows(): pl.pallas_call(functools.partial(expert_kernel, ksteps), grid=(ksteps + n...]
    all_to_all x9 -> x4, starting transfers between devices: 41 us -> 25 us  [exchange(): return lax.all_to_all(a, axis, split_axis=0, concat_axis=0, tiled=True)]
    all_gather x1 -> x0, blocking collectives: 10.5 us -> none  [local(): all_ids = lax.all_gather(ids, 'exp', axis=0)]
    reduce_sum x4 -> x0, other arithmetic: 7.81 us -> none  [total(): return jnp.sum(parts.astype(F32), axis=0).astype(BF16)]
    ppermute x4 -> x5, waiting for transfers between devices: 0.01 us -> 7.23 us  [shift(): return lax.ppermute(a, axis, [(i, (i + by) % n) for i in range(n)])]
  transfers between devices with their start and end apart: 13 -> 11, of which waited for: 8 -> 7; matrix products, arithmetic and copies ran while one was open for 9% -> 1% of each run, Pallas kernels for 11% -> 16%
where the time goes in v2:
time: 265 us; the launch traced here: 264 us
  waiting for transfers between devices  74.9 us (28%)
  Pallas kernels  74.8 us (28%)
  blocking collectives  61 us (23%)
  starting transfers between devices  31.5 us (12%)
  between operations  14.2 us (5%)
  local copies, waits for them, and re-layouts  7.35 us (3%)
    all_to_all x3, blocking collectives, exchange(): return lax.all_to_all(a, axis, split_axis=0, concat_axis=0, tiled=True)  61 us
    all_gather x2, waiting for transfers between devices, gather(): return lax.all_gather(a, CTX, axis=0).reshape(32 * a.shape[0], a.shape[1])  41.9 us
    all_to_all x4, waiting for transfers between devices, exchange(): return lax.all_to_all(a, axis, split_axis=0, concat_axis=0, tiled=True)  25.1 us
    all_to_all x4, starting transfers between devices, exchange(): return lax.all_to_all(a, axis, split_axis=0, concat_axis=0, tiled=True)  25 us
    pallas_call x2, Pallas kernels, expert_rows(): pl.pallas_call(functools.partial(expert_kernel, ksteps), grid=(ksteps + n...  22.2 us
    pallas_call x1, Pallas kernels, inside_blocks(): pl.pallas_call(functools.partial(inside_kernel, group), grid=(heads // gr...  11.7 us
    pallas_call x2, Pallas kernels, pair_sum(): pl.pallas_call(pair_kernel, grid=(steps,), out_shape=jax.ShapeDtypeStruct...  8.01 us
    unnamed x30, local copies, waits for them, and re-layouts  7.35 us
  transfers between devices with their start and end apart: 11, of which 7 were waited for; matrix products, arithmetic and copies ran while one was open for 1% of the time, Pallas kernels for 16%

profile of v2, /device:TPU:0, one launch (start us, length us, event | category | flops | bytes accessed | tf_op | source)
XLA Modules:
  0.0 263.7 jit_solution(1317331977008503298)
XLA Ops:
  7.2 5.5 %local_states.1 = (f32[512,12]{1,0:T(8,128)}, bf16[32,64,128]{2,1,0:T(8,128)(2,1)}) custom-call(bf16[512,1536]{1,0:T(8,128)(2,1)} %k_ref.3, bf16[512,1536]{1,0:T(8,128)(2,1)} %v_ref.3, f32[12,512]{1,0:T(8,128)} %bitcast.21), custom_call_target="tpu_custom_call" | custom-call | flops 201326592 | bytes 3145728 | tf_op jit(solution)/shard_map/local_states/pallas_call | solution.py:106
  12.6 8.2 %all-to-all-start = ((bf16[32,64,128]{2,1,0:T(8,128)(2,1)}), bf16[32,64,128]{2,1,0:T(8,128)(2,1)S(1)}, u32[]{:S(2)}, u32[]{:S(2)}) async-start(bf16[32,64,128]{2,1,0:T(8,128)(2,1)} %get-tuple-element.33), calls=%async_computation | async-start | bytes 1048576 | tf_op jit(solution)/shard_map/all_to_all | solution.py:591
  20.9 4.4 %route_rows.1 = (bf16[8,6400]{1,0:T(8,128)(2,1)}, bf16[8,6400]{1,0:T(8,128)(2,1)}, bf16[8,6400]{1,0:T(8,128)(2,1)}, bf16[8,6400]{1,0:T(8,128)(2,1)}, f32[16,128]{1,0:T(8,128)}) custom-call(s32[1]{0:T(128)} %bitcast.1.me_ref, s32[2,128]{1,0:T(2,128)} %bitcast.24, bf16[128,6144]{1,0:T(8,128)(2,1)} %res_ref.3, bf16[128,6144]{1,0:T(8,128)(2,1)} %gate_ref.3), custom_call_target="tpu_custom_call" | custom-call | flops 50331648 | bytes 3932160 | tf_op jit(solution)/shard_map/route_rows/pallas_call | solution.py:298
  25.3 11.7 %inside_blocks.1 = (f32[512,1536]{1,0:T(8,128)}, bf16[512,1536]{1,0:T(8,128)(2,1)}) custom-call(bf16[512,1536]{1,0:T(8,128)(2,1)} %q_ref.1, bf16[512,1536]{1,0:T(8,128)(2,1)} %k_ref.3, bf16[512,1536]{1,0:T(8,128)(2,1)} %v_ref.3, f32[512,12]{1,0:T(8,128)} %get-tuple-element.34.cum_ref, f32[12,512]{1,0:T(8,128)} %bitcast.22), custom_call_target="tpu_custom_call" | custom-call | flops 1610612736 | bytes 9437184 | tf_op jit(solution)/shard_map/inside_blocks/pallas_call | solution.py:198
  39.8 7.4 %all-to-all-start.1 = ((bf16[32,48,128]{2,1,0:T(8,128)(2,1)}), bf16[32,48,128]{2,1,0:T(8,128)(2,1)S(1)}, u32[]{:S(2)}, u32[]{:S(2)}) async-start(bf16[32,48,128]{2,1,0:T(8,128)(2,1)} %scan_blocks.1), calls=%async_computation.1 | async-start | bytes 786432 | tf_op jit(solution)/shard_map/all_to_all | solution.py:591
  48.9 2.9 %collective-permute-start.1 = (bf16[8,6400]{1,0:T(8,128)(2,1)S(1)}, bf16[8,6400]{1,0:T(8,128)(2,1)S(1)}, u32[]{:S(2)}, u32[]{:S(2)}) collective-permute-start(bf16[8,6400]{1,0:T(8,128)(2,1)S(1)} %copy-done.12), channel_id=1, source_target_pairs={{0,2},{1,3},{2,0},{3,1},{4,6},{5,7},{6,4},{7,5},{8,10},{9,11},{10,... | collective-permute-start | bytes 307208 | tf_op jit(solution)/shard_map/ppermute | solution.py:596
  53.6 3.4 %collective-permute-done.1.refs_2_ = bf16[8,6400]{1,0:T(8,128)(2,1)S(1)} collective-permute-done((bf16[8,6400]{1,0:T(8,128)(2,1)S(1)}, bf16[8,6400]{1,0:T(8,128)(2,1)S(1)}, u32[]{:S(2)}, u32[]{:S(2)}) %collective-permute-start.1) | collective-permute-done | bytes 102432 | tf_op jit(solution)/shard_map/ppermute | solution.py:596
  60.6 5.6 %carried_blocks.1 = (bf16[512,1536]{1,0:T(8,128)(2,1)}, bf16[64,1536]{1,0:T(8,128)(2,1)}) custom-call(f32[512,1536]{1,0:T(8,128)} %get-tuple-element.41.inside_ref, bf16[512,1536]{1,0:T(8,128)(2,1)} %get-tuple-element.42.qs_ref, bf16[12,128,128]{2,1,0:T(8,128)(2,1)} %bitcast.17, bf16[64,512]{1,0:T(8,128)(2,1)} %place_rows.1.place_ref), custom_call_target="tpu_custom_call" | custom-call | flops 402653184 | bytes 6291456 | tf_op jit(solution)/shard_map/carried_blocks/pallas_call | solution.py:238
  66.2 10.4 %all_to_all.35.att_ref = bf16[4,16,1536]{2,1,0:T(8,128)(2,1)} all-to-all(bf16[4,16,1536]{2,1,0:T(8,128)(2,1)} %bitcast.18), channel_id=1, replica_groups=mesh['z'=4,'x'=4,'core'=2,'exp'=4] {'exp'}, dimensions={0} | all-to-all | bytes 393216 | tf_op jit(solution)/shard_map/all_to_all | solution.py:591
  79.8 23.9 %all_to_all.36.att_ref = bf16[4,128,1536]{2,1,0:T(8,128)(2,1)} all-to-all(bf16[4,128,1536]{2,1,0:T(8,128)(2,1)} %bitcast.16), channel_id=1, replica_groups=mesh['z'=4,'x'=4,'core'=2,'exp'=4] {'exp'}, dimensions={0} | all-to-all | bytes 3145728 | tf_op jit(solution)/shard_map/all_to_all | solution.py:591
  103.7 5.0 %hidden_rows.1 = bf16[128,6144]{1,0:T(8,128)(2,1)} custom-call(bf16[4,128,1536]{2,1,0:T(8,128)(2,1)} %all_to_all.36.att_ref, bf16[128,6144]{1,0:T(8,128)(2,1)} %res_ref.3, bf16[128,6144]{1,0:T(8,128)(2,1)} %gate_ref.3, f32[1,6144]{1,0:T(1,128)} %bitcast.20), custom_call_target="tpu_custom_call" | custom-call | flops 15728640 | bytes 6291456 | tf_op jit(solution)/shard_map/hidden_rows/pallas_call | solution.py:419
  108.7 15.1 %all-gather.5.cloned.1.call-done.x_ref = bf16[256,6144]{1,0:T(8,128)(2,1)} async-done(((bf16[8,6144]{1,0:T(8,128)(2,1)}), bf16[256,6144]{1,0:T(8,128)(2,1)}) %all-gather.5.cloned.1.call-update) | async-done | bytes 3145744 | tf_op jit(solution)/shard_map/all_gather | solution.py:643
  123.8 11.1 %expert_rows.2 = (bf16[16,8,6144]{2,1,0:T(8,128)(2,1)}, bf16[16,8,6144]{2,1,0:T(8,128)(2,1)}) custom-call(s32[1]{0:T(128)} %bitcast.9.core_ref, bf16[256,6144]{1,0:T(8,128)(2,1)} %all-gather.5.cloned.1.call-done.x_ref, bf16[1,288,6144]{2,1,0:T(8,128)(2,1)} %bitcast.12, bf16[1,288,6144]{2,1,0:T(8,128)(2,1)} %bitcast.14, bf16[1,288,6144]{2,1,0:T(8,128)(2,1)} %wd_ref.3), custom_call_target="tpu_custom_call" | custom-call | flops 2717908992 | bytes 16908288 | tf_op jit(solution)/shard_map/expert_rows/pallas_call | solution.py:493
  135.1 3.4 %collective-permute-done.3.b_ref = bf16[16,8,6144]{2,1,0:T(8,128)(2,1)S(1)} collective-permute-done((bf16[16,8,6144]{2,1,0:T(8,128)(2,1)}, bf16[16,8,6144]{2,1,0:T(8,128)(2,1)S(1)}, u32[]{:S(2)}, u32[]{:S(2)}) %collective-permute-start.3) | collective-permute-done | bytes 1572896 | tf_op jit(solution)/shard_map/ppermute | solution.py:596
  139.7 4.0 %pair_sum.2 = bf16[16,8,6144]{2,1,0:T(8,128)(2,1)} custom-call(bf16[16,8,6144]{2,1,0:T(8,128)(2,1)} %get-tuple-element.57.a_ref, bf16[16,8,6144]{2,1,0:T(8,128)(2,1)} %copy-done.4), custom_call_target="tpu_custom_call" | custom-call | flops 786432 | bytes 4718592 | tf_op jit(solution)/shard_map/pair_sum/pallas_call | solution.py:524
  143.7 26.8 %all-gather.7.cloned.1.call-done.x_ref = bf16[256,6144]{1,0:T(8,128)(2,1)} async-done(((bf16[8,6144]{1,0:T(8,128)(2,1)}), bf16[256,6144]{1,0:T(8,128)(2,1)}) %all-gather.7.cloned.1.call-update) | async-done | bytes 3145744 | tf_op jit(solution)/shard_map/all_gather | solution.py:643
  170.5 11.1 %expert_rows.3 = (bf16[16,8,6144]{2,1,0:T(8,128)(2,1)}, bf16[16,8,6144]{2,1,0:T(8,128)(2,1)}) custom-call(s32[1]{0:T(128)} %bitcast.9.core_ref, bf16[256,6144]{1,0:T(8,128)(2,1)} %all-gather.7.cloned.1.call-done.x_ref, bf16[1,288,6144]{2,1,0:T(8,128)(2,1)} %bitcast.13, bf16[1,288,6144]{2,1,0:T(8,128)(2,1)} %bitcast.15, bf16[1,288,6144]{2,1,0:T(8,128)(2,1)} %wd_ref.3), custom_call_target="tpu_custom_call" | custom-call | flops 2717908992 | bytes 16908288 | tf_op jit(solution)/shard_map/expert_rows/pallas_call | solution.py:493
  181.9 5.0 %all-to-all-start.4 = ((bf16[16,8,6144]{2,1,0:T(8,128)(2,1)}), bf16[16,8,6144]{2,1,0:T(8,128)(2,1)S(1)}, u32[]{:S(2)}, u32[]{:S(2)}) async-start(bf16[16,8,6144]{2,1,0:T(8,128)(2,1)} %pair_sum.2), calls=%async_computation.4 | async-start | bytes 3145728 | tf_op jit(solution)/shard_map/all_to_all | solution.py:591
  188.0 4.0 %pair_sum.3 = bf16[16,8,6144]{2,1,0:T(8,128)(2,1)} custom-call(bf16[16,8,6144]{2,1,0:T(8,128)(2,1)} %get-tuple-element.62.a_ref, bf16[16,8,6144]{2,1,0:T(8,128)(2,1)} %copy-done.3), custom_call_target="tpu_custom_call" | custom-call | flops 786432 | bytes 4718592 | tf_op jit(solution)/shard_map/pair_sum/pallas_call | solution.py:524
  192.0 20.2 %all-to-all-done.4.one_ref = bf16[16,8,6144]{2,1,0:T(8,128)(2,1)S(1)} async-done(((bf16[16,8,6144]{2,1,0:T(8,128)(2,1)}), bf16[16,8,6144]{2,1,0:T(8,128)(2,1)S(1)}, u32[]{:S(2)}, u32[]{:S(2)}) %all-to-all-start.4) | async-done | bytes 1572896 | tf_op jit(solution)/shard_map/all_to_all | solution.py:591
  212.2 26.8 %all_to_all.37.two_ref = bf16[16,8,6144]{2,1,0:T(8,128)(2,1)} all-to-all(bf16[16,8,6144]{2,1,0:T(8,128)(2,1)} %pair_sum.3), channel_id=1, replica_groups=mesh['z'=4,'x'=4,'core'=2,'exp'=4] {'z','x'}, dimensions={0} | all-to-all | bytes 3145728 | tf_op jit(solution)/shard_map/all_to_all | solution.py:591
  239.0 3.8 %chip_sum.1 = bf16[4,4,6144]{2,1,0:T(4,128)(2,1)} custom-call(bf16[16,8,6144]{2,1,0:T(8,128)(2,1)} %copy-done, bf16[16,8,6144]{2,1,0:T(8,128)(2,1)} %all_to_all.37.two_ref), custom_call_target="tpu_custom_call" | custom-call | flops 1572864 | bytes 3145728 | tf_op jit(solution)/shard_map/chip_sum/pallas_call | solution.py:554
  242.8 4.3 %all-to-all-start.6 = ((bf16[4,4,6144]{2,1,0:T(4,128)(2,1)}), bf16[4,4,6144]{2,1,0:T(4,128)(2,1)S(1)}, u32[]{:S(2)}, u32[]{:S(2)}) async-start(bf16[4,4,6144]{2,1,0:T(4,128)(2,1)} %chip_sum.1), calls=%async_computation.6 | async-start | bytes 393216 | tf_op jit(solution)/shard_map/all_to_all | solution.py:591
  248.6 4.9 %all-to-all-done.6.rows_ref = bf16[4,4,6144]{2,1,0:T(4,128)(2,1)S(1)} async-done(((bf16[4,4,6144]{2,1,0:T(4,128)(2,1)}), bf16[4,4,6144]{2,1,0:T(4,128)(2,1)S(1)}, u32[]{:S(2)}, u32[]{:S(2)}) %all-to-all-start.6) | async-done | bytes 196640 | tf_op jit(solution)/shard_map/all_to_all | solution.py:591
  (47 shorter events, 20.8 us)
Async XLA Ops:
  12.6 24.4 %all-to-all-start = ((bf16[32,64,128]{2,1,0:T(8,128)(2,1)}), bf16[32,64,128]{2,1,0:T(8,128)(2,1)S(1)}, u32[]{:S(2)}, u32[]{:S(2)}) async-start(bf16[32,64,128]{2,1,0:T(8,128)(2,1)} %get-tuple-element.33), calls=%async_computation | async-start | bytes 1048576 | tf_op jit(solution)/shard_map/all_to_all | solution.py:591
  37.0 10.2 %copy-start.13 = (bf16[8,6400]{1,0:T(8,128)(2,1)S(1)}, bf16[8,6400]{1,0:T(8,128)(2,1)}, u32[]{:S(2)}) copy-start(bf16[8,6400]{1,0:T(8,128)(2,1)} %get-tuple-element.45) | copy-start | bytes 307204
  37.0 11.9 %copy-start.12 = (bf16[8,6400]{1,0:T(8,128)(2,1)S(1)}, bf16[8,6400]{1,0:T(8,128)(2,1)}, u32[]{:S(2)}) copy-start(bf16[8,6400]{1,0:T(8,128)(2,1)} %get-tuple-element.46) | copy-start | bytes 307204
  37.0 14.8 %copy-start.11 = (bf16[8,6400]{1,0:T(8,128)(2,1)S(1)}, bf16[8,6400]{1,0:T(8,128)(2,1)}, u32[]{:S(2)}) copy-start(bf16[8,6400]{1,0:T(8,128)(2,1)} %get-tuple-element.47) | copy-start | bytes 307204
  37.0 0.8 copy-start.1
  39.8 20.0 %all-to-all-start.1 = ((bf16[32,48,128]{2,1,0:T(8,128)(2,1)}), bf16[32,48,128]{2,1,0:T(8,128)(2,1)S(1)}, u32[]{:S(2)}, u32[]{:S(2)}) async-start(bf16[32,48,128]{2,1,0:T(8,128)(2,1)} %scan_blocks.1), calls=%async_computation.1 | async-start | bytes 786432 | tf_op jit(solution)/shard_map/all_to_all | solution.py:591
  47.2 76.6 %all-gather.5.cloned.1.call-start = ((), (), s32[]{:S(2)}) async-start(), calls=%async_computation.7 | async-start | bytes 3244032 | tf_op jit(solution)/shard_map/all_gather | solution.py:643
  47.2 6.4 %collective-permute-start = (bf16[8,6400]{1,0:T(8,128)(2,1)S(1)}, bf16[8,6400]{1,0:T(8,128)(2,1)S(1)}, u32[]{:S(2)}, u32[]{:S(2)}) collective-permute-start(bf16[8,6400]{1,0:T(8,128)(2,1)S(1)} %copy-done.13), channel_id=1, source_target_pairs={{0,1},{1,2},{2,3},{3,0},{4,5},{5,6},{6,7},{7,4},{8,9},{9,10},{10,1... | collective-permute-start | bytes 307208 | tf_op jit(solution)/shard_map/ppermute | solution.py:596
  48.9 8.1 %collective-permute-start.1 = (bf16[8,6400]{1,0:T(8,128)(2,1)S(1)}, bf16[8,6400]{1,0:T(8,128)(2,1)S(1)}, u32[]{:S(2)}, u32[]{:S(2)}) collective-permute-start(bf16[8,6400]{1,0:T(8,128)(2,1)S(1)} %copy-done.12), channel_id=1, source_target_pairs={{0,2},{1,3},{2,0},{3,1},{4,6},{5,7},{6,4},{7,5},{8,10},{9,11},{10,... | collective-permute-start | bytes 307208 | tf_op jit(solution)/shard_map/ppermute | solution.py:596
  51.8 5.2 %collective-permute-start.2 = (bf16[8,6400]{1,0:T(8,128)(2,1)S(1)}, bf16[8,6400]{1,0:T(8,128)(2,1)S(1)}, u32[]{:S(2)}, u32[]{:S(2)}) collective-permute-start(bf16[8,6400]{1,0:T(8,128)(2,1)S(1)} %copy-done.11), channel_id=1, source_target_pairs={{0,3},{1,0},{2,1},{3,2},{4,7},{5,4},{6,5},{7,6},{8,11},{9,8},{10,9... | collective-permute-start | bytes 307208 | tf_op jit(solution)/shard_map/ppermute | solution.py:596
  53.6 3.4 %copy-start.6 = (bf16[8,6400]{1,0:T(8,128)(2,1)}, bf16[8,6400]{1,0:T(8,128)(2,1)S(1)}, u32[]{:S(2)}) copy-start(bf16[8,6400]{1,0:T(8,128)(2,1)S(1)} %collective-permute-done.refs_1_) | copy-start | bytes 307204
  57.6 0.7 copy-start.8
  59.8 0.8 copy-start.2
  79.0 91.5 %all-gather.7.cloned.1.call-start = ((), (), s32[]{:S(2)}) async-start(), calls=%async_computation.8 | async-start | bytes 3244032 | tf_op jit(solution)/shard_map/all_gather | solution.py:643
  134.9 3.6 %collective-permute-start.3 = (bf16[16,8,6144]{2,1,0:T(8,128)(2,1)}, bf16[16,8,6144]{2,1,0:T(8,128)(2,1)S(1)}, u32[]{:S(2)}, u32[]{:S(2)}) collective-permute-start(bf16[16,8,6144]{2,1,0:T(8,128)(2,1)} %get-tuple-element.58), channel_id=1, source_target_pairs={{0,4},{4,0},{1,5},{5,1},{2,6},{6,2},{3,7},{7,3},{8,12},{12,8},{9,1... | collective-permute-start | bytes 4718600 | tf_op jit(solution)/shard_map/ppermute | solution.py:596
  138.5 1.2 copy-start.4
  181.6 5.3 %collective-permute-start.4 = (bf16[16,8,6144]{2,1,0:T(8,128)(2,1)}, bf16[16,8,6144]{2,1,0:T(8,128)(2,1)S(1)}, u32[]{:S(2)}, u32[]{:S(2)}) collective-permute-start(bf16[16,8,6144]{2,1,0:T(8,128)(2,1)} %get-tuple-element.63), channel_id=1, source_target_pairs={{0,4},{4,0},{1,5},{5,1},{2,6},{6,2},{3,7},{7,3},{8,12},{12,8},{9,1... | collective-permute-start | bytes 4718600 | tf_op jit(solution)/shard_map/ppermute | solution.py:596
  181.9 30.3 %all-to-all-start.4 = ((bf16[16,8,6144]{2,1,0:T(8,128)(2,1)}), bf16[16,8,6144]{2,1,0:T(8,128)(2,1)S(1)}, u32[]{:S(2)}, u32[]{:S(2)}) async-start(bf16[16,8,6144]{2,1,0:T(8,128)(2,1)} %pair_sum.2), calls=%async_computation.4 | async-start | bytes 3145728 | tf_op jit(solution)/shard_map/all_to_all | solution.py:591
  186.9 1.1 copy-start.3
  212.2 26.8 %copy-start = (bf16[16,8,6144]{2,1,0:T(8,128)(2,1)}, bf16[16,8,6144]{2,1,0:T(8,128)(2,1)S(1)}, u32[]{:S(2)}) copy-start(bf16[16,8,6144]{2,1,0:T(8,128)(2,1)S(1)} %all-to-all-done.4.one_ref) | copy-start | bytes 4718596
  239.0 8.2 %copy-start.9 = (s32[128,2]{0,1:T(2,128)S(1)}, s32[128,2]{0,1:T(2,128)}, u32[]{:S(2)}) copy-start(s32[128,2]{0,1:T(2,128)} %param.21) | copy-start | bytes 3076
  239.0 8.9 %copy-start.10 = (f32[128,2]{0,1:T(2,128)S(1)}, f32[128,2]{0,1:T(2,128)}, u32[]{:S(2)}) copy-start(f32[128,2]{0,1:T(2,128)} %param.22) | copy-start | bytes 3076
  242.8 10.7 %all-to-all-start.6 = ((bf16[4,4,6144]{2,1,0:T(4,128)(2,1)}), bf16[4,4,6144]{2,1,0:T(4,128)(2,1)S(1)}, u32[]{:S(2)}, u32[]{:S(2)}) async-start(bf16[4,4,6144]{2,1,0:T(4,128)(2,1)} %chip_sum.1), calls=%async_computation.6 | async-start | bytes 393216 | tf_op jit(solution)/shard_map/all_to_all | solution.py:591
  253.4 0.7 copy-start.5
  (1 other events, 0.6 us)
Sparse Core Ops, SparseCore 0:
  79.1 44.6 all-gather.4
  126.0 44.4 all-gather.6

commit v3 on v2

--- a/solution.py
+++ b/solution.py
@@ -14,11 +14,19 @@
 BF16 = jnp.bfloat16
 HIGHEST = lax.Precision.HIGHEST
 CTX = ("z", "x", "core")
-VMEM_LIMIT = 60 * 1024 * 1024
+VMEM_LIMIT = 24 * 1024 * 1024
 
 
 def iota(shape, dim):
     return lax.broadcasted_iota(jnp.int32, shape, dim)
+
+
+def hbm(a):
+    return pltpu.with_memory_space_constraint(a, pltpu.HBM)
+
+
+def far(shape, dtype=BF16):
+    return pltpu.HBM(shape, dtype)
 
 
 def params(**kw):
@@ -44,9 +52,18 @@
     return total
 
 
-def column(table, h):
-    lane = iota(table.shape, 1)
-    return jnp.sum(jnp.where(lane == h, table, 0.0), axis=1, keepdims=True)
+def spread(table, first, count, terms):
+    n = table.shape[1]
+    shape = (n, count * HEAD_DIM)
+    pick = (iota(shape, 0) == first + iota(shape, 1) // HEAD_DIM).astype(BF16)
+    total = None
+    rest = table
+    for _ in range(terms):
+        part = rest.astype(BF16)
+        rest = rest - part.astype(F32)
+        term = jnp.dot(part, pick, preferred_element_type=F32)
+        total = term if total is None else total + term
+    return total
 
 
 def state_kernel(group, k_ref, v_ref, ld_ref, cum_ref, msg_ref, fade_ref, decay_ref):
@@ -63,14 +80,13 @@
         fade_ref[...] = jnp.exp(final - cum)
         decay_ref[...] = jnp.broadcast_to(jnp.exp(final), decay_ref.shape)
 
-    fade = fade_ref[...]
-    decay = decay_ref[...]
+    fade = spread(fade_ref[...], g * group, group, 2)
+    decay = spread(decay_ref[...], g * group, group, 2)
     row16 = iota((16, HEAD_DIM), 0)
     tiles = []
     for j in range(group):
-        h = g * group + j
         cols = slice(j * HEAD_DIM, (j + 1) * HEAD_DIM)
-        wk = (k_ref[:, cols].astype(F32) * column(fade, h)).astype(BF16)
+        wk = (k_ref[:, cols].astype(F32) * fade[:, cols]).astype(BF16)
         state = lax.dot_general(
             wk, v_ref[:, cols], (((0,), (0,)), ((), ())), preferred_element_type=F32
         ).astype(BF16)
@@ -81,7 +97,7 @@
             lo = row - j * HEAD_DIM
             msg_ref[part, at : at + take, :] = state[lo : lo + take, :]
             row += take
-        whole = jnp.broadcast_to(column(decay, h), (16, HEAD_DIM))
+        whole = decay[:, cols]
         high = whole.astype(BF16).astype(F32)
         tiles.append((high, whole - high))
     for part in range(parts):
@@ -108,7 +124,7 @@
         grid=(heads // group,),
         out_shape=(
             jax.ShapeDtypeStruct((rows, heads), F32),
-            jax.ShapeDtypeStruct((32, per + 16, HEAD_DIM), BF16),
+            far((32, per + 16, HEAD_DIM)),
         ),
         in_specs=[block, block, pl.BlockSpec((heads, rows), lambda g: (0, 0))],
         out_specs=(
@@ -142,7 +158,7 @@
     split = (HEAD_DIM - (per * part) % HEAD_DIM).astype(jnp.int32).reshape(1)
     return pl.pallas_call(
         scan_kernel,
-        out_shape=jax.ShapeDtypeStruct((parts, per, width), BF16),
+        out_shape=far((parts, per, width)),
         in_specs=[
             pl.BlockSpec(memory_space=pltpu.SMEM),
             pl.BlockSpec(memory_space=pltpu.VMEM),
@@ -161,12 +177,12 @@
     def _():
         cumt_ref[...] = running_sum(ld_ref[...], 1)
 
-    cum = cum_ref[...]
+    cum = spread(cum_ref[...], pl.program_id(0) * group, group, 3)
     causal = iota((HEAD_DIM, HEAD_DIM), 0) >= iota((HEAD_DIM, HEAD_DIM), 1)
     for j in range(group):
         h = pl.program_id(0) * group + j
         cols = slice(j * HEAD_DIM, (j + 1) * HEAD_DIM)
-        col = column(cum, h)
+        col = cum[:, cols]
         row = cumt_ref[pl.ds(h, 1), :]
         q = q_ref[:, cols]
         k = k_ref[:, cols]
@@ -186,7 +202,8 @@
                 s = lax.dot_general(
                     qi, k[:lo], (((1,), (1,)), ((), ())), preferred_element_type=F32
                 )
-                w = (s * jnp.exp(jnp.minimum(ci - row[:, :lo], 0.0))).astype(BF16)
+                gap = jnp.concatenate([ci] * i, axis=1) - row[:, :lo]
+                w = (s * jnp.exp(jnp.minimum(gap, 0.0))).astype(BF16)
                 total = total + jnp.dot(w, v[:lo], preferred_element_type=F32)
             inside_ref[lo:hi, cols] = total
 
@@ -217,42 +234,50 @@
     )(q, k, v, cum, ld)
 
 
-def carried_kernel(group, inside_ref, qs_ref, state_ref, place_ref, att_ref, sel_ref):
+def carried_kernel(group, me_ref, inside_ref, qs_ref, state_ref, place_ref, sel_ref, *refs):
+    outs, att_ref = refs[:-1], refs[-1]
+    held = len(outs)
+    tokens = outs[0].shape[0]
     for j in range(group):
         cols = slice(j * HEAD_DIM, (j + 1) * HEAD_DIM)
-        att = (
+        att_ref[:, cols] = (
             inside_ref[:, cols]
             + jnp.dot(qs_ref[:, cols], state_ref[j], preferred_element_type=F32)
         ).astype(BF16)
-        att_ref[:, cols] = att
-        sel_ref[:, cols] = jnp.dot(
-            place_ref[...], att, preferred_element_type=F32
-        ).astype(BF16)
-
-
-def carried_blocks(inside, qs, state, place, group=3):
+    sel_ref[...] = jnp.dot(
+        place_ref[...], att_ref[...], preferred_element_type=F32
+    ).astype(BF16)
+    for d in range(held):
+        at = pl.multiple_of(lax.rem(me_ref[0] + d, held) * tokens, tokens)
+        outs[d][...] = att_ref[pl.ds(at, tokens), :]
+
+
+def carried_blocks(me, inside, qs, state, place, held, group=3):
     rows, width = inside.shape
     heads = width // HEAD_DIM
     chosen = place.shape[0]
-    block = pl.BlockSpec((rows, group * HEAD_DIM), lambda g: (0, g))
-    return pl.pallas_call(
+    wide = group * HEAD_DIM
+    tokens = rows // held
+    block = pl.BlockSpec((rows, wide), lambda g: (0, g))
+    outs = pl.pallas_call(
         functools.partial(carried_kernel, group),
         grid=(heads // group,),
-        out_shape=(
-            jax.ShapeDtypeStruct((rows, width), BF16),
-            jax.ShapeDtypeStruct((chosen, width), BF16),
-        ),
+        out_shape=(far((chosen, width)),) + (far((tokens, width)),) * held,
         in_specs=[
+            pl.BlockSpec(memory_space=pltpu.SMEM),
             block,
             block,
             pl.BlockSpec((group, HEAD_DIM, HEAD_DIM), lambda g: (g, 0, 0)),
             pl.BlockSpec((chosen, rows), lambda g: (0, 0)),
         ],
-        out_specs=(block, pl.BlockSpec((chosen, group * HEAD_DIM), lambda g: (0, g))),
+        out_specs=(pl.BlockSpec((chosen, wide), lambda g: (0, g)),)
+        + (pl.BlockSpec((tokens, wide), lambda g: (0, g)),) * held,
+        scratch_shapes=[pltpu.VMEM((rows, wide), BF16)],
         compiler_params=params(),
         cost_estimate=cost(4 * rows * width * HEAD_DIM, 8 * rows * width),
         name="carried_blocks",
-    )(inside, qs, state, place)
+    )(me, inside, qs, state, place)
+    return outs[0], list(outs[1:])
 
 
 def route_kernel(me_ref, ids_ref, res_ref, gate_ref, *refs):
@@ -294,7 +319,7 @@
 def route_rows(me, ids, residual, out_gate, held):
     tokens, width = residual.shape
     whole = pl.BlockSpec(memory_space=pltpu.VMEM)
-    piece = jax.ShapeDtypeStruct((2 * CAP, width + 2 * tokens), BF16)
+    piece = far((2 * CAP, width + 2 * tokens))
     outs = pl.pallas_call(
         route_kernel,
         out_shape=(piece,) * held + (jax.ShapeDtypeStruct((held * CAP, tokens), F32),),
@@ -386,18 +411,19 @@
     normed = (
         hidden * lax.rsqrt(jnp.mean(hidden * hidden, axis=-1, keepdims=True) + EPS) * mg_ref[...]
     )
-    one_ref[...] = normed[: rows // 2].astype(BF16)
+    one = normed[: rows // 2].astype(BF16)
+    for i in range(one_ref.shape[0]):
+        one_ref[i] = one
     two_ref[...] = normed[rows // 2 :].astype(BF16)
 
 
-def routed_norm(me, att, pieces, attn_gain, moe_gain):
+def routed_norm(me, att, pieces, attn_gain, moe_gain, copies):
     sources, rows, part = att.shape
     width = sources * part
     whole = pl.BlockSpec(memory_space=pltpu.VMEM)
-    shape = jax.ShapeDtypeStruct((rows // 2, width), BF16)
     return pl.pallas_call(
         routed_norm_kernel,
-        out_shape=(shape, shape),
+        out_shape=(far((copies, rows // 2, width)), far((rows // 2, width))),
         in_specs=[pl.BlockSpec(memory_space=pltpu.SMEM)] + [whole] * (3 + len(pieces)),
         out_specs=(whole, whole),
         compiler_params=params(),
@@ -406,111 +432,138 @@
     )(me, att, attn_gain, moe_gain, *pieces)
 
 
-def hidden_kernel(att_ref, res_ref, gate_ref, ag_ref, out_ref):
-    sources = att_ref.shape[0]
-    att = jnp.concatenate([att_ref[s].astype(F32) for s in range(sources)], axis=1)
+def hidden_kernel(me_ref, res_ref, gate_ref, ag_ref, *refs):
+    pieces, out_ref = refs[:-1], refs[-1]
+    me = me_ref[0]
+    tables = [p[...].astype(F32) for p in pieces]
+    att = jnp.concatenate([by_source(me, tables, j) for j in range(len(pieces))], axis=1)
     out_ref[...] = gated(att, res_ref[...].astype(F32), gate_ref[...].astype(F32), ag_ref[...])
 
 
-def hidden_rows(att, residual, out_gate, attn_gain, tile=32):
-    sources, rows, part = att.shape
-    width = sources * part
+def hidden_rows(me, pieces, residual, out_gate, attn_gain, tile=32):
+    rows, part = pieces[0].shape
+    width = len(pieces) * part
     block = pl.BlockSpec((tile, width), lambda i: (i, 0))
     return pl.pallas_call(
         hidden_kernel,
         grid=(rows // tile,),
         out_shape=jax.ShapeDtypeStruct((rows, width), BF16),
         in_specs=[
-            pl.BlockSpec((sources, tile, part), lambda i: (0, i, 0)),
+            pl.BlockSpec(memory_space=pltpu.SMEM),
             block,
             block,
             pl.BlockSpec((1, width), lambda i: (0, 0)),
-        ],
+        ]
+        + [pl.BlockSpec((tile, part), lambda i: (i, 0))] * len(pieces),
         out_specs=block,
         compiler_params=params(),
         cost_estimate=cost(20 * rows * width, 8 * rows * width),
         name="hidden_rows",
-    )(att, residual, out_gate, attn_gain)
-
-
-def expert_kernel(
-    ksteps, core_ref, x_ref, wg_ref, wu_ref, wd_ref, own_ref, other_ref, gate_acc, up_acc, act
-):
-    step = pl.program_id(0)
-    chips, rows, wide = own_ref.shape
+    )(me, residual, out_gate, attn_gain, *pieces)
+
+
+def act_kernel(steps, streamed, wg_hbm, wu_hbm, *refs):
+    count = len(refs) - 4
+    xs, (act_ref, w_ref, x_ref, sem) = refs[:count], refs[count:]
+    units, width = wg_hbm.shape
     nt = (((1,), (1,)), ((), ()))
-
-    @pl.when(step < ksteps)
-    def _():
-        x = x_ref[...]
-        g = lax.dot_general(wg_ref[0], x, nt, preferred_element_type=F32)
-        u = lax.dot_general(wu_ref[0], x, nt, preferred_element_type=F32)
-
-        @pl.when(step == 0)
-        def _():
-            gate_acc[...] = g
-            up_acc[...] = u
-
-        @pl.when(step > 0)
-        def _():
-            gate_acc[...] += g
-            up_acc[...] += u
-
-    @pl.when(step == ksteps - 1)
-    def _():
-        g = gate_acc[...]
-        act[...] = (g * jax.nn.sigmoid(g) * up_acc[...]).T.astype(BF16)
-
-    @pl.when(step >= ksteps)
-    def _():
-        out = jnp.dot(act[...], wd_ref[0], preferred_element_type=F32)
-        out = out.reshape(chips, 2, rows, wide)
-        first = core_ref[0] == 0
-
-        @pl.when(first)
-        def _():
-            own_ref[...] = out[:, 0].astype(BF16)
-            other_ref[...] = out[:, 1].astype(BF16)
-
-        @pl.when(jnp.logical_not(first))
-        def _():
-            own_ref[...] = out[:, 1].astype(BF16)
-            other_ref[...] = out[:, 0].astype(BF16)
-
-
-def expert_rows(core, x, w_gate, w_up, w_down, ksteps=4, nsteps=4):
-    count, width = x.shape
-    units = w_gate.shape[1]
-    depth, wide = width // ksteps, width // nsteps
+    wide = width // steps
+    copies = []
+    for s in range(steps):
+        cols = pl.ds(s * wide, wide)
+        pairs = [(wg_hbm.at[:, cols], w_ref.at[0, :, cols]), (wu_hbm.at[:, cols], w_ref.at[1, :, cols])]
+        if streamed:
+            pairs.append((xs[0].at[:, cols], x_ref.at[:, cols]))
+        copies.append(
+            [pltpu.make_async_copy(a, b, sem.at[s, n]) for n, (a, b) in enumerate(pairs)]
+        )
+    for group in copies:
+        for c in group:
+            c.start()
+    sources = [x_ref] if streamed else xs
+    gate = up = None
+    for s in range(steps):
+        cols = slice(s * wide, (s + 1) * wide)
+        for c in copies[s]:
+            c.wait()
+        x = [r[:, cols] for r in sources]
+        x = x[0] if len(x) == 1 else jnp.concatenate(x, axis=0)
+        g = lax.dot_general(w_ref[0, :, cols], x, nt, preferred_element_type=F32)
+        u = lax.dot_general(w_ref[1, :, cols], x, nt, preferred_element_type=F32)
+        gate = g if gate is None else gate + g
+        up = u if up is None else up + u
+    act_ref[...] = (gate * jax.nn.sigmoid(gate) * up).T.astype(BF16)
+
+
+def expert_act(xs, w_gate, w_up, steps=6):
+    count = sum(x.shape[0] for x in xs)
+    units, width = w_gate.shape
+    whole = pl.BlockSpec(memory_space=pltpu.VMEM)
+    away = pl.BlockSpec(memory_space=pl.ANY)
+    streamed = len(xs) == 1
+    if streamed:
+        xs = (hbm(xs[0]),)
+    return pl.pallas_call(
+        functools.partial(act_kernel, steps, streamed),
+        out_shape=jax.ShapeDtypeStruct((count, units), BF16),
+        in_specs=[away, away] + [away if streamed else whole] * len(xs),
+        out_specs=whole,
+        scratch_shapes=[
+            pltpu.VMEM((2, units, width), BF16),
+            pltpu.VMEM((count, width) if streamed else (16, HEAD_DIM), BF16),
+            pltpu.SemaphoreType.DMA((steps, 3)),
+        ],
+        compiler_params=params(),
+        cost_estimate=cost(4 * count * width * units, 4 * width * units + 2 * count * width),
+        name="expert_act",
+    )(hbm(w_gate), hbm(w_up), *xs)
+
+
+def down_kernel(steps, mixed, core_ref, act_ref, wd_hbm, own_ref, other_ref, wd_ref, sem):
+    chips, rows, width = own_ref.shape
+    wide = width // steps
+    act = act_ref[...]
+    first = core_ref[0] == 0
+    copies = []
+    for s in range(steps):
+        cols = pl.ds(s * wide, wide)
+        copies.append(pltpu.make_async_copy(wd_hbm.at[:, cols], wd_ref.at[:, cols], sem.at[s]))
+    for c in copies:
+        c.start()
+    for s in range(steps):
+        cols = slice(s * wide, (s + 1) * wide)
+        copies[s].wait()
+        out = jnp.dot(act, wd_ref[:, cols], preferred_element_type=F32)
+        if mixed:
+            out = out.reshape(chips, 2, rows, wide)
+            a, b = out[:, 0].astype(BF16), out[:, 1].astype(BF16)
+            own_ref[:, :, cols] = jnp.where(first, a, b)
+            other_ref[:, :, cols] = jnp.where(first, b, a)
+        else:
+            out = out.reshape(2, chips, rows, wide).astype(BF16)
+            own_ref[:, :, cols] = out[0]
+            other_ref[:, :, cols] = out[1]
+
+
+def expert_down(core, act, w_down, mixed, steps=6):
+    count, units = act.shape
+    width = w_down.shape[1]
     rows = count // 32
-
-    def k_at(i):
-        return jnp.minimum(i, ksteps - 1)
-
-    def n_at(i):
-        return jnp.maximum(i - ksteps, 0)
-
-    return pl.pallas_call(
-        functools.partial(expert_kernel, ksteps),
-        grid=(ksteps + nsteps,),
+    whole = pl.BlockSpec(memory_space=pltpu.VMEM)
+    return pl.pallas_call(
+        functools.partial(down_kernel, steps, mixed),
         out_shape=(jax.ShapeDtypeStruct((16, rows, width), BF16),) * 2,
         in_specs=[
             pl.BlockSpec(memory_space=pltpu.SMEM),
-            pl.BlockSpec((count, depth), lambda i: (0, k_at(i))),
-            pl.BlockSpec((1, units, depth), lambda i: (0, 0, k_at(i))),
-            pl.BlockSpec((1, units, depth), lambda i: (0, 0, k_at(i))),
-            pl.BlockSpec((1, units, wide), lambda i: (0, 0, n_at(i))),
+            whole,
+            pl.BlockSpec(memory_space=pl.ANY),
         ],
-        out_specs=(pl.BlockSpec((16, rows, wide), lambda i: (0, 0, n_at(i))),) * 2,
-        scratch_shapes=[
-            pltpu.VMEM((units, count), F32),
-            pltpu.VMEM((units, count), F32),
-            pltpu.VMEM((count, units), BF16),
-        ],
-        compiler_params=params(),
-        cost_estimate=cost(6 * count * width * units, 6 * width * units + 4 * count * width),
-        name="expert_rows",
-    )(core, x, w_gate, w_up, w_down)
+        out_specs=(whole, whole),
+        scratch_shapes=[pltpu.VMEM((units, width), BF16), pltpu.SemaphoreType.DMA((steps,))],
+        compiler_params=params(),
+        cost_estimate=cost(2 * count * width * units, 2 * width * units + 2 * count * width),
+        name="expert_down",
+    )(core, act, hbm(w_down))
 
 
 def pair_kernel(a_ref, b_ref, out_ref):
@@ -524,7 +577,7 @@
     return pl.pallas_call(
         pair_kernel,
         grid=(steps,),
-        out_shape=jax.ShapeDtypeStruct((chips, rows, width), BF16),
+        out_shape=far((chips, rows, width)),
         in_specs=[block, block],
         out_specs=block,
         compiler_params=params(),
@@ -554,7 +607,7 @@
     return pl.pallas_call(
         chip_sum_kernel,
         grid=(steps,),
-        out_shape=jax.ShapeDtypeStruct((held, CAP, width), BF16),
+        out_shape=far((held, CAP, width)),
         in_specs=[block, block],
         out_specs=pl.BlockSpec((held, CAP, wide), lambda i: (0, 0, i)),
         compiler_params=params(),
@@ -617,45 +670,47 @@
     tokens = residual.shape[0]
     attn_gain = attn_gain.reshape(1, -1)
     moe_gain = moe_gain.reshape(1, -1)
-    w_gate = jnp.swapaxes(w_gate, 1, 2)
-    w_up = jnp.swapaxes(w_up, 1, 2)
+    w_gate = jnp.swapaxes(w_gate, 1, 2)[0]
+    w_up = jnp.swapaxes(w_up, 1, 2)[0]
+    w_down = w_down[0]
     ids = expert_ids.T
     ld = log_decay.T
     me = lax.axis_index("exp").reshape(1)
     core = lax.axis_index("core").reshape(1)
     keep = lax.optimization_barrier
-
-    cum, msg = local_states(key_vectors, values, ld)
+    chips = lax.axis_size("z") * lax.axis_size("x")
+
+    cum, msg = local_states(hbm(key_vectors), hbm(values), ld)
     sent = exchange(msg, CTX)
-    inside, qs = inside_blocks(queries, key_vectors, values, cum, ld)
-    pieces, place_own = route_rows(me, ids, residual, out_gate, held)
+    inside, qs = inside_blocks(hbm(queries), hbm(key_vectors), hbm(values), cum, ld)
+    pieces, place_own = route_rows(me, ids, hbm(residual), hbm(out_gate), held)
     sent, inside, qs, pieces = keep((sent, inside, qs, pieces))
     prior = scan_blocks(sent, lax.axis_index(CTX))
     state = exchange(prior, CTX).reshape(heads, HEAD_DIM, HEAD_DIM)
     pieces = [pieces[0]] + [shift(pieces[d], "exp", d) for d in range(1, held)]
     place = place_rows(me, pieces, tokens)
 
-    attention, routed = carried_blocks(inside, qs, state, place)
+    routed, attention = carried_blocks(me, inside, qs, state, place, held)
     routed = exchange(routed.reshape(held, held * CAP, width), "exp")
-    one, two = routed_norm(me, routed, pieces, attn_gain, moe_gain)
-
-    def gather(a):
-        return lax.all_gather(a, CTX, axis=0).reshape(32 * a.shape[0], a.shape[1])
-
-    attention, one, two = keep((attention, one, two))
-    one, two = gather(one), gather(two)
-    whole = exchange(attention.reshape(held, tokens, width), "exp")
-    hidden = hidden_rows(whole, residual, out_gate, attn_gain)
-    one, hidden = keep((one, hidden))
-
-    def expert(a):
-        own, other = expert_rows(core, a, w_gate, w_up, w_down)
-        return pair_sum(own, shift(other, "core", 1))
-
-    one = expert(one)
-    one, two = keep((one, two))
+    one, two = routed_norm(me, routed, pieces, attn_gain, moe_gain, chips)
+
+    attention, two = keep((attention, two))
+    two = lax.all_gather(two, CTX, axis=0).reshape(32 * two.shape[0], two.shape[1])
     one = exchange(one, ("z", "x"))
-    two = exchange(expert(two), ("z", "x"))
+    one = one.reshape(-1, one.shape[2])
+    attention = [attention[0]] + [shift(attention[d], "exp", d) for d in range(1, held)]
+    one, attention = keep((one, attention))
+
+    act = expert_act((one, shift(one, "core", 1)), w_gate, w_up)
+    own, other = expert_down(core, act, w_down, False)
+    one = pair_sum(own, shift(other, "core", 1))
+    _, two = keep((one, two))
+    one = exchange(one, ("z", "x"))
+    act = expert_act((two,), w_gate, w_up)
+    one, act = keep((one, act))
+    own, other = expert_down(core, act, w_down, True)
+    two = exchange(pair_sum(own, shift(other, "core", 1)), ("z", "x"))
+    hidden = hidden_rows(me, attention, hbm(residual), hbm(out_gate), attn_gain)
     back = exchange(chip_sum(one, two, held), "exp")
     moe_out = combine_rows(place_own, back, expert_ids, route_weights)
     return (hidden, moe_out)

time: 265 us -> 215 us (0.81)
  blocking collectives: 61 us -> 37.3 us
  waiting for transfers between devices: 74.9 us -> 53.7 us
  Pallas kernels: 74.8 us -> 58.5 us
  starting transfers between devices: 31.5 us -> 42.4 us
    all_gather x2 -> x1, waiting for transfers between devices: 41.9 us -> 9.41 us  [local(): lax.all_gather(two, CTX, axis=0).reshape(32 * two.shape[0], two.shape[1])]
    all_to_all x3 -> x2, blocking collectives: 61 us -> 37.3 us  [exchange(): return lax.all_to_all(a, axis, split_axis=0, concat_axis=0, tiled=True)]
    ppermute x5 -> x9, waiting for transfers between devices: 7.23 us -> 29.2 us  [shift(): return lax.ppermute(a, axis, [(i, (i + by) % n) for i in range(n)])]
    pallas_call x7 -> x9, Pallas kernels: 38.3 us -> 26.1 us  [the longest x2 8.96 us: expert_act(): pl.pallas_call(functools.partial(act_kernel, steps, streamed), out_shape=...]
    all_to_all x4 -> x5, waiting for transfers between devices: 25.1 us -> 14.4 us  [exchange(): return lax.all_to_all(a, axis, split_axis=0, concat_axis=0, tiled=True)]
    all_to_all x4 -> x5, starting transfers between devices: 25 us -> 32.5 us  [exchange(): return lax.all_to_all(a, axis, split_axis=0, concat_axis=0, tiled=True)]
    ppermute x5 -> x9, starting transfers between devices: 6.42 us -> 9.88 us  [shift(): return lax.ppermute(a, axis, [(i, (i + by) % n) for i in range(n)])]
    unnamed x30 -> x46, local copies, waits for them, and re-layouts: 7.35 us -> 7.86 us
  transfers between devices with their start and end apart: 11 -> 15, of which waited for: 7 -> 11; matrix products, arithmetic and copies ran while one was open for 1% -> 0% of each run, Pallas kernels for 16% -> 17%
where the time goes in v3:
time: 215 us; the launch traced here: 214 us
  Pallas kernels  58.5 us (27%)
  waiting for transfers between devices  53.7 us (25%)
  starting transfers between devices  42.4 us (20%)
  blocking collectives  37.3 us (17%)
  between operations  14.3 us (7%)
  local copies, waits for them, and re-layouts  7.86 us (4%)
    all_to_all x2, blocking collectives, exchange(): return lax.all_to_all(a, axis, split_axis=0, concat_axis=0, tiled=True)  37.3 us
    all_to_all x5, starting transfers between devices, exchange(): return lax.all_to_all(a, axis, split_axis=0, concat_axis=0, tiled=True)  32.5 us
    ppermute x9, waiting for transfers between devices, shift(): return lax.ppermute(a, axis, [(i, (i + by) % n) for i in range(n)])  29.2 us
    all_to_all x5, waiting for transfers between devices, exchange(): return lax.all_to_all(a, axis, split_axis=0, concat_axis=0, tiled=True)  14.4 us
    pallas_call x1, Pallas kernels, inside_blocks(): pl.pallas_call(functools.partial(inside_kernel, group), grid=(heads // gr...  11.9 us
    ppermute x9, starting transfers between devices, shift(): return lax.ppermute(a, axis, [(i, (i + by) % n) for i in range(n)])  9.88 us
    all_gather x1, waiting for transfers between devices, local(): lax.all_gather(two, CTX, axis=0).reshape(32 * two.shape[0], two.shape[1])  9.41 us
    pallas_call x2, Pallas kernels, expert_act(): pl.pallas_call(functools.partial(act_kernel, steps, streamed), out_shape=...  8.96 us
  transfers between devices with their start and end apart: 15, of which 11 were waited for; matrix products, arithmetic and copies ran while one was open for 0% of the time, Pallas kernels for 17%

profile of v3, /device:TPU:0, one launch (start us, length us, event | category | flops | bytes accessed | tf_op | source)
XLA Modules:
  0.0 214.0 jit_solution(15231325540911111108)
XLA Ops:
  7.9 5.8 %local_states.1 = (f32[512,12]{1,0:T(8,128)S(1)}, bf16[32,64,128]{2,1,0:T(8,128)(2,1)}) custom-call(bf16[512,1536]{1,0:T(8,128)(2,1)} %k_ref.3, bf16[512,1536]{1,0:T(8,128)(2,1)} %v_ref.3, f32[12,512]{1,0:T(8,128)S(1)} %bitcast.22), custom_call_target="tpu_custom_call" | custom-call | flops 201326592 | bytes 3145728 | tf_op jit(solution)/shard_map/local_states/pallas_call | solution.py:122
  13.7 8.4 %all-to-all-start = ((bf16[32,64,128]{2,1,0:T(8,128)(2,1)}), bf16[32,64,128]{2,1,0:T(8,128)(2,1)}, u32[]{:S(2)}, u32[]{:S(2)}) async-start(bf16[32,64,128]{2,1,0:T(8,128)(2,1)} %get-tuple-element.42), calls=%async_computation | async-start | bytes 1048576 | tf_op jit(solution)/shard_map/all_to_all | solution.py:644
  22.2 4.4 %route_rows.1 = (bf16[8,6400]{1,0:T(8,128)(2,1)}, bf16[8,6400]{1,0:T(8,128)(2,1)}, bf16[8,6400]{1,0:T(8,128)(2,1)}, bf16[8,6400]{1,0:T(8,128)(2,1)}, f32[16,128]{1,0:T(8,128)S(1)}) custom-call(s32[1]{0:T(128)} %bitcast.me_ref, s32[2,128]{1,0:T(2,128)S(1)} %bitcast.25, bf16[128,6144]{1,0:T(8,128)(2,1)} %res_ref.3, bf16[128,6144]{1,0:T(8,128)(2,1)} %gate_ref.3), custom_call_target="tpu_custom_call" | custom-call | flops 50331648 | bytes 3932160 | tf_op jit(solution)/shard_map/route_rows/pallas_call | solution.py:323
  26.6 11.9 %inside_blocks.1 = (f32[512,1536]{1,0:T(8,128)S(1)}, bf16[512,1536]{1,0:T(8,128)(2,1)S(1)}) custom-call(bf16[512,1536]{1,0:T(8,128)(2,1)} %q_ref.1, bf16[512,1536]{1,0:T(8,128)(2,1)} %k_ref.3, bf16[512,1536]{1,0:T(8,128)(2,1)} %v_ref.3, f32[512,12]{1,0:T(8,128)S(1)} %get-tuple-element.43.cum_ref, f32[12,512]{1,0:T(8,128)S(1)} %bitcast.23), custom_call_target="tpu_custom_call" | custom-call | flops 1610612736 | bytes 9437184 | tf_op jit(solution)/shard_map/inside_blocks/pallas_call | solution.py:215
  41.6 7.3 %all-to-all-start.1 = ((bf16[32,48,128]{2,1,0:T(8,128)(2,1)}), bf16[32,48,128]{2,1,0:T(8,128)(2,1)S(1)}, u32[]{:S(2)}, u32[]{:S(2)}) async-start(bf16[32,48,128]{2,1,0:T(8,128)(2,1)} %scan_blocks.1), calls=%async_computation.1 | async-start | bytes 786432 | tf_op jit(solution)/shard_map/all_to_all | solution.py:644
  50.6 2.9 %collective-permute-start.1 = (bf16[8,6400]{1,0:T(8,128)(2,1)}, bf16[8,6400]{1,0:T(8,128)(2,1)S(1)}, u32[]{:S(2)}, u32[]{:S(2)}) collective-permute-start(bf16[8,6400]{1,0:T(8,128)(2,1)} %get-tuple-element.55), channel_id=1, source_target_pairs={{0,2},{1,3},{2,0},{3,1},{4,6},{5,7},{6,4},{7,5},{8,10},{9,11},{10,... | collective-permute-start | bytes 307208 | tf_op jit(solution)/shard_map/ppermute | solution.py:649
  55.5 3.4 %collective-permute-done.1.refs_2_ = bf16[8,6400]{1,0:T(8,128)(2,1)S(1)} collective-permute-done((bf16[8,6400]{1,0:T(8,128)(2,1)}, bf16[8,6400]{1,0:T(8,128)(2,1)S(1)}, u32[]{:S(2)}, u32[]{:S(2)}) %collective-permute-start.1) | collective-permute-done | bytes 102432 | tf_op jit(solution)/shard_map/ppermute | solution.py:649
  64.8 3.4 %carried_blocks.1 = (bf16[64,1536]{1,0:T(8,128)(2,1)}, bf16[128,1536]{1,0:T(8,128)(2,1)}, bf16[128,1536]{1,0:T(8,128)(2,1)}, bf16[128,1536]{1,0:T(8,128)(2,1)}, bf16[128,1536]{1,0:T(8,128)(2,1)}) custom-call(s32[1]{0:T(128)} %bitcast.me_ref, f32[512,1536]{1,0:T(8,128)S(1)} %get-tuple-element.50.inside_ref, bf16[512,1536]{1,0:T(8,128)(2,1)S(1)} %copy-done.1, ...), custom_call_target="tpu_custom_call" | custom-call | flops 402653184 | bytes 6291456 | tf_op jit(solution)/shard_map/carried_blocks/pallas_call | solution.py:262
  68.2 10.2 %all_to_all.35.att_ref = bf16[4,16,1536]{2,1,0:T(8,128)(2,1)S(1)} all-to-all(bf16[4,16,1536]{2,1,0:T(8,128)(2,1)} %bitcast.32), channel_id=1, replica_groups=mesh['z'=4,'x'=4,'core'=2,'exp'=4] {'exp'}, dimensions={0} | all-to-all | bytes 393216 | tf_op jit(solution)/shard_map/all_to_all | solution.py:644
  80.3 7.1 %all-to-all-start.3 = ((bf16[16,8,6144]{2,1,0:T(8,128)(2,1)}), bf16[16,8,6144]{2,1,0:T(8,128)(2,1)S(1)}, u32[]{:S(2)}, u32[]{:S(2)}) async-start(bf16[16,8,6144]{2,1,0:T(8,128)(2,1)} %get-tuple-element.58), calls=%async_computation.3 | async-start | bytes 3145728 | tf_op jit(solution)/shard_map/all_to_all | solution.py:644
  91.9 14.6 %collective-permute-done.3.refs_1_ = bf16[128,1536]{1,0:T(8,128)(2,1)S(1)} collective-permute-done((bf16[128,1536]{1,0:T(8,128)(2,1)}, bf16[128,1536]{1,0:T(8,128)(2,1)S(1)}, u32[]{:S(2)}, u32[]{:S(2)}) %collective-permute-start.3) | collective-permute-done | bytes 393248 | tf_op jit(solution)/shard_map/ppermute | solution.py:649
  109.3 3.4 %collective-permute-done.6.refs_1_ = bf16[128,6144]{1,0:T(8,128)(2,1)S(1)} collective-permute-done((bf16[128,6144]{1,0:T(8,128)(2,1)S(1)}, bf16[128,6144]{1,0:T(8,128)(2,1)S(1)}, u32[]{:S(2)}, u32[]{:S(2)}) %collective-permute-start.6) | collective-permute-done | bytes 1572896 | tf_op jit(solution)/shard_map/ppermute | solution.py:649
  112.7 4.3 %expert_act.2.act_ref = bf16[256,288]{1,0:T(8,128)(2,1)S(1)} custom-call(bf16[288,6144]{1,0:T(8,128)(2,1)} %bitcast.26, bf16[288,6144]{1,0:T(8,128)(2,1)} %bitcast.28, bf16[128,6144]{1,0:T(8,128)(2,1)S(1)} %bitcast.18, bf16[128,6144]{1,0:T(8,128)(2,1)S(1)} %collective-permute-done.6.refs_1_), custom_call_target="tpu_custom_call" | custom-call | flops 1811939328 | bytes 10223616 | tf_op jit(solution)/shard_map/expert_act/pallas_call | solution.py:506
  117.0 3.7 %expert_down.2 = (bf16[16,8,6144]{2,1,0:T(8,128)(2,1)S(1)}, bf16[16,8,6144]{2,1,0:T(8,128)(2,1)S(1)}) custom-call(s32[1]{0:T(128)} %bitcast.9.core_ref, bf16[256,288]{1,0:T(8,128)(2,1)S(1)} %expert_act.2.act_ref, bf16[288,6144]{1,0:T(8,128)(2,1)} %bitcast.30), custom_call_target="tpu_custom_call" | custom-call | flops 905969664 | bytes 6684672 | tf_op jit(solution)/shard_map/expert_down/pallas_call | solution.py:553
  120.9 3.3 %collective-permute-done.7.b_ref = bf16[16,8,6144]{2,1,0:T(8,128)(2,1)S(1)} collective-permute-done((bf16[16,8,6144]{2,1,0:T(8,128)(2,1)S(1)}, bf16[16,8,6144]{2,1,0:T(8,128)(2,1)S(1)}, u32[]{:S(2)}, u32[]{:S(2)}) %collective-permute-start.7) | collective-permute-done | bytes 1572896 | tf_op jit(solution)/shard_map/ppermute | solution.py:649
  126.2 4.6 %all-to-all-start.4 = ((bf16[16,8,6144]{2,1,0:T(8,128)(2,1)}), bf16[16,8,6144]{2,1,0:T(8,128)(2,1)S(1)}, u32[]{:S(2)}, u32[]{:S(2)}) async-start(bf16[16,8,6144]{2,1,0:T(8,128)(2,1)} %pair_sum.2), calls=%async_computation.4 | async-start | bytes 3145728 | tf_op jit(solution)/shard_map/all_to_all | solution.py:644
  130.8 9.4 %all-gather.3.cloned.1.call-done.refs_0_ = bf16[256,6144]{1,0:T(8,128)(2,1)} async-done(((bf16[8,6144]{1,0:T(8,128)(2,1)}), bf16[256,6144]{1,0:T(8,128)(2,1)}) %all-gather.3.cloned.1.call-update) | async-done | bytes 3145744 | tf_op jit(solution)/shard_map/all_gather | solution.py:698
  140.2 4.7 %expert_act.3.act_ref = bf16[256,288]{1,0:T(8,128)(2,1)S(1)} custom-call(bf16[288,6144]{1,0:T(8,128)(2,1)} %bitcast.27, bf16[288,6144]{1,0:T(8,128)(2,1)} %bitcast.29, bf16[256,6144]{1,0:T(8,128)(2,1)} %all-gather.3.cloned.1.call-done.refs_0_), custom_call_target="tpu_custom_call" | custom-call | flops 1811939328 | bytes 10223616 | tf_op jit(solution)/shard_map/expert_act/pallas_call | solution.py:506
  144.9 10.9 %all-to-all-done.4.one_ref = bf16[16,8,6144]{2,1,0:T(8,128)(2,1)S(1)} async-done(((bf16[16,8,6144]{2,1,0:T(8,128)(2,1)}), bf16[16,8,6144]{2,1,0:T(8,128)(2,1)S(1)}, u32[]{:S(2)}, u32[]{:S(2)}) %all-to-all-start.4) | async-done | bytes 1572896 | tf_op jit(solution)/shard_map/all_to_all | solution.py:644
  155.8 3.7 %expert_down.3 = (bf16[16,8,6144]{2,1,0:T(8,128)(2,1)S(1)}, bf16[16,8,6144]{2,1,0:T(8,128)(2,1)S(1)}) custom-call(s32[1]{0:T(128)} %bitcast.9.core_ref, bf16[256,288]{1,0:T(8,128)(2,1)S(1)} %expert_act.3.act_ref, bf16[288,6144]{1,0:T(8,128)(2,1)} %bitcast.31), custom_call_target="tpu_custom_call" | custom-call | flops 905969664 | bytes 6684672 | tf_op jit(solution)/shard_map/expert_down/pallas_call | solution.py:553
  159.7 3.4 %collective-permute-done.8.b_ref = bf16[16,8,6144]{2,1,0:T(8,128)(2,1)S(1)} collective-permute-done((bf16[16,8,6144]{2,1,0:T(8,128)(2,1)S(1)}, bf16[16,8,6144]{2,1,0:T(8,128)(2,1)S(1)}, u32[]{:S(2)}, u32[]{:S(2)}) %collective-permute-start.8) | collective-permute-done | bytes 1572896 | tf_op jit(solution)/shard_map/ppermute | solution.py:649
  165.1 27.1 %all_to_all.36.two_ref = bf16[16,8,6144]{2,1,0:T(8,128)(2,1)S(1)} all-to-all(bf16[16,8,6144]{2,1,0:T(8,128)(2,1)} %pair_sum.3), channel_id=1, replica_groups=mesh['z'=4,'x'=4,'core'=2,'exp'=4] {'z','x'}, dimensions={0} | all-to-all | bytes 3145728 | tf_op jit(solution)/shard_map/all_to_all | solution.py:644
  194.0 5.1 %all-to-all-start.6 = ((bf16[4,4,6144]{2,1,0:T(4,128)(2,1)}), bf16[4,4,6144]{2,1,0:T(4,128)(2,1)S(1)}, u32[]{:S(2)}, u32[]{:S(2)}) async-start(bf16[4,4,6144]{2,1,0:T(4,128)(2,1)} %chip_sum.1), calls=%async_computation.6 | async-start | bytes 393216 | tf_op jit(solution)/shard_map/all_to_all | solution.py:644
  199.4 4.9 %hidden_rows.1 = bf16[128,6144]{1,0:T(8,128)(2,1)} custom-call(s32[1]{0:T(128)} %bitcast.me_ref, bf16[128,6144]{1,0:T(8,128)(2,1)} %res_ref.3, bf16[128,6144]{1,0:T(8,128)(2,1)} %gate_ref.3, f32[1,6144]{1,0:T(1,128)S(1)} %bitcast.21, bf16[128,1536]{1,0:T(8,128)(2,1)S(1)} %copy-done.10, bf16[128,1536]{1,0:T(8,128)(2,1)S(1)} %collective-permute-done.3.refs_1_, ...), custom_call_target="tpu_custom_call" | custom-call | flops 15728640 | bytes 6291456 | tf_op jit(solution)/shard_map/hidden_rows/pallas_call | solution.py:447
  (71 shorter events, 31.8 us)
Async XLA Ops:
  7.9 14.2 %copy-start.18 = (s32[128,2]{0,1:T(2,128)S(1)}, s32[128,2]{0,1:T(2,128)}, u32[]{:S(2)}) copy-start(s32[128,2]{0,1:T(2,128)} %param.21) | copy-start | bytes 3076
  13.7 25.9 %all-to-all-start = ((bf16[32,64,128]{2,1,0:T(8,128)(2,1)}), bf16[32,64,128]{2,1,0:T(8,128)(2,1)}, u32[]{:S(2)}, u32[]{:S(2)}) async-start(bf16[32,64,128]{2,1,0:T(8,128)(2,1)} %get-tuple-element.42), calls=%async_computation | async-start | bytes 1048576 | tf_op jit(solution)/shard_map/all_to_all | solution.py:644
  41.6 21.0 %all-to-all-start.1 = ((bf16[32,48,128]{2,1,0:T(8,128)(2,1)}), bf16[32,48,128]{2,1,0:T(8,128)(2,1)S(1)}, u32[]{:S(2)}, u32[]{:S(2)}) async-start(bf16[32,48,128]{2,1,0:T(8,128)(2,1)} %scan_blocks.1), calls=%async_computation.1 | async-start | bytes 786432 | tf_op jit(solution)/shard_map/all_to_all | solution.py:644
  48.9 6.6 %collective-permute-start = (bf16[8,6400]{1,0:T(8,128)(2,1)}, bf16[8,6400]{1,0:T(8,128)(2,1)S(1)}, u32[]{:S(2)}, u32[]{:S(2)}) collective-permute-start(bf16[8,6400]{1,0:T(8,128)(2,1)} %get-tuple-element.54), channel_id=1, source_target_pairs={{0,1},{1,2},{2,3},{3,0},{4,5},{5,6},{6,7},{7,4},{8,9},{9,10},{10,1... | collective-permute-start | bytes 307208 | tf_op jit(solution)/shard_map/ppermute | solution.py:649
  50.6 8.3 %collective-permute-start.1 = (bf16[8,6400]{1,0:T(8,128)(2,1)}, bf16[8,6400]{1,0:T(8,128)(2,1)S(1)}, u32[]{:S(2)}, u32[]{:S(2)}) collective-permute-start(bf16[8,6400]{1,0:T(8,128)(2,1)} %get-tuple-element.55), channel_id=1, source_target_pairs={{0,2},{1,3},{2,0},{3,1},{4,6},{5,7},{6,4},{7,5},{8,10},{9,11},{10,... | collective-permute-start | bytes 307208 | tf_op jit(solution)/shard_map/ppermute | solution.py:649
  53.5 5.4 %collective-permute-start.2 = (bf16[8,6400]{1,0:T(8,128)(2,1)}, bf16[8,6400]{1,0:T(8,128)(2,1)S(1)}, u32[]{:S(2)}, u32[]{:S(2)}) collective-permute-start(bf16[8,6400]{1,0:T(8,128)(2,1)} %get-tuple-element.56), channel_id=1, source_target_pairs={{0,3},{1,0},{2,1},{3,2},{4,7},{5,4},{6,5},{7,6},{8,11},{9,8},{10,9... | collective-permute-start | bytes 307208 | tf_op jit(solution)/shard_map/ppermute | solution.py:649
  64.8 13.6 %copy-start.3 = (bf16[8,6400]{1,0:T(8,128)(2,1)S(1)}, bf16[8,6400]{1,0:T(8,128)(2,1)}, u32[]{:S(2)}) copy-start(bf16[8,6400]{1,0:T(8,128)(2,1)} %get-tuple-element.53.refs_0_) | copy-start | bytes 307204
  64.8 13.6 %copy-start.5 = (bf16[8,6400]{1,0:T(8,128)(2,1)S(1)}, bf16[8,6400]{1,0:T(8,128)(2,1)}, u32[]{:S(2)}) copy-start(bf16[8,6400]{1,0:T(8,128)(2,1)} %copy-done.4) | copy-start | bytes 307204
  64.8 13.6 %copy-start.7 = (bf16[8,6400]{1,0:T(8,128)(2,1)S(1)}, bf16[8,6400]{1,0:T(8,128)(2,1)}, u32[]{:S(2)}) copy-start(bf16[8,6400]{1,0:T(8,128)(2,1)} %copy-done.6) | copy-start | bytes 307204
  64.8 13.6 %copy-start.9 = (bf16[8,6400]{1,0:T(8,128)(2,1)S(1)}, bf16[8,6400]{1,0:T(8,128)(2,1)}, u32[]{:S(2)}) copy-start(bf16[8,6400]{1,0:T(8,128)(2,1)} %copy-done.8) | copy-start | bytes 307204
  64.8 13.6 %copy-start.13 = (f32[6144]{0:T(1024)S(1)}, f32[6144]{0:T(1024)}, u32[]{:S(2)}) copy-start(f32[6144]{0:T(1024)} %param.19) | copy-start | bytes 73732
  64.8 13.6 %copy-start.17 = (f32[6144]{0:T(1024)S(1)}, f32[6144]{0:T(1024)}, u32[]{:S(2)}) copy-start(f32[6144]{0:T(1024)} %param.20) | copy-start | bytes 73732
  80.3 8.5 %copy-start.21 = (bf16[128,1536]{1,0:T(8,128)(2,1)S(1)}, bf16[128,1536]{1,0:T(8,128)(2,1)}, u32[]{:S(2)}) copy-start(bf16[128,1536]{1,0:T(8,128)(2,1)} %get-tuple-element.66) | copy-start | bytes 1179652
  80.3 10.6 %copy-start.20 = (bf16[128,1536]{1,0:T(8,128)(2,1)S(1)}, bf16[128,1536]{1,0:T(8,128)(2,1)}, u32[]{:S(2)}) copy-start(bf16[128,1536]{1,0:T(8,128)(2,1)} %get-tuple-element.67) | copy-start | bytes 1179652
  80.3 28.9 %all-to-all-start.3 = ((bf16[16,8,6144]{2,1,0:T(8,128)(2,1)}), bf16[16,8,6144]{2,1,0:T(8,128)(2,1)S(1)}, u32[]{:S(2)}, u32[]{:S(2)}) async-start(bf16[16,8,6144]{2,1,0:T(8,128)(2,1)} %get-tuple-element.58), calls=%async_computation.3 | async-start | bytes 3145728 | tf_op jit(solution)/shard_map/all_to_all | solution.py:644
  87.5 52.7 %all-gather.3.cloned.1.call-start = ((), (), s32[]{:S(2)}) async-start(), calls=%async_computation.7 | async-start | bytes 3244032 | tf_op jit(solution)/shard_map/all_gather | solution.py:698
  88.2 18.3 %collective-permute-start.3 = (bf16[128,1536]{1,0:T(8,128)(2,1)}, bf16[128,1536]{1,0:T(8,128)(2,1)S(1)}, u32[]{:S(2)}, u32[]{:S(2)}) collective-permute-start(bf16[128,1536]{1,0:T(8,128)(2,1)} %get-tuple-element.65), channel_id=1, source_target_pairs={{0,1},{1,2},{2,3},{3,0},{4,5},{5,6},{6,7},{7,4},{8,9},{9,10},{10,1... | collective-permute-start | bytes 1179656 | tf_op jit(solution)/shard_map/ppermute | solution.py:649
  88.8 17.7 %collective-permute-start.4 = (bf16[128,1536]{1,0:T(8,128)(2,1)S(1)}, bf16[128,1536]{1,0:T(8,128)(2,1)S(1)}, u32[]{:S(2)}, u32[]{:S(2)}) collective-permute-start(bf16[128,1536]{1,0:T(8,128)(2,1)S(1)} %copy-done.21), channel_id=1, source_target_pairs={{0,2},{1,3},{2,0},{3,1},{4,6},{5,7},{6,4},{7,5},{8,10},{9,11},{10,... | collective-permute-start | bytes 1179656 | tf_op jit(solution)/shard_map/ppermute | solution.py:649
  90.9 16.0 %collective-permute-start.5 = (bf16[128,1536]{1,0:T(8,128)(2,1)S(1)}, bf16[128,1536]{1,0:T(8,128)(2,1)S(1)}, u32[]{:S(2)}, u32[]{:S(2)}) collective-permute-start(bf16[128,1536]{1,0:T(8,128)(2,1)S(1)} %copy-done.20), channel_id=1, source_target_pairs={{0,3},{1,0},{2,1},{3,2},{4,7},{5,4},{6,5},{7,6},{8,11},{9,8},{10,9... | collective-permute-start | bytes 1179656 | tf_op jit(solution)/shard_map/ppermute | solution.py:649
  109.3 3.4 %collective-permute-start.6 = (bf16[128,6144]{1,0:T(8,128)(2,1)S(1)}, bf16[128,6144]{1,0:T(8,128)(2,1)S(1)}, u32[]{:S(2)}, u32[]{:S(2)}) collective-permute-start(bf16[128,6144]{1,0:T(8,128)(2,1)S(1)} %bitcast.17), channel_id=1, source_target_pairs={{0,4},{4,0},{1,5},{5,1},{2,6},{6,2},{3,7},{7,3},{8,12},{12,8},{9,1... | collective-permute-start | bytes 4718600 | tf_op jit(solution)/shard_map/ppermute | solution.py:649
  120.7 3.5 %collective-permute-start.7 = (bf16[16,8,6144]{2,1,0:T(8,128)(2,1)S(1)}, bf16[16,8,6144]{2,1,0:T(8,128)(2,1)S(1)}, u32[]{:S(2)}, u32[]{:S(2)}) collective-permute-start(bf16[16,8,6144]{2,1,0:T(8,128)(2,1)S(1)} %get-tuple-element.75), channel_id=1, source_target_pairs={{0,4},{4,0},{1,5},{5,1},{2,6},{6,2},{3,7},{7,3},{8,12},{12,8},{9,1... | collective-permute-start | bytes 4718600 | tf_op jit(solution)/shard_map/ppermute | solution.py:649
  126.2 29.7 %all-to-all-start.4 = ((bf16[16,8,6144]{2,1,0:T(8,128)(2,1)}), bf16[16,8,6144]{2,1,0:T(8,128)(2,1)S(1)}, u32[]{:S(2)}, u32[]{:S(2)}) async-start(bf16[16,8,6144]{2,1,0:T(8,128)(2,1)} %pair_sum.2), calls=%async_computation.4 | async-start | bytes 3145728 | tf_op jit(solution)/shard_map/all_to_all | solution.py:644
  159.6 3.5 %collective-permute-start.8 = (bf16[16,8,6144]{2,1,0:T(8,128)(2,1)S(1)}, bf16[16,8,6144]{2,1,0:T(8,128)(2,1)S(1)}, u32[]{:S(2)}, u32[]{:S(2)}) collective-permute-start(bf16[16,8,6144]{2,1,0:T(8,128)(2,1)S(1)} %get-tuple-element.81), channel_id=1, source_target_pairs={{0,4},{4,0},{1,5},{5,1},{2,6},{6,2},{3,7},{7,3},{8,12},{12,8},{9,1... | collective-permute-start | bytes 4718600 | tf_op jit(solution)/shard_map/ppermute | solution.py:649
  194.0 11.5 %all-to-all-start.6 = ((bf16[4,4,6144]{2,1,0:T(4,128)(2,1)}), bf16[4,4,6144]{2,1,0:T(4,128)(2,1)S(1)}, u32[]{:S(2)}, u32[]{:S(2)}) async-start(bf16[4,4,6144]{2,1,0:T(4,128)(2,1)} %chip_sum.1), calls=%async_computation.6 | async-start | bytes 393216 | tf_op jit(solution)/shard_map/all_to_all | solution.py:644
  (13 other events, 33.5 us)
Sparse Core Ops, SparseCore 0:
  90.5 49.5 all-gather.2

commit v4 on v3

--- a/solution.py
+++ b/solution.py
@@ -178,7 +178,8 @@
         cumt_ref[...] = running_sum(ld_ref[...], 1)
 
     cum = spread(cum_ref[...], pl.program_id(0) * group, group, 3)
-    causal = iota((HEAD_DIM, HEAD_DIM), 0) >= iota((HEAD_DIM, HEAD_DIM), 1)
+    size = 2 * HEAD_DIM
+    causal = iota((size, size), 0) >= iota((size, size), 1)
     for j in range(group):
         h = pl.program_id(0) * group + j
         cols = slice(j * HEAD_DIM, (j + 1) * HEAD_DIM)
@@ -188,24 +189,24 @@
         k = k_ref[:, cols]
         v = v_ref[:, cols]
         qs_ref[:, cols] = (q.astype(F32) * jnp.exp(col)).astype(BF16)
-        for i in range(rows // HEAD_DIM):
-            lo, hi = i * HEAD_DIM, (i + 1) * HEAD_DIM
-            qi = q[lo:hi]
-            ci = col[lo:hi]
+        wide = jnp.concatenate([col, col], axis=1)
+        total = None
+        for lo in range(0, rows, size):
+            hi = lo + size
             s = lax.dot_general(
-                qi, k[lo:hi], (((1,), (1,)), ((), ())), preferred_element_type=F32
+                q[lo:], k[lo:hi], (((1,), (1,)), ((), ())), preferred_element_type=F32
             )
-            gap = jnp.minimum(ci - row[:, lo:hi], 0.0)
-            w = jnp.where(causal, s * jnp.exp(gap), 0.0).astype(BF16)
-            total = jnp.dot(w, v[lo:hi], preferred_element_type=F32)
-            if i:
-                s = lax.dot_general(
-                    qi, k[:lo], (((1,), (1,)), ((), ())), preferred_element_type=F32
-                )
-                gap = jnp.concatenate([ci] * i, axis=1) - row[:, :lo]
-                w = (s * jnp.exp(jnp.minimum(gap, 0.0))).astype(BF16)
-                total = total + jnp.dot(w, v[:lo], preferred_element_type=F32)
-            inside_ref[lo:hi, cols] = total
+            decay = jnp.exp(jnp.minimum(wide[lo:] - row[:, lo:hi], 0.0))
+            w = s * decay
+            w = jnp.concatenate([jnp.where(causal, w[:size], 0.0), w[size:]], axis=0) if (
+                hi < rows
+            ) else jnp.where(causal, w, 0.0)
+            part = jnp.dot(w.astype(BF16), v[lo:hi], preferred_element_type=F32)
+            if total is None:
+                total = part
+            else:
+                total = jnp.concatenate([total[:lo], total[lo:] + part], axis=0)
+        inside_ref[:, cols] = total
 
 
 def inside_blocks(q, k, v, cum, ld, group=3):
@@ -217,7 +218,7 @@
         grid=(heads // group,),
         out_shape=(
             jax.ShapeDtypeStruct((rows, width), F32),
-            jax.ShapeDtypeStruct((rows, width), BF16),
+            far((rows, width)),
         ),
         in_specs=[
             block,
@@ -280,9 +281,17 @@
     return outs[0], list(outs[1:])
 
 
-def route_kernel(me_ref, ids_ref, res_ref, gate_ref, *refs):
-    outs, place_ref = refs[:-1], refs[-1]
+def route_kernel(pieces, me_ref, ids_ref, res_hbm, gate_hbm, *refs):
+    outs, (place_ref, res_ref, gate_ref, sem) = refs[:-4], refs[-4:]
     held = len(outs)
+    size = res_ref.shape[0] // pieces
+    copies = []
+    for n, (a, b) in enumerate(((res_hbm, res_ref), (gate_hbm, gate_ref))):
+        for i in range(pieces):
+            at = pl.ds(i * size, size)
+            copies.append(pltpu.make_async_copy(a.at[at], b.at[at], sem.at[n, i]))
+    for c in copies:
+        c.start()
     tokens, width = res_ref.shape
     me = me_ref[0]
     ids = ids_ref[...]
@@ -298,6 +307,8 @@
     ]
     place = jnp.concatenate(places, axis=0)
     place_ref[...] = place
+    for c in copies:
+        c.wait()
     for d in range(held):
         expert = lax.rem(me + d, held)
         mine = places[0]
@@ -316,15 +327,21 @@
             ).astype(BF16)
 
 
-def route_rows(me, ids, residual, out_gate, held):
+def route_rows(me, ids, residual, out_gate, held, pieces=4):
     tokens, width = residual.shape
     whole = pl.BlockSpec(memory_space=pltpu.VMEM)
+    away = pl.BlockSpec(memory_space=pl.ANY)
     piece = far((2 * CAP, width + 2 * tokens))
     outs = pl.pallas_call(
-        route_kernel,
+        functools.partial(route_kernel, pieces),
         out_shape=(piece,) * held + (jax.ShapeDtypeStruct((held * CAP, tokens), F32),),
-        in_specs=[pl.BlockSpec(memory_space=pltpu.SMEM), whole, whole, whole],
+        in_specs=[pl.BlockSpec(memory_space=pltpu.SMEM), whole, away, away],
         out_specs=(whole,) * (held + 1),
+        scratch_shapes=[
+            pltpu.VMEM((tokens, width), BF16),
+            pltpu.VMEM((tokens, width), BF16),
+            pltpu.SemaphoreType.DMA((2, pieces)),
+        ],
         compiler_params=params(),
         cost_estimate=cost(64 * tokens * width, 5 * tokens * width),
         name="route_rows",
@@ -377,7 +394,7 @@
     return pl.pallas_call(
         place_kernel,
         grid=(1,),
-        out_shape=jax.ShapeDtypeStruct((held * held * CAP, held * tokens), BF16),
+        out_shape=far((held * held * CAP, held * tokens)),
         in_specs=[pl.BlockSpec(memory_space=pltpu.SMEM)]
         + [pl.BlockSpec((2 * CAP, 2 * tokens), lambda i: (0, at))] * held,
         out_specs=pl.BlockSpec((held * held * CAP, held * tokens), lambda i: (0, 0)),
@@ -674,7 +691,7 @@
     w_up = jnp.swapaxes(w_up, 1, 2)[0]
     w_down = w_down[0]
     ids = expert_ids.T
-    ld = log_decay.T
+    ld = hbm(log_decay.T)
     me = lax.axis_index("exp").reshape(1)
     core = lax.axis_index("core").reshape(1)
     keep = lax.optimization_barrier
@@ -685,12 +702,13 @@
     inside, qs = inside_blocks(hbm(queries), hbm(key_vectors), hbm(values), cum, ld)
     pieces, place_own = route_rows(me, ids, hbm(residual), hbm(out_gate), held)
     sent, inside, qs, pieces = keep((sent, inside, qs, pieces))
-    prior = scan_blocks(sent, lax.axis_index(CTX))
+    prior = scan_blocks(hbm(sent), lax.axis_index(CTX))
     state = exchange(prior, CTX).reshape(heads, HEAD_DIM, HEAD_DIM)
     pieces = [pieces[0]] + [shift(pieces[d], "exp", d) for d in range(1, held)]
+    pieces = [hbm(a) for a in pieces]
     place = place_rows(me, pieces, tokens)
 
-    routed, attention = carried_blocks(me, inside, qs, state, place, held)
+    routed, attention = carried_blocks(me, inside, hbm(qs), state, hbm(place), held)
     routed = exchange(routed.reshape(held, held * CAP, width), "exp")
     one, two = routed_norm(me, routed, pieces, attn_gain, moe_gain, chips)
 
@@ -707,8 +725,8 @@
     _, two = keep((one, two))
     one = exchange(one, ("z", "x"))
     act = expert_act((two,), w_gate, w_up)
-    one, act = keep((one, act))
     own, other = expert_down(core, act, w_down, True)
+    one, other = keep((one, other))
     two = exchange(pair_sum(own, shift(other, "core", 1)), ("z", "x"))
     hidden = hidden_rows(me, attention, hbm(residual), hbm(out_gate), attn_gain)
     back = exchange(chip_sum(one, two, held), "exp")

time: 215 us -> 203 us (0.944)
  local copies, waits for them, and re-layouts: 7.86 us -> 2.69 us
  waiting for transfers between devices: 53.7 us -> 49.2 us
    unnamed x46 -> x34, local copies, waits for them, and re-layouts: 7.86 us -> 2.69 us
    pallas_call x1, Pallas kernels: 11.9 us -> 7.81 us  [inside_blocks(): pl.pallas_call(functools.partial(inside_kernel, group), grid=(heads // gr...]
    all_to_all x5, waiting for transfers between devices: 14.4 us -> 10.9 us  [exchange(): return lax.all_to_all(a, axis, split_axis=0, concat_axis=0, tiled=True)]
  transfers between devices with their start and end apart: 15 -> 15, of which waited for: 11 -> 11; matrix products, arithmetic and copies ran while one was open for 0% -> 0% of each run, Pallas kernels for 17% -> 18%
where the time goes in v4:
time: 203 us; the launch traced here: 202 us
  Pallas kernels  58 us (29%)
  waiting for transfers between devices  49.2 us (24%)
  starting transfers between devices  41.5 us (20%)
  blocking collectives  36.8 us (18%)
  between operations  14.2 us (7%)
  local copies, waits for them, and re-layouts  2.69 us (1%)
    all_to_all x2, blocking collectives, exchange(): return lax.all_to_all(a, axis, split_axis=0, concat_axis=0, tiled=True)  36.8 us
    all_to_all x5, starting transfers between devices, exchange(): return lax.all_to_all(a, axis, split_axis=0, concat_axis=0, tiled=True)  31.6 us
    ppermute x9, waiting for transfers between devices, shift(): return lax.ppermute(a, axis, [(i, (i + by) % n) for i in range(n)])  29.9 us
    all_to_all x5, waiting for transfers between devices, exchange(): return lax.all_to_all(a, axis, split_axis=0, concat_axis=0, tiled=True)  10.9 us
    ppermute x9, starting transfers between devices, shift(): return lax.ppermute(a, axis, [(i, (i + by) % n) for i in range(n)])  9.8 us
    pallas_call x2, Pallas kernels, expert_act(): pl.pallas_call(functools.partial(act_kernel, steps, streamed), out_shape=...  8.98 us
    pallas_call x1, Pallas kernels, inside_blocks(): pl.pallas_call(functools.partial(inside_kernel, group), grid=(heads // gr...  7.81 us
    all_gather x1, waiting for transfers between devices, local(): lax.all_gather(two, CTX, axis=0).reshape(32 * two.shape[0], two.shape[1])  7.64 us
  transfers between devices with their start and end apart: 15, of which 11 were waited for; matrix products, arithmetic and copies ran while one was open for 0% of the time, Pallas kernels for 18%

profile of v4, /device:TPU:0, one launch (start us, length us, event | category | flops | bytes accessed | tf_op | source)
XLA Modules:
  0.0 202.3 jit_solution(16114298128312107028)
XLA Ops:
  7.2 5.8 %local_states.1 = (f32[512,12]{1,0:T(8,128)S(1)}, bf16[32,64,128]{2,1,0:T(8,128)(2,1)}) custom-call(bf16[512,1536]{1,0:T(8,128)(2,1)} %k_ref.3, bf16[512,1536]{1,0:T(8,128)(2,1)} %v_ref.3, f32[12,512]{1,0:T(8,128)} %bitcast.31), custom_call_target="tpu_custom_call" | custom-call | flops 201326592 | bytes 3145728 | tf_op jit(solution)/shard_map/local_states/pallas_call | solution.py:122
  13.0 8.4 %all-to-all-start = ((bf16[32,64,128]{2,1,0:T(8,128)(2,1)}), bf16[32,64,128]{2,1,0:T(8,128)(2,1)}, u32[]{:S(2)}, u32[]{:S(2)}) async-start(bf16[32,64,128]{2,1,0:T(8,128)(2,1)} %get-tuple-element.42), calls=%async_computation | async-start | bytes 1048576 | tf_op jit(solution)/shard_map/all_to_all | solution.py:661
  21.4 4.3 %route_rows.1 = (bf16[8,6400]{1,0:T(8,128)(2,1)}, bf16[8,6400]{1,0:T(8,128)(2,1)}, bf16[8,6400]{1,0:T(8,128)(2,1)}, bf16[8,6400]{1,0:T(8,128)(2,1)}, f32[16,128]{1,0:T(8,128)S(1)}) custom-call(s32[1]{0:T(128)} %bitcast.me_ref, s32[2,128]{1,0:T(2,128)S(1)} %bitcast.23, bf16[128,6144]{1,0:T(8,128)(2,1)} %res_ref.1, bf16[128,6144]{1,0:T(8,128)(2,1)} %gate_ref.1), custom_call_target="tpu_custom_call" | custom-call | flops 50331648 | bytes 3932160 | tf_op jit(solution)/shard_map/route_rows/pallas_call | solution.py:335
  25.7 7.8 %inside_blocks.1 = (f32[512,1536]{1,0:T(8,128)S(1)}, bf16[512,1536]{1,0:T(8,128)(2,1)}) custom-call(bf16[512,1536]{1,0:T(8,128)(2,1)} %q_ref.1, bf16[512,1536]{1,0:T(8,128)(2,1)} %k_ref.3, bf16[512,1536]{1,0:T(8,128)(2,1)} %v_ref.3, f32[512,12]{1,0:T(8,128)S(1)} %get-tuple-element.43.cum_ref, f32[12,512]{1,0:T(8,128)} %bitcast.32), custom_call_target="tpu_custom_call" | custom-call | flops 1610612736 | bytes 9437184 | tf_op jit(solution)/shard_map/inside_blocks/pallas_call | solution.py:216
  35.5 7.3 %all-to-all-start.1 = ((bf16[32,48,128]{2,1,0:T(8,128)(2,1)}), bf16[32,48,128]{2,1,0:T(8,128)(2,1)S(1)}, u32[]{:S(2)}, u32[]{:S(2)}) async-start(bf16[32,48,128]{2,1,0:T(8,128)(2,1)} %scan_blocks.1), calls=%async_computation.1 | async-start | bytes 786432 | tf_op jit(solution)/shard_map/all_to_all | solution.py:661
  49.4 3.4 %collective-permute-done.1.refs_2_ = bf16[8,6400]{1,0:T(8,128)(2,1)S(1)} collective-permute-done((bf16[8,6400]{1,0:T(8,128)(2,1)}, bf16[8,6400]{1,0:T(8,128)(2,1)S(1)}, u32[]{:S(2)}, u32[]{:S(2)}) %collective-permute-start.1) | collective-permute-done | bytes 102432 | tf_op jit(solution)/shard_map/ppermute | solution.py:666
  55.6 4.6 %carried_blocks.1 = (bf16[64,1536]{1,0:T(8,128)(2,1)}, bf16[128,1536]{1,0:T(8,128)(2,1)}, bf16[128,1536]{1,0:T(8,128)(2,1)}, bf16[128,1536]{1,0:T(8,128)(2,1)}, bf16[128,1536]{1,0:T(8,128)(2,1)}) custom-call(s32[1]{0:T(128)} %bitcast.me_ref, f32[512,1536]{1,0:T(8,128)S(1)} %get-tuple-element.50.inside_ref, bf16[512,1536]{1,0:T(8,128)(2,1)} %get-tuple-element.51.qs_ref, ...), custom_call_target="tpu_custom_call" | custom-call | flops 402653184 | bytes 6291456 | tf_op jit(solution)/shard_map/carried_blocks/pallas_call | solution.py:263
  60.2 9.7 %all_to_all.35.att_ref = bf16[4,16,1536]{2,1,0:T(8,128)(2,1)S(1)} all-to-all(bf16[4,16,1536]{2,1,0:T(8,128)(2,1)} %bitcast.30), channel_id=1, replica_groups=mesh['z'=4,'x'=4,'core'=2,'exp'=4] {'exp'}, dimensions={0} | all-to-all | bytes 393216 | tf_op jit(solution)/shard_map/all_to_all | solution.py:661
  69.9 3.0 %routed_norm.1 = (bf16[16,8,6144]{2,1,0:T(8,128)(2,1)}, bf16[8,6144]{1,0:T(8,128)(2,1)}) custom-call(s32[1]{0:T(128)} %bitcast.me_ref, bf16[4,16,1536]{2,1,0:T(8,128)(2,1)S(1)} %all_to_all.35.att_ref, f32[1,6144]{1,0:T(1,128)S(1)} %bitcast.20, f32[1,6144]{1,0:T(1,128)S(1)} %bitcast.22, bf16[8,6400]{1,0:T(8,128)(2,1)} %get-tuple-element.53.refs_0_, ...), custom_call_target="tpu_custom_call" | custom-call | flops 1966080 | bytes 1966080 | tf_op jit(solution)/shard_map/routed_norm/pallas_call | solution.py:441
  72.9 7.1 %all-to-all-start.3 = ((bf16[16,8,6144]{2,1,0:T(8,128)(2,1)}), bf16[16,8,6144]{2,1,0:T(8,128)(2,1)S(1)}, u32[]{:S(2)}, u32[]{:S(2)}) async-start(bf16[16,8,6144]{2,1,0:T(8,128)(2,1)} %get-tuple-element.58), calls=%async_computation.3 | async-start | bytes 3145728 | tf_op jit(solution)/shard_map/all_to_all | solution.py:661
  84.5 15.1 %collective-permute-done.3.refs_1_ = bf16[128,1536]{1,0:T(8,128)(2,1)S(1)} collective-permute-done((bf16[128,1536]{1,0:T(8,128)(2,1)}, bf16[128,1536]{1,0:T(8,128)(2,1)S(1)}, u32[]{:S(2)}, u32[]{:S(2)}) %collective-permute-start.3) | collective-permute-done | bytes 393248 | tf_op jit(solution)/shard_map/ppermute | solution.py:666
  102.0 3.4 %collective-permute-done.6.refs_1_ = bf16[128,6144]{1,0:T(8,128)(2,1)S(1)} collective-permute-done((bf16[128,6144]{1,0:T(8,128)(2,1)S(1)}, bf16[128,6144]{1,0:T(8,128)(2,1)S(1)}, u32[]{:S(2)}, u32[]{:S(2)}) %collective-permute-start.6) | collective-permute-done | bytes 1572896 | tf_op jit(solution)/shard_map/ppermute | solution.py:666
  105.4 4.3 %expert_act.2.act_ref = bf16[256,288]{1,0:T(8,128)(2,1)S(1)} custom-call(bf16[288,6144]{1,0:T(8,128)(2,1)} %bitcast.24, bf16[288,6144]{1,0:T(8,128)(2,1)} %bitcast.26, bf16[128,6144]{1,0:T(8,128)(2,1)S(1)} %bitcast.18, bf16[128,6144]{1,0:T(8,128)(2,1)S(1)} %collective-permute-done.6.refs_1_), custom_call_target="tpu_custom_call" | custom-call | flops 1811939328 | bytes 10223616 | tf_op jit(solution)/shard_map/expert_act/pallas_call | solution.py:523
  109.7 3.7 %expert_down.2 = (bf16[16,8,6144]{2,1,0:T(8,128)(2,1)S(1)}, bf16[16,8,6144]{2,1,0:T(8,128)(2,1)S(1)}) custom-call(s32[1]{0:T(128)} %bitcast.9.core_ref, bf16[256,288]{1,0:T(8,128)(2,1)S(1)} %expert_act.2.act_ref, bf16[288,6144]{1,0:T(8,128)(2,1)} %bitcast.28), custom_call_target="tpu_custom_call" | custom-call | flops 905969664 | bytes 6684672 | tf_op jit(solution)/shard_map/expert_down/pallas_call | solution.py:570
  113.7 3.3 %collective-permute-done.7.b_ref = bf16[16,8,6144]{2,1,0:T(8,128)(2,1)S(1)} collective-permute-done((bf16[16,8,6144]{2,1,0:T(8,128)(2,1)S(1)}, bf16[16,8,6144]{2,1,0:T(8,128)(2,1)S(1)}, u32[]{:S(2)}, u32[]{:S(2)}) %collective-permute-start.7) | collective-permute-done | bytes 1572896 | tf_op jit(solution)/shard_map/ppermute | solution.py:666
  118.9 4.9 %all-to-all-start.4 = ((bf16[16,8,6144]{2,1,0:T(8,128)(2,1)}), bf16[16,8,6144]{2,1,0:T(8,128)(2,1)S(1)}, u32[]{:S(2)}, u32[]{:S(2)}) async-start(bf16[16,8,6144]{2,1,0:T(8,128)(2,1)} %pair_sum.2), calls=%async_computation.4 | async-start | bytes 3145728 | tf_op jit(solution)/shard_map/all_to_all | solution.py:661
  123.9 7.6 %all-gather.3.cloned.1.call-done.refs_0_ = bf16[256,6144]{1,0:T(8,128)(2,1)} async-done(((bf16[8,6144]{1,0:T(8,128)(2,1)}), bf16[256,6144]{1,0:T(8,128)(2,1)}) %all-gather.3.cloned.1.call-update) | async-done | bytes 3145744 | tf_op jit(solution)/shard_map/all_gather | solution.py:716
  131.5 4.7 %expert_act.3.act_ref = bf16[256,288]{1,0:T(8,128)(2,1)S(1)} custom-call(bf16[288,6144]{1,0:T(8,128)(2,1)} %bitcast.25, bf16[288,6144]{1,0:T(8,128)(2,1)} %bitcast.27, bf16[256,6144]{1,0:T(8,128)(2,1)} %all-gather.3.cloned.1.call-done.refs_0_), custom_call_target="tpu_custom_call" | custom-call | flops 1811939328 | bytes 10223616 | tf_op jit(solution)/shard_map/expert_act/pallas_call | solution.py:523
  136.2 3.8 %expert_down.3 = (bf16[16,8,6144]{2,1,0:T(8,128)(2,1)S(1)}, bf16[16,8,6144]{2,1,0:T(8,128)(2,1)S(1)}) custom-call(s32[1]{0:T(128)} %bitcast.9.core_ref, bf16[256,288]{1,0:T(8,128)(2,1)S(1)} %expert_act.3.act_ref, bf16[288,6144]{1,0:T(8,128)(2,1)} %bitcast.29), custom_call_target="tpu_custom_call" | custom-call | flops 905969664 | bytes 6684672 | tf_op jit(solution)/shard_map/expert_down/pallas_call | solution.py:570
  141.1 7.8 %all-to-all-done.4.one_ref = bf16[16,8,6144]{2,1,0:T(8,128)(2,1)S(1)} async-done(((bf16[16,8,6144]{2,1,0:T(8,128)(2,1)}), bf16[16,8,6144]{2,1,0:T(8,128)(2,1)S(1)}, u32[]{:S(2)}, u32[]{:S(2)}) %all-to-all-start.4) | async-done | bytes 1572896 | tf_op jit(solution)/shard_map/all_to_all | solution.py:661
  148.9 3.6 %collective-permute-done.8.b_ref = bf16[16,8,6144]{2,1,0:T(8,128)(2,1)S(1)} collective-permute-done((bf16[16,8,6144]{2,1,0:T(8,128)(2,1)}, bf16[16,8,6144]{2,1,0:T(8,128)(2,1)S(1)}, u32[]{:S(2)}, u32[]{:S(2)}) %collective-permute-start.8) | collective-permute-done | bytes 1572896 | tf_op jit(solution)/shard_map/ppermute | solution.py:666
  154.5 27.1 %all_to_all.36.two_ref = bf16[16,8,6144]{2,1,0:T(8,128)(2,1)S(1)} all-to-all(bf16[16,8,6144]{2,1,0:T(8,128)(2,1)} %pair_sum.3), channel_id=1, replica_groups=mesh['z'=4,'x'=4,'core'=2,'exp'=4] {'z','x'}, dimensions={0} | all-to-all | bytes 3145728 | tf_op jit(solution)/shard_map/all_to_all | solution.py:661
  183.5 3.9 %all-to-all-start.6 = ((bf16[4,4,6144]{2,1,0:T(4,128)(2,1)}), bf16[4,4,6144]{2,1,0:T(4,128)(2,1)S(1)}, u32[]{:S(2)}, u32[]{:S(2)}) async-start(bf16[4,4,6144]{2,1,0:T(4,128)(2,1)} %chip_sum.1), calls=%async_computation.6 | async-start | bytes 393216 | tf_op jit(solution)/shard_map/all_to_all | solution.py:661
  187.7 5.0 %hidden_rows.1 = bf16[128,6144]{1,0:T(8,128)(2,1)} custom-call(s32[1]{0:T(128)} %bitcast.me_ref, bf16[128,6144]{1,0:T(8,128)(2,1)} %res_ref.1, bf16[128,6144]{1,0:T(8,128)(2,1)} %gate_ref.1, f32[1,6144]{1,0:T(1,128)S(1)} %bitcast.21, bf16[128,1536]{1,0:T(8,128)(2,1)S(1)} %copy-done, bf16[128,1536]{1,0:T(8,128)(2,1)S(1)} %collective-permute-done.3.refs_1_, ...), custom_call_target="tpu_custom_call" | custom-call | flops 15728640 | bytes 6291456 | tf_op jit(solution)/shard_map/hidden_rows/pallas_call | solution.py:464
  (59 shorter events, 28.5 us)
Async XLA Ops:
  7.2 14.2 %copy-start.8 = (s32[128,2]{0,1:T(2,128)S(1)}, s32[128,2]{0,1:T(2,128)}, u32[]{:S(2)}) copy-start(s32[128,2]{0,1:T(2,128)} %param.21) | copy-start | bytes 3076
  13.0 20.6 %all-to-all-start = ((bf16[32,64,128]{2,1,0:T(8,128)(2,1)}), bf16[32,64,128]{2,1,0:T(8,128)(2,1)}, u32[]{:S(2)}, u32[]{:S(2)}) async-start(bf16[32,64,128]{2,1,0:T(8,128)(2,1)} %get-tuple-element.42), calls=%async_computation | async-start | bytes 1048576 | tf_op jit(solution)/shard_map/all_to_all | solution.py:661
  35.5 20.1 %all-to-all-start.1 = ((bf16[32,48,128]{2,1,0:T(8,128)(2,1)}), bf16[32,48,128]{2,1,0:T(8,128)(2,1)S(1)}, u32[]{:S(2)}, u32[]{:S(2)}) async-start(bf16[32,48,128]{2,1,0:T(8,128)(2,1)} %scan_blocks.1), calls=%async_computation.1 | async-start | bytes 786432 | tf_op jit(solution)/shard_map/all_to_all | solution.py:661
  42.8 6.6 %collective-permute-start = (bf16[8,6400]{1,0:T(8,128)(2,1)}, bf16[8,6400]{1,0:T(8,128)(2,1)S(1)}, u32[]{:S(2)}, u32[]{:S(2)}) collective-permute-start(bf16[8,6400]{1,0:T(8,128)(2,1)} %get-tuple-element.54), channel_id=1, source_target_pairs={{0,1},{1,2},{2,3},{3,0},{4,5},{5,6},{6,7},{7,4},{8,9},{9,10},{10,1... | collective-permute-start | bytes 307208 | tf_op jit(solution)/shard_map/ppermute | solution.py:666
  44.4 8.3 %collective-permute-start.1 = (bf16[8,6400]{1,0:T(8,128)(2,1)}, bf16[8,6400]{1,0:T(8,128)(2,1)S(1)}, u32[]{:S(2)}, u32[]{:S(2)}) collective-permute-start(bf16[8,6400]{1,0:T(8,128)(2,1)} %get-tuple-element.55), channel_id=1, source_target_pairs={{0,2},{1,3},{2,0},{3,1},{4,6},{5,7},{6,4},{7,5},{8,10},{9,11},{10,... | collective-permute-start | bytes 307208 | tf_op jit(solution)/shard_map/ppermute | solution.py:666
  47.3 5.4 %collective-permute-start.2 = (bf16[8,6400]{1,0:T(8,128)(2,1)}, bf16[8,6400]{1,0:T(8,128)(2,1)S(1)}, u32[]{:S(2)}, u32[]{:S(2)}) collective-permute-start(bf16[8,6400]{1,0:T(8,128)(2,1)} %get-tuple-element.56), channel_id=1, source_target_pairs={{0,3},{1,0},{2,1},{3,2},{4,7},{5,4},{6,5},{7,6},{8,11},{9,8},{10,9... | collective-permute-start | bytes 307208 | tf_op jit(solution)/shard_map/ppermute | solution.py:666
  55.6 14.3 %copy-start.5 = (f32[6144]{0:T(1024)S(1)}, f32[6144]{0:T(1024)}, u32[]{:S(2)}) copy-start(f32[6144]{0:T(1024)} %param.19) | copy-start | bytes 73732
  55.6 14.3 %copy-start.7 = (f32[6144]{0:T(1024)S(1)}, f32[6144]{0:T(1024)}, u32[]{:S(2)}) copy-start(f32[6144]{0:T(1024)} %param.20) | copy-start | bytes 73732
  72.9 8.5 %copy-start.15 = (bf16[128,1536]{1,0:T(8,128)(2,1)S(1)}, bf16[128,1536]{1,0:T(8,128)(2,1)}, u32[]{:S(2)}) copy-start(bf16[128,1536]{1,0:T(8,128)(2,1)} %get-tuple-element.66) | copy-start | bytes 1179652
  72.9 10.6 %copy-start.14 = (bf16[128,1536]{1,0:T(8,128)(2,1)S(1)}, bf16[128,1536]{1,0:T(8,128)(2,1)}, u32[]{:S(2)}) copy-start(bf16[128,1536]{1,0:T(8,128)(2,1)} %get-tuple-element.67) | copy-start | bytes 1179652
  72.9 29.1 %all-to-all-start.3 = ((bf16[16,8,6144]{2,1,0:T(8,128)(2,1)}), bf16[16,8,6144]{2,1,0:T(8,128)(2,1)S(1)}, u32[]{:S(2)}, u32[]{:S(2)}) async-start(bf16[16,8,6144]{2,1,0:T(8,128)(2,1)} %get-tuple-element.58), calls=%async_computation.3 | async-start | bytes 3145728 | tf_op jit(solution)/shard_map/all_to_all | solution.py:661
  80.0 51.5 %all-gather.3.cloned.1.call-start = ((), (), s32[]{:S(2)}) async-start(), calls=%async_computation.7 | async-start | bytes 3244032 | tf_op jit(solution)/shard_map/all_gather | solution.py:716
  80.7 18.8 %collective-permute-start.3 = (bf16[128,1536]{1,0:T(8,128)(2,1)}, bf16[128,1536]{1,0:T(8,128)(2,1)S(1)}, u32[]{:S(2)}, u32[]{:S(2)}) collective-permute-start(bf16[128,1536]{1,0:T(8,128)(2,1)} %get-tuple-element.65), channel_id=1, source_target_pairs={{0,1},{1,2},{2,3},{3,0},{4,5},{5,6},{6,7},{7,4},{8,9},{9,10},{10,1... | collective-permute-start | bytes 1179656 | tf_op jit(solution)/shard_map/ppermute | solution.py:666
  81.4 18.2 %collective-permute-start.4 = (bf16[128,1536]{1,0:T(8,128)(2,1)S(1)}, bf16[128,1536]{1,0:T(8,128)(2,1)S(1)}, u32[]{:S(2)}, u32[]{:S(2)}) collective-permute-start(bf16[128,1536]{1,0:T(8,128)(2,1)S(1)} %copy-done.15), channel_id=1, source_target_pairs={{0,2},{1,3},{2,0},{3,1},{4,6},{5,7},{6,4},{7,5},{8,10},{9,11},{10,... | collective-permute-start | bytes 1179656 | tf_op jit(solution)/shard_map/ppermute | solution.py:666
  83.5 16.5 %collective-permute-start.5 = (bf16[128,1536]{1,0:T(8,128)(2,1)S(1)}, bf16[128,1536]{1,0:T(8,128)(2,1)S(1)}, u32[]{:S(2)}, u32[]{:S(2)}) collective-permute-start(bf16[128,1536]{1,0:T(8,128)(2,1)S(1)} %copy-done.14), channel_id=1, source_target_pairs={{0,3},{1,0},{2,1},{3,2},{4,7},{5,4},{6,5},{7,6},{8,11},{9,8},{10,9... | collective-permute-start | bytes 1179656 | tf_op jit(solution)/shard_map/ppermute | solution.py:666
  99.6 10.1 %copy-start.1 = (bf16[128,1536]{1,0:T(8,128)(2,1)}, bf16[128,1536]{1,0:T(8,128)(2,1)S(1)}, u32[]{:S(2)}) copy-start(bf16[128,1536]{1,0:T(8,128)(2,1)S(1)} %collective-permute-done.4.refs_2_) | copy-start | bytes 1179652
  100.0 9.7 %copy-start.3 = (bf16[128,1536]{1,0:T(8,128)(2,1)}, bf16[128,1536]{1,0:T(8,128)(2,1)S(1)}, u32[]{:S(2)}) copy-start(bf16[128,1536]{1,0:T(8,128)(2,1)S(1)} %collective-permute-done.5.refs_3_) | copy-start | bytes 1179652
  102.0 3.4 %collective-permute-start.6 = (bf16[128,6144]{1,0:T(8,128)(2,1)S(1)}, bf16[128,6144]{1,0:T(8,128)(2,1)S(1)}, u32[]{:S(2)}, u32[]{:S(2)}) collective-permute-start(bf16[128,6144]{1,0:T(8,128)(2,1)S(1)} %bitcast.17), channel_id=1, source_target_pairs={{0,4},{4,0},{1,5},{5,1},{2,6},{6,2},{3,7},{7,3},{8,12},{12,8},{9,1... | collective-permute-start | bytes 4718600 | tf_op jit(solution)/shard_map/ppermute | solution.py:666
  113.5 3.5 %collective-permute-start.7 = (bf16[16,8,6144]{2,1,0:T(8,128)(2,1)S(1)}, bf16[16,8,6144]{2,1,0:T(8,128)(2,1)S(1)}, u32[]{:S(2)}, u32[]{:S(2)}) collective-permute-start(bf16[16,8,6144]{2,1,0:T(8,128)(2,1)S(1)} %get-tuple-element.75), channel_id=1, source_target_pairs={{0,4},{4,0},{1,5},{5,1},{2,6},{6,2},{3,7},{7,3},{8,12},{12,8},{9,1... | collective-permute-start | bytes 4718600 | tf_op jit(solution)/shard_map/ppermute | solution.py:666
  118.9 30.0 %all-to-all-start.4 = ((bf16[16,8,6144]{2,1,0:T(8,128)(2,1)}), bf16[16,8,6144]{2,1,0:T(8,128)(2,1)S(1)}, u32[]{:S(2)}, u32[]{:S(2)}) async-start(bf16[16,8,6144]{2,1,0:T(8,128)(2,1)} %pair_sum.2), calls=%async_computation.4 | async-start | bytes 3145728 | tf_op jit(solution)/shard_map/all_to_all | solution.py:661
  148.9 3.6 %collective-permute-start.8 = (bf16[16,8,6144]{2,1,0:T(8,128)(2,1)}, bf16[16,8,6144]{2,1,0:T(8,128)(2,1)S(1)}, u32[]{:S(2)}, u32[]{:S(2)}) collective-permute-start(bf16[16,8,6144]{2,1,0:T(8,128)(2,1)} %copy-done.9), channel_id=1, source_target_pairs={{0,4},{4,0},{1,5},{5,1},{2,6},{6,2},{3,7},{7,3},{8,12},{12,8},{9,1... | collective-permute-start | bytes 4718600 | tf_op jit(solution)/shard_map/ppermute | solution.py:666
  181.6 6.0 %copy-start.4 = (bf16[128,1536]{1,0:T(8,128)(2,1)S(1)}, bf16[128,1536]{1,0:T(8,128)(2,1)}, u32[]{:S(2)}) copy-start(bf16[128,1536]{1,0:T(8,128)(2,1)} %copy-done.3) | copy-start | bytes 1179652
  181.6 6.0 %copy-start.6 = (f32[6144]{0:T(1024)S(1)}, f32[6144]{0:T(1024)}, u32[]{:S(2)}) copy-start(f32[6144]{0:T(1024)} %param.19) | copy-start | bytes 73732
  183.5 10.2 %all-to-all-start.6 = ((bf16[4,4,6144]{2,1,0:T(4,128)(2,1)}), bf16[4,4,6144]{2,1,0:T(4,128)(2,1)S(1)}, u32[]{:S(2)}, u32[]{:S(2)}) async-start(bf16[4,4,6144]{2,1,0:T(4,128)(2,1)} %chip_sum.1), calls=%async_computation.6 | async-start | bytes 393216 | tf_op jit(solution)/shard_map/all_to_all | solution.py:661
  (7 other events, 23.7 us)
Sparse Core Ops, SparseCore 0:
  83.1 48.3 all-gather.2

commit v5 on v4

--- a/solution.py
+++ b/solution.py
@@ -479,32 +479,26 @@
     )(me, residual, out_gate, attn_gain, *pieces)
 
 
-def act_kernel(steps, streamed, wg_hbm, wu_hbm, *refs):
-    count = len(refs) - 4
-    xs, (act_ref, w_ref, x_ref, sem) = refs[:count], refs[count:]
+def act_kernel(steps, wg_hbm, wu_hbm, *refs):
+    xs, (act_ref, w_ref, sem) = refs[:-3], refs[-3:]
     units, width = wg_hbm.shape
     nt = (((1,), (1,)), ((), ()))
     wide = width // steps
     copies = []
     for s in range(steps):
         cols = pl.ds(s * wide, wide)
-        pairs = [(wg_hbm.at[:, cols], w_ref.at[0, :, cols]), (wu_hbm.at[:, cols], w_ref.at[1, :, cols])]
-        if streamed:
-            pairs.append((xs[0].at[:, cols], x_ref.at[:, cols]))
-        copies.append(
-            [pltpu.make_async_copy(a, b, sem.at[s, n]) for n, (a, b) in enumerate(pairs)]
-        )
-    for group in copies:
-        for c in group:
-            c.start()
-    sources = [x_ref] if streamed else xs
+        for n, a in enumerate((wg_hbm, wu_hbm)):
+            copies.append(
+                pltpu.make_async_copy(a.at[:, cols], w_ref.at[n, :, cols], sem.at[s, n])
+            )
+    for c in copies:
+        c.start()
     gate = up = None
     for s in range(steps):
         cols = slice(s * wide, (s + 1) * wide)
-        for c in copies[s]:
-            c.wait()
-        x = [r[:, cols] for r in sources]
-        x = x[0] if len(x) == 1 else jnp.concatenate(x, axis=0)
+        copies[2 * s].wait()
+        copies[2 * s + 1].wait()
+        x = jnp.concatenate([r[:, cols] for r in xs], axis=0)
         g = lax.dot_general(w_ref[0, :, cols], x, nt, preferred_element_type=F32)
         u = lax.dot_general(w_ref[1, :, cols], x, nt, preferred_element_type=F32)
         gate = g if gate is None else gate + g
@@ -517,18 +511,14 @@
     units, width = w_gate.shape
     whole = pl.BlockSpec(memory_space=pltpu.VMEM)
     away = pl.BlockSpec(memory_space=pl.ANY)
-    streamed = len(xs) == 1
-    if streamed:
-        xs = (hbm(xs[0]),)
-    return pl.pallas_call(
-        functools.partial(act_kernel, steps, streamed),
+    return pl.pallas_call(
+        functools.partial(act_kernel, steps),
         out_shape=jax.ShapeDtypeStruct((count, units), BF16),
-        in_specs=[away, away] + [away if streamed else whole] * len(xs),
+        in_specs=[away, away] + [whole] * len(xs),
         out_specs=whole,
         scratch_shapes=[
             pltpu.VMEM((2, units, width), BF16),
-            pltpu.VMEM((count, width) if streamed else (16, HEAD_DIM), BF16),
-            pltpu.SemaphoreType.DMA((steps, 3)),
+            pltpu.SemaphoreType.DMA((steps, 2)),
         ],
         compiler_params=params(),
         cost_estimate=cost(4 * count * width * units, 4 * width * units + 2 * count * width),
@@ -536,11 +526,11 @@
     )(hbm(w_gate), hbm(w_up), *xs)
 
 
-def down_kernel(steps, mixed, core_ref, act_ref, wd_hbm, own_ref, other_ref, wd_ref, sem):
-    chips, rows, width = own_ref.shape
+def down_kernel(steps, act_ref, wd_hbm, *refs):
+    outs, (wd_ref, sem) = refs[:-2], refs[-2:]
+    chips, rows, width = outs[0].shape
     wide = width // steps
     act = act_ref[...]
-    first = core_ref[0] == 0
     copies = []
     for s in range(steps):
         cols = pl.ds(s * wide, wide)
@@ -551,86 +541,106 @@
         cols = slice(s * wide, (s + 1) * wide)
         copies[s].wait()
         out = jnp.dot(act, wd_ref[:, cols], preferred_element_type=F32)
-        if mixed:
-            out = out.reshape(chips, 2, rows, wide)
-            a, b = out[:, 0].astype(BF16), out[:, 1].astype(BF16)
-            own_ref[:, :, cols] = jnp.where(first, a, b)
-            other_ref[:, :, cols] = jnp.where(first, b, a)
-        else:
-            out = out.reshape(2, chips, rows, wide).astype(BF16)
-            own_ref[:, :, cols] = out[0]
-            other_ref[:, :, cols] = out[1]
-
-
-def expert_down(core, act, w_down, mixed, steps=6):
+        out = out.reshape(len(outs), chips, rows, wide).astype(BF16)
+        for n, ref in enumerate(outs):
+            ref[:, :, cols] = out[n]
+
+
+def expert_down(act, w_down, chips, rows, steps=6):
     count, units = act.shape
     width = w_down.shape[1]
-    rows = count // 32
+    pieces = count // (chips * rows)
     whole = pl.BlockSpec(memory_space=pltpu.VMEM)
     return pl.pallas_call(
-        functools.partial(down_kernel, steps, mixed),
-        out_shape=(jax.ShapeDtypeStruct((16, rows, width), BF16),) * 2,
-        in_specs=[
-            pl.BlockSpec(memory_space=pltpu.SMEM),
-            whole,
-            pl.BlockSpec(memory_space=pl.ANY),
-        ],
-        out_specs=(whole, whole),
+        functools.partial(down_kernel, steps),
+        out_shape=(jax.ShapeDtypeStruct((chips, rows, width), BF16),) * pieces,
+        in_specs=[whole, pl.BlockSpec(memory_space=pl.ANY)],
+        out_specs=(whole,) * pieces,
         scratch_shapes=[pltpu.VMEM((units, width), BF16), pltpu.SemaphoreType.DMA((steps,))],
         compiler_params=params(),
         cost_estimate=cost(2 * count * width * units, 2 * width * units + 2 * count * width),
         name="expert_down",
-    )(core, act, hbm(w_down))
-
-
-def pair_kernel(a_ref, b_ref, out_ref):
-    out_ref[...] = (a_ref[...].astype(F32) + b_ref[...].astype(F32)).astype(BF16)
-
-
-def pair_sum(own, other, steps=4):
+    )(act, hbm(w_down))
+
+
+def pair_kernel(a_ref, b_ref, *outs):
+    total = (a_ref[...].astype(F32) + b_ref[...].astype(F32)).astype(BF16)
+    size = outs[0].shape[0]
+    for n, out in enumerate(outs):
+        out[...] = total[n * size : (n + 1) * size]
+
+
+def pair_sum(own, other, pieces=1, steps=4):
     chips, rows, width = own.shape
     wide = width // steps
     block = pl.BlockSpec((chips, rows, wide), lambda i: (0, 0, i))
+    part = pl.BlockSpec((chips // pieces, rows, wide), lambda i: (0, 0, i))
     return pl.pallas_call(
         pair_kernel,
         grid=(steps,),
-        out_shape=far((chips, rows, width)),
+        out_shape=(far((chips // pieces, rows, width)),) * pieces,
         in_specs=[block, block],
-        out_specs=block,
+        out_specs=(part,) * pieces,
         compiler_params=params(),
         cost_estimate=cost(chips * rows * width, 6 * chips * rows * width),
         name="pair_sum",
     )(own, other)
 
 
-def chip_sum_kernel(one_ref, two_ref, out_ref):
-    def total(ref):
-        out = ref[0].astype(F32)
-        for i in range(1, ref.shape[0]):
-            out = out + ref[i].astype(F32)
-        return out
-
-    one, two = total(one_ref), total(two_ref)
+def line_kernel(*refs):
+    half = len(refs) // 2
+    total = refs[0][...].astype(F32)
+    for ref in refs[1:half]:
+        total = total + ref[...].astype(F32)
+    total = total.astype(BF16)
+    for n, out in enumerate(refs[half:]):
+        out[...] = total[n]
+
+
+def line_sum(parts, steps=2):
+    n, rows, width = parts[0].shape
+    wide = width // steps
+    block = pl.BlockSpec((n, rows, wide), lambda i: (0, 0, i))
+    return pl.pallas_call(
+        line_kernel,
+        grid=(steps,),
+        out_shape=(far((rows, width)),) * n,
+        in_specs=[block] * len(parts),
+        out_specs=(pl.BlockSpec((rows, wide), lambda i: (0, i)),) * n,
+        compiler_params=params(),
+        cost_estimate=cost(n * n * rows * width, 2 * n * (n + 1) * rows * width),
+        name="line_sum",
+    )(*parts)
+
+
+def chip_sum_kernel(one_ref, *refs):
+    parts, out_ref = refs[:-1], refs[-1]
+    one = one_ref[0].astype(F32)
+    for i in range(1, one_ref.shape[0]):
+        one = one + one_ref[i].astype(F32)
+    two = parts[0][...].astype(F32)
+    for ref in parts[1:]:
+        two = two + ref[...].astype(F32)
     half = CAP // 2
     for j in range(out_ref.shape[0]):
         at = slice(j * half, (j + 1) * half)
         out_ref[j] = jnp.concatenate([one[at], two[at]], axis=0).astype(BF16)
 
 
-def chip_sum(one, two, held, steps=4):
+def chip_sum(one, parts, held, steps=4):
     chips, rows, width = one.shape
     wide = width // steps
-    block = pl.BlockSpec((chips, rows, wide), lambda i: (0, 0, i))
     return pl.pallas_call(
         chip_sum_kernel,
         grid=(steps,),
         out_shape=far((held, CAP, width)),
-        in_specs=[block, block],
+        in_specs=[pl.BlockSpec((chips, rows, wide), lambda i: (0, 0, i))]
+        + [pl.BlockSpec((rows, wide), lambda i: (0, i))] * len(parts),
         out_specs=pl.BlockSpec((held, CAP, wide), lambda i: (0, 0, i)),
         compiler_params=params(),
-        cost_estimate=cost(2 * chips * rows * width, 4 * chips * rows * width),
+        cost_estimate=cost(chips * rows * width, 3 * chips * rows * width),
         name="chip_sum",
-    )(one, two)
+    )(one, *parts)
 
 
 def combine_kernel(place_ref, rows_ref, ids_ref, weights_ref, out_ref):
@@ -693,7 +703,6 @@
     ids = expert_ids.T
     ld = hbm(log_decay.T)
     me = lax.axis_index("exp").reshape(1)
-    core = lax.axis_index("core").reshape(1)
     keep = lax.optimization_barrier
     chips = lax.axis_size("z") * lax.axis_size("x")
 
@@ -713,23 +722,23 @@
     one, two = routed_norm(me, routed, pieces, attn_gain, moe_gain, chips)
 
     attention, two = keep((attention, two))
-    two = lax.all_gather(two, CTX, axis=0).reshape(32 * two.shape[0], two.shape[1])
     one = exchange(one, ("z", "x"))
-    one = one.reshape(-1, one.shape[2])
+    line = jnp.stack([two] + [shift(two, "x", d) for d in range(1, 4)])
+    plane = [line] + [shift(line, "z", d) for d in range(1, 4)]
     attention = [attention[0]] + [shift(attention[d], "exp", d) for d in range(1, held)]
-    one, attention = keep((one, attention))
-
-    act = expert_act((one, shift(one, "core", 1)), w_gate, w_up)
-    own, other = expert_down(core, act, w_down, False)
-    one = pair_sum(own, shift(other, "core", 1))
-    _, two = keep((one, two))
+    one, plane, attention = keep((one, plane, attention))
+    near = [a.reshape(-1, a.shape[2]) for a in [one] + plane]
+    act = expert_act(near + [shift(a, "core", 1) for a in near], w_gate, w_up)
+    own1, own2, other1, other2 = expert_down(act, w_down, chips, two.shape[0])
+    (one,) = pair_sum(own1, shift(other1, "core", 1))
     one = exchange(one, ("z", "x"))
-    act = expert_act((two,), w_gate, w_up)
-    own, other = expert_down(core, act, w_down, True)
-    one, other = keep((one, other))
-    two = exchange(pair_sum(own, shift(other, "core", 1)), ("z", "x"))
+    parts = pair_sum(own2, shift(other2, "core", 1), pieces=4)
+    parts = [parts[0]] + [shift(parts[d], "z", -d) for d in range(1, 4)]
+    one, parts = keep((one, parts))
+    parts = line_sum(parts)
+    parts = [parts[0]] + [shift(parts[d], "x", -d) for d in range(1, 4)]
     hidden = hidden_rows(me, attention, hbm(residual), hbm(out_gate), attn_gain)
-    back = exchange(chip_sum(one, two, held), "exp")
+    back = exchange(chip_sum(one, parts, held), "exp")
     moe_out = combine_rows(place_own, back, expert_ids, route_weights)
     return (hidden, moe_out)
 

time: 203 us -> 216 us (1.064)
  waiting for transfers between devices: 49.2 us -> 79.3 us
  blocking collectives: 36.8 us -> 9.66 us
  starting transfers between devices: 41.5 us -> 61.9 us
  between operations: 14.2 us -> 0.86 us
  local copies, waits for them, and re-layouts: 2.69 us -> 5.17 us
    ppermute x9 -> x25, waiting for transfers between devices: 29.9 us -> 78.2 us  [shift(): return lax.ppermute(a, axis, [(i, (i + by) % n) for i in range(n)])]
    all_to_all x2 -> x1, blocking collectives: 36.8 us -> 9.66 us  [exchange(): return lax.all_to_all(a, axis, split_axis=0, concat_axis=0, tiled=True)]
    ppermute x9 -> x25, starting transfers between devices: 9.8 us -> 31.1 us  [shift(): return lax.ppermute(a, axis, [(i, (i + by) % n) for i in range(n)])]
    all_to_all x5, waiting for transfers between devices: 10.9 us -> 1.09 us  [exchange(): return lax.all_to_all(a, axis, split_axis=0, concat_axis=0, tiled=True)]
    all_gather x1 -> x0, waiting for transfers between devices: 7.64 us -> none  [local(): lax.all_gather(two, CTX, axis=0).reshape(32 * two.shape[0], two.shape[1])]
    unnamed x34 -> x38, local copies, waits for them, and re-layouts: 2.69 us -> 5.17 us
    pallas_call x6 -> x5, Pallas kernels: 20.4 us -> 20.1 us  [the longest x1 7.01 us: expert_act(): pl.pallas_call(functools.partial(act_kernel, steps), out_shape=jax.ShapeD...]
  transfers between devices with their start and end apart: 15 -> 30, of which waited for: 11 -> 19; matrix products, arithmetic and copies ran while one was open for 0% -> 0% of each run, Pallas kernels for 18% -> 11%
where the time goes in v5:
time: 216 us; the launch traced here: 214 us
  waiting for transfers between devices  79.3 us (37%)
  starting transfers between devices  61.9 us (29%)
  Pallas kernels  57.4 us (27%)
  blocking collectives  9.66 us (4%)
  local copies, waits for them, and re-layouts  5.17 us (2%)
    ppermute x25, waiting for transfers between devices, shift(): return lax.ppermute(a, axis, [(i, (i + by) % n) for i in range(n)])  78.2 us
    ppermute x25, starting transfers between devices, shift(): return lax.ppermute(a, axis, [(i, (i + by) % n) for i in range(n)])  31.1 us
    all_to_all x5, starting transfers between devices, exchange(): return lax.all_to_all(a, axis, split_axis=0, concat_axis=0, tiled=True)  30.8 us
    all_to_all x1, blocking collectives, exchange(): return lax.all_to_all(a, axis, split_axis=0, concat_axis=0, tiled=True)  9.66 us
    pallas_call x1, Pallas kernels, inside_blocks(): pl.pallas_call(functools.partial(inside_kernel, group), grid=(heads // gr...  7.82 us
    pallas_call x1, Pallas kernels, expert_act(): pl.pallas_call(functools.partial(act_kernel, steps), out_shape=jax.ShapeD...  7.01 us
    pallas_call x1, Pallas kernels, expert_down(): pl.pallas_call(functools.partial(down_kernel, steps), out_shape=(jax.Shap...  6.54 us
    pallas_call x1, Pallas kernels, local_states(): pl.pallas_call(functools.partial(state_kernel, group), grid=(heads // gro...  5.85 us
  transfers between devices with their start and end apart: 30, of which 19 were waited for; matrix products, arithmetic and copies ran while one was open for 0% of the time, Pallas kernels for 11%

profile of v5, /device:TPU:0, one launch (start us, length us, event | category | flops | bytes accessed | tf_op | source)
XLA Modules:
  0.0 214.3 jit_solution(1577095505334901691)
XLA Ops:
  0.6 5.9 %local_states.1 = (f32[512,12]{1,0:T(8,128)S(1)}, bf16[32,64,128]{2,1,0:T(8,128)(2,1)}) custom-call(bf16[512,1536]{1,0:T(8,128)(2,1)} %k_ref.3, bf16[512,1536]{1,0:T(8,128)(2,1)} %v_ref.3, f32[12,512]{1,0:T(8,128)} %bitcast.44), custom_call_target="tpu_custom_call" | custom-call | flops 201326592 | bytes 3145728 | tf_op jit(solution)/shard_map/local_states/pallas_call | solution.py:122
  6.5 8.4 %all-to-all-start = ((bf16[32,64,128]{2,1,0:T(8,128)(2,1)}), bf16[32,64,128]{2,1,0:T(8,128)(2,1)}, u32[]{:S(2)}, u32[]{:S(2)}) async-start(bf16[32,64,128]{2,1,0:T(8,128)(2,1)} %get-tuple-element.56), calls=%async_computation | async-start | bytes 1048576 | tf_op jit(solution)/shard_map/all_to_all | solution.py:671
  14.9 4.3 %route_rows.1 = (bf16[8,6400]{1,0:T(8,128)(2,1)}, bf16[8,6400]{1,0:T(8,128)(2,1)}, bf16[8,6400]{1,0:T(8,128)(2,1)}, bf16[8,6400]{1,0:T(8,128)(2,1)}, f32[16,128]{1,0:T(8,128)S(1)}) custom-call(s32[1]{0:T(128)} %bitcast.me_ref, s32[2,128]{1,0:T(2,128)S(1)} %bitcast.36, bf16[128,6144]{1,0:T(8,128)(2,1)} %res_ref.1, bf16[128,6144]{1,0:T(8,128)(2,1)} %gate_ref.1), custom_call_target="tpu_custom_call" | custom-call | flops 50331648 | bytes 3932160 | tf_op jit(solution)/shard_map/route_rows/pallas_call | solution.py:335
  19.2 7.8 %inside_blocks.1 = (f32[512,1536]{1,0:T(8,128)S(1)}, bf16[512,1536]{1,0:T(8,128)(2,1)}) custom-call(bf16[512,1536]{1,0:T(8,128)(2,1)} %q_ref.1, bf16[512,1536]{1,0:T(8,128)(2,1)} %k_ref.3, bf16[512,1536]{1,0:T(8,128)(2,1)} %v_ref.3, f32[512,12]{1,0:T(8,128)S(1)} %get-tuple-element.57.cum_ref, f32[12,512]{1,0:T(8,128)} %bitcast.45), custom_call_target="tpu_custom_call" | custom-call | flops 1610612736 | bytes 9437184 | tf_op jit(solution)/shard_map/inside_blocks/pallas_call | solution.py:216
  29.0 7.3 %all-to-all-start.1 = ((bf16[32,48,128]{2,1,0:T(8,128)(2,1)}), bf16[32,48,128]{2,1,0:T(8,128)(2,1)S(1)}, u32[]{:S(2)}, u32[]{:S(2)}) async-start(bf16[32,48,128]{2,1,0:T(8,128)(2,1)} %scan_blocks.1), calls=%async_computation.1 | async-start | bytes 786432 | tf_op jit(solution)/shard_map/all_to_all | solution.py:671
  42.9 3.4 %collective-permute-done.1.refs_2_ = bf16[8,6400]{1,0:T(8,128)(2,1)S(1)} collective-permute-done((bf16[8,6400]{1,0:T(8,128)(2,1)}, bf16[8,6400]{1,0:T(8,128)(2,1)S(1)}, u32[]{:S(2)}, u32[]{:S(2)}) %collective-permute-start.1) | collective-permute-done | bytes 102432 | tf_op jit(solution)/shard_map/ppermute | solution.py:676
  49.1 4.6 %carried_blocks.1 = (bf16[64,1536]{1,0:T(8,128)(2,1)}, bf16[128,1536]{1,0:T(8,128)(2,1)}, bf16[128,1536]{1,0:T(8,128)(2,1)}, bf16[128,1536]{1,0:T(8,128)(2,1)}, bf16[128,1536]{1,0:T(8,128)(2,1)}) custom-call(s32[1]{0:T(128)} %bitcast.me_ref, f32[512,1536]{1,0:T(8,128)S(1)} %get-tuple-element.64.inside_ref, bf16[512,1536]{1,0:T(8,128)(2,1)} %get-tuple-element.65.qs_ref, ...), custom_call_target="tpu_custom_call" | custom-call | flops 402653184 | bytes 6291456 | tf_op jit(solution)/shard_map/carried_blocks/pallas_call | solution.py:263
  53.7 9.7 %all_to_all.30.att_ref = bf16[4,16,1536]{2,1,0:T(8,128)(2,1)S(1)} all-to-all(bf16[4,16,1536]{2,1,0:T(8,128)(2,1)} %bitcast.39), channel_id=1, replica_groups=mesh['z'=4,'x'=4,'core'=2,'exp'=4] {'exp'}, dimensions={0} | all-to-all | bytes 393216 | tf_op jit(solution)/shard_map/all_to_all | solution.py:671
  66.3 7.1 %all-to-all-start.3 = ((bf16[16,8,6144]{2,1,0:T(8,128)(2,1)}), bf16[16,8,6144]{2,1,0:T(8,128)(2,1)S(1)}, u32[]{:S(2)}, u32[]{:S(2)}) async-start(bf16[16,8,6144]{2,1,0:T(8,128)(2,1)} %get-tuple-element.72), calls=%async_computation.3 | async-start | bytes 3145728 | tf_op jit(solution)/shard_map/all_to_all | solution.py:671
  73.4 3.2 %collective-permute-start.5 = (bf16[8,6144]{1,0:T(8,128)(2,1)S(1)}, bf16[8,6144]{1,0:T(8,128)(2,1)S(1)}, u32[]{:S(2)}, u32[]{:S(2)}) collective-permute-start(bf16[8,6144]{1,0:T(8,128)(2,1)S(1)} %copy-done.16), channel_id=1, source_target_pairs={{0,24},{8,0},{16,8},{24,16},{1,25},{9,1},{17,9},{25,17},{2,26},{10... | collective-permute-start | bytes 294920 | tf_op jit(solution)/shard_map/ppermute | solution.py:676
  81.0 13.2 %collective-permute-done.5 = bf16[8,6144]{1,0:T(8,128)(2,1)S(1)} collective-permute-done((bf16[8,6144]{1,0:T(8,128)(2,1)S(1)}, bf16[8,6144]{1,0:T(8,128)(2,1)S(1)}, u32[]{:S(2)}, u32[]{:S(2)}) %collective-permute-start.5) | collective-permute-done | bytes 98336 | tf_op jit(solution)/shard_map/ppermute | solution.py:676
  102.1 6.6 %collective-permute-done.6 = bf16[4,8,6144]{2,1,0:T(8,128)(2,1)S(1)} collective-permute-done((bf16[4,8,6144]{2,1,0:T(8,128)(2,1)S(1)}, bf16[4,8,6144]{2,1,0:T(8,128)(2,1)S(1)}, u32[]{:S(2)}, u32[]{:S(2)}) %collective-permute-start.6) | collective-permute-done | bytes 393248 | tf_op jit(solution)/shard_map/ppermute | solution.py:676
  108.8 8.9 %collective-permute-done.7 = bf16[4,8,6144]{2,1,0:T(8,128)(2,1)S(1)} collective-permute-done((bf16[4,8,6144]{2,1,0:T(8,128)(2,1)S(1)}, bf16[4,8,6144]{2,1,0:T(8,128)(2,1)S(1)}, u32[]{:S(2)}, u32[]{:S(2)}) %collective-permute-start.7) | collective-permute-done | bytes 393248 | tf_op jit(solution)/shard_map/ppermute | solution.py:676
  119.5 3.4 %collective-permute-done.13.refs_6_ = bf16[32,6144]{1,0:T(8,128)(2,1)S(1)} collective-permute-done((bf16[32,6144]{1,0:T(8,128)(2,1)S(1)}, bf16[32,6144]{1,0:T(8,128)(2,1)S(1)}, u32[]{:S(2)}, u32[]{:S(2)}) %collective-permute-start.13) | collective-permute-done | bytes 393248 | tf_op jit(solution)/shard_map/ppermute | solution.py:676
  125.3 7.0 %expert_act.1.act_ref = bf16[512,288]{1,0:T(8,128)(2,1)S(1)} custom-call(bf16[288,6144]{1,0:T(8,128)(2,1)} %bitcast.37, bf16[288,6144]{1,0:T(8,128)(2,1)} %bitcast.38, bf16[128,6144]{1,0:T(8,128)(2,1)S(1)} %bitcast.25, bf16[32,6144]{1,0:T(8,128)(2,1)S(1)} %bitcast.27, bf16[32,6144]{1,0:T(8,128)(2,1)S(1)} %bitcast.30, bf16[32,6144]{1,0:T(8,128)(2,1)S(1)} %bitcast.32, ...), custom_call_target="tpu_custom_call" | custom-call | flops 3623878656 | bytes 13369344 | tf_op jit(solution)/shard_map/expert_act/pallas_call | solution.py:514
  132.3 6.5 %expert_down.1 = (bf16[16,8,6144]{2,1,0:T(8,128)(2,1)S(1)}, bf16[16,8,6144]{2,1,0:T(8,128)(2,1)S(1)}, bf16[16,8,6144]{2,1,0:T(8,128)(2,1)S(1)}, bf16[16,8,6144]{2,1,0:T(8,128)(2,1)}) custom-call(bf16[512,288]{1,0:T(8,128)(2,1)S(1)} %expert_act.1.act_ref, bf16[288,6144]{1,0:T(8,128)(2,1)} %bitcast.46), custom_call_target="tpu_custom_call" | custom-call | flops 1811939328 | bytes 9830400 | tf_op jit(solution)/shard_map/expert_down/pallas_call | solution.py:554
  139.4 3.8 %collective-permute-done.17.b_ref = bf16[16,8,6144]{2,1,0:T(8,128)(2,1)S(1)} collective-permute-done((bf16[16,8,6144]{2,1,0:T(8,128)(2,1)S(1)}, bf16[16,8,6144]{2,1,0:T(8,128)(2,1)S(1)}, u32[]{:S(2)}, u32[]{:S(2)}) %collective-permute-start.17) | collective-permute-done | bytes 1572896 | tf_op jit(solution)/shard_map/ppermute | solution.py:676
  145.3 4.7 %all-to-all-start.4 = ((bf16[16,8,6144]{2,1,0:T(8,128)(2,1)}), bf16[16,8,6144]{2,1,0:T(8,128)(2,1)S(1)}, u32[]{:S(2)}, u32[]{:S(2)}) async-start(bf16[16,8,6144]{2,1,0:T(8,128)(2,1)} %pair_sum.2), calls=%async_computation.4 | async-start | bytes 3145728 | tf_op jit(solution)/shard_map/all_to_all | solution.py:671
  150.0 3.6 %pair_sum.3 = (bf16[4,8,6144]{2,1,0:T(8,128)(2,1)}, bf16[4,8,6144]{2,1,0:T(8,128)(2,1)}, bf16[4,8,6144]{2,1,0:T(8,128)(2,1)}, bf16[4,8,6144]{2,1,0:T(8,128)(2,1)}) custom-call(bf16[16,8,6144]{2,1,0:T(8,128)(2,1)S(1)} %get-tuple-element.95.a_ref, bf16[16,8,6144]{2,1,0:T(8,128)(2,1)} %collective-permute-done.18.b_ref), custom_call_target="tpu_custom_call" | custom-call | flops 786432 | bytes 4718592 | tf_op jit(solution)/shard_map/pair_sum/pallas_call | solution.py:578
  153.6 3.1 %collective-permute-start.19 = (bf16[4,8,6144]{2,1,0:T(8,128)(2,1)}, bf16[4,8,6144]{2,1,0:T(8,128)(2,1)S(1)}, u32[]{:S(2)}, u32[]{:S(2)}) collective-permute-start(bf16[4,8,6144]{2,1,0:T(8,128)(2,1)} %get-tuple-element.98), channel_id=1, source_target_pairs={{0,96},{32,0},{64,32},{96,64},{1,97},{33,1},{65,33},{97,65},{2,98}... | collective-permute-start | bytes 1179656 | tf_op jit(solution)/shard_map/ppermute | solution.py:676
  158.4 20.5 %collective-permute-done.19.refs_1_ = bf16[4,8,6144]{2,1,0:T(8,128)(2,1)S(1)} collective-permute-done((bf16[4,8,6144]{2,1,0:T(8,128)(2,1)}, bf16[4,8,6144]{2,1,0:T(8,128)(2,1)S(1)}, u32[]{:S(2)}, u32[]{:S(2)}) %collective-permute-start.19) | collective-permute-done | bytes 393248 | tf_op jit(solution)/shard_map/ppermute | solution.py:676
  179.7 8.0 %collective-permute-done.21.refs_3_ = bf16[4,8,6144]{2,1,0:T(8,128)(2,1)S(1)} collective-permute-done((bf16[4,8,6144]{2,1,0:T(8,128)(2,1)}, bf16[4,8,6144]{2,1,0:T(8,128)(2,1)S(1)}, u32[]{:S(2)}, u32[]{:S(2)}) %collective-permute-start.21) | collective-permute-done | bytes 393248 | tf_op jit(solution)/shard_map/ppermute | solution.py:676
  202.9 3.4 %all-to-all-start.5 = ((bf16[4,4,6144]{2,1,0:T(4,128)(2,1)}), bf16[4,4,6144]{2,1,0:T(4,128)(2,1)S(1)}, u32[]{:S(2)}, u32[]{:S(2)}) async-start(bf16[4,4,6144]{2,1,0:T(4,128)(2,1)} %chip_sum.1), calls=%async_computation.5 | async-start | bytes 393216 | tf_op jit(solution)/shard_map/all_to_all | solution.py:671
  206.5 4.9 %hidden_rows.1 = bf16[128,6144]{1,0:T(8,128)(2,1)} custom-call(s32[1]{0:T(128)} %bitcast.me_ref, bf16[128,6144]{1,0:T(8,128)(2,1)} %res_ref.1, bf16[128,6144]{1,0:T(8,128)(2,1)} %gate_ref.1, f32[1,6144]{1,0:T(1,128)S(1)} %bitcast.34, bf16[128,1536]{1,0:T(8,128)(2,1)S(1)} %copy-done, bf16[128,1536]{1,0:T(8,128)(2,1)S(1)} %collective-permute-done.9.refs_1_, ...), custom_call_target="tpu_custom_call" | custom-call | flops 15728640 | bytes 6291456 | tf_op jit(solution)/shard_map/hidden_rows/pallas_call | solution.py:464
  (91 shorter events, 54.2 us)
Async XLA Ops:
  6.5 20.5 %all-to-all-start = ((bf16[32,64,128]{2,1,0:T(8,128)(2,1)}), bf16[32,64,128]{2,1,0:T(8,128)(2,1)}, u32[]{:S(2)}, u32[]{:S(2)}) async-start(bf16[32,64,128]{2,1,0:T(8,128)(2,1)} %get-tuple-element.56), calls=%async_computation | async-start | bytes 1048576 | tf_op jit(solution)/shard_map/all_to_all | solution.py:671
  29.0 20.1 %all-to-all-start.1 = ((bf16[32,48,128]{2,1,0:T(8,128)(2,1)}), bf16[32,48,128]{2,1,0:T(8,128)(2,1)S(1)}, u32[]{:S(2)}, u32[]{:S(2)}) async-start(bf16[32,48,128]{2,1,0:T(8,128)(2,1)} %scan_blocks.1), calls=%async_computation.1 | async-start | bytes 786432 | tf_op jit(solution)/shard_map/all_to_all | solution.py:671
  36.3 6.6 %collective-permute-start = (bf16[8,6400]{1,0:T(8,128)(2,1)}, bf16[8,6400]{1,0:T(8,128)(2,1)S(1)}, u32[]{:S(2)}, u32[]{:S(2)}) collective-permute-start(bf16[8,6400]{1,0:T(8,128)(2,1)} %get-tuple-element.68), channel_id=1, source_target_pairs={{0,1},{1,2},{2,3},{3,0},{4,5},{5,6},{6,7},{7,4},{8,9},{9,10},{10,1... | collective-permute-start | bytes 307208 | tf_op jit(solution)/shard_map/ppermute | solution.py:676
  37.9 8.3 %collective-permute-start.1 = (bf16[8,6400]{1,0:T(8,128)(2,1)}, bf16[8,6400]{1,0:T(8,128)(2,1)S(1)}, u32[]{:S(2)}, u32[]{:S(2)}) collective-permute-start(bf16[8,6400]{1,0:T(8,128)(2,1)} %get-tuple-element.69), channel_id=1, source_target_pairs={{0,2},{1,3},{2,0},{3,1},{4,6},{5,7},{6,4},{7,5},{8,10},{9,11},{10,... | collective-permute-start | bytes 307208 | tf_op jit(solution)/shard_map/ppermute | solution.py:676
  66.3 52.1 %all-to-all-start.3 = ((bf16[16,8,6144]{2,1,0:T(8,128)(2,1)}), bf16[16,8,6144]{2,1,0:T(8,128)(2,1)S(1)}, u32[]{:S(2)}, u32[]{:S(2)}) async-start(bf16[16,8,6144]{2,1,0:T(8,128)(2,1)} %get-tuple-element.72), calls=%async_computation.3 | async-start | bytes 3145728 | tf_op jit(solution)/shard_map/all_to_all | solution.py:671
  73.4 20.7 %collective-permute-start.5 = (bf16[8,6144]{1,0:T(8,128)(2,1)S(1)}, bf16[8,6144]{1,0:T(8,128)(2,1)S(1)}, u32[]{:S(2)}, u32[]{:S(2)}) collective-permute-start(bf16[8,6144]{1,0:T(8,128)(2,1)S(1)} %copy-done.16), channel_id=1, source_target_pairs={{0,24},{8,0},{16,8},{24,16},{1,25},{9,1},{17,9},{25,17},{2,26},{10... | collective-permute-start | bytes 294920 | tf_op jit(solution)/shard_map/ppermute | solution.py:676
  76.6 19.1 %collective-permute-start.4 = (bf16[8,6144]{1,0:T(8,128)(2,1)S(1)}, bf16[8,6144]{1,0:T(8,128)(2,1)S(1)}, u32[]{:S(2)}, u32[]{:S(2)}) collective-permute-start(bf16[8,6144]{1,0:T(8,128)(2,1)S(1)} %copy-done.16), channel_id=1, source_target_pairs={{0,16},{8,24},{16,0},{24,8},{1,17},{9,25},{17,1},{25,9},{2,18},{10... | collective-permute-start | bytes 294920 | tf_op jit(solution)/shard_map/ppermute | solution.py:676
  77.5 18.8 %collective-permute-start.3 = (bf16[8,6144]{1,0:T(8,128)(2,1)S(1)}, bf16[8,6144]{1,0:T(8,128)(2,1)S(1)}, u32[]{:S(2)}, u32[]{:S(2)}) collective-permute-start(bf16[8,6144]{1,0:T(8,128)(2,1)S(1)} %copy-done.16), channel_id=1, source_target_pairs={{0,8},{8,16},{16,24},{24,0},{1,9},{9,17},{17,25},{25,1},{2,10},{10... | collective-permute-start | bytes 294920 | tf_op jit(solution)/shard_map/ppermute | solution.py:676
  78.3 22.2 %collective-permute-start.9 = (bf16[128,1536]{1,0:T(8,128)(2,1)}, bf16[128,1536]{1,0:T(8,128)(2,1)S(1)}, u32[]{:S(2)}, u32[]{:S(2)}) collective-permute-start(bf16[128,1536]{1,0:T(8,128)(2,1)} %get-tuple-element.80), channel_id=1, source_target_pairs={{0,1},{1,2},{2,3},{3,0},{4,5},{5,6},{6,7},{7,4},{8,9},{9,10},{10,1... | collective-permute-start | bytes 1179656 | tf_op jit(solution)/shard_map/ppermute | solution.py:676
  78.9 23.1 %collective-permute-start.10 = (bf16[128,1536]{1,0:T(8,128)(2,1)}, bf16[128,1536]{1,0:T(8,128)(2,1)S(1)}, u32[]{:S(2)}, u32[]{:S(2)}) collective-permute-start(bf16[128,1536]{1,0:T(8,128)(2,1)} %get-tuple-element.81), channel_id=1, source_target_pairs={{0,2},{1,3},{2,0},{3,1},{4,6},{5,7},{6,4},{7,5},{8,10},{9,11},{10,... | collective-permute-start | bytes 1179656 | tf_op jit(solution)/shard_map/ppermute | solution.py:676
  94.1 8.0 %collective-permute-start.11 = (bf16[128,1536]{1,0:T(8,128)(2,1)}, bf16[128,1536]{1,0:T(8,128)(2,1)S(1)}, u32[]{:S(2)}, u32[]{:S(2)}) collective-permute-start(bf16[128,1536]{1,0:T(8,128)(2,1)} %get-tuple-element.82), channel_id=1, source_target_pairs={{0,3},{1,0},{2,1},{3,2},{4,7},{5,4},{6,5},{7,6},{8,11},{9,8},{10,9... | collective-permute-start | bytes 1179656 | tf_op jit(solution)/shard_map/ppermute | solution.py:676
  96.3 12.4 %collective-permute-start.6 = (bf16[4,8,6144]{2,1,0:T(8,128)(2,1)S(1)}, bf16[4,8,6144]{2,1,0:T(8,128)(2,1)S(1)}, u32[]{:S(2)}, u32[]{:S(2)}) collective-permute-start(bf16[4,8,6144]{2,1,0:T(8,128)(2,1)S(1)} %pad_maximum_fusion), channel_id=1, source_target_pairs={{0,32},{32,64},{64,96},{96,0},{1,33},{33,65},{65,97},{97,1},{2,34}... | collective-permute-start | bytes 1179656 | tf_op jit(solution)/shard_map/ppermute | solution.py:676
  97.9 19.8 %collective-permute-start.7 = (bf16[4,8,6144]{2,1,0:T(8,128)(2,1)S(1)}, bf16[4,8,6144]{2,1,0:T(8,128)(2,1)S(1)}, u32[]{:S(2)}, u32[]{:S(2)}) collective-permute-start(bf16[4,8,6144]{2,1,0:T(8,128)(2,1)S(1)} %pad_maximum_fusion), channel_id=1, source_target_pairs={{0,64},{32,96},{64,0},{96,32},{1,65},{33,97},{65,1},{97,33},{2,66}... | collective-permute-start | bytes 1179656 | tf_op jit(solution)/shard_map/ppermute | solution.py:676
  100.6 17.8 %collective-permute-start.8 = (bf16[4,8,6144]{2,1,0:T(8,128)(2,1)S(1)}, bf16[4,8,6144]{2,1,0:T(8,128)(2,1)}, u32[]{:S(2)}, u32[]{:S(2)}) collective-permute-start(bf16[4,8,6144]{2,1,0:T(8,128)(2,1)S(1)} %pad_maximum_fusion), channel_id=1, source_target_pairs={{0,96},{32,0},{64,32},{96,64},{1,97},{33,1},{65,33},{97,65},{2,98}... | collective-permute-start | bytes 1179656 | tf_op jit(solution)/shard_map/ppermute | solution.py:676
  118.4 5.9 %collective-permute-start.12 = (bf16[128,6144]{1,0:T(8,128)(2,1)S(1)}, bf16[128,6144]{1,0:T(8,128)(2,1)S(1)}, u32[]{:S(2)}, u32[]{:S(2)}) collective-permute-start(bf16[128,6144]{1,0:T(8,128)(2,1)S(1)} %bitcast.24), channel_id=1, source_target_pairs={{0,4},{4,0},{1,5},{5,1},{2,6},{6,2},{3,7},{7,3},{8,12},{12,8},{9,1... | collective-permute-start | bytes 4718600 | tf_op jit(solution)/shard_map/ppermute | solution.py:676
  139.1 10.9 %collective-permute-start.18 = (bf16[16,8,6144]{2,1,0:T(8,128)(2,1)}, bf16[16,8,6144]{2,1,0:T(8,128)(2,1)}, u32[]{:S(2)}, u32[]{:S(2)}) collective-permute-start(bf16[16,8,6144]{2,1,0:T(8,128)(2,1)} %get-tuple-element.96), channel_id=1, source_target_pairs={{0,4},{4,0},{1,5},{5,1},{2,6},{6,2},{3,7},{7,3},{8,12},{12,8},{9,1... | collective-permute-start | bytes 4718600 | tf_op jit(solution)/shard_map/ppermute | solution.py:676
  145.3 42.5 %all-to-all-start.4 = ((bf16[16,8,6144]{2,1,0:T(8,128)(2,1)}), bf16[16,8,6144]{2,1,0:T(8,128)(2,1)S(1)}, u32[]{:S(2)}, u32[]{:S(2)}) async-start(bf16[16,8,6144]{2,1,0:T(8,128)(2,1)} %pair_sum.2), calls=%async_computation.4 | async-start | bytes 3145728 | tf_op jit(solution)/shard_map/all_to_all | solution.py:671
  153.6 25.3 %collective-permute-start.19 = (bf16[4,8,6144]{2,1,0:T(8,128)(2,1)}, bf16[4,8,6144]{2,1,0:T(8,128)(2,1)S(1)}, u32[]{:S(2)}, u32[]{:S(2)}) collective-permute-start(bf16[4,8,6144]{2,1,0:T(8,128)(2,1)} %get-tuple-element.98), channel_id=1, source_target_pairs={{0,96},{32,0},{64,32},{96,64},{1,97},{33,1},{65,33},{97,65},{2,98}... | collective-permute-start | bytes 1179656 | tf_op jit(solution)/shard_map/ppermute | solution.py:676
  156.7 23.0 %collective-permute-start.20 = (bf16[4,8,6144]{2,1,0:T(8,128)(2,1)}, bf16[4,8,6144]{2,1,0:T(8,128)(2,1)S(1)}, u32[]{:S(2)}, u32[]{:S(2)}) collective-permute-start(bf16[4,8,6144]{2,1,0:T(8,128)(2,1)} %get-tuple-element.99), channel_id=1, source_target_pairs={{0,64},{32,96},{64,0},{96,32},{1,65},{33,97},{65,1},{97,33},{2,66}... | collective-permute-start | bytes 1179656 | tf_op jit(solution)/shard_map/ppermute | solution.py:676
  157.6 30.1 %collective-permute-start.21 = (bf16[4,8,6144]{2,1,0:T(8,128)(2,1)}, bf16[4,8,6144]{2,1,0:T(8,128)(2,1)S(1)}, u32[]{:S(2)}, u32[]{:S(2)}) collective-permute-start(bf16[4,8,6144]{2,1,0:T(8,128)(2,1)} %get-tuple-element.100), channel_id=1, source_target_pairs={{0,32},{32,64},{64,96},{96,0},{1,33},{33,65},{65,97},{97,1},{2,34}... | collective-permute-start | bytes 1179656 | tf_op jit(solution)/shard_map/ppermute | solution.py:676
  189.7 7.1 %collective-permute-start.22 = (bf16[8,6144]{1,0:T(8,128)(2,1)}, bf16[8,6144]{1,0:T(8,128)(2,1)S(1)}, u32[]{:S(2)}, u32[]{:S(2)}) collective-permute-start(bf16[8,6144]{1,0:T(8,128)(2,1)} %get-tuple-element.107), channel_id=1, source_target_pairs={{0,24},{8,0},{16,8},{24,16},{1,25},{9,1},{17,9},{25,17},{2,26},{10... | collective-permute-start | bytes 294920 | tf_op jit(solution)/shard_map/ppermute | solution.py:676
  192.2 7.2 %collective-permute-start.23 = (bf16[8,6144]{1,0:T(8,128)(2,1)}, bf16[8,6144]{1,0:T(8,128)(2,1)S(1)}, u32[]{:S(2)}, u32[]{:S(2)}) collective-permute-start(bf16[8,6144]{1,0:T(8,128)(2,1)} %get-tuple-element.108), channel_id=1, source_target_pairs={{0,16},{8,24},{16,0},{24,8},{1,17},{9,25},{17,1},{25,9},{2,18},{10... | collective-permute-start | bytes 294920 | tf_op jit(solution)/shard_map/ppermute | solution.py:676
  193.4 7.0 %collective-permute-start.24 = (bf16[8,6144]{1,0:T(8,128)(2,1)}, bf16[8,6144]{1,0:T(8,128)(2,1)S(1)}, u32[]{:S(2)}, u32[]{:S(2)}) collective-permute-start(bf16[8,6144]{1,0:T(8,128)(2,1)} %get-tuple-element.109), channel_id=1, source_target_pairs={{0,8},{8,16},{16,24},{24,0},{1,9},{9,17},{17,25},{25,1},{2,10},{10... | collective-permute-start | bytes 294920 | tf_op jit(solution)/shard_map/ppermute | solution.py:676
  202.9 9.7 %all-to-all-start.5 = ((bf16[4,4,6144]{2,1,0:T(4,128)(2,1)}), bf16[4,4,6144]{2,1,0:T(4,128)(2,1)S(1)}, u32[]{:S(2)}, u32[]{:S(2)}) async-start(bf16[4,4,6144]{2,1,0:T(4,128)(2,1)} %chip_sum.1), calls=%async_computation.5 | async-start | bytes 393216 | tf_op jit(solution)/shard_map/all_to_all | solution.py:671
  (24 other events, 232.9 us)

commit v6 on v5

--- a/solution.py
+++ b/solution.py
@@ -309,18 +309,19 @@
     place_ref[...] = place
     for c in copies:
         c.wait()
+    ordered = []
     for d in range(held):
         expert = lax.rem(me + d, held)
         mine = places[0]
         for e in range(1, held):
             mine = jnp.where(expert == e, places[e], mine)
-        mine = mine.astype(BF16)
-        outs[d][0:CAP, 0:width] = jnp.dot(
-            mine, res_ref[...], preferred_element_type=F32
-        ).astype(BF16)
-        outs[d][CAP : 2 * CAP, 0:width] = jnp.dot(
-            mine, gate_ref[...], preferred_element_type=F32
-        ).astype(BF16)
+        ordered.append(mine)
+    chosen = jnp.concatenate(ordered, axis=0).astype(BF16)
+    res = jnp.dot(chosen, res_ref[...], preferred_element_type=F32)
+    gate = jnp.dot(chosen, gate_ref[...], preferred_element_type=F32)
+    for d in range(held):
+        at = slice(d * CAP, (d + 1) * CAP)
+        outs[d][:, 0:width] = jnp.concatenate([res[at], gate[at]], axis=0).astype(BF16)
         for n in range(2):
             outs[d][:, width + n * tokens : width + (n + 1) * tokens] = jnp.broadcast_to(
                 ids[n : n + 1, :].astype(F32), (2 * CAP, tokens)
@@ -377,11 +378,8 @@
     rows = held * CAP
     r = iota((rows, total), 0)
     t = iota((rows, total), 1)
-    chunk = r // (rows // 2)
-    inner = r % (rows // 2)
-    source = inner // (CAP // 2)
-    slot = (chunk * (CAP // 2) + inner % (CAP // 2)).astype(F32)
-    here = (t // tokens == source).astype(F32)
+    here = (t // tokens == r // CAP).astype(F32)
+    slot = (r % CAP).astype(F32)
     for e in range(held):
         hit = jnp.where(rank[e : e + 1, :] == slot, m[e : e + 1, :] * here, 0.0)
         place_ref[e * rows : (e + 1) * rows, :] = hit.astype(BF16)
@@ -417,21 +415,15 @@
     att = jnp.concatenate([att_ref[s].astype(F32) for s in range(sources)], axis=1)
     tables = [p[...][:, :width].astype(F32) for p in pieces]
     ordered = [by_source(me, tables, j) for j in range(sources)]
-    half = CAP // 2
-    res = jnp.concatenate(
-        [a[c * half : (c + 1) * half] for c in range(2) for a in ordered], axis=0
-    )
-    gate = jnp.concatenate(
-        [a[CAP + c * half : CAP + (c + 1) * half] for c in range(2) for a in ordered], axis=0
-    )
+    res = jnp.concatenate([a[:CAP] for a in ordered], axis=0)
+    gate = jnp.concatenate([a[CAP:] for a in ordered], axis=0)
     hidden = gated(att, res, gate, ag_ref[...]).astype(F32)
     normed = (
         hidden * lax.rsqrt(jnp.mean(hidden * hidden, axis=-1, keepdims=True) + EPS) * mg_ref[...]
-    )
-    one = normed[: rows // 2].astype(BF16)
-    for i in range(one_ref.shape[0]):
-        one_ref[i] = one
-    two_ref[...] = normed[rows // 2 :].astype(BF16)
+    ).astype(BF16)
+    one_ref[...] = normed[:, : width // 2]
+    for i in range(two_ref.shape[0]):
+        two_ref[i] = normed[:, width // 2 :]
 
 
 def routed_norm(me, att, pieces, attn_gain, moe_gain, copies):
@@ -440,7 +432,7 @@
     whole = pl.BlockSpec(memory_space=pltpu.VMEM)
     return pl.pallas_call(
         routed_norm_kernel,
-        out_shape=(far((copies, rows // 2, width)), far((rows // 2, width))),
+        out_shape=(far((rows, width // 2)), far((copies, rows, width // 2))),
         in_specs=[pl.BlockSpec(memory_space=pltpu.SMEM)] + [whole] * (3 + len(pieces)),
         out_specs=(whole, whole),
         compiler_params=params(),
@@ -479,9 +471,38 @@
     )(me, residual, out_gate, attn_gain, *pieces)
 
 
-def act_kernel(steps, wg_hbm, wu_hbm, *refs):
-    xs, (act_ref, w_ref, sem) = refs[:-3], refs[-3:]
+def repeat_kernel(*refs):
+    ins, (out, sem) = refs[:-2], refs[-2:]
+    copies = [
+        pltpu.make_async_copy(a, out.at[n, k], sem.at[n, k])
+        for n in range(out.shape[0])
+        for k, a in enumerate(ins)
+    ]
+    for c in copies:
+        c.start()
+    for c in copies:
+        c.wait()
+
+
+def repeat(arrays, copies):
+    rows, width = arrays[0].shape
+    count = len(arrays)
+    return pl.pallas_call(
+        repeat_kernel,
+        out_shape=far((copies, count, rows, width)),
+        in_specs=[pl.BlockSpec(memory_space=pltpu.VMEM)] * count,
+        out_specs=pl.BlockSpec(memory_space=pl.ANY),
+        scratch_shapes=[pltpu.SemaphoreType.DMA((copies, count))],
+        compiler_params=params(),
+        cost_estimate=cost(0, 2 * (copies + 1) * count * rows * width),
+        name="repeat",
+    )(*arrays)
+
+
+def act_kernel(steps, wg_hbm, wu_hbm, one_ref, *refs):
+    twos, (act_ref, w_ref, sem) = refs[:-3], refs[-3:]
     units, width = wg_hbm.shape
+    nz, nx, rows, half = one_ref.shape
     nt = (((1,), (1,)), ((), ()))
     wide = width // steps
     copies = []
@@ -498,7 +519,12 @@
         cols = slice(s * wide, (s + 1) * wide)
         copies[2 * s].wait()
         copies[2 * s + 1].wait()
-        x = jnp.concatenate([r[:, cols] for r in xs], axis=0)
+        if s < steps // 2:
+            x = [one_ref[z, k, :, cols] for k in range(nx) for z in range(nz)]
+        else:
+            near = slice(s * wide - half, (s + 1) * wide - half)
+            x = [r[z, :, near] for r in twos for z in range(nz)]
+        x = jnp.concatenate(x, axis=0)
         g = lax.dot_general(w_ref[0, :, cols], x, nt, preferred_element_type=F32)
         u = lax.dot_general(w_ref[1, :, cols], x, nt, preferred_element_type=F32)
         gate = g if gate is None else gate + g
@@ -506,15 +532,16 @@
     act_ref[...] = (gate * jax.nn.sigmoid(gate) * up).T.astype(BF16)
 
 
-def expert_act(xs, w_gate, w_up, steps=6):
-    count = sum(x.shape[0] for x in xs)
+def expert_act(one, twos, w_gate, w_up, steps=6):
+    nz, nx, rows, half = one.shape
+    count = nz * nx * rows
     units, width = w_gate.shape
     whole = pl.BlockSpec(memory_space=pltpu.VMEM)
     away = pl.BlockSpec(memory_space=pl.ANY)
     return pl.pallas_call(
         functools.partial(act_kernel, steps),
         out_shape=jax.ShapeDtypeStruct((count, units), BF16),
-        in_specs=[away, away] + [whole] * len(xs),
+        in_specs=[away, away] + [whole] * (1 + len(twos)),
         out_specs=whole,
         scratch_shapes=[
             pltpu.VMEM((2, units, width), BF16),
@@ -523,13 +550,12 @@
         compiler_params=params(),
         cost_estimate=cost(4 * count * width * units, 4 * width * units + 2 * count * width),
         name="expert_act",
-    )(hbm(w_gate), hbm(w_up), *xs)
-
-
-def down_kernel(steps, act_ref, wd_hbm, *refs):
-    outs, (wd_ref, sem) = refs[:-2], refs[-2:]
-    chips, rows, width = outs[0].shape
-    wide = width // steps
+    )(hbm(w_gate), hbm(w_up), one, *twos)
+
+
+def down_kernel(steps, act_ref, wd_hbm, one_ref, two_ref, wd_ref, sem):
+    nz, nx, rows, half = one_ref.shape
+    wide = 2 * half // steps
     act = act_ref[...]
     copies = []
     for s in range(steps):
@@ -541,21 +567,27 @@
         cols = slice(s * wide, (s + 1) * wide)
         copies[s].wait()
         out = jnp.dot(act, wd_ref[:, cols], preferred_element_type=F32)
-        out = out.reshape(len(outs), chips, rows, wide).astype(BF16)
-        for n, ref in enumerate(outs):
-            ref[:, :, cols] = out[n]
-
-
-def expert_down(act, w_down, chips, rows, steps=6):
+        out = out.reshape(nx, nz, rows, wide).astype(BF16)
+        if s < steps // 2:
+            for z in range(nz):
+                one_ref[z, :, :, cols] = out[:, z]
+        else:
+            two_ref[:, :, :, s * wide - half : (s + 1) * wide - half] = out
+
+
+def expert_down(act, w_down, nz, nx, steps=6):
     count, units = act.shape
     width = w_down.shape[1]
-    pieces = count // (chips * rows)
+    rows = count // (nz * nx)
     whole = pl.BlockSpec(memory_space=pltpu.VMEM)
     return pl.pallas_call(
         functools.partial(down_kernel, steps),
-        out_shape=(jax.ShapeDtypeStruct((chips, rows, width), BF16),) * pieces,
+        out_shape=(
+            jax.ShapeDtypeStruct((nz, nx, rows, width // 2), BF16),
+            jax.ShapeDtypeStruct((nx, nz, rows, width // 2), BF16),
+        ),
         in_specs=[whole, pl.BlockSpec(memory_space=pl.ANY)],
-        out_specs=(whole,) * pieces,
+        out_specs=(whole, whole),
         scratch_shapes=[pltpu.VMEM((units, width), BF16), pltpu.SemaphoreType.DMA((steps,))],
         compiler_params=params(),
         cost_estimate=cost(2 * count * width * units, 2 * width * units + 2 * count * width),
@@ -565,82 +597,104 @@
 
 def pair_kernel(a_ref, b_ref, *outs):
     total = (a_ref[...].astype(F32) + b_ref[...].astype(F32)).astype(BF16)
-    size = outs[0].shape[0]
-    for n, out in enumerate(outs):
-        out[...] = total[n * size : (n + 1) * size]
-
-
-def pair_sum(own, other, pieces=1, steps=4):
-    chips, rows, width = own.shape
+    if len(outs) == 1:
+        outs[0][...] = total
+    else:
+        for n, out in enumerate(outs):
+            out[...] = total[n]
+
+
+def pair_sum(own, other, split, steps=3):
+    n, m, rows, width = own.shape
     wide = width // steps
-    block = pl.BlockSpec((chips, rows, wide), lambda i: (0, 0, i))
-    part = pl.BlockSpec((chips // pieces, rows, wide), lambda i: (0, 0, i))
+    block = pl.BlockSpec((n, m, rows, wide), lambda i: (0, 0, 0, i))
+    part = pl.BlockSpec((m, rows, wide), lambda i: (0, 0, i))
     return pl.pallas_call(
         pair_kernel,
         grid=(steps,),
-        out_shape=(far((chips // pieces, rows, width)),) * pieces,
+        out_shape=(far((m, rows, width)),) * n if split else (far(own.shape),),
         in_specs=[block, block],
-        out_specs=(part,) * pieces,
-        compiler_params=params(),
-        cost_estimate=cost(chips * rows * width, 6 * chips * rows * width),
+        out_specs=(part,) * n if split else (block,),
+        compiler_params=params(),
+        cost_estimate=cost(n * m * rows * width, 6 * n * m * rows * width),
         name="pair_sum",
     )(own, other)
 
 
-def line_kernel(*refs):
-    half = len(refs) // 2
+def block_kernel(in_ref, *outs):
+    total = in_ref[0].astype(F32)
+    for i in range(1, in_ref.shape[0]):
+        total = total + in_ref[i].astype(F32)
+    total = total.astype(BF16)
+    for n, out in enumerate(outs):
+        out[...] = total[n]
+
+
+def block_sum(parts, steps=2):
+    count, n, rows, width = parts.shape
+    wide = width // steps
+    return pl.pallas_call(
+        block_kernel,
+        grid=(steps,),
+        out_shape=(far((rows, width)),) * n,
+        in_specs=[pl.BlockSpec((count, n, rows, wide), lambda i: (0, 0, 0, i))],
+        out_specs=(pl.BlockSpec((rows, wide), lambda i: (0, i)),) * n,
+        compiler_params=params(),
+        cost_estimate=cost(count * n * rows * width, 2 * (count + 1) * n * rows * width),
+        name="block_sum",
+    )(parts)
+
+
+def stack_kernel(*refs):
     total = refs[0][...].astype(F32)
-    for ref in refs[1:half]:
+    for ref in refs[1:-1]:
         total = total + ref[...].astype(F32)
-    total = total.astype(BF16)
-    for n, out in enumerate(refs[half:]):
-        out[...] = total[n]
-
-
-def line_sum(parts, steps=2):
+    refs[-1][...] = total.astype(BF16)
+
+
+def stack_sum(parts, steps=2):
     n, rows, width = parts[0].shape
     wide = width // steps
     block = pl.BlockSpec((n, rows, wide), lambda i: (0, 0, i))
     return pl.pallas_call(
-        line_kernel,
+        stack_kernel,
         grid=(steps,),
-        out_shape=(far((rows, width)),) * n,
+        out_shape=far(parts[0].shape),
         in_specs=[block] * len(parts),
-        out_specs=(pl.BlockSpec((rows, wide), lambda i: (0, i)),) * n,
-        compiler_params=params(),
-        cost_estimate=cost(n * n * rows * width, 2 * n * (n + 1) * rows * width),
-        name="line_sum",
+        out_specs=block,
+        compiler_params=params(),
+        cost_estimate=cost(len(parts) * n * rows * width, 2 * (len(parts) + 1) * n * rows * width),
+        name="stack_sum",
     )(*parts)
 
 
-def chip_sum_kernel(one_ref, *refs):
+def row_sum_kernel(two_ref, *refs):
     parts, out_ref = refs[:-1], refs[-1]
-    one = one_ref[0].astype(F32)
-    for i in range(1, one_ref.shape[0]):
-        one = one + one_ref[i].astype(F32)
-    two = parts[0][...].astype(F32)
+    one = parts[0][...].astype(F32)
     for ref in parts[1:]:
-        two = two + ref[...].astype(F32)
-    half = CAP // 2
+        one = one + ref[...].astype(F32)
+    two = two_ref[0].astype(F32)
+    for i in range(1, two_ref.shape[0]):
+        two = two + two_ref[i].astype(F32)
+    half = one.shape[1]
     for j in range(out_ref.shape[0]):
-        at = slice(j * half, (j + 1) * half)
-        out_ref[j] = jnp.concatenate([one[at], two[at]], axis=0).astype(BF16)
-
-
-def chip_sum(one, parts, held, steps=4):
-    chips, rows, width = one.shape
-    wide = width // steps
-    return pl.pallas_call(
-        chip_sum_kernel,
-        grid=(steps,),
-        out_shape=far((held, CAP, width)),
-        in_specs=[pl.BlockSpec((chips, rows, wide), lambda i: (0, 0, i))]
-        + [pl.BlockSpec((rows, wide), lambda i: (0, i))] * len(parts),
-        out_specs=pl.BlockSpec((held, CAP, wide), lambda i: (0, 0, i)),
-        compiler_params=params(),
-        cost_estimate=cost(chips * rows * width, 3 * chips * rows * width),
-        name="chip_sum",
-    )(one, *parts)
+        at = slice(j * CAP, (j + 1) * CAP)
+        out_ref[j, :, :half] = one[at].astype(BF16)
+        out_ref[j, :, half:] = two[at].astype(BF16)
+
+
+def row_sum(parts, two, held):
+    count, rows, half = two.shape
+    whole = pl.BlockSpec(memory_space=pltpu.VMEM)
+    return pl.pallas_call(
+        row_sum_kernel,
+        out_shape=far((held, CAP, 2 * half)),
+        in_specs=[whole] * (1 + len(parts)),
+        out_specs=whole,
+        compiler_params=params(),
+        cost_estimate=cost(8 * rows * half, 20 * rows * half),
+        name="row_sum",
+    )(two, *parts)
 
 
 def combine_kernel(place_ref, rows_ref, ids_ref, weights_ref, out_ref):
@@ -704,7 +758,7 @@
     ld = hbm(log_decay.T)
     me = lax.axis_index("exp").reshape(1)
     keep = lax.optimization_barrier
-    chips = lax.axis_size("z") * lax.axis_size("x")
+    nz, nx = lax.axis_size("z"), lax.axis_size("x")
 
     cum, msg = local_states(hbm(key_vectors), hbm(values), ld)
     sent = exchange(msg, CTX)
@@ -719,26 +773,35 @@
 
     routed, attention = carried_blocks(me, inside, hbm(qs), state, hbm(place), held)
     routed = exchange(routed.reshape(held, held * CAP, width), "exp")
-    one, two = routed_norm(me, routed, pieces, attn_gain, moe_gain, chips)
-
-    attention, two = keep((attention, two))
-    one = exchange(one, ("z", "x"))
-    line = jnp.stack([two] + [shift(two, "x", d) for d in range(1, 4)])
-    plane = [line] + [shift(line, "z", d) for d in range(1, 4)]
+    one, two = routed_norm(me, routed, pieces, attn_gain, moe_gain, nz)
+
+    others = range(1, nx)
+    attention, one = keep((attention, one))
+    ones = [one] + [shift(one, "x", d) for d in others]
+    two = exchange(two, "z")
+    ones, two = keep((ones, two))
+    one = exchange(repeat(ones, nz), "z")
+    twos = [two] + [shift(two, "x", d) for d in others]
     attention = [attention[0]] + [shift(attention[d], "exp", d) for d in range(1, held)]
-    one, plane, attention = keep((one, plane, attention))
-    near = [a.reshape(-1, a.shape[2]) for a in [one] + plane]
-    act = expert_act(near + [shift(a, "core", 1) for a in near], w_gate, w_up)
-    own1, own2, other1, other2 = expert_down(act, w_down, chips, two.shape[0])
-    (one,) = pair_sum(own1, shift(other1, "core", 1))
-    one = exchange(one, ("z", "x"))
-    parts = pair_sum(own2, shift(other2, "core", 1), pieces=4)
-    parts = [parts[0]] + [shift(parts[d], "z", -d) for d in range(1, 4)]
-    one, parts = keep((one, parts))
-    parts = line_sum(parts)
-    parts = [parts[0]] + [shift(parts[d], "x", -d) for d in range(1, 4)]
+    one, twos, attention = keep((one, twos, attention))
+
+    act_own = expert_act(one, twos, w_gate, w_up)
+    one, twos = shift(one, "core", 1), [shift(a, "core", 1) for a in twos]
+    one, twos, act_own = keep((one, twos, act_own))
+    other1, other2 = expert_down(expert_act(one, twos, w_gate, w_up), w_down, nz, nx)
+    other1, other2, act_own = keep((other1, other2, act_own))
+    own1, own2 = expert_down(act_own, w_down, nz, nx)
+    (one,) = pair_sum(own1, shift(other1, "core", 1), False)
+    twos = pair_sum(own2, shift(other2, "core", 1), True)
+
+    one = exchange(one, "z")
+    twos = [twos[0]] + [shift(twos[d], "x", -d) for d in others]
+    one, twos = keep((one, twos))
+    ones = block_sum(one)
+    ones = [ones[0]] + [shift(ones[d], "x", -d) for d in others]
+    two = exchange(stack_sum(twos), "z")
     hidden = hidden_rows(me, attention, hbm(residual), hbm(out_gate), attn_gain)
-    back = exchange(chip_sum(one, parts, held), "exp")
+    back = exchange(row_sum(ones, two, held), "exp")
     moe_out = combine_rows(place_own, back, expert_ids, route_weights)
     return (hidden, moe_out)
 

time: 216 us -> 194 us (0.90)
  waiting for transfers between devices: 79.3 us -> 47.5 us
  starting transfers between devices: 61.9 us -> 66.6 us
  local copies, waits for them, and re-layouts: 5.17 us -> 9.12 us
    ppermute x25, waiting for transfers between devices: 78.2 us -> 46.5 us  [shift(): return lax.ppermute(a, axis, [(i, (i + by) % n) for i in range(n)])]
    all_to_all x5 -> x7, starting transfers between devices: 30.8 us -> 36.8 us  [exchange(): return lax.all_to_all(a, axis, split_axis=0, concat_axis=0, tiled=True)]
    unnamed x38 -> x40, local copies, waits for them, and re-layouts: 5.17 us -> 9.12 us
    pallas_call x1 -> x2, Pallas kernels: 6.54 us -> 8.56 us  [expert_down(): pl.pallas_call(functools.partial(down_kernel, steps), out_shape=(jax.Shap...]
    pallas_call x1 -> x2, Pallas kernels: 7.01 us -> 8.38 us  [expert_act(): pl.pallas_call(functools.partial(act_kernel, steps), out_shape=jax.ShapeD...]
    pallas_call x5 -> x7, Pallas kernels: 11.2 us -> 10.3 us  [the longest x2 3.92 us: pair_sum(): pl.pallas_call(pair_kernel, grid=(steps,), out_shape=(far((m, rows, width...]
  transfers between devices with their start and end apart: 30 -> 32, of which waited for: 19 -> 15; matrix products, arithmetic and copies ran while one was open for 0% -> 0% of each run, Pallas kernels for 11% -> 16%
where the time goes in v6:
time: 194 us; the launch traced here: 193 us
  starting transfers between devices  66.6 us (34%)
  Pallas kernels  58.8 us (30%)
  waiting for transfers between devices  47.5 us (24%)
  blocking collectives  9.67 us (5%)
  local copies, waits for them, and re-layouts  9.12 us (5%)
    ppermute x25, waiting for transfers between devices, shift(): return lax.ppermute(a, axis, [(i, (i + by) % n) for i in range(n)])  46.5 us
    all_to_all x7, starting transfers between devices, exchange(): return lax.all_to_all(a, axis, split_axis=0, concat_axis=0, tiled=True)  36.8 us
    ppermute x25, starting transfers between devices, shift(): return lax.ppermute(a, axis, [(i, (i + by) % n) for i in range(n)])  29.8 us
    all_to_all x1, blocking collectives, exchange(): return lax.all_to_all(a, axis, split_axis=0, concat_axis=0, tiled=True)  9.67 us
    unnamed x40, local copies, waits for them, and re-layouts  9.12 us
    pallas_call x2, Pallas kernels, expert_down(): pl.pallas_call(functools.partial(down_kernel, steps), out_shape=(jax.Shap...  8.56 us
    pallas_call x2, Pallas kernels, expert_act(): pl.pallas_call(functools.partial(act_kernel, steps), out_shape=jax.ShapeD...  8.38 us
    pallas_call x1, Pallas kernels, inside_blocks(): pl.pallas_call(functools.partial(inside_kernel, group), grid=(heads // gr...  7.82 us
  transfers between devices with their start and end apart: 32, of which 15 were waited for; matrix products, arithmetic and copies ran while one was open for 0% of the time, Pallas kernels for 16%

profile of v6, /device:TPU:0, one launch (start us, length us, event | category | flops | bytes accessed | tf_op | source)
XLA Modules:
  0.0 192.5 jit_solution(11126610909904396086)
XLA Ops:
  0.6 5.9 %local_states.1 = (f32[512,12]{1,0:T(8,128)S(1)}, bf16[32,64,128]{2,1,0:T(8,128)(2,1)}) custom-call(bf16[512,1536]{1,0:T(8,128)(2,1)} %k_ref.3, bf16[512,1536]{1,0:T(8,128)(2,1)} %v_ref.3, f32[12,512]{1,0:T(8,128)} %bitcast.27), custom_call_target="tpu_custom_call" | custom-call | flops 201326592 | bytes 3145728 | tf_op jit(solution)/shard_map/local_states/pallas_call | solution.py:122
  6.5 8.4 %all-to-all-start = ((bf16[32,64,128]{2,1,0:T(8,128)(2,1)}), bf16[32,64,128]{2,1,0:T(8,128)(2,1)}, u32[]{:S(2)}, u32[]{:S(2)}) async-start(bf16[32,64,128]{2,1,0:T(8,128)(2,1)} %get-tuple-element.70), calls=%async_computation | async-start | bytes 1048576 | tf_op jit(solution)/shard_map/all_to_all | solution.py:725
  14.9 3.2 %route_rows.1 = (bf16[8,6400]{1,0:T(8,128)(2,1)}, bf16[8,6400]{1,0:T(8,128)(2,1)}, bf16[8,6400]{1,0:T(8,128)(2,1)}, bf16[8,6400]{1,0:T(8,128)(2,1)}, f32[16,128]{1,0:T(8,128)S(1)}) custom-call(s32[1]{0:T(128)} %bitcast.me_ref, s32[2,128]{1,0:T(2,128)S(1)} %bitcast.19, bf16[128,6144]{1,0:T(8,128)(2,1)} %res_ref.1, bf16[128,6144]{1,0:T(8,128)(2,1)} %gate_ref.1), custom_call_target="tpu_custom_call" | custom-call | flops 50331648 | bytes 3932160 | tf_op jit(solution)/shard_map/route_rows/pallas_call | solution.py:336
  18.1 7.8 %inside_blocks.1 = (f32[512,1536]{1,0:T(8,128)S(1)}, bf16[512,1536]{1,0:T(8,128)(2,1)}) custom-call(bf16[512,1536]{1,0:T(8,128)(2,1)} %q_ref.1, bf16[512,1536]{1,0:T(8,128)(2,1)} %k_ref.3, bf16[512,1536]{1,0:T(8,128)(2,1)} %v_ref.3, f32[512,12]{1,0:T(8,128)S(1)} %get-tuple-element.71.cum_ref, f32[12,512]{1,0:T(8,128)} %bitcast.28), custom_call_target="tpu_custom_call" | custom-call | flops 1610612736 | bytes 9437184 | tf_op jit(solution)/shard_map/inside_blocks/pallas_call | solution.py:216
  28.5 6.7 %all-to-all-start.1 = ((bf16[32,48,128]{2,1,0:T(8,128)(2,1)}), bf16[32,48,128]{2,1,0:T(8,128)(2,1)S(1)}, u32[]{:S(2)}, u32[]{:S(2)}) async-start(bf16[32,48,128]{2,1,0:T(8,128)(2,1)} %scan_blocks.1), calls=%async_computation.1 | async-start | bytes 786432 | tf_op jit(solution)/shard_map/all_to_all | solution.py:725
  41.8 3.4 %collective-permute-done.1.refs_2_ = bf16[8,6400]{1,0:T(8,128)(2,1)S(1)} collective-permute-done((bf16[8,6400]{1,0:T(8,128)(2,1)}, bf16[8,6400]{1,0:T(8,128)(2,1)S(1)}, u32[]{:S(2)}, u32[]{:S(2)}) %collective-permute-start.1) | collective-permute-done | bytes 102432 | tf_op jit(solution)/shard_map/ppermute | solution.py:730
  48.0 4.6 %carried_blocks.1 = (bf16[64,1536]{1,0:T(8,128)(2,1)}, bf16[128,1536]{1,0:T(8,128)(2,1)}, bf16[128,1536]{1,0:T(8,128)(2,1)}, bf16[128,1536]{1,0:T(8,128)(2,1)}, bf16[128,1536]{1,0:T(8,128)(2,1)}) custom-call(s32[1]{0:T(128)} %bitcast.me_ref, f32[512,1536]{1,0:T(8,128)S(1)} %get-tuple-element.78.inside_ref, bf16[512,1536]{1,0:T(8,128)(2,1)} %get-tuple-element.79.qs_ref, ...), custom_call_target="tpu_custom_call" | custom-call | flops 402653184 | bytes 6291456 | tf_op jit(solution)/shard_map/carried_blocks/pallas_call | solution.py:263
  52.5 9.7 %all_to_all.40.att_ref = bf16[4,16,1536]{2,1,0:T(8,128)(2,1)S(1)} all-to-all(bf16[4,16,1536]{2,1,0:T(8,128)(2,1)} %bitcast.26), channel_id=1, replica_groups=mesh['z'=4,'x'=4,'core'=2,'exp'=4] {'exp'}, dimensions={0} | all-to-all | bytes 393216 | tf_op jit(solution)/shard_map/all_to_all | solution.py:725
  64.5 4.4 %all-to-all-start.3 = ((bf16[4,16,3072]{2,1,0:T(8,128)(2,1)}), bf16[4,16,3072]{2,1,0:T(8,128)(2,1)S(1)}, u32[]{:S(2)}, u32[]{:S(2)}) async-start(bf16[4,16,3072]{2,1,0:T(8,128)(2,1)} %get-tuple-element.92), calls=%async_computation.3 | async-start | bytes 786432 | tf_op jit(solution)/shard_map/all_to_all | solution.py:725
  80.1 4.9 %all-to-all-start.4 = ((bf16[4,4,16,3072]{3,2,1,0:T(8,128)(2,1)}), bf16[4,4,16,3072]{3,2,1,0:T(8,128)(2,1)S(1)}, u32[]{:S(2)}, u32[]{:S(2)}) async-start(bf16[4,4,16,3072]{3,2,1,0:T(8,128)(2,1)} %repeat.1), calls=%async_computation.4 | async-start | bytes 3145728 | tf_op jit(solution)/shard_map/all_to_all | solution.py:725
  92.8 8.8 %collective-permute-done.9.refs_1_ = bf16[128,1536]{1,0:T(8,128)(2,1)S(1)} collective-permute-done((bf16[128,1536]{1,0:T(8,128)(2,1)S(1)}, bf16[128,1536]{1,0:T(8,128)(2,1)S(1)}, u32[]{:S(2)}, u32[]{:S(2)}) %collective-permute-start.9) | collective-permute-done | bytes 393248 | tf_op jit(solution)/shard_map/ppermute | solution.py:730
  105.6 3.9 %collective-permute-done.8.refs_3_ = bf16[4,16,3072]{2,1,0:T(8,128)(2,1)S(1)} collective-permute-done((bf16[4,16,3072]{2,1,0:T(8,128)(2,1)S(1)}, bf16[4,16,3072]{2,1,0:T(8,128)(2,1)S(1)}, u32[]{:S(2)}, u32[]{:S(2)}) %collective-permute-start.8) | collective-permute-done | bytes 393248 | tf_op jit(solution)/shard_map/ppermute | solution.py:730
  110.5 4.2 %expert_act.2.act_ref = bf16[256,288]{1,0:T(8,128)(2,1)S(1)} custom-call(bf16[288,6144]{1,0:T(8,128)(2,1)} %bitcast.20, bf16[288,6144]{1,0:T(8,128)(2,1)} %bitcast.22, bf16[4,4,16,3072]{3,2,1,0:T(8,128)(2,1)S(1)} %all-to-all-done.4.one_ref, bf16[4,16,3072]{2,1,0:T(8,128)(2,1)S(1)} %all-to-all-done.3.refs_0_, ...), custom_call_target="tpu_custom_call" | custom-call | flops 1811939328 | bytes 10223616 | tf_op jit(solution)/shard_map/expert_act/pallas_call | solution.py:541
  115.1 4.2 %expert_act.3.act_ref = bf16[256,288]{1,0:T(8,128)(2,1)S(1)} custom-call(bf16[288,6144]{1,0:T(8,128)(2,1)} %bitcast.21, bf16[288,6144]{1,0:T(8,128)(2,1)} %bitcast.23, bf16[4,4,16,3072]{3,2,1,0:T(8,128)(2,1)S(1)} %collective-permute-done.12.one_ref, bf16[4,16,3072]{2,1,0:T(8,128)(2,1)S(1)} %collective-permute-done.13.refs_0_, ...), custom_call_target="tpu_custom_call" | custom-call | flops 1811939328 | bytes 10223616 | tf_op jit(solution)/shard_map/expert_act/pallas_call | solution.py:541
  119.3 4.9 %expert_down.2 = (bf16[4,4,16,3072]{3,2,1,0:T(8,128)(2,1)S(1)}, bf16[4,4,16,3072]{3,2,1,0:T(8,128)(2,1)}) custom-call(bf16[256,288]{1,0:T(8,128)(2,1)S(1)} %expert_act.3.act_ref, bf16[288,6144]{1,0:T(8,128)(2,1)} %bitcast.24), custom_call_target="tpu_custom_call" | custom-call | flops 905969664 | bytes 6684672 | tf_op jit(solution)/shard_map/expert_down/pallas_call | solution.py:583
  124.8 3.7 %expert_down.3 = (bf16[4,4,16,3072]{3,2,1,0:T(8,128)(2,1)S(1)}, bf16[4,4,16,3072]{3,2,1,0:T(8,128)(2,1)S(1)}) custom-call(bf16[256,288]{1,0:T(8,128)(2,1)S(1)} %expert_act.2.act_ref, bf16[288,6144]{1,0:T(8,128)(2,1)} %bitcast.25), custom_call_target="tpu_custom_call" | custom-call | flops 905969664 | bytes 6684672 | tf_op jit(solution)/shard_map/expert_down/pallas_call | solution.py:583
  131.7 4.5 %all-to-all-start.5 = ((bf16[4,4,16,3072]{3,2,1,0:T(8,128)(2,1)}), bf16[4,4,16,3072]{3,2,1,0:T(8,128)(2,1)S(1)}, u32[]{:S(2)}, u32[]{:S(2)}) async-start(bf16[4,4,16,3072]{3,2,1,0:T(8,128)(2,1)} %pair_sum.2), calls=%async_computation.5 | async-start | bytes 3145728 | tf_op jit(solution)/shard_map/all_to_all | solution.py:725
  139.5 3.6 %collective-permute-start.19 = (bf16[4,16,3072]{2,1,0:T(8,128)(2,1)}, bf16[4,16,3072]{2,1,0:T(8,128)(2,1)S(1)}, u32[]{:S(2)}, u32[]{:S(2)}) collective-permute-start(bf16[4,16,3072]{2,1,0:T(8,128)(2,1)} %get-tuple-element.126), channel_id=1, source_target_pairs={{0,24},{8,0},{16,8},{24,16},{1,25},{9,1},{17,9},{25,17},{2,26},{10... | collective-permute-start | bytes 1179656 | tf_op jit(solution)/shard_map/ppermute | solution.py:730
  144.0 16.2 %collective-permute-done.19.refs_1_ = bf16[4,16,3072]{2,1,0:T(8,128)(2,1)S(1)} collective-permute-done((bf16[4,16,3072]{2,1,0:T(8,128)(2,1)}, bf16[4,16,3072]{2,1,0:T(8,128)(2,1)S(1)}, u32[]{:S(2)}, u32[]{:S(2)}) %collective-permute-start.19) | collective-permute-done | bytes 393248 | tf_op jit(solution)/shard_map/ppermute | solution.py:730
  160.2 3.3 %collective-permute-done.21.refs_3_ = bf16[4,16,3072]{2,1,0:T(8,128)(2,1)S(1)} collective-permute-done((bf16[4,16,3072]{2,1,0:T(8,128)(2,1)}, bf16[4,16,3072]{2,1,0:T(8,128)(2,1)S(1)}, u32[]{:S(2)}, u32[]{:S(2)}) %collective-permute-start.21) | collective-permute-done | bytes 393248 | tf_op jit(solution)/shard_map/ppermute | solution.py:730
  165.5 4.5 %all-to-all-start.6 = ((bf16[4,16,3072]{2,1,0:T(8,128)(2,1)}), bf16[4,16,3072]{2,1,0:T(8,128)(2,1)S(1)}, u32[]{:S(2)}, u32[]{:S(2)}) async-start(bf16[4,16,3072]{2,1,0:T(8,128)(2,1)} %stack_sum.1), calls=%async_computation.6 | async-start | bytes 786432 | tf_op jit(solution)/shard_map/all_to_all | solution.py:725
  173.1 3.3 %collective-permute-done.22.refs_1_ = bf16[16,3072]{1,0:T(8,128)(2,1)S(1)} collective-permute-done((bf16[16,3072]{1,0:T(8,128)(2,1)}, bf16[16,3072]{1,0:T(8,128)(2,1)S(1)}, u32[]{:S(2)}, u32[]{:S(2)}) %collective-permute-start.22) | collective-permute-done | bytes 98336 | tf_op jit(solution)/shard_map/ppermute | solution.py:730
  181.1 3.4 %all-to-all-start.7 = ((bf16[4,4,6144]{2,1,0:T(4,128)(2,1)}), bf16[4,4,6144]{2,1,0:T(4,128)(2,1)S(1)}, u32[]{:S(2)}, u32[]{:S(2)}) async-start(bf16[4,4,6144]{2,1,0:T(4,128)(2,1)} %row_sum.1), calls=%async_computation.7 | async-start | bytes 393216 | tf_op jit(solution)/shard_map/all_to_all | solution.py:725
  185.5 4.9 %hidden_rows.1 = bf16[128,6144]{1,0:T(8,128)(2,1)} custom-call(s32[1]{0:T(128)} %bitcast.me_ref, bf16[128,6144]{1,0:T(8,128)(2,1)} %res_ref.1, bf16[128,6144]{1,0:T(8,128)(2,1)} %gate_ref.1, f32[1,6144]{1,0:T(1,128)S(1)} %bitcast.17, bf16[128,1536]{1,0:T(8,128)(2,1)S(1)} %copy-done.2, bf16[128,1536]{1,0:T(8,128)(2,1)S(1)} %collective-permute-done.9.refs_1_, ...), custom_call_target="tpu_custom_call" | custom-call | flops 15728640 | bytes 6291456 | tf_op jit(solution)/shard_map/hidden_rows/pallas_call | solution.py:456
  (100 shorter events, 59.3 us)
Async XLA Ops:
  6.5 20.1 %all-to-all-start = ((bf16[32,64,128]{2,1,0:T(8,128)(2,1)}), bf16[32,64,128]{2,1,0:T(8,128)(2,1)}, u32[]{:S(2)}, u32[]{:S(2)}) async-start(bf16[32,64,128]{2,1,0:T(8,128)(2,1)} %get-tuple-element.70), calls=%async_computation | async-start | bytes 1048576 | tf_op jit(solution)/shard_map/all_to_all | solution.py:725
  28.5 19.4 %all-to-all-start.1 = ((bf16[32,48,128]{2,1,0:T(8,128)(2,1)}), bf16[32,48,128]{2,1,0:T(8,128)(2,1)S(1)}, u32[]{:S(2)}, u32[]{:S(2)}) async-start(bf16[32,48,128]{2,1,0:T(8,128)(2,1)} %scan_blocks.1), calls=%async_computation.1 | async-start | bytes 786432 | tf_op jit(solution)/shard_map/all_to_all | solution.py:725
  35.2 6.6 %collective-permute-start = (bf16[8,6400]{1,0:T(8,128)(2,1)}, bf16[8,6400]{1,0:T(8,128)(2,1)S(1)}, u32[]{:S(2)}, u32[]{:S(2)}) collective-permute-start(bf16[8,6400]{1,0:T(8,128)(2,1)} %get-tuple-element.82), channel_id=1, source_target_pairs={{0,1},{1,2},{2,3},{3,0},{4,5},{5,6},{6,7},{7,4},{8,9},{9,10},{10,1... | collective-permute-start | bytes 307208 | tf_op jit(solution)/shard_map/ppermute | solution.py:730
  36.8 8.3 %collective-permute-start.1 = (bf16[8,6400]{1,0:T(8,128)(2,1)}, bf16[8,6400]{1,0:T(8,128)(2,1)S(1)}, u32[]{:S(2)}, u32[]{:S(2)}) collective-permute-start(bf16[8,6400]{1,0:T(8,128)(2,1)} %get-tuple-element.83), channel_id=1, source_target_pairs={{0,2},{1,3},{2,0},{3,1},{4,6},{5,7},{6,4},{7,5},{8,10},{9,11},{10,... | collective-permute-start | bytes 307208 | tf_op jit(solution)/shard_map/ppermute | solution.py:730
  64.5 13.4 %all-to-all-start.3 = ((bf16[4,16,3072]{2,1,0:T(8,128)(2,1)}), bf16[4,16,3072]{2,1,0:T(8,128)(2,1)S(1)}, u32[]{:S(2)}, u32[]{:S(2)}) async-start(bf16[4,16,3072]{2,1,0:T(8,128)(2,1)} %get-tuple-element.92), calls=%async_computation.3 | async-start | bytes 786432 | tf_op jit(solution)/shard_map/all_to_all | solution.py:725
  69.0 6.0 %collective-permute-start.3 = (bf16[16,3072]{1,0:T(8,128)(2,1)}, bf16[16,3072]{1,0:T(8,128)(2,1)S(1)}, u32[]{:S(2)}, u32[]{:S(2)}) collective-permute-start(bf16[16,3072]{1,0:T(8,128)(2,1)} %get-tuple-element.93.refs_0_), channel_id=1, source_target_pairs={{0,8},{8,16},{16,24},{24,0},{1,9},{9,17},{17,25},{25,1},{2,10},{10... | collective-permute-start | bytes 294920 | tf_op jit(solution)/shard_map/ppermute | solution.py:730
  70.4 6.6 %collective-permute-start.4 = (bf16[16,3072]{1,0:T(8,128)(2,1)}, bf16[16,3072]{1,0:T(8,128)(2,1)S(1)}, u32[]{:S(2)}, u32[]{:S(2)}) collective-permute-start(bf16[16,3072]{1,0:T(8,128)(2,1)} %get-tuple-element.93.refs_0_), channel_id=1, source_target_pairs={{0,16},{8,24},{16,0},{24,8},{1,17},{9,25},{17,1},{25,9},{2,18},{10... | collective-permute-start | bytes 294920 | tf_op jit(solution)/shard_map/ppermute | solution.py:730
  80.1 29.3 %all-to-all-start.4 = ((bf16[4,4,16,3072]{3,2,1,0:T(8,128)(2,1)}), bf16[4,4,16,3072]{3,2,1,0:T(8,128)(2,1)S(1)}, u32[]{:S(2)}, u32[]{:S(2)}) async-start(bf16[4,4,16,3072]{3,2,1,0:T(8,128)(2,1)} %repeat.1), calls=%async_computation.4 | async-start | bytes 3145728 | tf_op jit(solution)/shard_map/all_to_all | solution.py:725
  85.1 16.6 %collective-permute-start.9 = (bf16[128,1536]{1,0:T(8,128)(2,1)S(1)}, bf16[128,1536]{1,0:T(8,128)(2,1)S(1)}, u32[]{:S(2)}, u32[]{:S(2)}) collective-permute-start(bf16[128,1536]{1,0:T(8,128)(2,1)S(1)} %copy-done.18), channel_id=1, source_target_pairs={{0,1},{1,2},{2,3},{3,0},{4,5},{5,6},{6,7},{7,4},{8,9},{9,10},{10,1... | collective-permute-start | bytes 1179656 | tf_op jit(solution)/shard_map/ppermute | solution.py:730
  85.7 18.4 %collective-permute-start.10 = (bf16[128,1536]{1,0:T(8,128)(2,1)}, bf16[128,1536]{1,0:T(8,128)(2,1)S(1)}, u32[]{:S(2)}, u32[]{:S(2)}) collective-permute-start(bf16[128,1536]{1,0:T(8,128)(2,1)} %get-tuple-element.100), channel_id=1, source_target_pairs={{0,2},{1,3},{2,0},{3,1},{4,6},{5,7},{6,4},{7,5},{8,10},{9,11},{10,... | collective-permute-start | bytes 1179656 | tf_op jit(solution)/shard_map/ppermute | solution.py:730
  87.7 17.1 %collective-permute-start.11 = (bf16[128,1536]{1,0:T(8,128)(2,1)}, bf16[128,1536]{1,0:T(8,128)(2,1)S(1)}, u32[]{:S(2)}, u32[]{:S(2)}) collective-permute-start(bf16[128,1536]{1,0:T(8,128)(2,1)} %get-tuple-element.101), channel_id=1, source_target_pairs={{0,3},{1,0},{2,1},{3,2},{4,7},{5,4},{6,5},{7,6},{8,11},{9,8},{10,9... | collective-permute-start | bytes 1179656 | tf_op jit(solution)/shard_map/ppermute | solution.py:730
  88.7 16.9 %collective-permute-start.6 = (bf16[4,16,3072]{2,1,0:T(8,128)(2,1)S(1)}, bf16[4,16,3072]{2,1,0:T(8,128)(2,1)S(1)}, u32[]{:S(2)}, u32[]{:S(2)}) collective-permute-start(bf16[4,16,3072]{2,1,0:T(8,128)(2,1)S(1)} %all-to-all-done.3.refs_0_), channel_id=1, source_target_pairs={{0,8},{8,16},{16,24},{24,0},{1,9},{9,17},{17,25},{25,1},{2,10},{10... | collective-permute-start | bytes 1179656 | tf_op jit(solution)/shard_map/ppermute | solution.py:730
  89.7 15.9 %collective-permute-start.7 = (bf16[4,16,3072]{2,1,0:T(8,128)(2,1)S(1)}, bf16[4,16,3072]{2,1,0:T(8,128)(2,1)S(1)}, u32[]{:S(2)}, u32[]{:S(2)}) collective-permute-start(bf16[4,16,3072]{2,1,0:T(8,128)(2,1)S(1)} %all-to-all-done.3.refs_0_), channel_id=1, source_target_pairs={{0,16},{8,24},{16,0},{24,8},{1,17},{9,25},{17,1},{25,9},{2,18},{10... | collective-permute-start | bytes 1179656 | tf_op jit(solution)/shard_map/ppermute | solution.py:730
  101.7 7.8 %collective-permute-start.8 = (bf16[4,16,3072]{2,1,0:T(8,128)(2,1)S(1)}, bf16[4,16,3072]{2,1,0:T(8,128)(2,1)S(1)}, u32[]{:S(2)}, u32[]{:S(2)}) collective-permute-start(bf16[4,16,3072]{2,1,0:T(8,128)(2,1)S(1)} %all-to-all-done.3.refs_0_), channel_id=1, source_target_pairs={{0,24},{8,0},{16,8},{24,16},{1,25},{9,1},{17,9},{25,17},{2,26},{10... | collective-permute-start | bytes 1179656 | tf_op jit(solution)/shard_map/ppermute | solution.py:730
  109.4 5.7 %collective-permute-start.12 = (bf16[4,4,16,3072]{3,2,1,0:T(8,128)(2,1)S(1)}, bf16[4,4,16,3072]{3,2,1,0:T(8,128)(2,1)S(1)}, u32[]{:S(2)}, u32[]{:S(2)}) collective-permute-start(bf16[4,4,16,3072]{3,2,1,0:T(8,128)(2,1)S(1)} %all-to-all-done.4.one_ref), channel_id=1, source_target_pairs={{0,4},{4,0},{1,5},{5,1},{2,6},{6,2},{3,7},{7,3},{8,12},{12,8},{9,1... | collective-permute-start | bytes 4718600 | tf_op jit(solution)/shard_map/ppermute | solution.py:730
  124.4 11.8 %collective-permute-start.18 = (bf16[4,4,16,3072]{3,2,1,0:T(8,128)(2,1)}, bf16[4,4,16,3072]{3,2,1,0:T(8,128)(2,1)S(1)}, u32[]{:S(2)}, u32[]{:S(2)}) collective-permute-start(bf16[4,4,16,3072]{3,2,1,0:T(8,128)(2,1)} %get-tuple-element.124), channel_id=1, source_target_pairs={{0,4},{4,0},{1,5},{5,1},{2,6},{6,2},{3,7},{7,3},{8,12},{12,8},{9,1... | collective-permute-start | bytes 4718600 | tf_op jit(solution)/shard_map/ppermute | solution.py:730
  131.7 31.8 %all-to-all-start.5 = ((bf16[4,4,16,3072]{3,2,1,0:T(8,128)(2,1)}), bf16[4,4,16,3072]{3,2,1,0:T(8,128)(2,1)S(1)}, u32[]{:S(2)}, u32[]{:S(2)}) async-start(bf16[4,4,16,3072]{3,2,1,0:T(8,128)(2,1)} %pair_sum.2), calls=%async_computation.5 | async-start | bytes 3145728 | tf_op jit(solution)/shard_map/all_to_all | solution.py:725
  139.5 20.7 %collective-permute-start.19 = (bf16[4,16,3072]{2,1,0:T(8,128)(2,1)}, bf16[4,16,3072]{2,1,0:T(8,128)(2,1)S(1)}, u32[]{:S(2)}, u32[]{:S(2)}) collective-permute-start(bf16[4,16,3072]{2,1,0:T(8,128)(2,1)} %get-tuple-element.126), channel_id=1, source_target_pairs={{0,24},{8,0},{16,8},{24,16},{1,25},{9,1},{17,9},{25,17},{2,26},{10... | collective-permute-start | bytes 1179656 | tf_op jit(solution)/shard_map/ppermute | solution.py:730
  143.1 17.1 %collective-permute-start.20 = (bf16[4,16,3072]{2,1,0:T(8,128)(2,1)}, bf16[4,16,3072]{2,1,0:T(8,128)(2,1)S(1)}, u32[]{:S(2)}, u32[]{:S(2)}) collective-permute-start(bf16[4,16,3072]{2,1,0:T(8,128)(2,1)} %get-tuple-element.127), channel_id=1, source_target_pairs={{0,16},{8,24},{16,0},{24,8},{1,17},{9,25},{17,1},{25,9},{2,18},{10... | collective-permute-start | bytes 1179656 | tf_op jit(solution)/shard_map/ppermute | solution.py:730
  143.1 20.4 %collective-permute-start.21 = (bf16[4,16,3072]{2,1,0:T(8,128)(2,1)}, bf16[4,16,3072]{2,1,0:T(8,128)(2,1)S(1)}, u32[]{:S(2)}, u32[]{:S(2)}) collective-permute-start(bf16[4,16,3072]{2,1,0:T(8,128)(2,1)} %get-tuple-element.128), channel_id=1, source_target_pairs={{0,8},{8,16},{16,24},{24,0},{1,9},{9,17},{17,25},{25,1},{2,10},{10... | collective-permute-start | bytes 1179656 | tf_op jit(solution)/shard_map/ppermute | solution.py:730
  165.5 13.9 %all-to-all-start.6 = ((bf16[4,16,3072]{2,1,0:T(8,128)(2,1)}), bf16[4,16,3072]{2,1,0:T(8,128)(2,1)S(1)}, u32[]{:S(2)}, u32[]{:S(2)}) async-start(bf16[4,16,3072]{2,1,0:T(8,128)(2,1)} %stack_sum.1), calls=%async_computation.6 | async-start | bytes 786432 | tf_op jit(solution)/shard_map/all_to_all | solution.py:725
  172.0 7.1 %collective-permute-start.23 = (bf16[16,3072]{1,0:T(8,128)(2,1)}, bf16[16,3072]{1,0:T(8,128)(2,1)S(1)}, u32[]{:S(2)}, u32[]{:S(2)}) collective-permute-start(bf16[16,3072]{1,0:T(8,128)(2,1)} %get-tuple-element.136), channel_id=1, source_target_pairs={{0,16},{8,24},{16,0},{24,8},{1,17},{9,25},{17,1},{25,9},{2,18},{10... | collective-permute-start | bytes 294920 | tf_op jit(solution)/shard_map/ppermute | solution.py:730
  172.2 7.2 %collective-permute-start.24 = (bf16[16,3072]{1,0:T(8,128)(2,1)}, bf16[16,3072]{1,0:T(8,128)(2,1)S(1)}, u32[]{:S(2)}, u32[]{:S(2)}) collective-permute-start(bf16[16,3072]{1,0:T(8,128)(2,1)} %get-tuple-element.137), channel_id=1, source_target_pairs={{0,8},{8,16},{16,24},{24,0},{1,9},{9,17},{17,25},{25,1},{2,10},{10... | collective-permute-start | bytes 294920 | tf_op jit(solution)/shard_map/ppermute | solution.py:730
  181.1 9.7 %all-to-all-start.7 = ((bf16[4,4,6144]{2,1,0:T(4,128)(2,1)}), bf16[4,4,6144]{2,1,0:T(4,128)(2,1)S(1)}, u32[]{:S(2)}, u32[]{:S(2)}) async-start(bf16[4,4,6144]{2,1,0:T(4,128)(2,1)} %row_sum.1), calls=%async_computation.7 | async-start | bytes 393216 | tf_op jit(solution)/shard_map/all_to_all | solution.py:725
  (27 other events, 158.9 us)

commit v7 on v6

--- a/solution.py
+++ b/solution.py
@@ -235,50 +235,80 @@
     )(q, k, v, cum, ld)
 
 
-def carried_kernel(group, me_ref, inside_ref, qs_ref, state_ref, place_ref, sel_ref, *refs):
-    outs, att_ref = refs[:-1], refs[-1]
-    held = len(outs)
-    tokens = outs[0].shape[0]
+def attend(group, inside_ref, qs_ref, state_ref, att_ref):
     for j in range(group):
         cols = slice(j * HEAD_DIM, (j + 1) * HEAD_DIM)
         att_ref[:, cols] = (
             inside_ref[:, cols]
             + jnp.dot(qs_ref[:, cols], state_ref[j], preferred_element_type=F32)
         ).astype(BF16)
+
+
+def chosen_kernel(group, inside_ref, qs_ref, state_ref, place_ref, sel_ref, att_ref):
+    attend(group, inside_ref, qs_ref, state_ref, att_ref)
     sel_ref[...] = jnp.dot(
         place_ref[...], att_ref[...], preferred_element_type=F32
     ).astype(BF16)
+
+
+def carried_kernel(group, me_ref, inside_ref, qs_ref, state_ref, *refs):
+    outs, att_ref = refs[:-1], refs[-1]
+    held = len(outs)
+    tokens = outs[0].shape[0]
+    attend(group, inside_ref, qs_ref, state_ref, att_ref)
     for d in range(held):
         at = pl.multiple_of(lax.rem(me_ref[0] + d, held) * tokens, tokens)
         outs[d][...] = att_ref[pl.ds(at, tokens), :]
 
 
-def carried_blocks(me, inside, qs, state, place, held, group=3):
+def chosen_rows(inside, qs, state, place, group=3):
     rows, width = inside.shape
     heads = width // HEAD_DIM
     chosen = place.shape[0]
     wide = group * HEAD_DIM
-    tokens = rows // held
     block = pl.BlockSpec((rows, wide), lambda g: (0, g))
-    outs = pl.pallas_call(
-        functools.partial(carried_kernel, group),
+    return pl.pallas_call(
+        functools.partial(chosen_kernel, group),
         grid=(heads // group,),
-        out_shape=(far((chosen, width)),) + (far((tokens, width)),) * held,
+        out_shape=far((chosen, width)),
         in_specs=[
-            pl.BlockSpec(memory_space=pltpu.SMEM),
             block,
             block,
             pl.BlockSpec((group, HEAD_DIM, HEAD_DIM), lambda g: (g, 0, 0)),
             pl.BlockSpec((chosen, rows), lambda g: (0, 0)),
         ],
-        out_specs=(pl.BlockSpec((chosen, wide), lambda g: (0, g)),)
-        + (pl.BlockSpec((tokens, wide), lambda g: (0, g)),) * held,
+        out_specs=pl.BlockSpec((chosen, wide), lambda g: (0, g)),
         scratch_shapes=[pltpu.VMEM((rows, wide), BF16)],
         compiler_params=params(),
         cost_estimate=cost(4 * rows * width * HEAD_DIM, 8 * rows * width),
-        name="carried_blocks",
-    )(me, inside, qs, state, place)
-    return outs[0], list(outs[1:])
+        name="chosen_rows",
+    )(inside, qs, state, place)
+
+
+def carried_blocks(me, inside, qs, state, held, group=3):
+    rows, width = inside.shape
+    heads = width // HEAD_DIM
+    wide = group * HEAD_DIM
+    tokens = rows // held
+    block = pl.BlockSpec((rows, wide), lambda g: (0, g))
+    return list(
+        pl.pallas_call(
+            functools.partial(carried_kernel, group),
+            grid=(heads // group,),
+            out_shape=(far((tokens, width)),) * held,
+            in_specs=[
+                pl.BlockSpec(memory_space=pltpu.SMEM),
+                block,
+                block,
+                pl.BlockSpec((group, HEAD_DIM, HEAD_DIM), lambda g: (g, 0, 0)),
+            ],
+            out_specs=(pl.BlockSpec((tokens, wide), lambda g: (0, g)),) * held,
+            scratch_shapes=[pltpu.VMEM((rows, wide), BF16)],
+            compiler_params=params(),
+            cost_estimate=cost(4 * rows * width * HEAD_DIM, 8 * rows * width),
+            name="carried_blocks",
+        )(me, inside, qs, state)
+    )
 
 
 def route_kernel(pieces, me_ref, ids_ref, res_hbm, gate_hbm, *refs):
@@ -553,72 +583,77 @@
     )(hbm(w_gate), hbm(w_up), one, *twos)
 
 
-def down_kernel(steps, act_ref, wd_hbm, one_ref, two_ref, wd_ref, sem):
-    nz, nx, rows, half = one_ref.shape
-    wide = 2 * half // steps
-    act = act_ref[...]
+def down_kernel(steps, first, by_x, act_ref, wd_hbm, *refs):
+    wd_ref, sem = refs[-2:]
+    half = wd_ref.shape[1]
+    wide = half // steps
     copies = []
     for s in range(steps):
         cols = pl.ds(s * wide, wide)
-        copies.append(pltpu.make_async_copy(wd_hbm.at[:, cols], wd_ref.at[:, cols], sem.at[s]))
+        copies.append(
+            pltpu.make_async_copy(
+                wd_hbm.at[:, pl.ds(first + s * wide, wide)], wd_ref.at[:, cols], sem.at[s]
+            )
+        )
     for c in copies:
         c.start()
+    refs = refs[:-2]
+    added = refs[0] if len(refs) != 1 else None
+    outs = refs[1:] if len(refs) != 1 else refs
+    act = act_ref[...]
+    if by_x:
+        nx = outs[0].shape[0] if len(outs) == 1 else len(outs)
+        nz = outs[0].shape[-3]
+    else:
+        nz, nx = outs[0].shape[:2]
+    rows = outs[0].shape[-2]
     for s in range(steps):
         cols = slice(s * wide, (s + 1) * wide)
         copies[s].wait()
         out = jnp.dot(act, wd_ref[:, cols], preferred_element_type=F32)
-        out = out.reshape(nx, nz, rows, wide).astype(BF16)
-        if s < steps // 2:
+        out = out.reshape(nx, nz, rows, wide)
+        if by_x:
+            if added is not None:
+                out = out + added[:, :, :, cols].astype(F32)
+            out = out.astype(BF16)
+            if len(outs) == 1:
+                outs[0][:, :, :, cols] = out
+            else:
+                for k in range(nx):
+                    outs[k][:, :, cols] = out[k]
+        else:
             for z in range(nz):
-                one_ref[z, :, :, cols] = out[:, z]
-        else:
-            two_ref[:, :, :, s * wide - half : (s + 1) * wide - half] = out
-
-
-def expert_down(act, w_down, nz, nx, steps=6):
+                part = out[:, z]
+                if added is not None:
+                    part = part + added[z, :, :, cols].astype(F32)
+                outs[0][z, :, :, cols] = part.astype(BF16)
+
+
+def expert_down(act, w_down, last, nz, nx, added=None, steps=3):
     count, units = act.shape
-    width = w_down.shape[1]
+    half = w_down.shape[1] // 2
     rows = count // (nz * nx)
     whole = pl.BlockSpec(memory_space=pltpu.VMEM)
-    return pl.pallas_call(
-        functools.partial(down_kernel, steps),
-        out_shape=(
-            jax.ShapeDtypeStruct((nz, nx, rows, width // 2), BF16),
-            jax.ShapeDtypeStruct((nx, nz, rows, width // 2), BF16),
-        ),
-        in_specs=[whole, pl.BlockSpec(memory_space=pl.ANY)],
-        out_specs=(whole, whole),
-        scratch_shapes=[pltpu.VMEM((units, width), BF16), pltpu.SemaphoreType.DMA((steps,))],
-        compiler_params=params(),
-        cost_estimate=cost(2 * count * width * units, 2 * width * units + 2 * count * width),
+    if last:
+        if added is None:
+            shapes = (jax.ShapeDtypeStruct((nx, nz, rows, half), BF16),)
+        else:
+            shapes = (far((nz, rows, half)),) * nx
+    elif added is None:
+        shapes = (jax.ShapeDtypeStruct((nz, nx, rows, half), BF16),)
+    else:
+        shapes = (far((nz, nx, rows, half)),)
+    more = () if added is None else (added,)
+    return pl.pallas_call(
+        functools.partial(down_kernel, steps, half if last else 0, last),
+        out_shape=shapes,
+        in_specs=[whole, pl.BlockSpec(memory_space=pl.ANY)] + [whole] * len(more),
+        out_specs=(whole,) * len(shapes),
+        scratch_shapes=[pltpu.VMEM((units, half), BF16), pltpu.SemaphoreType.DMA((steps,))],
+        compiler_params=params(),
+        cost_estimate=cost(2 * count * half * units, 2 * half * units + 2 * count * half),
         name="expert_down",
-    )(act, hbm(w_down))
-
-
-def pair_kernel(a_ref, b_ref, *outs):
-    total = (a_ref[...].astype(F32) + b_ref[...].astype(F32)).astype(BF16)
-    if len(outs) == 1:
-        outs[0][...] = total
-    else:
-        for n, out in enumerate(outs):
-            out[...] = total[n]
-
-
-def pair_sum(own, other, split, steps=3):
-    n, m, rows, width = own.shape
-    wide = width // steps
-    block = pl.BlockSpec((n, m, rows, wide), lambda i: (0, 0, 0, i))
-    part = pl.BlockSpec((m, rows, wide), lambda i: (0, 0, i))
-    return pl.pallas_call(
-        pair_kernel,
-        grid=(steps,),
-        out_shape=(far((m, rows, width)),) * n if split else (far(own.shape),),
-        in_specs=[block, block],
-        out_specs=(part,) * n if split else (block,),
-        compiler_params=params(),
-        cost_estimate=cost(n * m * rows * width, 6 * n * m * rows * width),
-        name="pair_sum",
-    )(own, other)
+    )(act, hbm(w_down), *more)
 
 
 def block_kernel(in_ref, *outs):
@@ -771,35 +806,44 @@
     pieces = [hbm(a) for a in pieces]
     place = place_rows(me, pieces, tokens)
 
-    routed, attention = carried_blocks(me, inside, hbm(qs), state, hbm(place), held)
+    routed = chosen_rows(inside, hbm(qs), state, hbm(place))
+    _, inside, qs, state = keep((routed, inside, qs, state))
     routed = exchange(routed.reshape(held, held * CAP, width), "exp")
+    attention = carried_blocks(me, inside, hbm(qs), state, held)
+    routed, attention = keep((routed, attention))
     one, two = routed_norm(me, routed, pieces, attn_gain, moe_gain, nz)
 
     others = range(1, nx)
-    attention, one = keep((attention, one))
     ones = [one] + [shift(one, "x", d) for d in others]
     two = exchange(two, "z")
-    ones, two = keep((ones, two))
-    one = exchange(repeat(ones, nz), "z")
+    across = shift(attention[2], "exp", 2)
+    ones, two, across = keep((ones, two, across))
+    one = exchange(repeat([hbm(ones[0])] + ones[1:], nz), "z")
     twos = [two] + [shift(two, "x", d) for d in others]
-    attention = [attention[0]] + [shift(attention[d], "exp", d) for d in range(1, held)]
-    one, twos, attention = keep((one, twos, attention))
+    right = shift(attention[1], "exp", 1)
+    one, twos, right = keep((one, twos, right))
 
     act_own = expert_act(one, twos, w_gate, w_up)
     one, twos = shift(one, "core", 1), [shift(a, "core", 1) for a in twos]
     one, twos, act_own = keep((one, twos, act_own))
-    other1, other2 = expert_down(expert_act(one, twos, w_gate, w_up), w_down, nz, nx)
-    other1, other2, act_own = keep((other1, other2, act_own))
-    own1, own2 = expert_down(act_own, w_down, nz, nx)
-    (one,) = pair_sum(own1, shift(other1, "core", 1), False)
-    twos = pair_sum(own2, shift(other2, "core", 1), True)
+    act_far = expert_act(one, twos, w_gate, w_up)
+    (two,) = expert_down(act_far, w_down, True, nz, nx)
+    two, act_far = keep((two, act_far))
+    (one,) = expert_down(act_far, w_down, False, nz, nx)
+    one, two, act_own = keep((one, two, act_own))
+    one, two = shift(one, "core", 1), shift(two, "core", 1)
+    twos = expert_down(act_own, w_down, True, nz, nx, two)
+    one, twos, act_own = keep((one, twos, act_own))
+    (one,) = expert_down(act_own, w_down, False, nz, nx, one)
 
     one = exchange(one, "z")
     twos = [twos[0]] + [shift(twos[d], "x", -d) for d in others]
-    one, twos = keep((one, twos))
+    left = shift(attention[3], "exp", 3)
+    one, twos, left = keep((one, twos, left))
+    attention = [attention[0], right, across, left]
     ones = block_sum(one)
-    ones = [ones[0]] + [shift(ones[d], "x", -d) for d in others]
-    two = exchange(stack_sum(twos), "z")
+    ones = [hbm(ones[0])] + [shift(ones[d], "x", -d) for d in others]
+    two = exchange(stack_sum([hbm(twos[0])] + twos[1:]), "z")
     hidden = hidden_rows(me, attention, hbm(residual), hbm(out_gate), attn_gain)
     back = exchange(row_sum(ones, two, held), "exp")
     moe_out = combine_rows(place_own, back, expert_ids, route_weights)

time: 194 us -> 192 us (0.990)
  blocking collectives: 9.67 us -> 0 us
  Pallas kernels: 58.8 us -> 64.9 us
  local copies, waits for them, and re-layouts: 9.12 us -> 4.48 us
  waiting for transfers between devices: 47.5 us -> 51.1 us
  starting transfers between devices: 66.6 us -> 69.4 us
    all_to_all x1 -> x0, blocking collectives: 9.67 us -> none  [exchange(): return lax.all_to_all(a, axis, split_axis=0, concat_axis=0, tiled=True)]
    unnamed x40 -> x24, local copies, waits for them, and re-layouts: 9.12 us -> 4.48 us
    all_to_all x7 -> x8, starting transfers between devices: 36.8 us -> 40.7 us  [exchange(): return lax.all_to_all(a, axis, split_axis=0, concat_axis=0, tiled=True)]
    pallas_call x4 -> x5, Pallas kernels: 12.5 us -> 16.1 us  [the longest x4 11.8 us: expert_down(): pl.pallas_call(functools.partial(down_kernel, steps, half if last else 0,...]
    all_to_all x7 -> x8, waiting for transfers between devices: 1.03 us -> 3.17 us  [exchange(): return lax.all_to_all(a, axis, split_axis=0, concat_axis=0, tiled=True)]
  transfers between devices with their start and end apart: 32 -> 33, of which waited for: 15 -> 19; matrix products, arithmetic and copies ran while one was open for 0% -> 0% of each run, Pallas kernels for 16% -> 17%
where the time goes in v7:
time: 192 us; the launch traced here: 191 us
  starting transfers between devices  69.4 us (36%)
  Pallas kernels  64.9 us (34%)
  waiting for transfers between devices  51.1 us (27%)
  local copies, waits for them, and re-layouts  4.48 us (2%)
    ppermute x25, waiting for transfers between devices, shift(): return lax.ppermute(a, axis, [(i, (i + by) % n) for i in range(n)])  48 us
    all_to_all x8, starting transfers between devices, exchange(): return lax.all_to_all(a, axis, split_axis=0, concat_axis=0, tiled=True)  40.7 us
    ppermute x25, starting transfers between devices, shift(): return lax.ppermute(a, axis, [(i, (i + by) % n) for i in range(n)])  28.6 us
    pallas_call x4, Pallas kernels, expert_down(): pl.pallas_call(functools.partial(down_kernel, steps, half if last else 0,...  11.8 us
    pallas_call x2, Pallas kernels, expert_act(): pl.pallas_call(functools.partial(act_kernel, steps), out_shape=jax.ShapeD...  8.41 us
    pallas_call x1, Pallas kernels, inside_blocks(): pl.pallas_call(functools.partial(inside_kernel, group), grid=(heads // gr...  7.82 us
    pallas_call x1, Pallas kernels, local_states(): pl.pallas_call(functools.partial(state_kernel, group), grid=(heads // gro...  5.85 us
    pallas_call x1, Pallas kernels, hidden_rows(): pl.pallas_call(hidden_kernel, grid=(rows // tile,), out_shape=jax.ShapeDt...  4.93 us
  transfers between devices with their start and end apart: 33, of which 19 were waited for; matrix products, arithmetic and copies ran while one was open for 0% of the time, Pallas kernels for 17%

profile of v7, /device:TPU:0, one launch (start us, length us, event | category | flops | bytes accessed | tf_op | source)
XLA Modules:
  0.0 190.7 jit_solution(16809608000559279650)
XLA Ops:
  0.6 5.9 %local_states.1 = (f32[512,12]{1,0:T(8,128)S(1)}, bf16[32,64,128]{2,1,0:T(8,128)(2,1)}) custom-call(bf16[512,1536]{1,0:T(8,128)(2,1)} %k_ref.3, bf16[512,1536]{1,0:T(8,128)(2,1)} %v_ref.3, f32[12,512]{1,0:T(8,128)} %bitcast.30), custom_call_target="tpu_custom_call" | custom-call | flops 201326592 | bytes 3145728 | tf_op jit(solution)/shard_map/local_states/pallas_call | solution.py:122
  6.5 8.4 %all-to-all-start = ((bf16[32,64,128]{2,1,0:T(8,128)(2,1)}), bf16[32,64,128]{2,1,0:T(8,128)(2,1)}, u32[]{:S(2)}, u32[]{:S(2)}) async-start(bf16[32,64,128]{2,1,0:T(8,128)(2,1)} %get-tuple-element.75), calls=%async_computation | async-start | bytes 1048576 | tf_op jit(solution)/shard_map/all_to_all | solution.py:760
  18.1 7.8 %inside_blocks.1 = (f32[512,1536]{1,0:T(8,128)S(1)}, bf16[512,1536]{1,0:T(8,128)(2,1)}) custom-call(bf16[512,1536]{1,0:T(8,128)(2,1)} %q_ref.1, bf16[512,1536]{1,0:T(8,128)(2,1)} %k_ref.3, bf16[512,1536]{1,0:T(8,128)(2,1)} %v_ref.3, f32[512,12]{1,0:T(8,128)S(1)} %get-tuple-element.76.cum_ref, f32[12,512]{1,0:T(8,128)} %bitcast.31), custom_call_target="tpu_custom_call" | custom-call | flops 1610612736 | bytes 9437184 | tf_op jit(solution)/shard_map/inside_blocks/pallas_call | solution.py:216
  28.5 6.7 %all-to-all-start.1 = ((bf16[32,48,128]{2,1,0:T(8,128)(2,1)}), bf16[32,48,128]{2,1,0:T(8,128)(2,1)S(1)}, u32[]{:S(2)}, u32[]{:S(2)}) async-start(bf16[32,48,128]{2,1,0:T(8,128)(2,1)} %scan_blocks.1), calls=%async_computation.1 | async-start | bytes 786432 | tf_op jit(solution)/shard_map/all_to_all | solution.py:760
  41.8 3.4 %collective-permute-done.1.refs_2_ = bf16[8,6400]{1,0:T(8,128)(2,1)S(1)} collective-permute-done((bf16[8,6400]{1,0:T(8,128)(2,1)}, bf16[8,6400]{1,0:T(8,128)(2,1)S(1)}, u32[]{:S(2)}, u32[]{:S(2)}) %collective-permute-start.1) | collective-permute-done | bytes 102432 | tf_op jit(solution)/shard_map/ppermute | solution.py:765
  48.0 4.3 %chosen_rows.1 = bf16[64,1536]{1,0:T(8,128)(2,1)} custom-call(f32[512,1536]{1,0:T(8,128)S(1)} %get-tuple-element.90.inside_ref, bf16[512,1536]{1,0:T(8,128)(2,1)} %get-tuple-element.91.qs_ref, bf16[12,128,128]{2,1,0:T(8,128)(2,1)S(1)} %bitcast.15, bf16[64,512]{1,0:T(8,128)(2,1)} %place_rows.1.place_ref), custom_call_target="tpu_custom_call" | custom-call | flops 402653184 | bytes 6291456 | tf_op jit(solution)/shard_map/chosen_rows/pallas_call | solution.py:270
  52.3 4.0 %all-to-all-start.2 = ((bf16[4,16,1536]{2,1,0:T(8,128)(2,1)}), bf16[4,16,1536]{2,1,0:T(8,128)(2,1)}, u32[]{:S(2)}, u32[]{:S(2)}) async-start(bf16[4,16,1536]{2,1,0:T(8,128)(2,1)} %bitcast.29), calls=%async_computation.2 | async-start | bytes 393216 | tf_op jit(solution)/shard_map/all_to_all | solution.py:760
  56.3 4.3 %carried_blocks.1 = (bf16[128,1536]{1,0:T(8,128)(2,1)}, bf16[128,1536]{1,0:T(8,128)(2,1)}, bf16[128,1536]{1,0:T(8,128)(2,1)}, bf16[128,1536]{1,0:T(8,128)(2,1)}) custom-call(s32[1]{0:T(128)} %bitcast.me_ref, f32[512,1536]{1,0:T(8,128)S(1)} %get-tuple-element.90.inside_ref, bf16[512,1536]{1,0:T(8,128)(2,1)} %get-tuple-element.91.qs_ref, ...), custom_call_target="tpu_custom_call" | custom-call | flops 402653184 | bytes 6291456 | tf_op jit(solution)/shard_map/carried_blocks/pallas_call | solution.py:295
  68.0 4.4 %all-to-all-start.3 = ((bf16[4,16,3072]{2,1,0:T(8,128)(2,1)}), bf16[4,16,3072]{2,1,0:T(8,128)(2,1)S(1)}, u32[]{:S(2)}, u32[]{:S(2)}) async-start(bf16[4,16,3072]{2,1,0:T(8,128)(2,1)} %get-tuple-element.100), calls=%async_computation.3 | async-start | bytes 786432 | tf_op jit(solution)/shard_map/all_to_all | solution.py:760
  83.6 4.8 %all-to-all-start.4 = ((bf16[4,4,16,3072]{3,2,1,0:T(8,128)(2,1)}), bf16[4,4,16,3072]{3,2,1,0:T(8,128)(2,1)S(1)}, u32[]{:S(2)}, u32[]{:S(2)}) async-start(bf16[4,4,16,3072]{3,2,1,0:T(8,128)(2,1)} %repeat.1), calls=%async_computation.4 | async-start | bytes 3145728 | tf_op jit(solution)/shard_map/all_to_all | solution.py:760
  93.6 4.0 %collective-permute-done.10.refs_1_ = bf16[128,1536]{1,0:T(8,128)(2,1)S(1)} collective-permute-done((bf16[128,1536]{1,0:T(8,128)(2,1)}, bf16[128,1536]{1,0:T(8,128)(2,1)S(1)}, u32[]{:S(2)}, u32[]{:S(2)}) %collective-permute-start.10) | collective-permute-done | bytes 393248 | tf_op jit(solution)/shard_map/ppermute | solution.py:765
  98.4 3.9 %collective-permute-done.7.refs_1_ = bf16[4,16,3072]{2,1,0:T(8,128)(2,1)S(1)} collective-permute-done((bf16[4,16,3072]{2,1,0:T(8,128)(2,1)S(1)}, bf16[4,16,3072]{2,1,0:T(8,128)(2,1)S(1)}, u32[]{:S(2)}, u32[]{:S(2)}) %collective-permute-start.7) | collective-permute-done | bytes 393248 | tf_op jit(solution)/shard_map/ppermute | solution.py:765
  102.2 4.2 %collective-permute-done.8.refs_2_ = bf16[4,16,3072]{2,1,0:T(8,128)(2,1)S(1)} collective-permute-done((bf16[4,16,3072]{2,1,0:T(8,128)(2,1)S(1)}, bf16[4,16,3072]{2,1,0:T(8,128)(2,1)S(1)}, u32[]{:S(2)}, u32[]{:S(2)}) %collective-permute-start.8) | collective-permute-done | bytes 393248 | tf_op jit(solution)/shard_map/ppermute | solution.py:765
  107.6 4.2 %expert_act.2.act_ref = bf16[256,288]{1,0:T(8,128)(2,1)S(1)} custom-call(bf16[288,6144]{1,0:T(8,128)(2,1)} %bitcast.25, bf16[288,6144]{1,0:T(8,128)(2,1)} %bitcast.27, bf16[4,4,16,3072]{3,2,1,0:T(8,128)(2,1)S(1)} %all-to-all-done.4.one_ref, bf16[4,16,3072]{2,1,0:T(8,128)(2,1)S(1)} %all-to-all-done.3.refs_0_, ...), custom_call_target="tpu_custom_call" | custom-call | flops 1811939328 | bytes 10223616 | tf_op jit(solution)/shard_map/expert_act/pallas_call | solution.py:571
  112.1 4.2 %expert_act.3.act_ref = bf16[256,288]{1,0:T(8,128)(2,1)S(1)} custom-call(bf16[288,6144]{1,0:T(8,128)(2,1)} %bitcast.26, bf16[288,6144]{1,0:T(8,128)(2,1)} %bitcast.28, bf16[4,4,16,3072]{3,2,1,0:T(8,128)(2,1)S(1)} %collective-permute-done.11.one_ref, bf16[4,16,3072]{2,1,0:T(8,128)(2,1)S(1)} %collective-permute-done.12.refs_0_, ...), custom_call_target="tpu_custom_call" | custom-call | flops 1811939328 | bytes 10223616 | tf_op jit(solution)/shard_map/expert_act/pallas_call | solution.py:571
  124.6 3.5 %expert_down.6 = (bf16[4,16,3072]{2,1,0:T(8,128)(2,1)}, bf16[4,16,3072]{2,1,0:T(8,128)(2,1)}, bf16[4,16,3072]{2,1,0:T(8,128)(2,1)}, bf16[4,16,3072]{2,1,0:T(8,128)(2,1)}) custom-call(bf16[256,288]{1,0:T(8,128)(2,1)S(1)} %expert_act.2.act_ref, bf16[288,6144]{1,0:T(8,128)(2,1)} %bitcast.23, bf16[4,4,16,3072]{3,2,1,0:T(8,128)(2,1)S(1)} %collective-permute-done.17.refs_0_), custom_call_target="tpu_custom_call" | custom-call | flops 452984832 | bytes 3342336 | tf_op jit(solution)/shard_map/expert_down/pallas_call | solution.py:647
  128.1 3.5 %expert_down.7 = bf16[4,4,16,3072]{3,2,1,0:T(8,128)(2,1)} custom-call(bf16[256,288]{1,0:T(8,128)(2,1)S(1)} %expert_act.2.act_ref, bf16[288,6144]{1,0:T(8,128)(2,1)} %bitcast.24, bf16[4,4,16,3072]{3,2,1,0:T(8,128)(2,1)S(1)} %collective-permute-done.16.refs_0_), custom_call_target="tpu_custom_call" | custom-call | flops 452984832 | bytes 3342336 | tf_op jit(solution)/shard_map/expert_down/pallas_call | solution.py:647
  131.7 4.6 %all-to-all-start.5 = ((bf16[4,4,16,3072]{3,2,1,0:T(8,128)(2,1)}), bf16[4,4,16,3072]{3,2,1,0:T(8,128)(2,1)S(1)}, u32[]{:S(2)}, u32[]{:S(2)}) async-start(bf16[4,4,16,3072]{3,2,1,0:T(8,128)(2,1)} %expert_down.7), calls=%async_computation.5 | async-start | bytes 3145728 | tf_op jit(solution)/shard_map/all_to_all | solution.py:760
  142.6 5.1 %collective-permute-done.21.refs_3_ = bf16[128,1536]{1,0:T(8,128)(2,1)S(1)} collective-permute-done((bf16[128,1536]{1,0:T(8,128)(2,1)}, bf16[128,1536]{1,0:T(8,128)(2,1)S(1)}, u32[]{:S(2)}, u32[]{:S(2)}) %collective-permute-start.21) | collective-permute-done | bytes 393248 | tf_op jit(solution)/shard_map/ppermute | solution.py:765
  147.7 10.8 %collective-permute-done.18.refs_1_ = bf16[4,16,3072]{2,1,0:T(8,128)(2,1)S(1)} collective-permute-done((bf16[4,16,3072]{2,1,0:T(8,128)(2,1)}, bf16[4,16,3072]{2,1,0:T(8,128)(2,1)S(1)}, u32[]{:S(2)}, u32[]{:S(2)}) %collective-permute-start.18) | collective-permute-done | bytes 393248 | tf_op jit(solution)/shard_map/ppermute | solution.py:765
  158.4 3.6 %collective-permute-done.20.refs_3_ = bf16[4,16,3072]{2,1,0:T(8,128)(2,1)S(1)} collective-permute-done((bf16[4,16,3072]{2,1,0:T(8,128)(2,1)}, bf16[4,16,3072]{2,1,0:T(8,128)(2,1)S(1)}, u32[]{:S(2)}, u32[]{:S(2)}) %collective-permute-start.20) | collective-permute-done | bytes 393248 | tf_op jit(solution)/shard_map/ppermute | solution.py:765
  163.8 4.5 %all-to-all-start.6 = ((bf16[4,16,3072]{2,1,0:T(8,128)(2,1)}), bf16[4,16,3072]{2,1,0:T(8,128)(2,1)S(1)}, u32[]{:S(2)}, u32[]{:S(2)}) async-start(bf16[4,16,3072]{2,1,0:T(8,128)(2,1)} %stack_sum.1), calls=%async_computation.6 | async-start | bytes 786432 | tf_op jit(solution)/shard_map/all_to_all | solution.py:760
  179.3 3.4 %all-to-all-start.7 = ((bf16[4,4,6144]{2,1,0:T(4,128)(2,1)}), bf16[4,4,6144]{2,1,0:T(4,128)(2,1)S(1)}, u32[]{:S(2)}, u32[]{:S(2)}) async-start(bf16[4,4,6144]{2,1,0:T(4,128)(2,1)} %row_sum.1), calls=%async_computation.7 | async-start | bytes 393216 | tf_op jit(solution)/shard_map/all_to_all | solution.py:760
  183.7 4.9 %hidden_rows.1 = bf16[128,6144]{1,0:T(8,128)(2,1)} custom-call(s32[1]{0:T(128)} %bitcast.me_ref, bf16[128,6144]{1,0:T(8,128)(2,1)} %res_ref.1, bf16[128,6144]{1,0:T(8,128)(2,1)} %gate_ref.1, f32[1,6144]{1,0:T(1,128)S(1)} %bitcast.18, bf16[128,1536]{1,0:T(8,128)(2,1)S(1)} %copy-done, bf16[128,1536]{1,0:T(8,128)(2,1)S(1)} %copy-done.2, ...), custom_call_target="tpu_custom_call" | custom-call | flops 15728640 | bytes 6291456 | tf_op jit(solution)/shard_map/hidden_rows/pallas_call | solution.py:486
  (86 shorter events, 71.7 us)
Async XLA Ops:
  6.5 20.1 %all-to-all-start = ((bf16[32,64,128]{2,1,0:T(8,128)(2,1)}), bf16[32,64,128]{2,1,0:T(8,128)(2,1)}, u32[]{:S(2)}, u32[]{:S(2)}) async-start(bf16[32,64,128]{2,1,0:T(8,128)(2,1)} %get-tuple-element.75), calls=%async_computation | async-start | bytes 1048576 | tf_op jit(solution)/shard_map/all_to_all | solution.py:760
  28.5 19.5 %all-to-all-start.1 = ((bf16[32,48,128]{2,1,0:T(8,128)(2,1)}), bf16[32,48,128]{2,1,0:T(8,128)(2,1)S(1)}, u32[]{:S(2)}, u32[]{:S(2)}) async-start(bf16[32,48,128]{2,1,0:T(8,128)(2,1)} %scan_blocks.1), calls=%async_computation.1 | async-start | bytes 786432 | tf_op jit(solution)/shard_map/all_to_all | solution.py:760
  35.2 6.6 %collective-permute-start = (bf16[8,6400]{1,0:T(8,128)(2,1)}, bf16[8,6400]{1,0:T(8,128)(2,1)S(1)}, u32[]{:S(2)}, u32[]{:S(2)}) collective-permute-start(bf16[8,6400]{1,0:T(8,128)(2,1)} %get-tuple-element.87), channel_id=1, source_target_pairs={{0,1},{1,2},{2,3},{3,0},{4,5},{5,6},{6,7},{7,4},{8,9},{9,10},{10,1... | collective-permute-start | bytes 307208 | tf_op jit(solution)/shard_map/ppermute | solution.py:765
  36.8 8.3 %collective-permute-start.1 = (bf16[8,6400]{1,0:T(8,128)(2,1)}, bf16[8,6400]{1,0:T(8,128)(2,1)S(1)}, u32[]{:S(2)}, u32[]{:S(2)}) collective-permute-start(bf16[8,6400]{1,0:T(8,128)(2,1)} %get-tuple-element.88), channel_id=1, source_target_pairs={{0,2},{1,3},{2,0},{3,1},{4,6},{5,7},{6,4},{7,5},{8,10},{9,11},{10,... | collective-permute-start | bytes 307208 | tf_op jit(solution)/shard_map/ppermute | solution.py:765
  52.3 10.4 %all-to-all-start.2 = ((bf16[4,16,1536]{2,1,0:T(8,128)(2,1)}), bf16[4,16,1536]{2,1,0:T(8,128)(2,1)}, u32[]{:S(2)}, u32[]{:S(2)}) async-start(bf16[4,16,1536]{2,1,0:T(8,128)(2,1)} %bitcast.29), calls=%async_computation.2 | async-start | bytes 393216 | tf_op jit(solution)/shard_map/all_to_all | solution.py:760
  62.7 18.7 %collective-permute-start.6 = (bf16[128,1536]{1,0:T(8,128)(2,1)}, bf16[128,1536]{1,0:T(8,128)(2,1)S(1)}, u32[]{:S(2)}, u32[]{:S(2)}) collective-permute-start(bf16[128,1536]{1,0:T(8,128)(2,1)} %get-tuple-element.101), channel_id=1, source_target_pairs={{0,2},{1,3},{2,0},{3,1},{4,6},{5,7},{6,4},{7,5},{8,10},{9,11},{10,... | collective-permute-start | bytes 1179656 | tf_op jit(solution)/shard_map/ppermute | solution.py:765
  68.0 13.4 %all-to-all-start.3 = ((bf16[4,16,3072]{2,1,0:T(8,128)(2,1)}), bf16[4,16,3072]{2,1,0:T(8,128)(2,1)S(1)}, u32[]{:S(2)}, u32[]{:S(2)}) async-start(bf16[4,16,3072]{2,1,0:T(8,128)(2,1)} %get-tuple-element.100), calls=%async_computation.3 | async-start | bytes 786432 | tf_op jit(solution)/shard_map/all_to_all | solution.py:760
  72.4 6.6 %collective-permute-start.3 = (bf16[16,3072]{1,0:T(8,128)(2,1)}, bf16[16,3072]{1,0:T(8,128)(2,1)S(1)}, u32[]{:S(2)}, u32[]{:S(2)}) collective-permute-start(bf16[16,3072]{1,0:T(8,128)(2,1)} %get-tuple-element.102.refs_0_), channel_id=1, source_target_pairs={{0,8},{8,16},{16,24},{24,0},{1,9},{9,17},{17,25},{25,1},{2,10},{10... | collective-permute-start | bytes 294920 | tf_op jit(solution)/shard_map/ppermute | solution.py:765
  73.9 6.6 %collective-permute-start.4 = (bf16[16,3072]{1,0:T(8,128)(2,1)}, bf16[16,3072]{1,0:T(8,128)(2,1)S(1)}, u32[]{:S(2)}, u32[]{:S(2)}) collective-permute-start(bf16[16,3072]{1,0:T(8,128)(2,1)} %get-tuple-element.102.refs_0_), channel_id=1, source_target_pairs={{0,16},{8,24},{16,0},{24,8},{1,17},{9,25},{17,1},{25,9},{2,18},{10... | collective-permute-start | bytes 294920 | tf_op jit(solution)/shard_map/ppermute | solution.py:765
  83.6 22.9 %all-to-all-start.4 = ((bf16[4,4,16,3072]{3,2,1,0:T(8,128)(2,1)}), bf16[4,4,16,3072]{3,2,1,0:T(8,128)(2,1)S(1)}, u32[]{:S(2)}, u32[]{:S(2)}) async-start(bf16[4,4,16,3072]{3,2,1,0:T(8,128)(2,1)} %repeat.1), calls=%async_computation.4 | async-start | bytes 3145728 | tf_op jit(solution)/shard_map/all_to_all | solution.py:760
  88.4 9.2 %collective-permute-start.10 = (bf16[128,1536]{1,0:T(8,128)(2,1)}, bf16[128,1536]{1,0:T(8,128)(2,1)S(1)}, u32[]{:S(2)}, u32[]{:S(2)}) collective-permute-start(bf16[128,1536]{1,0:T(8,128)(2,1)} %get-tuple-element.107), channel_id=1, source_target_pairs={{0,1},{1,2},{2,3},{3,0},{4,5},{5,6},{6,7},{7,4},{8,9},{9,10},{10,1... | collective-permute-start | bytes 1179656 | tf_op jit(solution)/shard_map/ppermute | solution.py:765
  89.0 13.2 %collective-permute-start.7 = (bf16[4,16,3072]{2,1,0:T(8,128)(2,1)S(1)}, bf16[4,16,3072]{2,1,0:T(8,128)(2,1)S(1)}, u32[]{:S(2)}, u32[]{:S(2)}) collective-permute-start(bf16[4,16,3072]{2,1,0:T(8,128)(2,1)S(1)} %all-to-all-done.3.refs_0_), channel_id=1, source_target_pairs={{0,8},{8,16},{16,24},{24,0},{1,9},{9,17},{17,25},{25,1},{2,10},{10... | collective-permute-start | bytes 1179656 | tf_op jit(solution)/shard_map/ppermute | solution.py:765
  90.0 16.4 %collective-permute-start.8 = (bf16[4,16,3072]{2,1,0:T(8,128)(2,1)S(1)}, bf16[4,16,3072]{2,1,0:T(8,128)(2,1)S(1)}, u32[]{:S(2)}, u32[]{:S(2)}) collective-permute-start(bf16[4,16,3072]{2,1,0:T(8,128)(2,1)S(1)} %all-to-all-done.3.refs_0_), channel_id=1, source_target_pairs={{0,16},{8,24},{16,0},{24,8},{1,17},{9,25},{17,1},{25,9},{2,18},{10... | collective-permute-start | bytes 1179656 | tf_op jit(solution)/shard_map/ppermute | solution.py:765
  93.2 13.3 %collective-permute-start.9 = (bf16[4,16,3072]{2,1,0:T(8,128)(2,1)S(1)}, bf16[4,16,3072]{2,1,0:T(8,128)(2,1)S(1)}, u32[]{:S(2)}, u32[]{:S(2)}) collective-permute-start(bf16[4,16,3072]{2,1,0:T(8,128)(2,1)S(1)} %all-to-all-done.3.refs_0_), channel_id=1, source_target_pairs={{0,24},{8,0},{16,8},{24,16},{1,25},{9,1},{17,9},{25,17},{2,26},{10... | collective-permute-start | bytes 1179656 | tf_op jit(solution)/shard_map/ppermute | solution.py:765
  121.3 6.8 %collective-permute-start.16 = (bf16[4,4,16,3072]{3,2,1,0:T(8,128)(2,1)S(1)}, bf16[4,4,16,3072]{3,2,1,0:T(8,128)(2,1)S(1)}, u32[]{:S(2)}, u32[]{:S(2)}) collective-permute-start(bf16[4,4,16,3072]{3,2,1,0:T(8,128)(2,1)S(1)} %expert_down.5), channel_id=1, source_target_pairs={{0,4},{4,0},{1,5},{5,1},{2,6},{6,2},{3,7},{7,3},{8,12},{12,8},{9,1... | collective-permute-start | bytes 4718600 | tf_op jit(solution)/shard_map/ppermute | solution.py:765
  131.7 30.3 %all-to-all-start.5 = ((bf16[4,4,16,3072]{3,2,1,0:T(8,128)(2,1)}), bf16[4,4,16,3072]{3,2,1,0:T(8,128)(2,1)S(1)}, u32[]{:S(2)}, u32[]{:S(2)}) async-start(bf16[4,4,16,3072]{3,2,1,0:T(8,128)(2,1)} %expert_down.7), calls=%async_computation.5 | async-start | bytes 3145728 | tf_op jit(solution)/shard_map/all_to_all | solution.py:760
  136.3 11.4 %collective-permute-start.21 = (bf16[128,1536]{1,0:T(8,128)(2,1)}, bf16[128,1536]{1,0:T(8,128)(2,1)S(1)}, u32[]{:S(2)}, u32[]{:S(2)}) collective-permute-start(bf16[128,1536]{1,0:T(8,128)(2,1)} %get-tuple-element.136), channel_id=1, source_target_pairs={{0,3},{1,0},{2,1},{3,2},{4,7},{5,4},{6,5},{7,6},{8,11},{9,8},{10,9... | collective-permute-start | bytes 1179656 | tf_op jit(solution)/shard_map/ppermute | solution.py:765
  138.9 19.5 %collective-permute-start.18 = (bf16[4,16,3072]{2,1,0:T(8,128)(2,1)}, bf16[4,16,3072]{2,1,0:T(8,128)(2,1)S(1)}, u32[]{:S(2)}, u32[]{:S(2)}) collective-permute-start(bf16[4,16,3072]{2,1,0:T(8,128)(2,1)} %get-tuple-element.133), channel_id=1, source_target_pairs={{0,24},{8,0},{16,8},{24,16},{1,25},{9,1},{17,9},{25,17},{2,26},{10... | collective-permute-start | bytes 1179656 | tf_op jit(solution)/shard_map/ppermute | solution.py:765
  141.5 16.9 %collective-permute-start.19 = (bf16[4,16,3072]{2,1,0:T(8,128)(2,1)}, bf16[4,16,3072]{2,1,0:T(8,128)(2,1)S(1)}, u32[]{:S(2)}, u32[]{:S(2)}) collective-permute-start(bf16[4,16,3072]{2,1,0:T(8,128)(2,1)} %get-tuple-element.134), channel_id=1, source_target_pairs={{0,16},{8,24},{16,0},{24,8},{1,17},{9,25},{17,1},{25,9},{2,18},{10... | collective-permute-start | bytes 1179656 | tf_op jit(solution)/shard_map/ppermute | solution.py:765
  142.6 19.4 %collective-permute-start.20 = (bf16[4,16,3072]{2,1,0:T(8,128)(2,1)}, bf16[4,16,3072]{2,1,0:T(8,128)(2,1)S(1)}, u32[]{:S(2)}, u32[]{:S(2)}) collective-permute-start(bf16[4,16,3072]{2,1,0:T(8,128)(2,1)} %get-tuple-element.135), channel_id=1, source_target_pairs={{0,8},{8,16},{16,24},{24,0},{1,9},{9,17},{17,25},{25,1},{2,10},{10... | collective-permute-start | bytes 1179656 | tf_op jit(solution)/shard_map/ppermute | solution.py:765
  163.8 13.8 %all-to-all-start.6 = ((bf16[4,16,3072]{2,1,0:T(8,128)(2,1)}), bf16[4,16,3072]{2,1,0:T(8,128)(2,1)S(1)}, u32[]{:S(2)}, u32[]{:S(2)}) async-start(bf16[4,16,3072]{2,1,0:T(8,128)(2,1)} %stack_sum.1), calls=%async_computation.6 | async-start | bytes 786432 | tf_op jit(solution)/shard_map/all_to_all | solution.py:760
  169.9 7.2 %collective-permute-start.23 = (bf16[16,3072]{1,0:T(8,128)(2,1)}, bf16[16,3072]{1,0:T(8,128)(2,1)S(1)}, u32[]{:S(2)}, u32[]{:S(2)}) collective-permute-start(bf16[16,3072]{1,0:T(8,128)(2,1)} %get-tuple-element.146), channel_id=1, source_target_pairs={{0,16},{8,24},{16,0},{24,8},{1,17},{9,25},{17,1},{25,9},{2,18},{10... | collective-permute-start | bytes 294920 | tf_op jit(solution)/shard_map/ppermute | solution.py:765
  171.0 6.6 %collective-permute-start.24 = (bf16[16,3072]{1,0:T(8,128)(2,1)}, bf16[16,3072]{1,0:T(8,128)(2,1)S(1)}, u32[]{:S(2)}, u32[]{:S(2)}) collective-permute-start(bf16[16,3072]{1,0:T(8,128)(2,1)} %get-tuple-element.147), channel_id=1, source_target_pairs={{0,8},{8,16},{16,24},{24,0},{1,9},{9,17},{17,25},{25,1},{2,10},{10... | collective-permute-start | bytes 294920 | tf_op jit(solution)/shard_map/ppermute | solution.py:765
  179.3 9.7 %all-to-all-start.7 = ((bf16[4,4,6144]{2,1,0:T(4,128)(2,1)}), bf16[4,4,6144]{2,1,0:T(4,128)(2,1)S(1)}, u32[]{:S(2)}, u32[]{:S(2)}) async-start(bf16[4,4,6144]{2,1,0:T(4,128)(2,1)} %row_sum.1), calls=%async_computation.7 | async-start | bytes 393216 | tf_op jit(solution)/shard_map/all_to_all | solution.py:760
  (20 other events, 110.2 us)

commit v8 on v7

--- a/solution.py
+++ b/solution.py
@@ -244,11 +244,28 @@
         ).astype(BF16)
 
 
-def chosen_kernel(group, inside_ref, qs_ref, state_ref, place_ref, sel_ref, att_ref):
-    attend(group, inside_ref, qs_ref, state_ref, att_ref)
-    sel_ref[...] = jnp.dot(
-        place_ref[...], att_ref[...], preferred_element_type=F32
-    ).astype(BF16)
+def chosen_kernel(group, inside_ref, qs_hbm, state_ref, place_ref, sel_ref, att_ref, qs_ref, sem):
+    wide = group * HEAD_DIM
+    steps = sel_ref.shape[1] // wide
+    copies = []
+    for g in range(steps):
+        cols = pl.ds(g * wide, wide)
+        copies.append(pltpu.make_async_copy(qs_hbm.at[:, cols], qs_ref.at[:, cols], sem.at[g]))
+    for c in copies:
+        c.start()
+    for g in range(steps):
+        cols = slice(g * wide, (g + 1) * wide)
+        copies[g].wait()
+        attend(
+            group,
+            inside_ref.at[:, cols],
+            qs_ref.at[:, cols],
+            state_ref.at[g * group : (g + 1) * group],
+            att_ref,
+        )
+        sel_ref[:, cols] = jnp.dot(
+            place_ref[...], att_ref[...], preferred_element_type=F32
+        ).astype(BF16)
 
 
 def carried_kernel(group, me_ref, inside_ref, qs_ref, state_ref, *refs):
@@ -263,22 +280,19 @@
 
 def chosen_rows(inside, qs, state, place, group=3):
     rows, width = inside.shape
-    heads = width // HEAD_DIM
     chosen = place.shape[0]
     wide = group * HEAD_DIM
-    block = pl.BlockSpec((rows, wide), lambda g: (0, g))
+    whole = pl.BlockSpec(memory_space=pltpu.VMEM)
     return pl.pallas_call(
         functools.partial(chosen_kernel, group),
-        grid=(heads // group,),
         out_shape=far((chosen, width)),
-        in_specs=[
-            block,
-            block,
-            pl.BlockSpec((group, HEAD_DIM, HEAD_DIM), lambda g: (g, 0, 0)),
-            pl.BlockSpec((chosen, rows), lambda g: (0, 0)),
+        in_specs=[whole, pl.BlockSpec(memory_space=pl.ANY), whole, whole],
+        out_specs=whole,
+        scratch_shapes=[
+            pltpu.VMEM((rows, wide), BF16),
+            pltpu.VMEM((rows, width), BF16),
+            pltpu.SemaphoreType.DMA((width // wide,)),
         ],
-        out_specs=pl.BlockSpec((chosen, wide), lambda g: (0, g)),
-        scratch_shapes=[pltpu.VMEM((rows, wide), BF16)],
         compiler_params=params(),
         cost_estimate=cost(4 * rows * width * HEAD_DIM, 8 * rows * width),
         name="chosen_rows",
@@ -529,26 +543,15 @@
     )(*arrays)
 
 
-def act_kernel(steps, wg_hbm, wu_hbm, one_ref, *refs):
-    twos, (act_ref, w_ref, sem) = refs[:-3], refs[-3:]
-    units, width = wg_hbm.shape
+def act_rows(steps, w_ref, one_ref, twos, arrived):
+    width = w_ref.shape[2]
     nz, nx, rows, half = one_ref.shape
     nt = (((1,), (1,)), ((), ()))
     wide = width // steps
-    copies = []
-    for s in range(steps):
-        cols = pl.ds(s * wide, wide)
-        for n, a in enumerate((wg_hbm, wu_hbm)):
-            copies.append(
-                pltpu.make_async_copy(a.at[:, cols], w_ref.at[n, :, cols], sem.at[s, n])
-            )
-    for c in copies:
-        c.start()
     gate = up = None
     for s in range(steps):
         cols = slice(s * wide, (s + 1) * wide)
-        copies[2 * s].wait()
-        copies[2 * s + 1].wait()
+        arrived(s)
         if s < steps // 2:
             x = [one_ref[z, k, :, cols] for k in range(nx) for z in range(nz)]
         else:
@@ -559,28 +562,63 @@
         u = lax.dot_general(w_ref[1, :, cols], x, nt, preferred_element_type=F32)
         gate = g if gate is None else gate + g
         up = u if up is None else up + u
-    act_ref[...] = (gate * jax.nn.sigmoid(gate) * up).T.astype(BF16)
-
-
-def expert_act(one, twos, w_gate, w_up, steps=6):
+    return (gate * jax.nn.sigmoid(gate) * up).T.astype(BF16)
+
+
+def first_act_kernel(steps, wg_hbm, wu_hbm, one_ref, *refs):
+    twos, (act_ref, w_ref, sem) = refs[:-3], refs[-3:]
+    wide = w_ref.shape[2] // steps
+    copies = []
+    for s in range(steps):
+        cols = pl.ds(s * wide, wide)
+        for n, a in enumerate((wg_hbm, wu_hbm)):
+            copies.append(
+                pltpu.make_async_copy(a.at[:, cols], w_ref.at[n, :, cols], sem.at[s, n])
+            )
+    for c in copies:
+        c.start()
+
+    def arrived(s):
+        copies[2 * s].wait()
+        copies[2 * s + 1].wait()
+
+    act_ref[...] = act_rows(steps, w_ref, one_ref, twos, arrived)
+
+
+def next_act_kernel(steps, w_ref, one_ref, *refs):
+    refs[-1][...] = act_rows(steps, w_ref, one_ref, refs[:-1], lambda s: None)
+
+
+def expert_act(one, twos, weights, steps=6):
     nz, nx, rows, half = one.shape
     count = nz * nx * rows
-    units, width = w_gate.shape
     whole = pl.BlockSpec(memory_space=pltpu.VMEM)
     away = pl.BlockSpec(memory_space=pl.ANY)
-    return pl.pallas_call(
-        functools.partial(act_kernel, steps),
+    if isinstance(weights, tuple):
+        units, width = weights[0].shape
+        return pl.pallas_call(
+            functools.partial(first_act_kernel, steps),
+            out_shape=(
+                jax.ShapeDtypeStruct((count, units), BF16),
+                pltpu.VMEM((2, units, width), BF16),
+            ),
+            in_specs=[away, away] + [whole] * (1 + len(twos)),
+            out_specs=(whole, whole),
+            scratch_shapes=[pltpu.SemaphoreType.DMA((steps, 2))],
+            compiler_params=params(),
+            cost_estimate=cost(4 * count * width * units, 4 * width * units + 2 * count * width),
+            name="first_act",
+        )(hbm(weights[0]), hbm(weights[1]), one, *twos)
+    _, units, width = weights.shape
+    return pl.pallas_call(
+        functools.partial(next_act_kernel, steps),
         out_shape=jax.ShapeDtypeStruct((count, units), BF16),
-        in_specs=[away, away] + [whole] * (1 + len(twos)),
+        in_specs=[whole] * (2 + len(twos)),
         out_specs=whole,
-        scratch_shapes=[
-            pltpu.VMEM((2, units, width), BF16),
-            pltpu.SemaphoreType.DMA((steps, 2)),
-        ],
-        compiler_params=params(),
-        cost_estimate=cost(4 * count * width * units, 4 * width * units + 2 * count * width),
-        name="expert_act",
-    )(hbm(w_gate), hbm(w_up), one, *twos)
+        compiler_params=params(),
+        cost_estimate=cost(4 * count * width * units, 2 * count * width),
+        name="next_act",
+    )(pltpu.with_memory_space_constraint(weights, pltpu.VMEM), one, *twos)
 
 
 def down_kernel(steps, first, by_x, act_ref, wd_hbm, *refs):
@@ -629,9 +667,9 @@
                 outs[0][z, :, :, cols] = part.astype(BF16)
 
 
-def expert_down(act, w_down, last, nz, nx, added=None, steps=3):
+def expert_down(act, w_down, cut, last, nz, nx, added=None, steps=2):
     count, units = act.shape
-    half = w_down.shape[1] // 2
+    half = w_down.shape[1] - cut if last else cut
     rows = count // (nz * nx)
     whole = pl.BlockSpec(memory_space=pltpu.VMEM)
     if last:
@@ -645,7 +683,7 @@
         shapes = (far((nz, nx, rows, half)),)
     more = () if added is None else (added,)
     return pl.pallas_call(
-        functools.partial(down_kernel, steps, half if last else 0, last),
+        functools.partial(down_kernel, steps, cut if last else 0, last),
         out_shape=shapes,
         in_specs=[whole, pl.BlockSpec(memory_space=pl.ANY)] + [whole] * len(more),
         out_specs=(whole,) * len(shapes),
@@ -711,11 +749,11 @@
     two = two_ref[0].astype(F32)
     for i in range(1, two_ref.shape[0]):
         two = two + two_ref[i].astype(F32)
-    half = one.shape[1]
+    cut = one.shape[1]
     for j in range(out_ref.shape[0]):
         at = slice(j * CAP, (j + 1) * CAP)
-        out_ref[j, :, :half] = one[at].astype(BF16)
-        out_ref[j, :, half:] = two[at].astype(BF16)
+        out_ref[j, :, :cut] = one[at].astype(BF16)
+        out_ref[j, :, cut:] = two[at].astype(BF16)
 
 
 def row_sum(parts, two, held):
@@ -723,7 +761,7 @@
     whole = pl.BlockSpec(memory_space=pltpu.VMEM)
     return pl.pallas_call(
         row_sum_kernel,
-        out_shape=far((held, CAP, 2 * half)),
+        out_shape=far((held, CAP, parts[0].shape[1] + half)),
         in_specs=[whole] * (1 + len(parts)),
         out_specs=whole,
         compiler_params=params(),
@@ -784,8 +822,8 @@
     rows, width = queries.shape
     heads = log_decay.shape[1]
     tokens = residual.shape[0]
-    attn_gain = attn_gain.reshape(1, -1)
-    moe_gain = moe_gain.reshape(1, -1)
+    attn_gain = hbm(attn_gain.reshape(1, -1))
+    moe_gain = hbm(moe_gain.reshape(1, -1))
     w_gate = jnp.swapaxes(w_gate, 1, 2)[0]
     w_up = jnp.swapaxes(w_up, 1, 2)[0]
     w_down = w_down[0]
@@ -820,26 +858,26 @@
     ones, two, across = keep((ones, two, across))
     one = exchange(repeat([hbm(ones[0])] + ones[1:], nz), "z")
     twos = [two] + [shift(two, "x", d) for d in others]
-    right = shift(attention[1], "exp", 1)
-    one, twos, right = keep((one, twos, right))
-
-    act_own = expert_act(one, twos, w_gate, w_up)
+    right, left = shift(attention[1], "exp", 1), shift(attention[3], "exp", 3)
+    one, twos, right, left = keep((one, twos, right, left))
+
+    cut = moe_gain.shape[1] * 7 // 12
+    act_own, weights = expert_act(one, twos, (w_gate, w_up))
     one, twos = shift(one, "core", 1), [shift(a, "core", 1) for a in twos]
-    one, twos, act_own = keep((one, twos, act_own))
-    act_far = expert_act(one, twos, w_gate, w_up)
-    (two,) = expert_down(act_far, w_down, True, nz, nx)
-    two, act_far = keep((two, act_far))
-    (one,) = expert_down(act_far, w_down, False, nz, nx)
+    one, twos, weights = keep((one, twos, weights))
+    act_far = expert_act(one, twos, weights)
+    (one,) = expert_down(act_far, w_down, cut, False, nz, nx)
+    one, act_far = keep((one, act_far))
+    (two,) = expert_down(act_far, w_down, cut, True, nz, nx)
     one, two, act_own = keep((one, two, act_own))
     one, two = shift(one, "core", 1), shift(two, "core", 1)
-    twos = expert_down(act_own, w_down, True, nz, nx, two)
-    one, twos, act_own = keep((one, twos, act_own))
-    (one,) = expert_down(act_own, w_down, False, nz, nx, one)
+    (one,) = expert_down(act_own, w_down, cut, False, nz, nx, one)
+    one, two, act_own = keep((one, two, act_own))
+    twos = expert_down(act_own, w_down, cut, True, nz, nx, two)
 
     one = exchange(one, "z")
     twos = [twos[0]] + [shift(twos[d], "x", -d) for d in others]
-    left = shift(attention[3], "exp", 3)
-    one, twos, left = keep((one, twos, left))
+    one, twos = keep((one, twos))
     attention = [attention[0], right, across, left]
     ones = block_sum(one)
     ones = [hbm(ones[0])] + [shift(ones[d], "x", -d) for d in others]

time: 192 us -> 188 us (0.979)
    unnamed x24 -> x28, local copies, waits for them, and re-layouts: 4.48 us -> 3.01 us
  transfers between devices with their start and end apart: 33 -> 33, of which waited for: 19 -> 19; matrix products, arithmetic and copies ran while one was open for 0% -> 0% of each run, Pallas kernels for 17% -> 20%
where the time goes in v8:
time: 188 us; the launch traced here: 187 us
  starting transfers between devices  69.6 us (37%)
  Pallas kernels  63.2 us (34%)
  waiting for transfers between devices  50 us (27%)
  local copies, waits for them, and re-layouts  3.01 us (2%)
    ppermute x25, waiting for transfers between devices, shift(): return lax.ppermute(a, axis, [(i, (i + by) % n) for i in range(n)])  46.1 us
    all_to_all x8, starting transfers between devices, exchange(): return lax.all_to_all(a, axis, split_axis=0, concat_axis=0, tiled=True)  40.8 us
    ppermute x25, starting transfers between devices, shift(): return lax.ppermute(a, axis, [(i, (i + by) % n) for i in range(n)])  28.8 us
    pallas_call x4, Pallas kernels, expert_down(): pl.pallas_call(functools.partial(down_kernel, steps, cut if last else 0,...  12.1 us
    pallas_call x1, Pallas kernels, inside_blocks(): pl.pallas_call(functools.partial(inside_kernel, group), grid=(heads // gr...  7.82 us
    pallas_call x1, Pallas kernels, local_states(): pl.pallas_call(functools.partial(state_kernel, group), grid=(heads // gro...  5.85 us
    pallas_call x1, Pallas kernels, hidden_rows(): pl.pallas_call(hidden_kernel, grid=(rows // tile,), out_shape=jax.ShapeDt...  4.96 us
    pallas_call x1, Pallas kernels, chosen_rows(): pl.pallas_call(functools.partial(chosen_kernel, group), out_shape=far((ch...  4.42 us
  transfers between devices with their start and end apart: 33, of which 19 were waited for; matrix products, arithmetic and copies ran while one was open for 0% of the time, Pallas kernels for 20%

profile of v8, /device:TPU:0, one launch (start us, length us, event | category | flops | bytes accessed | tf_op | source)
XLA Modules:
  0.0 186.8 jit_solution(10499335939846844067)
XLA Ops:
  0.6 5.9 %local_states.1 = (f32[512,12]{1,0:T(8,128)S(1)}, bf16[32,64,128]{2,1,0:T(8,128)(2,1)}) custom-call(bf16[512,1536]{1,0:T(8,128)(2,1)} %k_ref.3, bf16[512,1536]{1,0:T(8,128)(2,1)} %v_ref.3, f32[12,512]{1,0:T(8,128)} %bitcast.27), custom_call_target="tpu_custom_call" | custom-call | flops 201326592 | bytes 3145728 | tf_op jit(solution)/shard_map/local_states/pallas_call | solution.py:122
  6.5 8.4 %all-to-all-start = ((bf16[32,64,128]{2,1,0:T(8,128)(2,1)}), bf16[32,64,128]{2,1,0:T(8,128)(2,1)}, u32[]{:S(2)}, u32[]{:S(2)}) async-start(bf16[32,64,128]{2,1,0:T(8,128)(2,1)} %get-tuple-element.74), calls=%async_computation | async-start | bytes 1048576 | tf_op jit(solution)/shard_map/all_to_all | solution.py:798
  14.9 3.2 %route_rows.1 = (bf16[8,6400]{1,0:T(8,128)(2,1)}, bf16[8,6400]{1,0:T(8,128)(2,1)}, bf16[8,6400]{1,0:T(8,128)(2,1)}, bf16[8,6400]{1,0:T(8,128)(2,1)}, f32[16,128]{1,0:T(8,128)S(1)}) custom-call(s32[1]{0:T(128)} %bitcast.me_ref, s32[2,128]{1,0:T(2,128)S(1)} %bitcast.17, bf16[128,6144]{1,0:T(8,128)(2,1)} %res_ref.1, bf16[128,6144]{1,0:T(8,128)(2,1)} %gate_ref.1), custom_call_target="tpu_custom_call" | custom-call | flops 50331648 | bytes 3932160 | tf_op jit(solution)/shard_map/route_rows/pallas_call | solution.py:380
  18.1 7.8 %inside_blocks.1 = (f32[512,1536]{1,0:T(8,128)S(1)}, bf16[512,1536]{1,0:T(8,128)(2,1)}) custom-call(bf16[512,1536]{1,0:T(8,128)(2,1)} %q_ref.1, bf16[512,1536]{1,0:T(8,128)(2,1)} %k_ref.3, bf16[512,1536]{1,0:T(8,128)(2,1)} %v_ref.3, f32[512,12]{1,0:T(8,128)S(1)} %get-tuple-element.75.cum_ref, f32[12,512]{1,0:T(8,128)} %bitcast.28), custom_call_target="tpu_custom_call" | custom-call | flops 1610612736 | bytes 9437184 | tf_op jit(solution)/shard_map/inside_blocks/pallas_call | solution.py:216
  28.5 6.6 %all-to-all-start.1 = ((bf16[32,48,128]{2,1,0:T(8,128)(2,1)}), bf16[32,48,128]{2,1,0:T(8,128)(2,1)S(1)}, u32[]{:S(2)}, u32[]{:S(2)}) async-start(bf16[32,48,128]{2,1,0:T(8,128)(2,1)} %scan_blocks.1), calls=%async_computation.1 | async-start | bytes 786432 | tf_op jit(solution)/shard_map/all_to_all | solution.py:798
  41.8 3.4 %collective-permute-done.1.refs_2_ = bf16[8,6400]{1,0:T(8,128)(2,1)S(1)} collective-permute-done((bf16[8,6400]{1,0:T(8,128)(2,1)}, bf16[8,6400]{1,0:T(8,128)(2,1)S(1)}, u32[]{:S(2)}, u32[]{:S(2)}) %collective-permute-start.1) | collective-permute-done | bytes 102432 | tf_op jit(solution)/shard_map/ppermute | solution.py:803
  47.9 4.4 %chosen_rows.1 = bf16[64,1536]{1,0:T(8,128)(2,1)} custom-call(f32[512,1536]{1,0:T(8,128)S(1)} %get-tuple-element.89.inside_ref, bf16[512,1536]{1,0:T(8,128)(2,1)} %get-tuple-element.90.qs_hbm.qs_ref, bf16[12,128,128]{2,1,0:T(8,128)(2,1)S(1)} %bitcast.15, bf16[64,512]{1,0:T(8,128)(2,1)} %place_rows.1.place_ref), custom_call_target="tpu_custom_call" | custom-call | flops 402653184 | bytes 6291456 | tf_op jit(solution)/shard_map/chosen_rows/pallas_call | solution.py:286
  52.3 4.0 %all-to-all-start.2 = ((bf16[4,16,1536]{2,1,0:T(8,128)(2,1)}), bf16[4,16,1536]{2,1,0:T(8,128)(2,1)}, u32[]{:S(2)}, u32[]{:S(2)}) async-start(bf16[4,16,1536]{2,1,0:T(8,128)(2,1)} %bitcast.24), calls=%async_computation.2 | async-start | bytes 393216 | tf_op jit(solution)/shard_map/all_to_all | solution.py:798
  56.4 4.3 %carried_blocks.1 = (bf16[128,1536]{1,0:T(8,128)(2,1)}, bf16[128,1536]{1,0:T(8,128)(2,1)}, bf16[128,1536]{1,0:T(8,128)(2,1)}, bf16[128,1536]{1,0:T(8,128)(2,1)}) custom-call(s32[1]{0:T(128)} %bitcast.me_ref, f32[512,1536]{1,0:T(8,128)S(1)} %get-tuple-element.89.inside_ref, bf16[512,1536]{1,0:T(8,128)(2,1)} %get-tuple-element.90.qs_hbm.qs_ref, ...), custom_call_target="tpu_custom_call" | custom-call | flops 402653184 | bytes 6291456 | tf_op jit(solution)/shard_map/carried_blocks/pallas_call | solution.py:309
  66.6 4.4 %all-to-all-start.3 = ((bf16[4,16,3072]{2,1,0:T(8,128)(2,1)}), bf16[4,16,3072]{2,1,0:T(8,128)(2,1)S(1)}, u32[]{:S(2)}, u32[]{:S(2)}) async-start(bf16[4,16,3072]{2,1,0:T(8,128)(2,1)} %get-tuple-element.99), calls=%async_computation.3 | async-start | bytes 786432 | tf_op jit(solution)/shard_map/all_to_all | solution.py:798
  82.3 4.9 %all-to-all-start.4 = ((bf16[4,4,16,3072]{3,2,1,0:T(8,128)(2,1)}), bf16[4,4,16,3072]{3,2,1,0:T(8,128)(2,1)S(1)}, u32[]{:S(2)}, u32[]{:S(2)}) async-start(bf16[4,4,16,3072]{3,2,1,0:T(8,128)(2,1)} %repeat.1), calls=%async_computation.4 | async-start | bytes 3145728 | tf_op jit(solution)/shard_map/all_to_all | solution.py:798
  97.9 5.5 %collective-permute-done.7.refs_1_ = bf16[4,16,3072]{2,1,0:T(8,128)(2,1)S(1)} collective-permute-done((bf16[4,16,3072]{2,1,0:T(8,128)(2,1)S(1)}, bf16[4,16,3072]{2,1,0:T(8,128)(2,1)S(1)}, u32[]{:S(2)}, u32[]{:S(2)}) %collective-permute-start.7) | collective-permute-done | bytes 393248 | tf_op jit(solution)/shard_map/ppermute | solution.py:803
  103.5 4.2 %collective-permute-done.8.refs_2_ = bf16[4,16,3072]{2,1,0:T(8,128)(2,1)S(1)} collective-permute-done((bf16[4,16,3072]{2,1,0:T(8,128)(2,1)S(1)}, bf16[4,16,3072]{2,1,0:T(8,128)(2,1)S(1)}, u32[]{:S(2)}, u32[]{:S(2)}) %collective-permute-start.8) | collective-permute-done | bytes 393248 | tf_op jit(solution)/shard_map/ppermute | solution.py:803
  108.8 4.2 %first_act.1 = (bf16[256,288]{1,0:T(8,128)(2,1)S(1)}, bf16[2,288,6144]{2,1,0:T(8,128)(2,1)S(1)}) custom-call(bf16[288,6144]{1,0:T(8,128)(2,1)} %bitcast.22, bf16[288,6144]{1,0:T(8,128)(2,1)} %bitcast.23, bf16[4,4,16,3072]{3,2,1,0:T(8,128)(2,1)S(1)} %all-to-all-done.4.one_ref, bf16[4,16,3072]{2,1,0:T(8,128)(2,1)S(1)} %all-to-all-done.3.refs_0_, ...), custom_call_target="tpu_custom_call" | custom-call | flops 1811939328 | bytes 10223616 | tf_op jit(solution)/shard_map/first_act/pallas_call | solution.py:599
  121.1 3.3 %collective-permute-done.17.refs_0_ = bf16[4,4,16,3584]{3,2,1,0:T(8,128)(2,1)S(1)} collective-permute-done((bf16[4,4,16,3584]{3,2,1,0:T(8,128)(2,1)S(1)}, bf16[4,4,16,3584]{3,2,1,0:T(8,128)(2,1)S(1)}, u32[]{:S(2)}, u32[]{:S(2)}) %collective-permute-start.17) | collective-permute-done | bytes 1835040 | tf_op jit(solution)/shard_map/ppermute | solution.py:803
  124.3 3.9 %expert_down.6 = bf16[4,4,16,3584]{3,2,1,0:T(8,128)(2,1)} custom-call(bf16[256,288]{1,0:T(8,128)(2,1)S(1)} %get-tuple-element.131.act_ref, bf16[288,6144]{1,0:T(8,128)(2,1)} %bitcast.20, bf16[4,4,16,3584]{3,2,1,0:T(8,128)(2,1)S(1)} %collective-permute-done.17.refs_0_), custom_call_target="tpu_custom_call" | custom-call | flops 528482304 | bytes 3899392 | tf_op jit(solution)/shard_map/expert_down/pallas_call | solution.py:685
  128.3 4.5 %all-to-all-start.5 = ((bf16[4,4,16,3584]{3,2,1,0:T(8,128)(2,1)}), bf16[4,4,16,3584]{3,2,1,0:T(8,128)(2,1)S(1)}, u32[]{:S(2)}, u32[]{:S(2)}) async-start(bf16[4,4,16,3584]{3,2,1,0:T(8,128)(2,1)} %expert_down.6), calls=%async_computation.5 | async-start | bytes 3670016 | tf_op jit(solution)/shard_map/all_to_all | solution.py:798
  132.8 3.3 %expert_down.7 = (bf16[4,16,2560]{2,1,0:T(8,128)(2,1)}, bf16[4,16,2560]{2,1,0:T(8,128)(2,1)}, bf16[4,16,2560]{2,1,0:T(8,128)(2,1)}, bf16[4,16,2560]{2,1,0:T(8,128)(2,1)}) custom-call(bf16[256,288]{1,0:T(8,128)(2,1)S(1)} %get-tuple-element.131.act_ref, bf16[288,6144]{1,0:T(8,128)(2,1)} %bitcast.21, bf16[4,4,16,2560]{3,2,1,0:T(8,128)(2,1)S(1)} %collective-permute-done.18.refs_0_), custom_call_target="tpu_custom_call" | custom-call | flops 377487360 | bytes 2785280 | tf_op jit(solution)/shard_map/expert_down/pallas_call | solution.py:685
  139.9 13.2 %collective-permute-done.19.refs_1_ = bf16[4,16,2560]{2,1,0:T(8,128)(2,1)S(1)} collective-permute-done((bf16[4,16,2560]{2,1,0:T(8,128)(2,1)}, bf16[4,16,2560]{2,1,0:T(8,128)(2,1)S(1)}, u32[]{:S(2)}, u32[]{:S(2)}) %collective-permute-start.19) | collective-permute-done | bytes 327712 | tf_op jit(solution)/shard_map/ppermute | solution.py:803
  153.1 3.6 %collective-permute-done.21.refs_3_ = bf16[4,16,2560]{2,1,0:T(8,128)(2,1)S(1)} collective-permute-done((bf16[4,16,2560]{2,1,0:T(8,128)(2,1)}, bf16[4,16,2560]{2,1,0:T(8,128)(2,1)S(1)}, u32[]{:S(2)}, u32[]{:S(2)}) %collective-permute-start.21) | collective-permute-done | bytes 327712 | tf_op jit(solution)/shard_map/ppermute | solution.py:803
  158.5 4.5 %all-to-all-start.6 = ((bf16[4,16,2560]{2,1,0:T(8,128)(2,1)}), bf16[4,16,2560]{2,1,0:T(8,128)(2,1)S(1)}, u32[]{:S(2)}, u32[]{:S(2)}) async-start(bf16[4,16,2560]{2,1,0:T(8,128)(2,1)} %stack_sum.1), calls=%async_computation.6 | async-start | bytes 655360 | tf_op jit(solution)/shard_map/all_to_all | solution.py:798
  166.7 3.6 %collective-permute-done.22.refs_1_ = bf16[16,3584]{1,0:T(8,128)(2,1)S(1)} collective-permute-done((bf16[16,3584]{1,0:T(8,128)(2,1)}, bf16[16,3584]{1,0:T(8,128)(2,1)S(1)}, u32[]{:S(2)}, u32[]{:S(2)}) %collective-permute-start.22) | collective-permute-done | bytes 114720 | tf_op jit(solution)/shard_map/ppermute | solution.py:803
  175.4 3.4 %all-to-all-start.7 = ((bf16[4,4,6144]{2,1,0:T(4,128)(2,1)}), bf16[4,4,6144]{2,1,0:T(4,128)(2,1)S(1)}, u32[]{:S(2)}, u32[]{:S(2)}) async-start(bf16[4,4,6144]{2,1,0:T(4,128)(2,1)} %row_sum.1), calls=%async_computation.7 | async-start | bytes 393216 | tf_op jit(solution)/shard_map/all_to_all | solution.py:798
  179.0 5.0 %hidden_rows.1 = bf16[128,6144]{1,0:T(8,128)(2,1)} custom-call(s32[1]{0:T(128)} %bitcast.me_ref, bf16[128,6144]{1,0:T(8,128)(2,1)} %res_ref.1, bf16[128,6144]{1,0:T(8,128)(2,1)} %gate_ref.1, f32[1,6144]{1,0:T(1,128)} %bitcast.26, bf16[128,1536]{1,0:T(8,128)(2,1)S(1)} %copy-done, bf16[128,1536]{1,0:T(8,128)(2,1)S(1)} %copy-done.4, ...), custom_call_target="tpu_custom_call" | custom-call | flops 15728640 | bytes 6291456 | tf_op jit(solution)/shard_map/hidden_rows/pallas_call | solution.py:500
  (90 shorter events, 66.4 us)
Async XLA Ops:
  6.5 20.1 %all-to-all-start = ((bf16[32,64,128]{2,1,0:T(8,128)(2,1)}), bf16[32,64,128]{2,1,0:T(8,128)(2,1)}, u32[]{:S(2)}, u32[]{:S(2)}) async-start(bf16[32,64,128]{2,1,0:T(8,128)(2,1)} %get-tuple-element.74), calls=%async_computation | async-start | bytes 1048576 | tf_op jit(solution)/shard_map/all_to_all | solution.py:798
  28.5 19.4 %all-to-all-start.1 = ((bf16[32,48,128]{2,1,0:T(8,128)(2,1)}), bf16[32,48,128]{2,1,0:T(8,128)(2,1)S(1)}, u32[]{:S(2)}, u32[]{:S(2)}) async-start(bf16[32,48,128]{2,1,0:T(8,128)(2,1)} %scan_blocks.1), calls=%async_computation.1 | async-start | bytes 786432 | tf_op jit(solution)/shard_map/all_to_all | solution.py:798
  35.1 6.6 %collective-permute-start = (bf16[8,6400]{1,0:T(8,128)(2,1)}, bf16[8,6400]{1,0:T(8,128)(2,1)S(1)}, u32[]{:S(2)}, u32[]{:S(2)}) collective-permute-start(bf16[8,6400]{1,0:T(8,128)(2,1)} %get-tuple-element.86), channel_id=1, source_target_pairs={{0,1},{1,2},{2,3},{3,0},{4,5},{5,6},{6,7},{7,4},{8,9},{9,10},{10,1... | collective-permute-start | bytes 307208 | tf_op jit(solution)/shard_map/ppermute | solution.py:803
  36.8 8.3 %collective-permute-start.1 = (bf16[8,6400]{1,0:T(8,128)(2,1)}, bf16[8,6400]{1,0:T(8,128)(2,1)S(1)}, u32[]{:S(2)}, u32[]{:S(2)}) collective-permute-start(bf16[8,6400]{1,0:T(8,128)(2,1)} %get-tuple-element.87), channel_id=1, source_target_pairs={{0,2},{1,3},{2,0},{3,1},{4,6},{5,7},{6,4},{7,5},{8,10},{9,11},{10,... | collective-permute-start | bytes 307208 | tf_op jit(solution)/shard_map/ppermute | solution.py:803
  52.3 10.4 %all-to-all-start.2 = ((bf16[4,16,1536]{2,1,0:T(8,128)(2,1)}), bf16[4,16,1536]{2,1,0:T(8,128)(2,1)}, u32[]{:S(2)}, u32[]{:S(2)}) async-start(bf16[4,16,1536]{2,1,0:T(8,128)(2,1)} %bitcast.24), calls=%async_computation.2 | async-start | bytes 393216 | tf_op jit(solution)/shard_map/all_to_all | solution.py:798
  62.7 17.3 %collective-permute-start.6 = (bf16[128,1536]{1,0:T(8,128)(2,1)}, bf16[128,1536]{1,0:T(8,128)(2,1)S(1)}, u32[]{:S(2)}, u32[]{:S(2)}) collective-permute-start(bf16[128,1536]{1,0:T(8,128)(2,1)} %get-tuple-element.100), channel_id=1, source_target_pairs={{0,2},{1,3},{2,0},{3,1},{4,6},{5,7},{6,4},{7,5},{8,10},{9,11},{10,... | collective-permute-start | bytes 1179656 | tf_op jit(solution)/shard_map/ppermute | solution.py:803
  66.6 13.4 %all-to-all-start.3 = ((bf16[4,16,3072]{2,1,0:T(8,128)(2,1)}), bf16[4,16,3072]{2,1,0:T(8,128)(2,1)S(1)}, u32[]{:S(2)}, u32[]{:S(2)}) async-start(bf16[4,16,3072]{2,1,0:T(8,128)(2,1)} %get-tuple-element.99), calls=%async_computation.3 | async-start | bytes 786432 | tf_op jit(solution)/shard_map/all_to_all | solution.py:798
  71.0 6.6 %collective-permute-start.3 = (bf16[16,3072]{1,0:T(8,128)(2,1)}, bf16[16,3072]{1,0:T(8,128)(2,1)S(1)}, u32[]{:S(2)}, u32[]{:S(2)}) collective-permute-start(bf16[16,3072]{1,0:T(8,128)(2,1)} %get-tuple-element.101.refs_0_), channel_id=1, source_target_pairs={{0,8},{8,16},{16,24},{24,0},{1,9},{9,17},{17,25},{25,1},{2,10},{10... | collective-permute-start | bytes 294920 | tf_op jit(solution)/shard_map/ppermute | solution.py:803
  72.5 6.6 %collective-permute-start.4 = (bf16[16,3072]{1,0:T(8,128)(2,1)}, bf16[16,3072]{1,0:T(8,128)(2,1)S(1)}, u32[]{:S(2)}, u32[]{:S(2)}) collective-permute-start(bf16[16,3072]{1,0:T(8,128)(2,1)} %get-tuple-element.101.refs_0_), channel_id=1, source_target_pairs={{0,16},{8,24},{16,0},{24,8},{1,17},{9,25},{17,1},{25,9},{2,18},{10... | collective-permute-start | bytes 294920 | tf_op jit(solution)/shard_map/ppermute | solution.py:803
  82.3 25.4 %all-to-all-start.4 = ((bf16[4,4,16,3072]{3,2,1,0:T(8,128)(2,1)}), bf16[4,4,16,3072]{3,2,1,0:T(8,128)(2,1)S(1)}, u32[]{:S(2)}, u32[]{:S(2)}) async-start(bf16[4,4,16,3072]{3,2,1,0:T(8,128)(2,1)} %repeat.1), calls=%async_computation.4 | async-start | bytes 3145728 | tf_op jit(solution)/shard_map/all_to_all | solution.py:798
  87.2 9.2 %collective-permute-start.10 = (bf16[128,1536]{1,0:T(8,128)(2,1)}, bf16[128,1536]{1,0:T(8,128)(2,1)S(1)}, u32[]{:S(2)}, u32[]{:S(2)}) collective-permute-start(bf16[128,1536]{1,0:T(8,128)(2,1)} %get-tuple-element.106), channel_id=1, source_target_pairs={{0,1},{1,2},{2,3},{3,0},{4,5},{5,6},{6,7},{7,4},{8,9},{9,10},{10,1... | collective-permute-start | bytes 1179656 | tf_op jit(solution)/shard_map/ppermute | solution.py:803
  87.9 9.3 %collective-permute-start.11 = (bf16[128,1536]{1,0:T(8,128)(2,1)S(1)}, bf16[128,1536]{1,0:T(8,128)(2,1)S(1)}, u32[]{:S(2)}, u32[]{:S(2)}) collective-permute-start(bf16[128,1536]{1,0:T(8,128)(2,1)S(1)} %copy-done.12), channel_id=1, source_target_pairs={{0,3},{1,0},{2,1},{3,2},{4,7},{5,4},{6,5},{7,6},{8,11},{9,8},{10,9... | collective-permute-start | bytes 1179656 | tf_op jit(solution)/shard_map/ppermute | solution.py:803
  90.5 13.0 %collective-permute-start.7 = (bf16[4,16,3072]{2,1,0:T(8,128)(2,1)S(1)}, bf16[4,16,3072]{2,1,0:T(8,128)(2,1)S(1)}, u32[]{:S(2)}, u32[]{:S(2)}) collective-permute-start(bf16[4,16,3072]{2,1,0:T(8,128)(2,1)S(1)} %all-to-all-done.3.refs_0_), channel_id=1, source_target_pairs={{0,8},{8,16},{16,24},{24,0},{1,9},{9,17},{17,25},{25,1},{2,10},{10... | collective-permute-start | bytes 1179656 | tf_op jit(solution)/shard_map/ppermute | solution.py:803
  91.5 16.2 %collective-permute-start.8 = (bf16[4,16,3072]{2,1,0:T(8,128)(2,1)S(1)}, bf16[4,16,3072]{2,1,0:T(8,128)(2,1)S(1)}, u32[]{:S(2)}, u32[]{:S(2)}) collective-permute-start(bf16[4,16,3072]{2,1,0:T(8,128)(2,1)S(1)} %all-to-all-done.3.refs_0_), channel_id=1, source_target_pairs={{0,16},{8,24},{16,0},{24,8},{1,17},{9,25},{17,1},{25,9},{2,18},{10... | collective-permute-start | bytes 1179656 | tf_op jit(solution)/shard_map/ppermute | solution.py:803
  94.6 13.1 %collective-permute-start.9 = (bf16[4,16,3072]{2,1,0:T(8,128)(2,1)S(1)}, bf16[4,16,3072]{2,1,0:T(8,128)(2,1)S(1)}, u32[]{:S(2)}, u32[]{:S(2)}) collective-permute-start(bf16[4,16,3072]{2,1,0:T(8,128)(2,1)S(1)} %all-to-all-done.3.refs_0_), channel_id=1, source_target_pairs={{0,24},{8,0},{16,8},{24,16},{1,25},{9,1},{17,9},{25,17},{2,26},{10... | collective-permute-start | bytes 1179656 | tf_op jit(solution)/shard_map/ppermute | solution.py:803
  120.7 7.6 %collective-permute-start.18 = (bf16[4,4,16,2560]{3,2,1,0:T(8,128)(2,1)S(1)}, bf16[4,4,16,2560]{3,2,1,0:T(8,128)(2,1)S(1)}, u32[]{:S(2)}, u32[]{:S(2)}) collective-permute-start(bf16[4,4,16,2560]{3,2,1,0:T(8,128)(2,1)S(1)} %expert_down.5), channel_id=1, source_target_pairs={{0,4},{4,0},{1,5},{5,1},{2,6},{6,2},{3,7},{7,3},{8,12},{12,8},{9,1... | collective-permute-start | bytes 3932168 | tf_op jit(solution)/shard_map/ppermute | solution.py:803
  128.3 28.4 %all-to-all-start.5 = ((bf16[4,4,16,3584]{3,2,1,0:T(8,128)(2,1)}), bf16[4,4,16,3584]{3,2,1,0:T(8,128)(2,1)S(1)}, u32[]{:S(2)}, u32[]{:S(2)}) async-start(bf16[4,4,16,3584]{3,2,1,0:T(8,128)(2,1)} %expert_down.6), calls=%async_computation.5 | async-start | bytes 3670016 | tf_op jit(solution)/shard_map/all_to_all | solution.py:798
  136.1 17.0 %collective-permute-start.19 = (bf16[4,16,2560]{2,1,0:T(8,128)(2,1)}, bf16[4,16,2560]{2,1,0:T(8,128)(2,1)S(1)}, u32[]{:S(2)}, u32[]{:S(2)}) collective-permute-start(bf16[4,16,2560]{2,1,0:T(8,128)(2,1)} %get-tuple-element.134), channel_id=1, source_target_pairs={{0,24},{8,0},{16,8},{24,16},{1,25},{9,1},{17,9},{25,17},{2,26},{10... | collective-permute-start | bytes 983048 | tf_op jit(solution)/shard_map/ppermute | solution.py:803
  138.7 14.4 %collective-permute-start.20 = (bf16[4,16,2560]{2,1,0:T(8,128)(2,1)}, bf16[4,16,2560]{2,1,0:T(8,128)(2,1)S(1)}, u32[]{:S(2)}, u32[]{:S(2)}) collective-permute-start(bf16[4,16,2560]{2,1,0:T(8,128)(2,1)} %get-tuple-element.135), channel_id=1, source_target_pairs={{0,16},{8,24},{16,0},{24,8},{1,17},{9,25},{17,1},{25,9},{2,18},{10... | collective-permute-start | bytes 983048 | tf_op jit(solution)/shard_map/ppermute | solution.py:803
  139.8 16.9 %collective-permute-start.21 = (bf16[4,16,2560]{2,1,0:T(8,128)(2,1)}, bf16[4,16,2560]{2,1,0:T(8,128)(2,1)S(1)}, u32[]{:S(2)}, u32[]{:S(2)}) collective-permute-start(bf16[4,16,2560]{2,1,0:T(8,128)(2,1)} %get-tuple-element.136), channel_id=1, source_target_pairs={{0,8},{8,16},{16,24},{24,0},{1,9},{9,17},{17,25},{25,1},{2,10},{10... | collective-permute-start | bytes 983048 | tf_op jit(solution)/shard_map/ppermute | solution.py:803
  158.5 15.2 %all-to-all-start.6 = ((bf16[4,16,2560]{2,1,0:T(8,128)(2,1)}), bf16[4,16,2560]{2,1,0:T(8,128)(2,1)S(1)}, u32[]{:S(2)}, u32[]{:S(2)}) async-start(bf16[4,16,2560]{2,1,0:T(8,128)(2,1)} %stack_sum.1), calls=%async_computation.6 | async-start | bytes 655360 | tf_op jit(solution)/shard_map/all_to_all | solution.py:798
  165.6 7.1 %collective-permute-start.23 = (bf16[16,3584]{1,0:T(8,128)(2,1)}, bf16[16,3584]{1,0:T(8,128)(2,1)S(1)}, u32[]{:S(2)}, u32[]{:S(2)}) collective-permute-start(bf16[16,3584]{1,0:T(8,128)(2,1)} %get-tuple-element.144), channel_id=1, source_target_pairs={{0,16},{8,24},{16,0},{24,8},{1,17},{9,25},{17,1},{25,9},{2,18},{10... | collective-permute-start | bytes 344072 | tf_op jit(solution)/shard_map/ppermute | solution.py:803
  166.6 7.0 %collective-permute-start.24 = (bf16[16,3584]{1,0:T(8,128)(2,1)}, bf16[16,3584]{1,0:T(8,128)(2,1)S(1)}, u32[]{:S(2)}, u32[]{:S(2)}) collective-permute-start(bf16[16,3584]{1,0:T(8,128)(2,1)} %get-tuple-element.145), channel_id=1, source_target_pairs={{0,8},{8,16},{16,24},{24,0},{1,9},{9,17},{17,25},{25,1},{2,10},{10... | collective-permute-start | bytes 344072 | tf_op jit(solution)/shard_map/ppermute | solution.py:803
  175.4 9.7 %all-to-all-start.7 = ((bf16[4,4,6144]{2,1,0:T(4,128)(2,1)}), bf16[4,4,6144]{2,1,0:T(4,128)(2,1)S(1)}, u32[]{:S(2)}, u32[]{:S(2)}) async-start(bf16[4,4,6144]{2,1,0:T(4,128)(2,1)} %row_sum.1), calls=%async_computation.7 | async-start | bytes 393216 | tf_op jit(solution)/shard_map/all_to_all | solution.py:798
  (22 other events, 152.5 us)

commit v9 on v8

--- a/solution.py
+++ b/solution.py
@@ -244,27 +244,12 @@
         ).astype(BF16)
 
 
-def chosen_kernel(group, inside_ref, qs_hbm, state_ref, place_ref, sel_ref, att_ref, qs_ref, sem):
-    wide = group * HEAD_DIM
-    steps = sel_ref.shape[1] // wide
-    copies = []
-    for g in range(steps):
-        cols = pl.ds(g * wide, wide)
-        copies.append(pltpu.make_async_copy(qs_hbm.at[:, cols], qs_ref.at[:, cols], sem.at[g]))
-    for c in copies:
-        c.start()
-    for g in range(steps):
-        cols = slice(g * wide, (g + 1) * wide)
-        copies[g].wait()
-        attend(
-            group,
-            inside_ref.at[:, cols],
-            qs_ref.at[:, cols],
-            state_ref.at[g * group : (g + 1) * group],
-            att_ref,
-        )
-        sel_ref[:, cols] = jnp.dot(
-            place_ref[...], att_ref[...], preferred_element_type=F32
+def chosen_kernel(inside_ref, qs_ref, state_ref, sel_ref):
+    for h in range(state_ref.shape[0]):
+        cols = slice(h * HEAD_DIM, (h + 1) * HEAD_DIM)
+        sel_ref[:, cols] = (
+            inside_ref[:, cols]
+            + jnp.dot(qs_ref[:, cols], state_ref[h], preferred_element_type=F32)
         ).astype(BF16)
 
 
@@ -278,25 +263,15 @@
         outs[d][...] = att_ref[pl.ds(at, tokens), :]
 
 
-def chosen_rows(inside, qs, state, place, group=3):
-    rows, width = inside.shape
-    chosen = place.shape[0]
-    wide = group * HEAD_DIM
-    whole = pl.BlockSpec(memory_space=pltpu.VMEM)
-    return pl.pallas_call(
-        functools.partial(chosen_kernel, group),
+def chosen_rows(inside, qs, state):
+    chosen, width = inside.shape
+    return pl.pallas_call(
+        chosen_kernel,
         out_shape=far((chosen, width)),
-        in_specs=[whole, pl.BlockSpec(memory_space=pl.ANY), whole, whole],
-        out_specs=whole,
-        scratch_shapes=[
-            pltpu.VMEM((rows, wide), BF16),
-            pltpu.VMEM((rows, width), BF16),
-            pltpu.SemaphoreType.DMA((width // wide,)),
-        ],
-        compiler_params=params(),
-        cost_estimate=cost(4 * rows * width * HEAD_DIM, 8 * rows * width),
+        compiler_params=params(),
+        cost_estimate=cost(2 * chosen * width * HEAD_DIM, 8 * chosen * width),
         name="chosen_rows",
-    )(inside, qs, state, place)
+    )(inside, qs, state)
 
 
 def carried_blocks(me, inside, qs, state, held, group=3):
@@ -402,8 +377,8 @@
     return out
 
 
-def place_kernel(me_ref, *refs):
-    pieces, place_ref = refs[:-1], refs[-1]
+def place_kernel(group, me_ref, inside_ref, qs_ref, *refs):
+    pieces, (some_inside_ref, some_qs_ref, place_ref) = refs[:-3], refs[-3:]
     held = len(pieces)
     tokens = pieces[0].shape[1] // 2
     total = held * tokens
@@ -427,23 +402,44 @@
     for e in range(held):
         hit = jnp.where(rank[e : e + 1, :] == slot, m[e : e + 1, :] * here, 0.0)
         place_ref[e * rows : (e + 1) * rows, :] = hit.astype(BF16)
-
-
-def place_rows(me, pieces, tokens):
+    place = place_ref[...]
+    wide = group * HEAD_DIM
+    for g in range(qs_ref.shape[1] // wide):
+        cols = slice(g * wide, (g + 1) * wide)
+        some_qs_ref[:, cols] = jnp.dot(
+            place, qs_ref[:, cols], preferred_element_type=F32
+        ).astype(BF16)
+        rest = inside_ref[:, cols]
+        picked = None
+        for _ in range(3):
+            part = rest.astype(BF16)
+            rest = rest - part.astype(F32)
+            term = jnp.dot(place, part, preferred_element_type=F32)
+            picked = term if picked is None else picked + term
+        some_inside_ref[:, cols] = picked
+
+
+def place_rows(me, inside, qs, pieces, tokens, group=3):
     held = len(pieces)
+    chosen = held * held * CAP
     width = pieces[0].shape[1] - 2 * tokens
     at = width // (2 * tokens)
-    return pl.pallas_call(
-        place_kernel,
+    whole = pl.BlockSpec(memory_space=pltpu.VMEM)
+    return pl.pallas_call(
+        functools.partial(place_kernel, group),
         grid=(1,),
-        out_shape=far((held * held * CAP, held * tokens)),
-        in_specs=[pl.BlockSpec(memory_space=pltpu.SMEM)]
+        out_shape=(
+            far((chosen, inside.shape[1]), F32),
+            far((chosen, inside.shape[1])),
+        ),
+        in_specs=[pl.BlockSpec(memory_space=pltpu.SMEM), whole, whole]
         + [pl.BlockSpec((2 * CAP, 2 * tokens), lambda i: (0, at))] * held,
-        out_specs=pl.BlockSpec((held * held * CAP, held * tokens), lambda i: (0, 0)),
+        out_specs=(whole, whole),
+        scratch_shapes=[pltpu.VMEM((chosen, held * tokens), BF16)],
         compiler_params=params(),
         cost_estimate=cost(1000000, 200000),
         name="place_rows",
-    )(me, *pieces)
+    )(me, inside, qs, *pieces)
 
 
 def gated(att, res, gate, attn_gain):
@@ -465,18 +461,20 @@
     normed = (
         hidden * lax.rsqrt(jnp.mean(hidden * hidden, axis=-1, keepdims=True) + EPS) * mg_ref[...]
     ).astype(BF16)
-    one_ref[...] = normed[:, : width // 2]
+    cut = one_ref.shape[1]
+    one_ref[...] = normed[:, :cut]
     for i in range(two_ref.shape[0]):
-        two_ref[i] = normed[:, width // 2 :]
+        two_ref[i] = normed[:, cut:]
 
 
 def routed_norm(me, att, pieces, attn_gain, moe_gain, copies):
     sources, rows, part = att.shape
     width = sources * part
+    cut = width * 7 // 12
     whole = pl.BlockSpec(memory_space=pltpu.VMEM)
     return pl.pallas_call(
         routed_norm_kernel,
-        out_shape=(far((rows, width // 2)), far((copies, rows, width // 2))),
+        out_shape=(far((rows, cut)), far((copies, rows, width - cut))),
         in_specs=[pl.BlockSpec(memory_space=pltpu.SMEM)] + [whole] * (3 + len(pieces)),
         out_specs=(whole, whole),
         compiler_params=params(),
@@ -552,7 +550,7 @@
     for s in range(steps):
         cols = slice(s * wide, (s + 1) * wide)
         arrived(s)
-        if s < steps // 2:
+        if s * wide < half:
             x = [one_ref[z, k, :, cols] for k in range(nx) for z in range(nz)]
         else:
             near = slice(s * wide - half, (s + 1) * wide - half)
@@ -589,7 +587,7 @@
     refs[-1][...] = act_rows(steps, w_ref, one_ref, refs[:-1], lambda s: None)
 
 
-def expert_act(one, twos, weights, steps=6):
+def expert_act(one, twos, weights, steps=12):
     nz, nx, rows, half = one.shape
     count = nz * nx * rows
     whole = pl.BlockSpec(memory_space=pltpu.VMEM)
@@ -636,8 +634,24 @@
     for c in copies:
         c.start()
     refs = refs[:-2]
-    added = refs[0] if len(refs) != 1 else None
-    outs = refs[1:] if len(refs) != 1 else refs
+    added, kept, ends = (refs[0], refs[-2], refs[-1]) if len(refs) != 1 else (None,) * 3
+    outs = refs[1:-2] if len(refs) != 1 else refs
+    leaving = []
+
+    def send(s, cols):
+        n = s * len(outs)
+        if len(outs) == 1:
+            leaving.append(
+                pltpu.make_async_copy(kept.at[:, :, :, cols], outs[0].at[:, :, :, cols], ends.at[n])
+            )
+            leaving[-1].start()
+            return
+        for k, ref in enumerate(outs):
+            leaving.append(
+                pltpu.make_async_copy(kept.at[k, :, :, cols], ref.at[:, :, cols], ends.at[n + k])
+            )
+            leaving[-1].start()
+
     act = act_ref[...]
     if by_x:
         nx = outs[0].shape[0] if len(outs) == 1 else len(outs)
@@ -653,18 +667,19 @@
         if by_x:
             if added is not None:
                 out = out + added[:, :, :, cols].astype(F32)
-            out = out.astype(BF16)
-            if len(outs) == 1:
-                outs[0][:, :, :, cols] = out
-            else:
-                for k in range(nx):
-                    outs[k][:, :, cols] = out[k]
+            target = outs[0] if added is None else kept
+            target[:, :, :, cols] = out.astype(BF16)
         else:
             for z in range(nz):
                 part = out[:, z]
                 if added is not None:
                     part = part + added[z, :, :, cols].astype(F32)
-                outs[0][z, :, :, cols] = part.astype(BF16)
+                target = outs[0] if added is None else kept
+                target[z, :, :, cols] = part.astype(BF16)
+        if added is not None:
+            send(s, pl.ds(s * wide, wide))
+    for c in leaving:
+        c.wait()
 
 
 def expert_down(act, w_down, cut, last, nz, nx, added=None, steps=2):
@@ -682,12 +697,19 @@
     else:
         shapes = (far((nz, nx, rows, half)),)
     more = () if added is None else (added,)
+    away = pl.BlockSpec(memory_space=pl.ANY)
+    scratch = [pltpu.VMEM((units, half), BF16), pltpu.SemaphoreType.DMA((steps,))]
+    if added is not None:
+        scratch = [
+            pltpu.VMEM(added.shape, BF16),
+            pltpu.SemaphoreType.DMA((steps * len(shapes),)),
+        ] + scratch
     return pl.pallas_call(
         functools.partial(down_kernel, steps, cut if last else 0, last),
         out_shape=shapes,
-        in_specs=[whole, pl.BlockSpec(memory_space=pl.ANY)] + [whole] * len(more),
-        out_specs=(whole,) * len(shapes),
-        scratch_shapes=[pltpu.VMEM((units, half), BF16), pltpu.SemaphoreType.DMA((steps,))],
+        in_specs=[whole, away] + [whole] * len(more),
+        out_specs=(whole if added is None else away,) * len(shapes),
+        scratch_shapes=scratch,
         compiler_params=params(),
         cost_estimate=cost(2 * count * half * units, 2 * half * units + 2 * count * half),
         name="expert_down",
@@ -842,9 +864,9 @@
     state = exchange(prior, CTX).reshape(heads, HEAD_DIM, HEAD_DIM)
     pieces = [pieces[0]] + [shift(pieces[d], "exp", d) for d in range(1, held)]
     pieces = [hbm(a) for a in pieces]
-    place = place_rows(me, pieces, tokens)
-
-    routed = chosen_rows(inside, hbm(qs), state, hbm(place))
+    some_inside, some_qs = place_rows(me, inside, hbm(qs), pieces, tokens)
+
+    routed = chosen_rows(hbm(some_inside), hbm(some_qs), state)
     _, inside, qs, state = keep((routed, inside, qs, state))
     routed = exchange(routed.reshape(held, held * CAP, width), "exp")
     attention = carried_blocks(me, inside, hbm(qs), state, held)
@@ -861,7 +883,7 @@
     right, left = shift(attention[1], "exp", 1), shift(attention[3], "exp", 3)
     one, twos, right, left = keep((one, twos, right, left))
 
-    cut = moe_gain.shape[1] * 7 // 12
+    cut = moe_gain.shape[1] * 2 // 3
     act_own, weights = expert_act(one, twos, (w_gate, w_up))
     one, twos = shift(one, "core", 1), [shift(a, "core", 1) for a in twos]
     one, twos, weights = keep((one, twos, weights))

time: 188 us -> 191 us (1.016)
  waiting for transfers between devices: 50 us -> 53.3 us
    all_to_all x8, waiting for transfers between devices: 3.93 us -> 11.8 us  [exchange(): return lax.all_to_all(a, axis, split_axis=0, concat_axis=0, tiled=True)]
    ppermute x25, waiting for transfers between devices: 46.1 us -> 41.5 us  [shift(): return lax.ppermute(a, axis, [(i, (i + by) % n) for i in range(n)])]
    all_to_all x8, starting transfers between devices: 40.8 us -> 38.8 us  [exchange(): return lax.all_to_all(a, axis, split_axis=0, concat_axis=0, tiled=True)]
  transfers between devices with their start and end apart: 33 -> 33, of which waited for: 19 -> 21; matrix products, arithmetic and copies ran while one was open for 0% -> 0% of each run, Pallas kernels for 20% -> 20%
where the time goes in v9:
time: 191 us; the launch traced here: 190 us
  starting transfers between devices  69 us (36%)
  Pallas kernels  62.5 us (33%)
  waiting for transfers between devices  53.3 us (28%)
  local copies, waits for them, and re-layouts  4.01 us (2%)
    ppermute x25, waiting for transfers between devices, shift(): return lax.ppermute(a, axis, [(i, (i + by) % n) for i in range(n)])  41.5 us
    all_to_all x8, starting transfers between devices, exchange(): return lax.all_to_all(a, axis, split_axis=0, concat_axis=0, tiled=True)  38.8 us
    ppermute x25, starting transfers between devices, shift(): return lax.ppermute(a, axis, [(i, (i + by) % n) for i in range(n)])  30.3 us
    all_to_all x8, waiting for transfers between devices, exchange(): return lax.all_to_all(a, axis, split_axis=0, concat_axis=0, tiled=True)  11.8 us
    pallas_call x4, Pallas kernels, expert_down(): pl.pallas_call(functools.partial(down_kernel, steps, cut if last else 0,...  11.3 us
    pallas_call x1, Pallas kernels, inside_blocks(): pl.pallas_call(functools.partial(inside_kernel, group), grid=(heads // gr...  7.82 us
    pallas_call x1, Pallas kernels, local_states(): pl.pallas_call(functools.partial(state_kernel, group), grid=(heads // gro...  5.85 us
    pallas_call x1, Pallas kernels, hidden_rows(): pl.pallas_call(hidden_kernel, grid=(rows // tile,), out_shape=jax.ShapeDt...  4.94 us
  transfers between devices with their start and end apart: 33, of which 21 were waited for; matrix products, arithmetic and copies ran while one was open for 0% of the time, Pallas kernels for 20%

profile of v9, /device:TPU:0, one launch (start us, length us, event | category | flops | bytes accessed | tf_op | source)
XLA Modules:
  0.0 189.8 jit_solution(1602702620134604272)
XLA Ops:
  0.6 5.9 %local_states.1 = (f32[512,12]{1,0:T(8,128)S(1)}, bf16[32,64,128]{2,1,0:T(8,128)(2,1)}) custom-call(bf16[512,1536]{1,0:T(8,128)(2,1)} %k_ref.3, bf16[512,1536]{1,0:T(8,128)(2,1)} %v_ref.3, f32[12,512]{1,0:T(8,128)} %bitcast.27), custom_call_target="tpu_custom_call" | custom-call | flops 201326592 | bytes 3145728 | tf_op jit(solution)/shard_map/local_states/pallas_call | solution.py:122
  6.5 8.4 %all-to-all-start = ((bf16[32,64,128]{2,1,0:T(8,128)(2,1)}), bf16[32,64,128]{2,1,0:T(8,128)(2,1)}, u32[]{:S(2)}, u32[]{:S(2)}) async-start(bf16[32,64,128]{2,1,0:T(8,128)(2,1)} %get-tuple-element.76), calls=%async_computation | async-start | bytes 1048576 | tf_op jit(solution)/shard_map/all_to_all | solution.py:820
  14.9 3.2 %route_rows.1 = (bf16[8,6400]{1,0:T(8,128)(2,1)}, bf16[8,6400]{1,0:T(8,128)(2,1)}, bf16[8,6400]{1,0:T(8,128)(2,1)}, bf16[8,6400]{1,0:T(8,128)(2,1)}, f32[16,128]{1,0:T(8,128)S(1)}) custom-call(s32[1]{0:T(128)} %bitcast.me_ref, s32[2,128]{1,0:T(2,128)S(1)} %bitcast.17, bf16[128,6144]{1,0:T(8,128)(2,1)} %res_ref.1, bf16[128,6144]{1,0:T(8,128)(2,1)} %gate_ref.1), custom_call_target="tpu_custom_call" | custom-call | flops 50331648 | bytes 3932160 | tf_op jit(solution)/shard_map/route_rows/pallas_call | solution.py:355
  18.1 7.8 %inside_blocks.1 = (f32[512,1536]{1,0:T(8,128)S(1)}, bf16[512,1536]{1,0:T(8,128)(2,1)}) custom-call(bf16[512,1536]{1,0:T(8,128)(2,1)} %q_ref.1, bf16[512,1536]{1,0:T(8,128)(2,1)} %k_ref.3, bf16[512,1536]{1,0:T(8,128)(2,1)} %v_ref.3, f32[512,12]{1,0:T(8,128)S(1)} %get-tuple-element.77.cum_ref, f32[12,512]{1,0:T(8,128)} %bitcast.28), custom_call_target="tpu_custom_call" | custom-call | flops 1610612736 | bytes 9437184 | tf_op jit(solution)/shard_map/inside_blocks/pallas_call | solution.py:216
  28.5 6.6 %all-to-all-start.1 = ((bf16[32,48,128]{2,1,0:T(8,128)(2,1)}), bf16[32,48,128]{2,1,0:T(8,128)(2,1)S(1)}, u32[]{:S(2)}, u32[]{:S(2)}) async-start(bf16[32,48,128]{2,1,0:T(8,128)(2,1)} %scan_blocks.1), calls=%async_computation.1 | async-start | bytes 786432 | tf_op jit(solution)/shard_map/all_to_all | solution.py:820
  41.8 3.4 %collective-permute-done.1.refs_2_ = bf16[8,6400]{1,0:T(8,128)(2,1)S(1)} collective-permute-done((bf16[8,6400]{1,0:T(8,128)(2,1)}, bf16[8,6400]{1,0:T(8,128)(2,1)S(1)}, u32[]{:S(2)}, u32[]{:S(2)}) %collective-permute-start.1) | collective-permute-done | bytes 102432 | tf_op jit(solution)/shard_map/ppermute | solution.py:825
  46.4 3.5 %place_rows.1 = (f32[64,1536]{1,0:T(8,128)}, bf16[64,1536]{1,0:T(8,128)(2,1)}) custom-call(s32[1]{0:T(128)} %bitcast.me_ref, f32[512,1536]{1,0:T(8,128)S(1)} %get-tuple-element.93.inside_ref, bf16[512,1536]{1,0:T(8,128)(2,1)} %get-tuple-element.94.qs_ref, bf16[8,6400]{1,0:T(8,128)(2,1)} %get-tuple-element.86.refs_0_, bf16[8,6400]{1,0:T(8,128)(2,1)} %copy-done.8, ...), custom_call_target="tpu_custom_call" | custom-call | flops 1000000 | bytes 200000 | tf_op jit(solution)/shard_map/place_rows/pallas_call | solution.py:428
  51.9 4.0 %all-to-all-start.2 = ((bf16[4,16,1536]{2,1,0:T(8,128)(2,1)}), bf16[4,16,1536]{2,1,0:T(8,128)(2,1)}, u32[]{:S(2)}, u32[]{:S(2)}) async-start(bf16[4,16,1536]{2,1,0:T(8,128)(2,1)} %bitcast.24), calls=%async_computation.2 | async-start | bytes 393216 | tf_op jit(solution)/shard_map/all_to_all | solution.py:820
  55.9 4.3 %carried_blocks.1 = (bf16[128,1536]{1,0:T(8,128)(2,1)}, bf16[128,1536]{1,0:T(8,128)(2,1)}, bf16[128,1536]{1,0:T(8,128)(2,1)}, bf16[128,1536]{1,0:T(8,128)(2,1)}) custom-call(s32[1]{0:T(128)} %bitcast.me_ref, f32[512,1536]{1,0:T(8,128)S(1)} %get-tuple-element.93.inside_ref, bf16[512,1536]{1,0:T(8,128)(2,1)} %get-tuple-element.94.qs_ref, ...), custom_call_target="tpu_custom_call" | custom-call | flops 402653184 | bytes 6291456 | tf_op jit(solution)/shard_map/carried_blocks/pallas_call | solution.py:284
  66.1 4.4 %all-to-all-start.3 = ((bf16[4,16,2560]{2,1,0:T(8,128)(2,1)}), bf16[4,16,2560]{2,1,0:T(8,128)(2,1)S(1)}, u32[]{:S(2)}, u32[]{:S(2)}) async-start(bf16[4,16,2560]{2,1,0:T(8,128)(2,1)} %get-tuple-element.103), calls=%async_computation.3 | async-start | bytes 655360 | tf_op jit(solution)/shard_map/all_to_all | solution.py:820
  82.1 4.9 %all-to-all-start.4 = ((bf16[4,4,16,3584]{3,2,1,0:T(8,128)(2,1)}), bf16[4,4,16,3584]{3,2,1,0:T(8,128)(2,1)S(1)}, u32[]{:S(2)}, u32[]{:S(2)}) async-start(bf16[4,4,16,3584]{3,2,1,0:T(8,128)(2,1)} %repeat.1), calls=%async_computation.4 | async-start | bytes 3670016 | tf_op jit(solution)/shard_map/all_to_all | solution.py:820
  97.8 3.4 %collective-permute-done.7.refs_1_ = bf16[4,16,2560]{2,1,0:T(8,128)(2,1)S(1)} collective-permute-done((bf16[4,16,2560]{2,1,0:T(8,128)(2,1)S(1)}, bf16[4,16,2560]{2,1,0:T(8,128)(2,1)S(1)}, u32[]{:S(2)}, u32[]{:S(2)}) %collective-permute-start.7) | collective-permute-done | bytes 327712 | tf_op jit(solution)/shard_map/ppermute | solution.py:825
  101.2 3.5 %collective-permute-done.8.refs_2_ = bf16[4,16,2560]{2,1,0:T(8,128)(2,1)S(1)} collective-permute-done((bf16[4,16,2560]{2,1,0:T(8,128)(2,1)S(1)}, bf16[4,16,2560]{2,1,0:T(8,128)(2,1)S(1)}, u32[]{:S(2)}, u32[]{:S(2)}) %collective-permute-start.8) | collective-permute-done | bytes 327712 | tf_op jit(solution)/shard_map/ppermute | solution.py:825
  108.6 4.5 %first_act.1 = (bf16[256,288]{1,0:T(8,128)(2,1)S(1)}, bf16[2,288,6144]{2,1,0:T(8,128)(2,1)S(1)}) custom-call(bf16[288,6144]{1,0:T(8,128)(2,1)} %bitcast.22, bf16[288,6144]{1,0:T(8,128)(2,1)} %bitcast.23, bf16[4,4,16,3584]{3,2,1,0:T(8,128)(2,1)S(1)} %all-to-all-done.4.one_ref, bf16[4,16,2560]{2,1,0:T(8,128)(2,1)S(1)} %all-to-all-done.3.refs_0_, ...), custom_call_target="tpu_custom_call" | custom-call | flops 1811939328 | bytes 10223616 | tf_op jit(solution)/shard_map/first_act/pallas_call | solution.py:597
  120.6 3.7 %collective-permute-done.17.refs_0_ = bf16[4,4,16,4096]{3,2,1,0:T(8,128)(2,1)S(1)} collective-permute-done((bf16[4,4,16,4096]{3,2,1,0:T(8,128)(2,1)S(1)}, bf16[4,4,16,4096]{3,2,1,0:T(8,128)(2,1)S(1)}, u32[]{:S(2)}, u32[]{:S(2)}) %collective-permute-start.17) | collective-permute-done | bytes 2097184 | tf_op jit(solution)/shard_map/ppermute | solution.py:825
  124.3 3.7 %expert_down.6 = bf16[4,4,16,4096]{3,2,1,0:T(8,128)(2,1)} custom-call(bf16[256,288]{1,0:T(8,128)(2,1)S(1)} %get-tuple-element.135.act_ref, bf16[288,6144]{1,0:T(8,128)(2,1)} %bitcast.20, bf16[4,4,16,4096]{3,2,1,0:T(8,128)(2,1)S(1)} %collective-permute-done.17.refs_0_), custom_call_target="tpu_custom_call" | custom-call | flops 603979776 | bytes 4456448 | tf_op jit(solution)/shard_map/expert_down/pallas_call | solution.py:707
  128.0 3.6 %all-to-all-start.5 = ((bf16[4,4,16,4096]{3,2,1,0:T(8,128)(2,1)}), bf16[4,4,16,4096]{3,2,1,0:T(8,128)(2,1)S(1)}, u32[]{:S(2)}, u32[]{:S(2)}) async-start(bf16[4,4,16,4096]{3,2,1,0:T(8,128)(2,1)} %expert_down.6), calls=%async_computation.5 | async-start | bytes 4194304 | tf_op jit(solution)/shard_map/all_to_all | solution.py:820
  138.5 10.6 %collective-permute-done.19.refs_1_ = bf16[4,16,2048]{2,1,0:T(8,128)(2,1)S(1)} collective-permute-done((bf16[4,16,2048]{2,1,0:T(8,128)(2,1)}, bf16[4,16,2048]{2,1,0:T(8,128)(2,1)S(1)}, u32[]{:S(2)}, u32[]{:S(2)}) %collective-permute-start.19) | collective-permute-done | bytes 262176 | tf_op jit(solution)/shard_map/ppermute | solution.py:825
  149.1 3.6 %collective-permute-done.21.refs_3_ = bf16[4,16,2048]{2,1,0:T(8,128)(2,1)S(1)} collective-permute-done((bf16[4,16,2048]{2,1,0:T(8,128)(2,1)}, bf16[4,16,2048]{2,1,0:T(8,128)(2,1)S(1)}, u32[]{:S(2)}, u32[]{:S(2)}) %collective-permute-start.21) | collective-permute-done | bytes 262176 | tf_op jit(solution)/shard_map/ppermute | solution.py:825
  152.6 6.2 %all-to-all-done.5.in_ref = bf16[4,4,16,4096]{3,2,1,0:T(8,128)(2,1)S(1)} async-done(((bf16[4,4,16,4096]{3,2,1,0:T(8,128)(2,1)}), bf16[4,4,16,4096]{3,2,1,0:T(8,128)(2,1)S(1)}, u32[]{:S(2)}, u32[]{:S(2)}) %all-to-all-start.5) | async-done | bytes 2097184 | tf_op jit(solution)/shard_map/all_to_all | solution.py:820
  160.5 3.4 %all-to-all-start.6 = ((bf16[4,16,2048]{2,1,0:T(8,128)(2,1)}), bf16[4,16,2048]{2,1,0:T(8,128)(2,1)S(1)}, u32[]{:S(2)}, u32[]{:S(2)}) async-start(bf16[4,16,2048]{2,1,0:T(8,128)(2,1)} %stack_sum.1), calls=%async_computation.6 | async-start | bytes 524288 | tf_op jit(solution)/shard_map/all_to_all | solution.py:820
  168.9 4.2 %collective-permute-done.22.refs_1_ = bf16[16,4096]{1,0:T(8,128)(2,1)S(1)} collective-permute-done((bf16[16,4096]{1,0:T(8,128)(2,1)}, bf16[16,4096]{1,0:T(8,128)(2,1)S(1)}, u32[]{:S(2)}, u32[]{:S(2)}) %collective-permute-start.22) | collective-permute-done | bytes 131104 | tf_op jit(solution)/shard_map/ppermute | solution.py:825
  178.4 3.4 %all-to-all-start.7 = ((bf16[4,4,6144]{2,1,0:T(4,128)(2,1)}), bf16[4,4,6144]{2,1,0:T(4,128)(2,1)S(1)}, u32[]{:S(2)}, u32[]{:S(2)}) async-start(bf16[4,4,6144]{2,1,0:T(4,128)(2,1)} %row_sum.1), calls=%async_computation.7 | async-start | bytes 393216 | tf_op jit(solution)/shard_map/all_to_all | solution.py:820
  183.0 4.9 %hidden_rows.1 = bf16[128,6144]{1,0:T(8,128)(2,1)} custom-call(s32[1]{0:T(128)} %bitcast.me_ref, bf16[128,6144]{1,0:T(8,128)(2,1)} %res_ref.1, bf16[128,6144]{1,0:T(8,128)(2,1)} %gate_ref.1, f32[1,6144]{1,0:T(1,128)} %bitcast.26, bf16[128,1536]{1,0:T(8,128)(2,1)S(1)} %copy-done, bf16[128,1536]{1,0:T(8,128)(2,1)S(1)} %copy-done.4, ...), custom_call_target="tpu_custom_call" | custom-call | flops 15728640 | bytes 6291456 | tf_op jit(solution)/shard_map/hidden_rows/pallas_call | solution.py:498
  (90 shorter events, 73.9 us)
Async XLA Ops:
  6.5 20.1 %all-to-all-start = ((bf16[32,64,128]{2,1,0:T(8,128)(2,1)}), bf16[32,64,128]{2,1,0:T(8,128)(2,1)}, u32[]{:S(2)}, u32[]{:S(2)}) async-start(bf16[32,64,128]{2,1,0:T(8,128)(2,1)} %get-tuple-element.76), calls=%async_computation | async-start | bytes 1048576 | tf_op jit(solution)/shard_map/all_to_all | solution.py:820
  28.5 21.4 %all-to-all-start.1 = ((bf16[32,48,128]{2,1,0:T(8,128)(2,1)}), bf16[32,48,128]{2,1,0:T(8,128)(2,1)S(1)}, u32[]{:S(2)}, u32[]{:S(2)}) async-start(bf16[32,48,128]{2,1,0:T(8,128)(2,1)} %scan_blocks.1), calls=%async_computation.1 | async-start | bytes 786432 | tf_op jit(solution)/shard_map/all_to_all | solution.py:820
  36.8 8.3 %collective-permute-start.1 = (bf16[8,6400]{1,0:T(8,128)(2,1)}, bf16[8,6400]{1,0:T(8,128)(2,1)S(1)}, u32[]{:S(2)}, u32[]{:S(2)}) collective-permute-start(bf16[8,6400]{1,0:T(8,128)(2,1)} %get-tuple-element.88), channel_id=1, source_target_pairs={{0,2},{1,3},{2,0},{3,1},{4,6},{5,7},{6,4},{7,5},{8,10},{9,11},{10,... | collective-permute-start | bytes 307208 | tf_op jit(solution)/shard_map/ppermute | solution.py:825
  51.9 10.4 %all-to-all-start.2 = ((bf16[4,16,1536]{2,1,0:T(8,128)(2,1)}), bf16[4,16,1536]{2,1,0:T(8,128)(2,1)}, u32[]{:S(2)}, u32[]{:S(2)}) async-start(bf16[4,16,1536]{2,1,0:T(8,128)(2,1)} %bitcast.24), calls=%async_computation.2 | async-start | bytes 393216 | tf_op jit(solution)/shard_map/all_to_all | solution.py:820
  62.3 17.4 %collective-permute-start.6 = (bf16[128,1536]{1,0:T(8,128)(2,1)}, bf16[128,1536]{1,0:T(8,128)(2,1)S(1)}, u32[]{:S(2)}, u32[]{:S(2)}) collective-permute-start(bf16[128,1536]{1,0:T(8,128)(2,1)} %get-tuple-element.104), channel_id=1, source_target_pairs={{0,2},{1,3},{2,0},{3,1},{4,6},{5,7},{6,4},{7,5},{8,10},{9,11},{10,... | collective-permute-start | bytes 1179656 | tf_op jit(solution)/shard_map/ppermute | solution.py:825
  66.1 13.6 %all-to-all-start.3 = ((bf16[4,16,2560]{2,1,0:T(8,128)(2,1)}), bf16[4,16,2560]{2,1,0:T(8,128)(2,1)S(1)}, u32[]{:S(2)}, u32[]{:S(2)}) async-start(bf16[4,16,2560]{2,1,0:T(8,128)(2,1)} %get-tuple-element.103), calls=%async_computation.3 | async-start | bytes 655360 | tf_op jit(solution)/shard_map/all_to_all | solution.py:820
  70.5 7.1 %collective-permute-start.3 = (bf16[16,3584]{1,0:T(8,128)(2,1)}, bf16[16,3584]{1,0:T(8,128)(2,1)S(1)}, u32[]{:S(2)}, u32[]{:S(2)}) collective-permute-start(bf16[16,3584]{1,0:T(8,128)(2,1)} %get-tuple-element.105.refs_0_), channel_id=1, source_target_pairs={{0,8},{8,16},{16,24},{24,0},{1,9},{9,17},{17,25},{25,1},{2,10},{10... | collective-permute-start | bytes 344072 | tf_op jit(solution)/shard_map/ppermute | solution.py:825
  72.0 6.9 %collective-permute-start.4 = (bf16[16,3584]{1,0:T(8,128)(2,1)}, bf16[16,3584]{1,0:T(8,128)(2,1)S(1)}, u32[]{:S(2)}, u32[]{:S(2)}) collective-permute-start(bf16[16,3584]{1,0:T(8,128)(2,1)} %get-tuple-element.105.refs_0_), channel_id=1, source_target_pairs={{0,16},{8,24},{16,0},{24,8},{1,17},{9,25},{17,1},{25,9},{2,18},{10... | collective-permute-start | bytes 344072 | tf_op jit(solution)/shard_map/ppermute | solution.py:825
  82.1 25.4 %all-to-all-start.4 = ((bf16[4,4,16,3584]{3,2,1,0:T(8,128)(2,1)}), bf16[4,4,16,3584]{3,2,1,0:T(8,128)(2,1)S(1)}, u32[]{:S(2)}, u32[]{:S(2)}) async-start(bf16[4,4,16,3584]{3,2,1,0:T(8,128)(2,1)} %repeat.1), calls=%async_computation.4 | async-start | bytes 3670016 | tf_op jit(solution)/shard_map/all_to_all | solution.py:820
  87.1 9.2 %collective-permute-start.10 = (bf16[128,1536]{1,0:T(8,128)(2,1)}, bf16[128,1536]{1,0:T(8,128)(2,1)S(1)}, u32[]{:S(2)}, u32[]{:S(2)}) collective-permute-start(bf16[128,1536]{1,0:T(8,128)(2,1)} %get-tuple-element.110), channel_id=1, source_target_pairs={{0,1},{1,2},{2,3},{3,0},{4,5},{5,6},{6,7},{7,4},{8,9},{9,10},{10,1... | collective-permute-start | bytes 1179656 | tf_op jit(solution)/shard_map/ppermute | solution.py:825
  87.7 9.3 %collective-permute-start.11 = (bf16[128,1536]{1,0:T(8,128)(2,1)S(1)}, bf16[128,1536]{1,0:T(8,128)(2,1)S(1)}, u32[]{:S(2)}, u32[]{:S(2)}) collective-permute-start(bf16[128,1536]{1,0:T(8,128)(2,1)S(1)} %copy-done.12), channel_id=1, source_target_pairs={{0,3},{1,0},{2,1},{3,2},{4,7},{5,4},{6,5},{7,6},{8,11},{9,8},{10,9... | collective-permute-start | bytes 1179656 | tf_op jit(solution)/shard_map/ppermute | solution.py:825
  90.3 10.9 %collective-permute-start.7 = (bf16[4,16,2560]{2,1,0:T(8,128)(2,1)S(1)}, bf16[4,16,2560]{2,1,0:T(8,128)(2,1)S(1)}, u32[]{:S(2)}, u32[]{:S(2)}) collective-permute-start(bf16[4,16,2560]{2,1,0:T(8,128)(2,1)S(1)} %all-to-all-done.3.refs_0_), channel_id=1, source_target_pairs={{0,8},{8,16},{16,24},{24,0},{1,9},{9,17},{17,25},{25,1},{2,10},{10... | collective-permute-start | bytes 983048 | tf_op jit(solution)/shard_map/ppermute | solution.py:825
  91.5 13.2 %collective-permute-start.8 = (bf16[4,16,2560]{2,1,0:T(8,128)(2,1)S(1)}, bf16[4,16,2560]{2,1,0:T(8,128)(2,1)S(1)}, u32[]{:S(2)}, u32[]{:S(2)}) collective-permute-start(bf16[4,16,2560]{2,1,0:T(8,128)(2,1)S(1)} %all-to-all-done.3.refs_0_), channel_id=1, source_target_pairs={{0,16},{8,24},{16,0},{24,8},{1,17},{9,25},{17,1},{25,9},{2,18},{10... | collective-permute-start | bytes 983048 | tf_op jit(solution)/shard_map/ppermute | solution.py:825
  94.4 10.3 %collective-permute-start.9 = (bf16[4,16,2560]{2,1,0:T(8,128)(2,1)S(1)}, bf16[4,16,2560]{2,1,0:T(8,128)(2,1)S(1)}, u32[]{:S(2)}, u32[]{:S(2)}) collective-permute-start(bf16[4,16,2560]{2,1,0:T(8,128)(2,1)S(1)} %all-to-all-done.3.refs_0_), channel_id=1, source_target_pairs={{0,24},{8,0},{16,8},{24,16},{1,25},{9,1},{17,9},{25,17},{2,26},{10... | collective-permute-start | bytes 983048 | tf_op jit(solution)/shard_map/ppermute | solution.py:825
  120.5 7.5 %collective-permute-start.18 = (bf16[4,4,16,2048]{3,2,1,0:T(8,128)(2,1)S(1)}, bf16[4,4,16,2048]{3,2,1,0:T(8,128)(2,1)S(1)}, u32[]{:S(2)}, u32[]{:S(2)}) collective-permute-start(bf16[4,4,16,2048]{3,2,1,0:T(8,128)(2,1)S(1)} %expert_down.5), channel_id=1, source_target_pairs={{0,4},{4,0},{1,5},{5,1},{2,6},{6,2},{3,7},{7,3},{8,12},{12,8},{9,1... | collective-permute-start | bytes 3145736 | tf_op jit(solution)/shard_map/ppermute | solution.py:825
  128.0 30.7 %all-to-all-start.5 = ((bf16[4,4,16,4096]{3,2,1,0:T(8,128)(2,1)}), bf16[4,4,16,4096]{3,2,1,0:T(8,128)(2,1)S(1)}, u32[]{:S(2)}, u32[]{:S(2)}) async-start(bf16[4,4,16,4096]{3,2,1,0:T(8,128)(2,1)} %expert_down.6), calls=%async_computation.5 | async-start | bytes 4194304 | tf_op jit(solution)/shard_map/all_to_all | solution.py:820
  134.6 14.5 %collective-permute-start.19 = (bf16[4,16,2048]{2,1,0:T(8,128)(2,1)}, bf16[4,16,2048]{2,1,0:T(8,128)(2,1)S(1)}, u32[]{:S(2)}, u32[]{:S(2)}) collective-permute-start(bf16[4,16,2048]{2,1,0:T(8,128)(2,1)} %get-tuple-element.138), channel_id=1, source_target_pairs={{0,24},{8,0},{16,8},{24,16},{1,25},{9,1},{17,9},{25,17},{2,26},{10... | collective-permute-start | bytes 786440 | tf_op jit(solution)/shard_map/ppermute | solution.py:825
  137.0 12.1 %collective-permute-start.20 = (bf16[4,16,2048]{2,1,0:T(8,128)(2,1)}, bf16[4,16,2048]{2,1,0:T(8,128)(2,1)S(1)}, u32[]{:S(2)}, u32[]{:S(2)}) collective-permute-start(bf16[4,16,2048]{2,1,0:T(8,128)(2,1)} %get-tuple-element.139), channel_id=1, source_target_pairs={{0,16},{8,24},{16,0},{24,8},{1,17},{9,25},{17,1},{25,9},{2,18},{10... | collective-permute-start | bytes 786440 | tf_op jit(solution)/shard_map/ppermute | solution.py:825
  137.9 14.7 %collective-permute-start.21 = (bf16[4,16,2048]{2,1,0:T(8,128)(2,1)}, bf16[4,16,2048]{2,1,0:T(8,128)(2,1)S(1)}, u32[]{:S(2)}, u32[]{:S(2)}) collective-permute-start(bf16[4,16,2048]{2,1,0:T(8,128)(2,1)} %get-tuple-element.140), channel_id=1, source_target_pairs={{0,8},{8,16},{16,24},{24,0},{1,9},{9,17},{17,25},{25,1},{2,10},{10... | collective-permute-start | bytes 786440 | tf_op jit(solution)/shard_map/ppermute | solution.py:825
  160.5 16.1 %all-to-all-start.6 = ((bf16[4,16,2048]{2,1,0:T(8,128)(2,1)}), bf16[4,16,2048]{2,1,0:T(8,128)(2,1)S(1)}, u32[]{:S(2)}, u32[]{:S(2)}) async-start(bf16[4,16,2048]{2,1,0:T(8,128)(2,1)} %stack_sum.1), calls=%async_computation.6 | async-start | bytes 524288 | tf_op jit(solution)/shard_map/all_to_all | solution.py:820
  165.1 8.0 %collective-permute-start.22 = (bf16[16,4096]{1,0:T(8,128)(2,1)}, bf16[16,4096]{1,0:T(8,128)(2,1)S(1)}, u32[]{:S(2)}, u32[]{:S(2)}) collective-permute-start(bf16[16,4096]{1,0:T(8,128)(2,1)} %get-tuple-element.147), channel_id=1, source_target_pairs={{0,24},{8,0},{16,8},{24,16},{1,25},{9,1},{17,9},{25,17},{2,26},{10... | collective-permute-start | bytes 393224 | tf_op jit(solution)/shard_map/ppermute | solution.py:825
  167.5 7.8 %collective-permute-start.23 = (bf16[16,4096]{1,0:T(8,128)(2,1)}, bf16[16,4096]{1,0:T(8,128)(2,1)S(1)}, u32[]{:S(2)}, u32[]{:S(2)}) collective-permute-start(bf16[16,4096]{1,0:T(8,128)(2,1)} %get-tuple-element.148), channel_id=1, source_target_pairs={{0,16},{8,24},{16,0},{24,8},{1,17},{9,25},{17,1},{25,9},{2,18},{10... | collective-permute-start | bytes 393224 | tf_op jit(solution)/shard_map/ppermute | solution.py:825
  168.4 8.3 %collective-permute-start.24 = (bf16[16,4096]{1,0:T(8,128)(2,1)}, bf16[16,4096]{1,0:T(8,128)(2,1)S(1)}, u32[]{:S(2)}, u32[]{:S(2)}) collective-permute-start(bf16[16,4096]{1,0:T(8,128)(2,1)} %get-tuple-element.149), channel_id=1, source_target_pairs={{0,8},{8,16},{16,24},{24,0},{1,9},{9,17},{17,25},{25,1},{2,10},{10... | collective-permute-start | bytes 393224 | tf_op jit(solution)/shard_map/ppermute | solution.py:825
  178.4 9.7 %all-to-all-start.7 = ((bf16[4,4,6144]{2,1,0:T(4,128)(2,1)}), bf16[4,4,6144]{2,1,0:T(4,128)(2,1)S(1)}, u32[]{:S(2)}, u32[]{:S(2)}) async-start(bf16[4,4,6144]{2,1,0:T(4,128)(2,1)} %row_sum.1), calls=%async_computation.7 | async-start | bytes 393216 | tf_op jit(solution)/shard_map/all_to_all | solution.py:820
  (22 other events, 148.6 us)

commit v10 on v9

--- a/solution.py
+++ b/solution.py
@@ -66,72 +66,94 @@
     return total
 
 
-def state_kernel(group, k_ref, v_ref, ld_ref, cum_ref, msg_ref, fade_ref, decay_ref):
+def state_kernel(
+    group, k_hbm, v_hbm, ld_ref, cum_ref, out_hbm, k_ref, v_ref, msg_ref, arrive, leave
+):
     heads, rows = ld_ref.shape
     per = heads * HEAD_DIM // 32
     parts = group * HEAD_DIM // per
-    g = pl.program_id(0)
-
-    @pl.when(g == 0)
-    def _():
-        cum = running_sum(ld_ref[...], 0)
-        cum_ref[...] = cum
-        final = cum[rows - 1 : rows, :]
-        fade_ref[...] = jnp.exp(final - cum)
-        decay_ref[...] = jnp.broadcast_to(jnp.exp(final), decay_ref.shape)
-
-    fade = spread(fade_ref[...], g * group, group, 2)
-    decay = spread(decay_ref[...], g * group, group, 2)
+    wide = group * HEAD_DIM
+    arriving = []
+    for g in range(heads // group):
+        cols = pl.ds(g * wide, wide)
+        for n, (a, b) in enumerate(((k_hbm, k_ref), (v_hbm, v_ref))):
+            arriving.append(pltpu.make_async_copy(a.at[:, cols], b.at[:, cols], arrive.at[g, n]))
+    for c in arriving:
+        c.start()
+    cum = running_sum(ld_ref[...], 0)
+    cum_ref[...] = cum
+    final = cum[rows - 1 : rows, :]
+    fades = jnp.exp(final - cum)
+    decays = jnp.broadcast_to(jnp.exp(final), (16, heads))
     row16 = iota((16, HEAD_DIM), 0)
-    tiles = []
-    for j in range(group):
-        cols = slice(j * HEAD_DIM, (j + 1) * HEAD_DIM)
-        wk = (k_ref[:, cols].astype(F32) * fade[:, cols]).astype(BF16)
-        state = lax.dot_general(
-            wk, v_ref[:, cols], (((0,), (0,)), ((), ())), preferred_element_type=F32
-        ).astype(BF16)
-        row = j * HEAD_DIM
-        while row < (j + 1) * HEAD_DIM:
-            part, at = row // per, row % per
-            take = min(per - at, (j + 1) * HEAD_DIM - row)
-            lo = row - j * HEAD_DIM
-            msg_ref[part, at : at + take, :] = state[lo : lo + take, :]
-            row += take
-        whole = decay[:, cols]
-        high = whole.astype(BF16).astype(F32)
-        tiles.append((high, whole - high))
-    for part in range(parts):
-        first = per * part // HEAD_DIM
-        last = (per * part + per - 1) // HEAD_DIM
-        tile = jnp.where(
-            row16 == 0,
-            tiles[first][0],
-            jnp.where(
-                row16 == 1, tiles[first][1], jnp.where(row16 == 2, tiles[last][0], tiles[last][1])
-            ),
-        )
-        msg_ref[part, per : per + 16, :] = tile.astype(BF16)
+    leaving = []
+    for g in range(heads // group):
+        fade = spread(fades, g * group, group, 2)
+        decay = spread(decays, g * group, group, 2)
+        arriving[2 * g].wait()
+        arriving[2 * g + 1].wait()
+        tiles = []
+        for j in range(group):
+            cols = slice(j * HEAD_DIM, (j + 1) * HEAD_DIM)
+            here = slice((g * group + j) * HEAD_DIM, (g * group + j + 1) * HEAD_DIM)
+            wk = (k_ref[:, here].astype(F32) * fade[:, cols]).astype(BF16)
+            state = lax.dot_general(
+                wk, v_ref[:, here], (((0,), (0,)), ((), ())), preferred_element_type=F32
+            ).astype(BF16)
+            row = (g * group + j) * HEAD_DIM
+            end = row + HEAD_DIM
+            lo = 0
+            while row < end:
+                part, at = row // per, row % per
+                take = min(per - at, end - row)
+                msg_ref[part, at : at + take, :] = state[lo : lo + take, :]
+                row += take
+                lo += take
+            whole = decay[:, cols]
+            high = whole.astype(BF16).astype(F32)
+            tiles.append((high, whole - high))
+        for part in range(parts):
+            first = per * part // HEAD_DIM
+            last = (per * part + per - 1) // HEAD_DIM
+            tile = jnp.where(
+                row16 == 0,
+                tiles[first][0],
+                jnp.where(
+                    row16 == 1,
+                    tiles[first][1],
+                    jnp.where(row16 == 2, tiles[last][0], tiles[last][1]),
+                ),
+            )
+            msg_ref[g * parts + part, per : per + 16, :] = tile.astype(BF16)
+        at = pl.ds(g * parts, parts)
+        leaving.append(pltpu.make_async_copy(msg_ref.at[at], out_hbm.at[at], leave.at[g]))
+        leaving[-1].start()
+    for c in leaving:
+        c.wait()
 
 
 def local_states(k, v, ld, group=3):
     rows, width = k.shape
     heads = ld.shape[0]
     per = heads * HEAD_DIM // 32
-    parts = group * HEAD_DIM // per
-    block = pl.BlockSpec((rows, group * HEAD_DIM), lambda g: (0, g))
+    whole = pl.BlockSpec(memory_space=pltpu.VMEM)
+    away = pl.BlockSpec(memory_space=pl.ANY)
+    steps = heads // group
     return pl.pallas_call(
         functools.partial(state_kernel, group),
-        grid=(heads // group,),
         out_shape=(
             jax.ShapeDtypeStruct((rows, heads), F32),
             far((32, per + 16, HEAD_DIM)),
         ),
-        in_specs=[block, block, pl.BlockSpec((heads, rows), lambda g: (0, 0))],
-        out_specs=(
-            pl.BlockSpec((rows, heads), lambda g: (0, 0)),
-            pl.BlockSpec((parts, per + 16, HEAD_DIM), lambda g: (g, 0, 0)),
-        ),
-        scratch_shapes=[pltpu.VMEM((rows, heads), F32), pltpu.VMEM((16, heads), F32)],
+        in_specs=[away, away, whole],
+        out_specs=(whole, away),
+        scratch_shapes=[
+            pltpu.VMEM((rows, width), BF16),
+            pltpu.VMEM((rows, width), BF16),
+            pltpu.VMEM((32, per + 16, HEAD_DIM), BF16),
+            pltpu.SemaphoreType.DMA((steps, 2)),
+            pltpu.SemaphoreType.DMA((steps,)),
+        ],
         compiler_params=params(),
         cost_estimate=cost(2 * rows * width * HEAD_DIM, 4 * rows * width),
         name="local_states",
@@ -470,7 +492,7 @@
 def routed_norm(me, att, pieces, attn_gain, moe_gain, copies):
     sources, rows, part = att.shape
     width = sources * part
-    cut = width * 7 // 12
+    cut = width // 2
     whole = pl.BlockSpec(memory_space=pltpu.VMEM)
     return pl.pallas_call(
         routed_norm_kernel,
@@ -532,7 +554,8 @@
     return pl.pallas_call(
         repeat_kernel,
         out_shape=far((copies, count, rows, width)),
-        in_specs=[pl.BlockSpec(memory_space=pltpu.VMEM)] * count,
+        in_specs=[pl.BlockSpec(memory_space=pl.ANY)]
+        + [pl.BlockSpec(memory_space=pltpu.VMEM)] * (count - 1),
         out_specs=pl.BlockSpec(memory_space=pl.ANY),
         scratch_shapes=[pltpu.SemaphoreType.DMA((copies, count))],
         compiler_params=params(),
@@ -587,7 +610,7 @@
     refs[-1][...] = act_rows(steps, w_ref, one_ref, refs[:-1], lambda s: None)
 
 
-def expert_act(one, twos, weights, steps=12):
+def expert_act(one, twos, weights, steps=6):
     nz, nx, rows, half = one.shape
     count = nz * nx * rows
     whole = pl.BlockSpec(memory_space=pltpu.VMEM)
@@ -883,7 +906,7 @@
     right, left = shift(attention[1], "exp", 1), shift(attention[3], "exp", 3)
     one, twos, right, left = keep((one, twos, right, left))
 
-    cut = moe_gain.shape[1] * 2 // 3
+    cut = moe_gain.shape[1] * 7 // 12
     act_own, weights = expert_act(one, twos, (w_gate, w_up))
     one, twos = shift(one, "core", 1), [shift(a, "core", 1) for a in twos]
     one, twos, weights = keep((one, twos, weights))

time: 191 us -> 198 us (1.037)
  Pallas kernels: 62.5 us -> 73.2 us
  waiting for transfers between devices: 53.3 us -> 50 us
    pallas_call x1, Pallas kernels: 2.4 us -> 13.2 us  [repeat(): pl.pallas_call(repeat_kernel, out_shape=far((copies, count, rows, width))...]
    all_to_all x8, waiting for transfers between devices: 11.8 us -> 3.95 us  [exchange(): return lax.all_to_all(a, axis, split_axis=0, concat_axis=0, tiled=True)]
    ppermute x25, waiting for transfers between devices: 41.5 us -> 46.1 us  [shift(): return lax.ppermute(a, axis, [(i, (i + by) % n) for i in range(n)])]
    all_to_all x8, starting transfers between devices: 38.8 us -> 40.8 us  [exchange(): return lax.all_to_all(a, axis, split_axis=0, concat_axis=0, tiled=True)]
  transfers between devices with their start and end apart: 33 -> 33, of which waited for: 21 -> 20; matrix products, arithmetic and copies ran while one was open for 0% -> 0% of each run, Pallas kernels for 20% -> 19%
where the time goes in v10:
time: 198 us; the launch traced here: 197 us
  Pallas kernels  73.2 us (37%)
  starting transfers between devices  69.7 us (35%)
  waiting for transfers between devices  50 us (25%)
  local copies, waits for them, and re-layouts  3.02 us (2%)
    ppermute x25, waiting for transfers between devices, shift(): return lax.ppermute(a, axis, [(i, (i + by) % n) for i in range(n)])  46.1 us
    all_to_all x8, starting transfers between devices, exchange(): return lax.all_to_all(a, axis, split_axis=0, concat_axis=0, tiled=True)  40.8 us
    ppermute x25, starting transfers between devices, shift(): return lax.ppermute(a, axis, [(i, (i + by) % n) for i in range(n)])  28.9 us
    pallas_call x1, Pallas kernels, repeat(): pl.pallas_call(repeat_kernel, out_shape=far((copies, count, rows, width))...  13.2 us
    pallas_call x4, Pallas kernels, expert_down(): pl.pallas_call(functools.partial(down_kernel, steps, cut if last else 0,...  11.7 us
    pallas_call x1, Pallas kernels, inside_blocks(): pl.pallas_call(functools.partial(inside_kernel, group), grid=(heads // gr...  7.82 us
    pallas_call x1, Pallas kernels, local_states(): pl.pallas_call(functools.partial(state_kernel, group), out_shape=(jax.Sha...  5.73 us
    pallas_call x1, Pallas kernels, hidden_rows(): pl.pallas_call(hidden_kernel, grid=(rows // tile,), out_shape=jax.ShapeDt...  4.96 us
  transfers between devices with their start and end apart: 33, of which 20 were waited for; matrix products, arithmetic and copies ran while one was open for 0% of the time, Pallas kernels for 19%

profile of v10, /device:TPU:0, one launch (start us, length us, event | category | flops | bytes accessed | tf_op | source)
XLA Modules:
  0.0 196.8 jit_solution(2575309985625157400)
XLA Ops:
  0.6 5.7 %local_states.1 = (f32[512,12]{1,0:T(8,128)S(1)}, bf16[32,64,128]{2,1,0:T(8,128)(2,1)}) custom-call(bf16[512,1536]{1,0:T(8,128)(2,1)} %k_ref.1, bf16[512,1536]{1,0:T(8,128)(2,1)} %v_ref.1, f32[12,512]{1,0:T(8,128)} %bitcast.27), custom_call_target="tpu_custom_call" | custom-call | flops 201326592 | bytes 3145728 | tf_op jit(solution)/shard_map/local_states/pallas_call | solution.py:142
  6.4 8.4 %all-to-all-start = ((bf16[32,64,128]{2,1,0:T(8,128)(2,1)}), bf16[32,64,128]{2,1,0:T(8,128)(2,1)}, u32[]{:S(2)}, u32[]{:S(2)}) async-start(bf16[32,64,128]{2,1,0:T(8,128)(2,1)} %get-tuple-element.76), calls=%async_computation | async-start | bytes 1048576 | tf_op jit(solution)/shard_map/all_to_all | solution.py:843
  14.8 3.2 %route_rows.1 = (bf16[8,6400]{1,0:T(8,128)(2,1)}, bf16[8,6400]{1,0:T(8,128)(2,1)}, bf16[8,6400]{1,0:T(8,128)(2,1)}, bf16[8,6400]{1,0:T(8,128)(2,1)}, f32[16,128]{1,0:T(8,128)S(1)}) custom-call(s32[1]{0:T(128)} %bitcast.me_ref, s32[2,128]{1,0:T(2,128)S(1)} %bitcast.17, bf16[128,6144]{1,0:T(8,128)(2,1)} %res_ref.1, bf16[128,6144]{1,0:T(8,128)(2,1)} %gate_ref.1), custom_call_target="tpu_custom_call" | custom-call | flops 50331648 | bytes 3932160 | tf_op jit(solution)/shard_map/route_rows/pallas_call | solution.py:377
  18.0 7.8 %inside_blocks.1 = (f32[512,1536]{1,0:T(8,128)S(1)}, bf16[512,1536]{1,0:T(8,128)(2,1)}) custom-call(bf16[512,1536]{1,0:T(8,128)(2,1)} %q_ref.1, bf16[512,1536]{1,0:T(8,128)(2,1)} %k_ref.1, bf16[512,1536]{1,0:T(8,128)(2,1)} %v_ref.1, f32[512,12]{1,0:T(8,128)S(1)} %get-tuple-element.77.cum_ref, f32[12,512]{1,0:T(8,128)} %bitcast.28), custom_call_target="tpu_custom_call" | custom-call | flops 1610612736 | bytes 9437184 | tf_op jit(solution)/shard_map/inside_blocks/pallas_call | solution.py:238
  28.4 6.6 %all-to-all-start.1 = ((bf16[32,48,128]{2,1,0:T(8,128)(2,1)}), bf16[32,48,128]{2,1,0:T(8,128)(2,1)S(1)}, u32[]{:S(2)}, u32[]{:S(2)}) async-start(bf16[32,48,128]{2,1,0:T(8,128)(2,1)} %scan_blocks.1), calls=%async_computation.1 | async-start | bytes 786432 | tf_op jit(solution)/shard_map/all_to_all | solution.py:843
  41.7 3.4 %collective-permute-done.1.refs_2_ = bf16[8,6400]{1,0:T(8,128)(2,1)S(1)} collective-permute-done((bf16[8,6400]{1,0:T(8,128)(2,1)}, bf16[8,6400]{1,0:T(8,128)(2,1)S(1)}, u32[]{:S(2)}, u32[]{:S(2)}) %collective-permute-start.1) | collective-permute-done | bytes 102432 | tf_op jit(solution)/shard_map/ppermute | solution.py:848
  46.3 3.5 %place_rows.1 = (f32[64,1536]{1,0:T(8,128)}, bf16[64,1536]{1,0:T(8,128)(2,1)}) custom-call(s32[1]{0:T(128)} %bitcast.me_ref, f32[512,1536]{1,0:T(8,128)S(1)} %get-tuple-element.93.inside_ref, bf16[512,1536]{1,0:T(8,128)(2,1)} %get-tuple-element.94.qs_ref, bf16[8,6400]{1,0:T(8,128)(2,1)} %get-tuple-element.86.refs_0_, bf16[8,6400]{1,0:T(8,128)(2,1)} %copy-done.8, ...), custom_call_target="tpu_custom_call" | custom-call | flops 1000000 | bytes 200000 | tf_op jit(solution)/shard_map/place_rows/pallas_call | solution.py:450
  51.8 4.0 %all-to-all-start.2 = ((bf16[4,16,1536]{2,1,0:T(8,128)(2,1)}), bf16[4,16,1536]{2,1,0:T(8,128)(2,1)}, u32[]{:S(2)}, u32[]{:S(2)}) async-start(bf16[4,16,1536]{2,1,0:T(8,128)(2,1)} %bitcast.24), calls=%async_computation.2 | async-start | bytes 393216 | tf_op jit(solution)/shard_map/all_to_all | solution.py:843
  55.8 4.3 %carried_blocks.1 = (bf16[128,1536]{1,0:T(8,128)(2,1)}, bf16[128,1536]{1,0:T(8,128)(2,1)}, bf16[128,1536]{1,0:T(8,128)(2,1)}, bf16[128,1536]{1,0:T(8,128)(2,1)}) custom-call(s32[1]{0:T(128)} %bitcast.me_ref, f32[512,1536]{1,0:T(8,128)S(1)} %get-tuple-element.93.inside_ref, bf16[512,1536]{1,0:T(8,128)(2,1)} %get-tuple-element.94.qs_ref, ...), custom_call_target="tpu_custom_call" | custom-call | flops 402653184 | bytes 6291456 | tf_op jit(solution)/shard_map/carried_blocks/pallas_call | solution.py:306
  66.0 4.5 %all-to-all-start.3 = ((bf16[4,16,3072]{2,1,0:T(8,128)(2,1)}), bf16[4,16,3072]{2,1,0:T(8,128)(2,1)S(1)}, u32[]{:S(2)}, u32[]{:S(2)}) async-start(bf16[4,16,3072]{2,1,0:T(8,128)(2,1)} %get-tuple-element.103), calls=%async_computation.3 | async-start | bytes 786432 | tf_op jit(solution)/shard_map/all_to_all | solution.py:843
  79.4 13.2 %repeat.1 = bf16[4,4,16,3072]{3,2,1,0:T(8,128)(2,1)} custom-call(bf16[16,3072]{1,0:T(8,128)(2,1)} %get-tuple-element.105.refs_0_, bf16[16,3072]{1,0:T(8,128)(2,1)S(1)} %collective-permute-done.3.refs_1_, bf16[16,3072]{1,0:T(8,128)(2,1)S(1)} %collective-permute-done.4.refs_2_, bf16[16,3072]{1,0:T(8,128)(2,1)S(1)} %collective-permute-done.5.refs_3_), custom_call_target="tpu_custom_call" | custom-call | bytes 1966080 | tf_op jit(solution)/shard_map/repeat/pallas_call | solution.py:554
  92.6 4.9 %all-to-all-start.4 = ((bf16[4,4,16,3072]{3,2,1,0:T(8,128)(2,1)}), bf16[4,4,16,3072]{3,2,1,0:T(8,128)(2,1)S(1)}, u32[]{:S(2)}, u32[]{:S(2)}) async-start(bf16[4,4,16,3072]{3,2,1,0:T(8,128)(2,1)} %repeat.1), calls=%async_computation.4 | async-start | bytes 3145728 | tf_op jit(solution)/shard_map/all_to_all | solution.py:843
  108.3 5.5 %collective-permute-done.7.refs_1_ = bf16[4,16,3072]{2,1,0:T(8,128)(2,1)S(1)} collective-permute-done((bf16[4,16,3072]{2,1,0:T(8,128)(2,1)S(1)}, bf16[4,16,3072]{2,1,0:T(8,128)(2,1)S(1)}, u32[]{:S(2)}, u32[]{:S(2)}) %collective-permute-start.7) | collective-permute-done | bytes 393248 | tf_op jit(solution)/shard_map/ppermute | solution.py:848
  113.8 4.2 %collective-permute-done.8.refs_2_ = bf16[4,16,3072]{2,1,0:T(8,128)(2,1)S(1)} collective-permute-done((bf16[4,16,3072]{2,1,0:T(8,128)(2,1)S(1)}, bf16[4,16,3072]{2,1,0:T(8,128)(2,1)S(1)}, u32[]{:S(2)}, u32[]{:S(2)}) %collective-permute-start.8) | collective-permute-done | bytes 393248 | tf_op jit(solution)/shard_map/ppermute | solution.py:848
  119.1 4.2 %first_act.1 = (bf16[256,288]{1,0:T(8,128)(2,1)S(1)}, bf16[2,288,6144]{2,1,0:T(8,128)(2,1)S(1)}) custom-call(bf16[288,6144]{1,0:T(8,128)(2,1)} %bitcast.22, bf16[288,6144]{1,0:T(8,128)(2,1)} %bitcast.23, bf16[4,4,16,3072]{3,2,1,0:T(8,128)(2,1)S(1)} %all-to-all-done.4.one_ref, bf16[4,16,3072]{2,1,0:T(8,128)(2,1)S(1)} %all-to-all-done.3.refs_0_, ...), custom_call_target="tpu_custom_call" | custom-call | flops 1811939328 | bytes 10223616 | tf_op jit(solution)/shard_map/first_act/pallas_call | solution.py:620
  131.4 3.3 %collective-permute-done.17.refs_0_ = bf16[4,4,16,3584]{3,2,1,0:T(8,128)(2,1)S(1)} collective-permute-done((bf16[4,4,16,3584]{3,2,1,0:T(8,128)(2,1)S(1)}, bf16[4,4,16,3584]{3,2,1,0:T(8,128)(2,1)S(1)}, u32[]{:S(2)}, u32[]{:S(2)}) %collective-permute-start.17) | collective-permute-done | bytes 1835040 | tf_op jit(solution)/shard_map/ppermute | solution.py:848
  134.7 3.6 %expert_down.6 = bf16[4,4,16,3584]{3,2,1,0:T(8,128)(2,1)} custom-call(bf16[256,288]{1,0:T(8,128)(2,1)S(1)} %get-tuple-element.135.act_ref, bf16[288,6144]{1,0:T(8,128)(2,1)} %bitcast.20, bf16[4,4,16,3584]{3,2,1,0:T(8,128)(2,1)S(1)} %collective-permute-done.17.refs_0_), custom_call_target="tpu_custom_call" | custom-call | flops 528482304 | bytes 3899392 | tf_op jit(solution)/shard_map/expert_down/pallas_call | solution.py:730
  138.3 4.5 %all-to-all-start.5 = ((bf16[4,4,16,3584]{3,2,1,0:T(8,128)(2,1)}), bf16[4,4,16,3584]{3,2,1,0:T(8,128)(2,1)S(1)}, u32[]{:S(2)}, u32[]{:S(2)}) async-start(bf16[4,4,16,3584]{3,2,1,0:T(8,128)(2,1)} %expert_down.6), calls=%async_computation.5 | async-start | bytes 3670016 | tf_op jit(solution)/shard_map/all_to_all | solution.py:843
  149.8 13.2 %collective-permute-done.19.refs_1_ = bf16[4,16,2560]{2,1,0:T(8,128)(2,1)S(1)} collective-permute-done((bf16[4,16,2560]{2,1,0:T(8,128)(2,1)}, bf16[4,16,2560]{2,1,0:T(8,128)(2,1)S(1)}, u32[]{:S(2)}, u32[]{:S(2)}) %collective-permute-start.19) | collective-permute-done | bytes 327712 | tf_op jit(solution)/shard_map/ppermute | solution.py:848
  163.1 3.6 %collective-permute-done.21.refs_3_ = bf16[4,16,2560]{2,1,0:T(8,128)(2,1)S(1)} collective-permute-done((bf16[4,16,2560]{2,1,0:T(8,128)(2,1)}, bf16[4,16,2560]{2,1,0:T(8,128)(2,1)S(1)}, u32[]{:S(2)}, u32[]{:S(2)}) %collective-permute-start.21) | collective-permute-done | bytes 327712 | tf_op jit(solution)/shard_map/ppermute | solution.py:848
  168.4 4.5 %all-to-all-start.6 = ((bf16[4,16,2560]{2,1,0:T(8,128)(2,1)}), bf16[4,16,2560]{2,1,0:T(8,128)(2,1)S(1)}, u32[]{:S(2)}, u32[]{:S(2)}) async-start(bf16[4,16,2560]{2,1,0:T(8,128)(2,1)} %stack_sum.1), calls=%async_computation.6 | async-start | bytes 655360 | tf_op jit(solution)/shard_map/all_to_all | solution.py:843
  176.7 3.5 %collective-permute-done.22.refs_1_ = bf16[16,3584]{1,0:T(8,128)(2,1)S(1)} collective-permute-done((bf16[16,3584]{1,0:T(8,128)(2,1)}, bf16[16,3584]{1,0:T(8,128)(2,1)S(1)}, u32[]{:S(2)}, u32[]{:S(2)}) %collective-permute-start.22) | collective-permute-done | bytes 114720 | tf_op jit(solution)/shard_map/ppermute | solution.py:848
  185.4 3.4 %all-to-all-start.7 = ((bf16[4,4,6144]{2,1,0:T(4,128)(2,1)}), bf16[4,4,6144]{2,1,0:T(4,128)(2,1)S(1)}, u32[]{:S(2)}, u32[]{:S(2)}) async-start(bf16[4,4,6144]{2,1,0:T(4,128)(2,1)} %row_sum.1), calls=%async_computation.7 | async-start | bytes 393216 | tf_op jit(solution)/shard_map/all_to_all | solution.py:843
  189.0 5.0 %hidden_rows.1 = bf16[128,6144]{1,0:T(8,128)(2,1)} custom-call(s32[1]{0:T(128)} %bitcast.me_ref, bf16[128,6144]{1,0:T(8,128)(2,1)} %res_ref.1, bf16[128,6144]{1,0:T(8,128)(2,1)} %gate_ref.1, f32[1,6144]{1,0:T(1,128)} %bitcast.26, bf16[128,1536]{1,0:T(8,128)(2,1)S(1)} %copy-done, bf16[128,1536]{1,0:T(8,128)(2,1)S(1)} %copy-done.4, ...), custom_call_target="tpu_custom_call" | custom-call | flops 15728640 | bytes 6291456 | tf_op jit(solution)/shard_map/hidden_rows/pallas_call | solution.py:520
  (90 shorter events, 68.0 us)
Async XLA Ops:
  6.4 20.1 %all-to-all-start = ((bf16[32,64,128]{2,1,0:T(8,128)(2,1)}), bf16[32,64,128]{2,1,0:T(8,128)(2,1)}, u32[]{:S(2)}, u32[]{:S(2)}) async-start(bf16[32,64,128]{2,1,0:T(8,128)(2,1)} %get-tuple-element.76), calls=%async_computation | async-start | bytes 1048576 | tf_op jit(solution)/shard_map/all_to_all | solution.py:843
  28.4 21.4 %all-to-all-start.1 = ((bf16[32,48,128]{2,1,0:T(8,128)(2,1)}), bf16[32,48,128]{2,1,0:T(8,128)(2,1)S(1)}, u32[]{:S(2)}, u32[]{:S(2)}) async-start(bf16[32,48,128]{2,1,0:T(8,128)(2,1)} %scan_blocks.1), calls=%async_computation.1 | async-start | bytes 786432 | tf_op jit(solution)/shard_map/all_to_all | solution.py:843
  35.1 6.6 %collective-permute-start = (bf16[8,6400]{1,0:T(8,128)(2,1)}, bf16[8,6400]{1,0:T(8,128)(2,1)S(1)}, u32[]{:S(2)}, u32[]{:S(2)}) collective-permute-start(bf16[8,6400]{1,0:T(8,128)(2,1)} %get-tuple-element.87), channel_id=1, source_target_pairs={{0,1},{1,2},{2,3},{3,0},{4,5},{5,6},{6,7},{7,4},{8,9},{9,10},{10,1... | collective-permute-start | bytes 307208 | tf_op jit(solution)/shard_map/ppermute | solution.py:848
  36.7 8.3 %collective-permute-start.1 = (bf16[8,6400]{1,0:T(8,128)(2,1)}, bf16[8,6400]{1,0:T(8,128)(2,1)S(1)}, u32[]{:S(2)}, u32[]{:S(2)}) collective-permute-start(bf16[8,6400]{1,0:T(8,128)(2,1)} %get-tuple-element.88), channel_id=1, source_target_pairs={{0,2},{1,3},{2,0},{3,1},{4,6},{5,7},{6,4},{7,5},{8,10},{9,11},{10,... | collective-permute-start | bytes 307208 | tf_op jit(solution)/shard_map/ppermute | solution.py:848
  51.8 10.4 %all-to-all-start.2 = ((bf16[4,16,1536]{2,1,0:T(8,128)(2,1)}), bf16[4,16,1536]{2,1,0:T(8,128)(2,1)}, u32[]{:S(2)}, u32[]{:S(2)}) async-start(bf16[4,16,1536]{2,1,0:T(8,128)(2,1)} %bitcast.24), calls=%async_computation.2 | async-start | bytes 393216 | tf_op jit(solution)/shard_map/all_to_all | solution.py:843
  62.2 17.3 %collective-permute-start.6 = (bf16[128,1536]{1,0:T(8,128)(2,1)}, bf16[128,1536]{1,0:T(8,128)(2,1)S(1)}, u32[]{:S(2)}, u32[]{:S(2)}) collective-permute-start(bf16[128,1536]{1,0:T(8,128)(2,1)} %get-tuple-element.104), channel_id=1, source_target_pairs={{0,2},{1,3},{2,0},{3,1},{4,6},{5,7},{6,4},{7,5},{8,10},{9,11},{10,... | collective-permute-start | bytes 1179656 | tf_op jit(solution)/shard_map/ppermute | solution.py:848
  66.0 13.5 %all-to-all-start.3 = ((bf16[4,16,3072]{2,1,0:T(8,128)(2,1)}), bf16[4,16,3072]{2,1,0:T(8,128)(2,1)S(1)}, u32[]{:S(2)}, u32[]{:S(2)}) async-start(bf16[4,16,3072]{2,1,0:T(8,128)(2,1)} %get-tuple-element.103), calls=%async_computation.3 | async-start | bytes 786432 | tf_op jit(solution)/shard_map/all_to_all | solution.py:843
  70.4 6.6 %collective-permute-start.3 = (bf16[16,3072]{1,0:T(8,128)(2,1)}, bf16[16,3072]{1,0:T(8,128)(2,1)S(1)}, u32[]{:S(2)}, u32[]{:S(2)}) collective-permute-start(bf16[16,3072]{1,0:T(8,128)(2,1)} %get-tuple-element.105.refs_0_), channel_id=1, source_target_pairs={{0,8},{8,16},{16,24},{24,0},{1,9},{9,17},{17,25},{25,1},{2,10},{10... | collective-permute-start | bytes 294920 | tf_op jit(solution)/shard_map/ppermute | solution.py:848
  71.9 6.6 %collective-permute-start.4 = (bf16[16,3072]{1,0:T(8,128)(2,1)}, bf16[16,3072]{1,0:T(8,128)(2,1)S(1)}, u32[]{:S(2)}, u32[]{:S(2)}) collective-permute-start(bf16[16,3072]{1,0:T(8,128)(2,1)} %get-tuple-element.105.refs_0_), channel_id=1, source_target_pairs={{0,16},{8,24},{16,0},{24,8},{1,17},{9,25},{17,1},{25,9},{2,18},{10... | collective-permute-start | bytes 294920 | tf_op jit(solution)/shard_map/ppermute | solution.py:848
  92.6 25.4 %all-to-all-start.4 = ((bf16[4,4,16,3072]{3,2,1,0:T(8,128)(2,1)}), bf16[4,4,16,3072]{3,2,1,0:T(8,128)(2,1)S(1)}, u32[]{:S(2)}, u32[]{:S(2)}) async-start(bf16[4,4,16,3072]{3,2,1,0:T(8,128)(2,1)} %repeat.1), calls=%async_computation.4 | async-start | bytes 3145728 | tf_op jit(solution)/shard_map/all_to_all | solution.py:843
  97.6 9.2 %collective-permute-start.10 = (bf16[128,1536]{1,0:T(8,128)(2,1)}, bf16[128,1536]{1,0:T(8,128)(2,1)S(1)}, u32[]{:S(2)}, u32[]{:S(2)}) collective-permute-start(bf16[128,1536]{1,0:T(8,128)(2,1)} %get-tuple-element.110), channel_id=1, source_target_pairs={{0,1},{1,2},{2,3},{3,0},{4,5},{5,6},{6,7},{7,4},{8,9},{9,10},{10,1... | collective-permute-start | bytes 1179656 | tf_op jit(solution)/shard_map/ppermute | solution.py:848
  98.2 9.3 %collective-permute-start.11 = (bf16[128,1536]{1,0:T(8,128)(2,1)S(1)}, bf16[128,1536]{1,0:T(8,128)(2,1)S(1)}, u32[]{:S(2)}, u32[]{:S(2)}) collective-permute-start(bf16[128,1536]{1,0:T(8,128)(2,1)S(1)} %copy-done.12), channel_id=1, source_target_pairs={{0,3},{1,0},{2,1},{3,2},{4,7},{5,4},{6,5},{7,6},{8,11},{9,8},{10,9... | collective-permute-start | bytes 1179656 | tf_op jit(solution)/shard_map/ppermute | solution.py:848
  100.8 13.0 %collective-permute-start.7 = (bf16[4,16,3072]{2,1,0:T(8,128)(2,1)S(1)}, bf16[4,16,3072]{2,1,0:T(8,128)(2,1)S(1)}, u32[]{:S(2)}, u32[]{:S(2)}) collective-permute-start(bf16[4,16,3072]{2,1,0:T(8,128)(2,1)S(1)} %all-to-all-done.3.refs_0_), channel_id=1, source_target_pairs={{0,8},{8,16},{16,24},{24,0},{1,9},{9,17},{17,25},{25,1},{2,10},{10... | collective-permute-start | bytes 1179656 | tf_op jit(solution)/shard_map/ppermute | solution.py:848
  101.8 16.2 %collective-permute-start.8 = (bf16[4,16,3072]{2,1,0:T(8,128)(2,1)S(1)}, bf16[4,16,3072]{2,1,0:T(8,128)(2,1)S(1)}, u32[]{:S(2)}, u32[]{:S(2)}) collective-permute-start(bf16[4,16,3072]{2,1,0:T(8,128)(2,1)S(1)} %all-to-all-done.3.refs_0_), channel_id=1, source_target_pairs={{0,16},{8,24},{16,0},{24,8},{1,17},{9,25},{17,1},{25,9},{2,18},{10... | collective-permute-start | bytes 1179656 | tf_op jit(solution)/shard_map/ppermute | solution.py:848
  104.9 13.1 %collective-permute-start.9 = (bf16[4,16,3072]{2,1,0:T(8,128)(2,1)S(1)}, bf16[4,16,3072]{2,1,0:T(8,128)(2,1)S(1)}, u32[]{:S(2)}, u32[]{:S(2)}) collective-permute-start(bf16[4,16,3072]{2,1,0:T(8,128)(2,1)S(1)} %all-to-all-done.3.refs_0_), channel_id=1, source_target_pairs={{0,24},{8,0},{16,8},{24,16},{1,25},{9,1},{17,9},{25,17},{2,26},{10... | collective-permute-start | bytes 1179656 | tf_op jit(solution)/shard_map/ppermute | solution.py:848
  131.0 7.3 %collective-permute-start.18 = (bf16[4,4,16,2560]{3,2,1,0:T(8,128)(2,1)S(1)}, bf16[4,4,16,2560]{3,2,1,0:T(8,128)(2,1)S(1)}, u32[]{:S(2)}, u32[]{:S(2)}) collective-permute-start(bf16[4,4,16,2560]{3,2,1,0:T(8,128)(2,1)S(1)} %expert_down.5), channel_id=1, source_target_pairs={{0,4},{4,0},{1,5},{5,1},{2,6},{6,2},{3,7},{7,3},{8,12},{12,8},{9,1... | collective-permute-start | bytes 3932168 | tf_op jit(solution)/shard_map/ppermute | solution.py:848
  138.3 28.4 %all-to-all-start.5 = ((bf16[4,4,16,3584]{3,2,1,0:T(8,128)(2,1)}), bf16[4,4,16,3584]{3,2,1,0:T(8,128)(2,1)S(1)}, u32[]{:S(2)}, u32[]{:S(2)}) async-start(bf16[4,4,16,3584]{3,2,1,0:T(8,128)(2,1)} %expert_down.6), calls=%async_computation.5 | async-start | bytes 3670016 | tf_op jit(solution)/shard_map/all_to_all | solution.py:843
  146.0 17.0 %collective-permute-start.19 = (bf16[4,16,2560]{2,1,0:T(8,128)(2,1)}, bf16[4,16,2560]{2,1,0:T(8,128)(2,1)S(1)}, u32[]{:S(2)}, u32[]{:S(2)}) collective-permute-start(bf16[4,16,2560]{2,1,0:T(8,128)(2,1)} %get-tuple-element.138), channel_id=1, source_target_pairs={{0,24},{8,0},{16,8},{24,16},{1,25},{9,1},{17,9},{25,17},{2,26},{10... | collective-permute-start | bytes 983048 | tf_op jit(solution)/shard_map/ppermute | solution.py:848
  148.7 14.4 %collective-permute-start.20 = (bf16[4,16,2560]{2,1,0:T(8,128)(2,1)}, bf16[4,16,2560]{2,1,0:T(8,128)(2,1)S(1)}, u32[]{:S(2)}, u32[]{:S(2)}) collective-permute-start(bf16[4,16,2560]{2,1,0:T(8,128)(2,1)} %get-tuple-element.139), channel_id=1, source_target_pairs={{0,16},{8,24},{16,0},{24,8},{1,17},{9,25},{17,1},{25,9},{2,18},{10... | collective-permute-start | bytes 983048 | tf_op jit(solution)/shard_map/ppermute | solution.py:848
  149.8 16.9 %collective-permute-start.21 = (bf16[4,16,2560]{2,1,0:T(8,128)(2,1)}, bf16[4,16,2560]{2,1,0:T(8,128)(2,1)S(1)}, u32[]{:S(2)}, u32[]{:S(2)}) collective-permute-start(bf16[4,16,2560]{2,1,0:T(8,128)(2,1)} %get-tuple-element.140), channel_id=1, source_target_pairs={{0,8},{8,16},{16,24},{24,0},{1,9},{9,17},{17,25},{25,1},{2,10},{10... | collective-permute-start | bytes 983048 | tf_op jit(solution)/shard_map/ppermute | solution.py:848
  168.4 15.3 %all-to-all-start.6 = ((bf16[4,16,2560]{2,1,0:T(8,128)(2,1)}), bf16[4,16,2560]{2,1,0:T(8,128)(2,1)S(1)}, u32[]{:S(2)}, u32[]{:S(2)}) async-start(bf16[4,16,2560]{2,1,0:T(8,128)(2,1)} %stack_sum.1), calls=%async_computation.6 | async-start | bytes 655360 | tf_op jit(solution)/shard_map/all_to_all | solution.py:843
  175.6 7.0 %collective-permute-start.23 = (bf16[16,3584]{1,0:T(8,128)(2,1)}, bf16[16,3584]{1,0:T(8,128)(2,1)S(1)}, u32[]{:S(2)}, u32[]{:S(2)}) collective-permute-start(bf16[16,3584]{1,0:T(8,128)(2,1)} %get-tuple-element.148), channel_id=1, source_target_pairs={{0,16},{8,24},{16,0},{24,8},{1,17},{9,25},{17,1},{25,9},{2,18},{10... | collective-permute-start | bytes 344072 | tf_op jit(solution)/shard_map/ppermute | solution.py:848
  176.7 7.0 %collective-permute-start.24 = (bf16[16,3584]{1,0:T(8,128)(2,1)}, bf16[16,3584]{1,0:T(8,128)(2,1)S(1)}, u32[]{:S(2)}, u32[]{:S(2)}) collective-permute-start(bf16[16,3584]{1,0:T(8,128)(2,1)} %get-tuple-element.149), channel_id=1, source_target_pairs={{0,8},{8,16},{16,24},{24,0},{1,9},{9,17},{17,25},{25,1},{2,10},{10... | collective-permute-start | bytes 344072 | tf_op jit(solution)/shard_map/ppermute | solution.py:848
  185.4 9.7 %all-to-all-start.7 = ((bf16[4,4,6144]{2,1,0:T(4,128)(2,1)}), bf16[4,4,6144]{2,1,0:T(4,128)(2,1)S(1)}, u32[]{:S(2)}, u32[]{:S(2)}) async-start(bf16[4,4,6144]{2,1,0:T(4,128)(2,1)} %row_sum.1), calls=%async_computation.7 | async-start | bytes 393216 | tf_op jit(solution)/shard_map/all_to_all | solution.py:843
  (22 other events, 163.9 us)

commit v11 on v10

--- a/solution.py
+++ b/solution.py
@@ -95,11 +95,15 @@
         tiles = []
         for j in range(group):
             cols = slice(j * HEAD_DIM, (j + 1) * HEAD_DIM)
-            here = slice((g * group + j) * HEAD_DIM, (g * group + j + 1) * HEAD_DIM)
-            wk = (k_ref[:, here].astype(F32) * fade[:, cols]).astype(BF16)
-            state = lax.dot_general(
-                wk, v_ref[:, here], (((0,), (0,)), ((), ())), preferred_element_type=F32
-            ).astype(BF16)
+            if j % 2 == 0:
+                two = slice(j * HEAD_DIM, (j + 2) * HEAD_DIM)
+                both = slice((g * group + j) * HEAD_DIM, (g * group + j + 2) * HEAD_DIM)
+                wk = (k_ref[:, both].astype(F32) * fade[:, two]).astype(BF16)
+                pair = lax.dot_general(
+                    wk, v_ref[:, both], (((0,), (0,)), ((), ())), preferred_element_type=F32
+                )
+            at = slice((j % 2) * HEAD_DIM, (j % 2 + 1) * HEAD_DIM)
+            state = pair[at, at].astype(BF16)
             row = (g * group + j) * HEAD_DIM
             end = row + HEAD_DIM
             lo = 0
@@ -132,7 +136,7 @@
         c.wait()
 
 
-def local_states(k, v, ld, group=3):
+def local_states(k, v, ld, group=6):
     rows, width = k.shape
     heads = ld.shape[0]
     per = heads * HEAD_DIM // 32
@@ -554,8 +558,7 @@
     return pl.pallas_call(
         repeat_kernel,
         out_shape=far((copies, count, rows, width)),
-        in_specs=[pl.BlockSpec(memory_space=pl.ANY)]
-        + [pl.BlockSpec(memory_space=pltpu.VMEM)] * (count - 1),
+        in_specs=[pl.BlockSpec(memory_space=pltpu.VMEM)] * count,
         out_specs=pl.BlockSpec(memory_space=pl.ANY),
         scratch_shapes=[pltpu.SemaphoreType.DMA((copies, count))],
         compiler_params=params(),

time: 198 us -> 187 us (0.944)
  Pallas kernels: 73.2 us -> 61.7 us
    pallas_call x1, Pallas kernels: 13.2 us -> 2.25 us  [repeat(): pl.pallas_call(repeat_kernel, out_shape=far((copies, count, rows, width))...]
  transfers between devices with their start and end apart: 33 -> 33, of which waited for: 20 -> 20; matrix products, arithmetic and copies ran while one was open for 0% -> 0% of each run, Pallas kernels for 19% -> 21%
where the time goes in v11:
time: 187 us; the launch traced here: 185 us
  starting transfers between devices  69.7 us (37%)
  Pallas kernels  61.7 us (33%)
  waiting for transfers between devices  50 us (27%)
  local copies, waits for them, and re-layouts  3.02 us (2%)
    ppermute x25, waiting for transfers between devices, shift(): return lax.ppermute(a, axis, [(i, (i + by) % n) for i in range(n)])  46.1 us
    all_to_all x8, starting transfers between devices, exchange(): return lax.all_to_all(a, axis, split_axis=0, concat_axis=0, tiled=True)  40.7 us
    ppermute x25, starting transfers between devices, shift(): return lax.ppermute(a, axis, [(i, (i + by) % n) for i in range(n)])  28.9 us
    pallas_call x4, Pallas kernels, expert_down(): pl.pallas_call(functools.partial(down_kernel, steps, cut if last else 0,...  11.7 us
    pallas_call x1, Pallas kernels, inside_blocks(): pl.pallas_call(functools.partial(inside_kernel, group), grid=(heads // gr...  7.82 us
    pallas_call x1, Pallas kernels, local_states(): pl.pallas_call(functools.partial(state_kernel, group), out_shape=(jax.Sha...  5.12 us
    pallas_call x1, Pallas kernels, hidden_rows(): pl.pallas_call(hidden_kernel, grid=(rows // tile,), out_shape=jax.ShapeDt...  4.96 us
    pallas_call x1, Pallas kernels, carried_blocks(): pl.pallas_call(functools.partial(carried_kernel, group), grid=(heads // g...  4.26 us
  transfers between devices with their start and end apart: 33, of which 20 were waited for; matrix products, arithmetic and copies ran while one was open for 0% of the time, Pallas kernels for 21%

profile of v11, /device:TPU:0, one launch (start us, length us, event | category | flops | bytes accessed | tf_op | source)
XLA Modules:
  0.0 185.3 jit_solution(8202664578538209897)
XLA Ops:
  0.6 5.1 %local_states.1 = (f32[512,12]{1,0:T(8,128)S(1)}, bf16[32,64,128]{2,1,0:T(8,128)(2,1)}) custom-call(bf16[512,1536]{1,0:T(8,128)(2,1)} %k_ref.1, bf16[512,1536]{1,0:T(8,128)(2,1)} %v_ref.1, f32[12,512]{1,0:T(8,128)} %bitcast.27), custom_call_target="tpu_custom_call" | custom-call | flops 201326592 | bytes 3145728 | tf_op jit(solution)/shard_map/local_states/pallas_call | solution.py:146
  5.8 8.4 %all-to-all-start = ((bf16[32,64,128]{2,1,0:T(8,128)(2,1)}), bf16[32,64,128]{2,1,0:T(8,128)(2,1)}, u32[]{:S(2)}, u32[]{:S(2)}) async-start(bf16[32,64,128]{2,1,0:T(8,128)(2,1)} %get-tuple-element.76), calls=%async_computation | async-start | bytes 1048576 | tf_op jit(solution)/shard_map/all_to_all | solution.py:846
  14.2 3.2 %route_rows.1 = (bf16[8,6400]{1,0:T(8,128)(2,1)}, bf16[8,6400]{1,0:T(8,128)(2,1)}, bf16[8,6400]{1,0:T(8,128)(2,1)}, bf16[8,6400]{1,0:T(8,128)(2,1)}, f32[16,128]{1,0:T(8,128)S(1)}) custom-call(s32[1]{0:T(128)} %bitcast.me_ref, s32[2,128]{1,0:T(2,128)S(1)} %bitcast.17, bf16[128,6144]{1,0:T(8,128)(2,1)} %res_ref.1, bf16[128,6144]{1,0:T(8,128)(2,1)} %gate_ref.1), custom_call_target="tpu_custom_call" | custom-call | flops 50331648 | bytes 3932160 | tf_op jit(solution)/shard_map/route_rows/pallas_call | solution.py:381
  17.4 7.8 %inside_blocks.1 = (f32[512,1536]{1,0:T(8,128)S(1)}, bf16[512,1536]{1,0:T(8,128)(2,1)}) custom-call(bf16[512,1536]{1,0:T(8,128)(2,1)} %q_ref.1, bf16[512,1536]{1,0:T(8,128)(2,1)} %k_ref.1, bf16[512,1536]{1,0:T(8,128)(2,1)} %v_ref.1, f32[512,12]{1,0:T(8,128)S(1)} %get-tuple-element.77.cum_ref, f32[12,512]{1,0:T(8,128)} %bitcast.28), custom_call_target="tpu_custom_call" | custom-call | flops 1610612736 | bytes 9437184 | tf_op jit(solution)/shard_map/inside_blocks/pallas_call | solution.py:242
  27.8 6.6 %all-to-all-start.1 = ((bf16[32,48,128]{2,1,0:T(8,128)(2,1)}), bf16[32,48,128]{2,1,0:T(8,128)(2,1)S(1)}, u32[]{:S(2)}, u32[]{:S(2)}) async-start(bf16[32,48,128]{2,1,0:T(8,128)(2,1)} %scan_blocks.1), calls=%async_computation.1 | async-start | bytes 786432 | tf_op jit(solution)/shard_map/all_to_all | solution.py:846
  41.1 3.4 %collective-permute-done.1.refs_2_ = bf16[8,6400]{1,0:T(8,128)(2,1)S(1)} collective-permute-done((bf16[8,6400]{1,0:T(8,128)(2,1)}, bf16[8,6400]{1,0:T(8,128)(2,1)S(1)}, u32[]{:S(2)}, u32[]{:S(2)}) %collective-permute-start.1) | collective-permute-done | bytes 102432 | tf_op jit(solution)/shard_map/ppermute | solution.py:851
  45.7 3.5 %place_rows.1 = (f32[64,1536]{1,0:T(8,128)}, bf16[64,1536]{1,0:T(8,128)(2,1)}) custom-call(s32[1]{0:T(128)} %bitcast.me_ref, f32[512,1536]{1,0:T(8,128)S(1)} %get-tuple-element.93.inside_ref, bf16[512,1536]{1,0:T(8,128)(2,1)} %get-tuple-element.94.qs_ref, bf16[8,6400]{1,0:T(8,128)(2,1)} %get-tuple-element.86.refs_0_, bf16[8,6400]{1,0:T(8,128)(2,1)} %copy-done.8, ...), custom_call_target="tpu_custom_call" | custom-call | flops 1000000 | bytes 200000 | tf_op jit(solution)/shard_map/place_rows/pallas_call | solution.py:454
  51.2 4.0 %all-to-all-start.2 = ((bf16[4,16,1536]{2,1,0:T(8,128)(2,1)}), bf16[4,16,1536]{2,1,0:T(8,128)(2,1)}, u32[]{:S(2)}, u32[]{:S(2)}) async-start(bf16[4,16,1536]{2,1,0:T(8,128)(2,1)} %bitcast.24), calls=%async_computation.2 | async-start | bytes 393216 | tf_op jit(solution)/shard_map/all_to_all | solution.py:846
  55.2 4.3 %carried_blocks.1 = (bf16[128,1536]{1,0:T(8,128)(2,1)}, bf16[128,1536]{1,0:T(8,128)(2,1)}, bf16[128,1536]{1,0:T(8,128)(2,1)}, bf16[128,1536]{1,0:T(8,128)(2,1)}) custom-call(s32[1]{0:T(128)} %bitcast.me_ref, f32[512,1536]{1,0:T(8,128)S(1)} %get-tuple-element.93.inside_ref, bf16[512,1536]{1,0:T(8,128)(2,1)} %get-tuple-element.94.qs_ref, ...), custom_call_target="tpu_custom_call" | custom-call | flops 402653184 | bytes 6291456 | tf_op jit(solution)/shard_map/carried_blocks/pallas_call | solution.py:310
  65.4 4.4 %all-to-all-start.3 = ((bf16[4,16,3072]{2,1,0:T(8,128)(2,1)}), bf16[4,16,3072]{2,1,0:T(8,128)(2,1)S(1)}, u32[]{:S(2)}, u32[]{:S(2)}) async-start(bf16[4,16,3072]{2,1,0:T(8,128)(2,1)} %get-tuple-element.103), calls=%async_computation.3 | async-start | bytes 786432 | tf_op jit(solution)/shard_map/all_to_all | solution.py:846
  81.1 4.9 %all-to-all-start.4 = ((bf16[4,4,16,3072]{3,2,1,0:T(8,128)(2,1)}), bf16[4,4,16,3072]{3,2,1,0:T(8,128)(2,1)S(1)}, u32[]{:S(2)}, u32[]{:S(2)}) async-start(bf16[4,4,16,3072]{3,2,1,0:T(8,128)(2,1)} %repeat.1), calls=%async_computation.4 | async-start | bytes 3145728 | tf_op jit(solution)/shard_map/all_to_all | solution.py:846
  96.7 5.5 %collective-permute-done.7.refs_1_ = bf16[4,16,3072]{2,1,0:T(8,128)(2,1)S(1)} collective-permute-done((bf16[4,16,3072]{2,1,0:T(8,128)(2,1)S(1)}, bf16[4,16,3072]{2,1,0:T(8,128)(2,1)S(1)}, u32[]{:S(2)}, u32[]{:S(2)}) %collective-permute-start.7) | collective-permute-done | bytes 393248 | tf_op jit(solution)/shard_map/ppermute | solution.py:851
  102.2 4.2 %collective-permute-done.8.refs_2_ = bf16[4,16,3072]{2,1,0:T(8,128)(2,1)S(1)} collective-permute-done((bf16[4,16,3072]{2,1,0:T(8,128)(2,1)S(1)}, bf16[4,16,3072]{2,1,0:T(8,128)(2,1)S(1)}, u32[]{:S(2)}, u32[]{:S(2)}) %collective-permute-start.8) | collective-permute-done | bytes 393248 | tf_op jit(solution)/shard_map/ppermute | solution.py:851
  107.6 4.2 %first_act.1 = (bf16[256,288]{1,0:T(8,128)(2,1)S(1)}, bf16[2,288,6144]{2,1,0:T(8,128)(2,1)S(1)}) custom-call(bf16[288,6144]{1,0:T(8,128)(2,1)} %bitcast.22, bf16[288,6144]{1,0:T(8,128)(2,1)} %bitcast.23, bf16[4,4,16,3072]{3,2,1,0:T(8,128)(2,1)S(1)} %all-to-all-done.4.one_ref, bf16[4,16,3072]{2,1,0:T(8,128)(2,1)S(1)} %all-to-all-done.3.refs_0_, ...), custom_call_target="tpu_custom_call" | custom-call | flops 1811939328 | bytes 10223616 | tf_op jit(solution)/shard_map/first_act/pallas_call | solution.py:623
  119.9 3.3 %collective-permute-done.17.refs_0_ = bf16[4,4,16,3584]{3,2,1,0:T(8,128)(2,1)S(1)} collective-permute-done((bf16[4,4,16,3584]{3,2,1,0:T(8,128)(2,1)S(1)}, bf16[4,4,16,3584]{3,2,1,0:T(8,128)(2,1)S(1)}, u32[]{:S(2)}, u32[]{:S(2)}) %collective-permute-start.17) | collective-permute-done | bytes 1835040 | tf_op jit(solution)/shard_map/ppermute | solution.py:851
  123.2 3.6 %expert_down.6 = bf16[4,4,16,3584]{3,2,1,0:T(8,128)(2,1)} custom-call(bf16[256,288]{1,0:T(8,128)(2,1)S(1)} %get-tuple-element.135.act_ref, bf16[288,6144]{1,0:T(8,128)(2,1)} %bitcast.20, bf16[4,4,16,3584]{3,2,1,0:T(8,128)(2,1)S(1)} %collective-permute-done.17.refs_0_), custom_call_target="tpu_custom_call" | custom-call | flops 528482304 | bytes 3899392 | tf_op jit(solution)/shard_map/expert_down/pallas_call | solution.py:733
  126.8 4.5 %all-to-all-start.5 = ((bf16[4,4,16,3584]{3,2,1,0:T(8,128)(2,1)}), bf16[4,4,16,3584]{3,2,1,0:T(8,128)(2,1)S(1)}, u32[]{:S(2)}, u32[]{:S(2)}) async-start(bf16[4,4,16,3584]{3,2,1,0:T(8,128)(2,1)} %expert_down.6), calls=%async_computation.5 | async-start | bytes 3670016 | tf_op jit(solution)/shard_map/all_to_all | solution.py:846
  131.3 3.2 %expert_down.7 = (bf16[4,16,2560]{2,1,0:T(8,128)(2,1)}, bf16[4,16,2560]{2,1,0:T(8,128)(2,1)}, bf16[4,16,2560]{2,1,0:T(8,128)(2,1)}, bf16[4,16,2560]{2,1,0:T(8,128)(2,1)}) custom-call(bf16[256,288]{1,0:T(8,128)(2,1)S(1)} %get-tuple-element.135.act_ref, bf16[288,6144]{1,0:T(8,128)(2,1)} %bitcast.21, bf16[4,4,16,2560]{3,2,1,0:T(8,128)(2,1)S(1)} %collective-permute-done.18.refs_0_), custom_call_target="tpu_custom_call" | custom-call | flops 377487360 | bytes 2785280 | tf_op jit(solution)/shard_map/expert_down/pallas_call | solution.py:733
  138.3 13.2 %collective-permute-done.19.refs_1_ = bf16[4,16,2560]{2,1,0:T(8,128)(2,1)S(1)} collective-permute-done((bf16[4,16,2560]{2,1,0:T(8,128)(2,1)}, bf16[4,16,2560]{2,1,0:T(8,128)(2,1)S(1)}, u32[]{:S(2)}, u32[]{:S(2)}) %collective-permute-start.19) | collective-permute-done | bytes 327712 | tf_op jit(solution)/shard_map/ppermute | solution.py:851
  151.5 3.6 %collective-permute-done.21.refs_3_ = bf16[4,16,2560]{2,1,0:T(8,128)(2,1)S(1)} collective-permute-done((bf16[4,16,2560]{2,1,0:T(8,128)(2,1)}, bf16[4,16,2560]{2,1,0:T(8,128)(2,1)S(1)}, u32[]{:S(2)}, u32[]{:S(2)}) %collective-permute-start.21) | collective-permute-done | bytes 327712 | tf_op jit(solution)/shard_map/ppermute | solution.py:851
  156.9 4.5 %all-to-all-start.6 = ((bf16[4,16,2560]{2,1,0:T(8,128)(2,1)}), bf16[4,16,2560]{2,1,0:T(8,128)(2,1)S(1)}, u32[]{:S(2)}, u32[]{:S(2)}) async-start(bf16[4,16,2560]{2,1,0:T(8,128)(2,1)} %stack_sum.1), calls=%async_computation.6 | async-start | bytes 655360 | tf_op jit(solution)/shard_map/all_to_all | solution.py:846
  165.2 3.5 %collective-permute-done.22.refs_1_ = bf16[16,3584]{1,0:T(8,128)(2,1)S(1)} collective-permute-done((bf16[16,3584]{1,0:T(8,128)(2,1)}, bf16[16,3584]{1,0:T(8,128)(2,1)S(1)}, u32[]{:S(2)}, u32[]{:S(2)}) %collective-permute-start.22) | collective-permute-done | bytes 114720 | tf_op jit(solution)/shard_map/ppermute | solution.py:851
  173.9 3.4 %all-to-all-start.7 = ((bf16[4,4,6144]{2,1,0:T(4,128)(2,1)}), bf16[4,4,6144]{2,1,0:T(4,128)(2,1)S(1)}, u32[]{:S(2)}, u32[]{:S(2)}) async-start(bf16[4,4,6144]{2,1,0:T(4,128)(2,1)} %row_sum.1), calls=%async_computation.7 | async-start | bytes 393216 | tf_op jit(solution)/shard_map/all_to_all | solution.py:846
  177.5 5.0 %hidden_rows.1 = bf16[128,6144]{1,0:T(8,128)(2,1)} custom-call(s32[1]{0:T(128)} %bitcast.me_ref, bf16[128,6144]{1,0:T(8,128)(2,1)} %res_ref.1, bf16[128,6144]{1,0:T(8,128)(2,1)} %gate_ref.1, f32[1,6144]{1,0:T(1,128)} %bitcast.26, bf16[128,1536]{1,0:T(8,128)(2,1)S(1)} %copy-done, bf16[128,1536]{1,0:T(8,128)(2,1)S(1)} %copy-done.4, ...), custom_call_target="tpu_custom_call" | custom-call | flops 15728640 | bytes 6291456 | tf_op jit(solution)/shard_map/hidden_rows/pallas_call | solution.py:524
  (90 shorter events, 67.1 us)
Async XLA Ops:
  5.8 20.1 %all-to-all-start = ((bf16[32,64,128]{2,1,0:T(8,128)(2,1)}), bf16[32,64,128]{2,1,0:T(8,128)(2,1)}, u32[]{:S(2)}, u32[]{:S(2)}) async-start(bf16[32,64,128]{2,1,0:T(8,128)(2,1)} %get-tuple-element.76), calls=%async_computation | async-start | bytes 1048576 | tf_op jit(solution)/shard_map/all_to_all | solution.py:846
  27.8 21.4 %all-to-all-start.1 = ((bf16[32,48,128]{2,1,0:T(8,128)(2,1)}), bf16[32,48,128]{2,1,0:T(8,128)(2,1)S(1)}, u32[]{:S(2)}, u32[]{:S(2)}) async-start(bf16[32,48,128]{2,1,0:T(8,128)(2,1)} %scan_blocks.1), calls=%async_computation.1 | async-start | bytes 786432 | tf_op jit(solution)/shard_map/all_to_all | solution.py:846
  34.4 6.6 %collective-permute-start = (bf16[8,6400]{1,0:T(8,128)(2,1)}, bf16[8,6400]{1,0:T(8,128)(2,1)S(1)}, u32[]{:S(2)}, u32[]{:S(2)}) collective-permute-start(bf16[8,6400]{1,0:T(8,128)(2,1)} %get-tuple-element.87), channel_id=1, source_target_pairs={{0,1},{1,2},{2,3},{3,0},{4,5},{5,6},{6,7},{7,4},{8,9},{9,10},{10,1... | collective-permute-start | bytes 307208 | tf_op jit(solution)/shard_map/ppermute | solution.py:851
  36.1 8.3 %collective-permute-start.1 = (bf16[8,6400]{1,0:T(8,128)(2,1)}, bf16[8,6400]{1,0:T(8,128)(2,1)S(1)}, u32[]{:S(2)}, u32[]{:S(2)}) collective-permute-start(bf16[8,6400]{1,0:T(8,128)(2,1)} %get-tuple-element.88), channel_id=1, source_target_pairs={{0,2},{1,3},{2,0},{3,1},{4,6},{5,7},{6,4},{7,5},{8,10},{9,11},{10,... | collective-permute-start | bytes 307208 | tf_op jit(solution)/shard_map/ppermute | solution.py:851
  51.2 10.4 %all-to-all-start.2 = ((bf16[4,16,1536]{2,1,0:T(8,128)(2,1)}), bf16[4,16,1536]{2,1,0:T(8,128)(2,1)}, u32[]{:S(2)}, u32[]{:S(2)}) async-start(bf16[4,16,1536]{2,1,0:T(8,128)(2,1)} %bitcast.24), calls=%async_computation.2 | async-start | bytes 393216 | tf_op jit(solution)/shard_map/all_to_all | solution.py:846
  61.5 17.3 %collective-permute-start.6 = (bf16[128,1536]{1,0:T(8,128)(2,1)}, bf16[128,1536]{1,0:T(8,128)(2,1)S(1)}, u32[]{:S(2)}, u32[]{:S(2)}) collective-permute-start(bf16[128,1536]{1,0:T(8,128)(2,1)} %get-tuple-element.104), channel_id=1, source_target_pairs={{0,2},{1,3},{2,0},{3,1},{4,6},{5,7},{6,4},{7,5},{8,10},{9,11},{10,... | collective-permute-start | bytes 1179656 | tf_op jit(solution)/shard_map/ppermute | solution.py:851
  65.4 13.4 %all-to-all-start.3 = ((bf16[4,16,3072]{2,1,0:T(8,128)(2,1)}), bf16[4,16,3072]{2,1,0:T(8,128)(2,1)S(1)}, u32[]{:S(2)}, u32[]{:S(2)}) async-start(bf16[4,16,3072]{2,1,0:T(8,128)(2,1)} %get-tuple-element.103), calls=%async_computation.3 | async-start | bytes 786432 | tf_op jit(solution)/shard_map/all_to_all | solution.py:846
  69.8 6.6 %collective-permute-start.3 = (bf16[16,3072]{1,0:T(8,128)(2,1)}, bf16[16,3072]{1,0:T(8,128)(2,1)S(1)}, u32[]{:S(2)}, u32[]{:S(2)}) collective-permute-start(bf16[16,3072]{1,0:T(8,128)(2,1)} %get-tuple-element.105.refs_0_), channel_id=1, source_target_pairs={{0,8},{8,16},{16,24},{24,0},{1,9},{9,17},{17,25},{25,1},{2,10},{10... | collective-permute-start | bytes 294920 | tf_op jit(solution)/shard_map/ppermute | solution.py:851
  71.3 6.5 %collective-permute-start.4 = (bf16[16,3072]{1,0:T(8,128)(2,1)}, bf16[16,3072]{1,0:T(8,128)(2,1)S(1)}, u32[]{:S(2)}, u32[]{:S(2)}) collective-permute-start(bf16[16,3072]{1,0:T(8,128)(2,1)} %get-tuple-element.105.refs_0_), channel_id=1, source_target_pairs={{0,16},{8,24},{16,0},{24,8},{1,17},{9,25},{17,1},{25,9},{2,18},{10... | collective-permute-start | bytes 294920 | tf_op jit(solution)/shard_map/ppermute | solution.py:851
  81.1 25.4 %all-to-all-start.4 = ((bf16[4,4,16,3072]{3,2,1,0:T(8,128)(2,1)}), bf16[4,4,16,3072]{3,2,1,0:T(8,128)(2,1)S(1)}, u32[]{:S(2)}, u32[]{:S(2)}) async-start(bf16[4,4,16,3072]{3,2,1,0:T(8,128)(2,1)} %repeat.1), calls=%async_computation.4 | async-start | bytes 3145728 | tf_op jit(solution)/shard_map/all_to_all | solution.py:846
  86.0 9.2 %collective-permute-start.10 = (bf16[128,1536]{1,0:T(8,128)(2,1)}, bf16[128,1536]{1,0:T(8,128)(2,1)S(1)}, u32[]{:S(2)}, u32[]{:S(2)}) collective-permute-start(bf16[128,1536]{1,0:T(8,128)(2,1)} %get-tuple-element.110), channel_id=1, source_target_pairs={{0,1},{1,2},{2,3},{3,0},{4,5},{5,6},{6,7},{7,4},{8,9},{9,10},{10,1... | collective-permute-start | bytes 1179656 | tf_op jit(solution)/shard_map/ppermute | solution.py:851
  86.7 9.3 %collective-permute-start.11 = (bf16[128,1536]{1,0:T(8,128)(2,1)S(1)}, bf16[128,1536]{1,0:T(8,128)(2,1)S(1)}, u32[]{:S(2)}, u32[]{:S(2)}) collective-permute-start(bf16[128,1536]{1,0:T(8,128)(2,1)S(1)} %copy-done.12), channel_id=1, source_target_pairs={{0,3},{1,0},{2,1},{3,2},{4,7},{5,4},{6,5},{7,6},{8,11},{9,8},{10,9... | collective-permute-start | bytes 1179656 | tf_op jit(solution)/shard_map/ppermute | solution.py:851
  89.3 13.0 %collective-permute-start.7 = (bf16[4,16,3072]{2,1,0:T(8,128)(2,1)S(1)}, bf16[4,16,3072]{2,1,0:T(8,128)(2,1)S(1)}, u32[]{:S(2)}, u32[]{:S(2)}) collective-permute-start(bf16[4,16,3072]{2,1,0:T(8,128)(2,1)S(1)} %all-to-all-done.3.refs_0_), channel_id=1, source_target_pairs={{0,8},{8,16},{16,24},{24,0},{1,9},{9,17},{17,25},{25,1},{2,10},{10... | collective-permute-start | bytes 1179656 | tf_op jit(solution)/shard_map/ppermute | solution.py:851
  90.3 16.2 %collective-permute-start.8 = (bf16[4,16,3072]{2,1,0:T(8,128)(2,1)S(1)}, bf16[4,16,3072]{2,1,0:T(8,128)(2,1)S(1)}, u32[]{:S(2)}, u32[]{:S(2)}) collective-permute-start(bf16[4,16,3072]{2,1,0:T(8,128)(2,1)S(1)} %all-to-all-done.3.refs_0_), channel_id=1, source_target_pairs={{0,16},{8,24},{16,0},{24,8},{1,17},{9,25},{17,1},{25,9},{2,18},{10... | collective-permute-start | bytes 1179656 | tf_op jit(solution)/shard_map/ppermute | solution.py:851
  93.4 13.1 %collective-permute-start.9 = (bf16[4,16,3072]{2,1,0:T(8,128)(2,1)S(1)}, bf16[4,16,3072]{2,1,0:T(8,128)(2,1)S(1)}, u32[]{:S(2)}, u32[]{:S(2)}) collective-permute-start(bf16[4,16,3072]{2,1,0:T(8,128)(2,1)S(1)} %all-to-all-done.3.refs_0_), channel_id=1, source_target_pairs={{0,24},{8,0},{16,8},{24,16},{1,25},{9,1},{17,9},{25,17},{2,26},{10... | collective-permute-start | bytes 1179656 | tf_op jit(solution)/shard_map/ppermute | solution.py:851
  119.5 7.3 %collective-permute-start.18 = (bf16[4,4,16,2560]{3,2,1,0:T(8,128)(2,1)S(1)}, bf16[4,4,16,2560]{3,2,1,0:T(8,128)(2,1)S(1)}, u32[]{:S(2)}, u32[]{:S(2)}) collective-permute-start(bf16[4,4,16,2560]{3,2,1,0:T(8,128)(2,1)S(1)} %expert_down.5), channel_id=1, source_target_pairs={{0,4},{4,0},{1,5},{5,1},{2,6},{6,2},{3,7},{7,3},{8,12},{12,8},{9,1... | collective-permute-start | bytes 3932168 | tf_op jit(solution)/shard_map/ppermute | solution.py:851
  126.8 28.4 %all-to-all-start.5 = ((bf16[4,4,16,3584]{3,2,1,0:T(8,128)(2,1)}), bf16[4,4,16,3584]{3,2,1,0:T(8,128)(2,1)S(1)}, u32[]{:S(2)}, u32[]{:S(2)}) async-start(bf16[4,4,16,3584]{3,2,1,0:T(8,128)(2,1)} %expert_down.6), calls=%async_computation.5 | async-start | bytes 3670016 | tf_op jit(solution)/shard_map/all_to_all | solution.py:846
  134.5 17.0 %collective-permute-start.19 = (bf16[4,16,2560]{2,1,0:T(8,128)(2,1)}, bf16[4,16,2560]{2,1,0:T(8,128)(2,1)S(1)}, u32[]{:S(2)}, u32[]{:S(2)}) collective-permute-start(bf16[4,16,2560]{2,1,0:T(8,128)(2,1)} %get-tuple-element.138), channel_id=1, source_target_pairs={{0,24},{8,0},{16,8},{24,16},{1,25},{9,1},{17,9},{25,17},{2,26},{10... | collective-permute-start | bytes 983048 | tf_op jit(solution)/shard_map/ppermute | solution.py:851
  137.2 14.4 %collective-permute-start.20 = (bf16[4,16,2560]{2,1,0:T(8,128)(2,1)}, bf16[4,16,2560]{2,1,0:T(8,128)(2,1)S(1)}, u32[]{:S(2)}, u32[]{:S(2)}) collective-permute-start(bf16[4,16,2560]{2,1,0:T(8,128)(2,1)} %get-tuple-element.139), channel_id=1, source_target_pairs={{0,16},{8,24},{16,0},{24,8},{1,17},{9,25},{17,1},{25,9},{2,18},{10... | collective-permute-start | bytes 983048 | tf_op jit(solution)/shard_map/ppermute | solution.py:851
  138.2 16.9 %collective-permute-start.21 = (bf16[4,16,2560]{2,1,0:T(8,128)(2,1)}, bf16[4,16,2560]{2,1,0:T(8,128)(2,1)S(1)}, u32[]{:S(2)}, u32[]{:S(2)}) collective-permute-start(bf16[4,16,2560]{2,1,0:T(8,128)(2,1)} %get-tuple-element.140), channel_id=1, source_target_pairs={{0,8},{8,16},{16,24},{24,0},{1,9},{9,17},{17,25},{25,1},{2,10},{10... | collective-permute-start | bytes 983048 | tf_op jit(solution)/shard_map/ppermute | solution.py:851
  156.9 15.3 %all-to-all-start.6 = ((bf16[4,16,2560]{2,1,0:T(8,128)(2,1)}), bf16[4,16,2560]{2,1,0:T(8,128)(2,1)S(1)}, u32[]{:S(2)}, u32[]{:S(2)}) async-start(bf16[4,16,2560]{2,1,0:T(8,128)(2,1)} %stack_sum.1), calls=%async_computation.6 | async-start | bytes 655360 | tf_op jit(solution)/shard_map/all_to_all | solution.py:846
  164.1 7.0 %collective-permute-start.23 = (bf16[16,3584]{1,0:T(8,128)(2,1)}, bf16[16,3584]{1,0:T(8,128)(2,1)S(1)}, u32[]{:S(2)}, u32[]{:S(2)}) collective-permute-start(bf16[16,3584]{1,0:T(8,128)(2,1)} %get-tuple-element.148), channel_id=1, source_target_pairs={{0,16},{8,24},{16,0},{24,8},{1,17},{9,25},{17,1},{25,9},{2,18},{10... | collective-permute-start | bytes 344072 | tf_op jit(solution)/shard_map/ppermute | solution.py:851
  165.1 7.0 %collective-permute-start.24 = (bf16[16,3584]{1,0:T(8,128)(2,1)}, bf16[16,3584]{1,0:T(8,128)(2,1)S(1)}, u32[]{:S(2)}, u32[]{:S(2)}) collective-permute-start(bf16[16,3584]{1,0:T(8,128)(2,1)} %get-tuple-element.149), channel_id=1, source_target_pairs={{0,8},{8,16},{16,24},{24,0},{1,9},{9,17},{17,25},{25,1},{2,10},{10... | collective-permute-start | bytes 344072 | tf_op jit(solution)/shard_map/ppermute | solution.py:851
  173.9 9.7 %all-to-all-start.7 = ((bf16[4,4,6144]{2,1,0:T(4,128)(2,1)}), bf16[4,4,6144]{2,1,0:T(4,128)(2,1)S(1)}, u32[]{:S(2)}, u32[]{:S(2)}) async-start(bf16[4,4,6144]{2,1,0:T(4,128)(2,1)} %row_sum.1), calls=%async_computation.7 | async-start | bytes 393216 | tf_op jit(solution)/shard_map/all_to_all | solution.py:846
  (22 other events, 152.5 us)

commit v12 on v11

--- a/solution.py
+++ b/solution.py
@@ -906,8 +906,11 @@
     ones, two, across = keep((ones, two, across))
     one = exchange(repeat([hbm(ones[0])] + ones[1:], nz), "z")
     twos = [two] + [shift(two, "x", d) for d in others]
-    right, left = shift(attention[1], "exp", 1), shift(attention[3], "exp", 3)
-    one, twos, right, left = keep((one, twos, right, left))
+    right = shift(attention[1], "exp", 1)
+    last, arrived = keep((attention[3], twos[1]))
+    twos = [twos[0], arrived] + twos[2:]
+    one, twos, right, last = keep((one, twos, right, last))
+    left = shift(last, "exp", 3)
 
     cut = moe_gain.shape[1] * 7 // 12
     act_own, weights = expert_act(one, twos, (w_gate, w_up))
@@ -917,7 +920,7 @@
     (one,) = expert_down(act_far, w_down, cut, False, nz, nx)
     one, act_far = keep((one, act_far))
     (two,) = expert_down(act_far, w_down, cut, True, nz, nx)
-    one, two, act_own = keep((one, two, act_own))
+    one, two, act_own, left = keep((one, two, act_own, left))
     one, two = shift(one, "core", 1), shift(two, "core", 1)
     (one,) = expert_down(act_own, w_down, cut, False, nz, nx, one)
     one, two, act_own = keep((one, two, act_own))

time: 187 us -> 190 us (1.016)
  waiting for transfers between devices: 50 us -> 53.5 us
    ppermute x25, waiting for transfers between devices: 46.1 us -> 49.6 us  [shift(): return lax.ppermute(a, axis, [(i, (i + by) % n) for i in range(n)])]
  transfers between devices with their start and end apart: 33 -> 33, of which waited for: 20 -> 18; matrix products, arithmetic and copies ran while one was open for 0% -> 0% of each run, Pallas kernels for 21% -> 24%
where the time goes in v12:
time: 190 us; the launch traced here: 189 us
  starting transfers between devices  69.6 us (37%)
  Pallas kernels  61.8 us (33%)
  waiting for transfers between devices  53.5 us (28%)
  local copies, waits for them, and re-layouts  3 us (2%)
    ppermute x25, waiting for transfers between devices, shift(): return lax.ppermute(a, axis, [(i, (i + by) % n) for i in range(n)])  49.6 us
    all_to_all x8, starting transfers between devices, exchange(): return lax.all_to_all(a, axis, split_axis=0, concat_axis=0, tiled=True)  40.8 us
    ppermute x25, starting transfers between devices, shift(): return lax.ppermute(a, axis, [(i, (i + by) % n) for i in range(n)])  28.8 us
    pallas_call x4, Pallas kernels, expert_down(): pl.pallas_call(functools.partial(down_kernel, steps, cut if last else 0,...  11.8 us
    pallas_call x1, Pallas kernels, inside_blocks(): pl.pallas_call(functools.partial(inside_kernel, group), grid=(heads // gr...  7.82 us
    pallas_call x1, Pallas kernels, local_states(): pl.pallas_call(functools.partial(state_kernel, group), out_shape=(jax.Sha...  5.12 us
    pallas_call x1, Pallas kernels, hidden_rows(): pl.pallas_call(hidden_kernel, grid=(rows // tile,), out_shape=jax.ShapeDt...  4.96 us
    pallas_call x1, Pallas kernels, carried_blocks(): pl.pallas_call(functools.partial(carried_kernel, group), grid=(heads // g...  4.26 us
  transfers between devices with their start and end apart: 33, of which 18 were waited for; matrix products, arithmetic and copies ran while one was open for 0% of the time, Pallas kernels for 24%

profile of v12, /device:TPU:0, one launch (start us, length us, event | category | flops | bytes accessed | tf_op | source)
XLA Modules:
  0.0 188.8 jit_solution(5467472292287423576)
XLA Ops:
  0.6 5.1 %local_states.1 = (f32[512,12]{1,0:T(8,128)S(1)}, bf16[32,64,128]{2,1,0:T(8,128)(2,1)}) custom-call(bf16[512,1536]{1,0:T(8,128)(2,1)} %k_ref.1, bf16[512,1536]{1,0:T(8,128)(2,1)} %v_ref.1, f32[12,512]{1,0:T(8,128)} %bitcast.27), custom_call_target="tpu_custom_call" | custom-call | flops 201326592 | bytes 3145728 | tf_op jit(solution)/shard_map/local_states/pallas_call | solution.py:146
  5.8 8.4 %all-to-all-start = ((bf16[32,64,128]{2,1,0:T(8,128)(2,1)}), bf16[32,64,128]{2,1,0:T(8,128)(2,1)}, u32[]{:S(2)}, u32[]{:S(2)}) async-start(bf16[32,64,128]{2,1,0:T(8,128)(2,1)} %get-tuple-element.79), calls=%async_computation | async-start | bytes 1048576 | tf_op jit(solution)/shard_map/all_to_all | solution.py:846
  14.2 3.2 %route_rows.1 = (bf16[8,6400]{1,0:T(8,128)(2,1)}, bf16[8,6400]{1,0:T(8,128)(2,1)}, bf16[8,6400]{1,0:T(8,128)(2,1)}, bf16[8,6400]{1,0:T(8,128)(2,1)}, f32[16,128]{1,0:T(8,128)S(1)}) custom-call(s32[1]{0:T(128)} %bitcast.me_ref, s32[2,128]{1,0:T(2,128)S(1)} %bitcast.17, bf16[128,6144]{1,0:T(8,128)(2,1)} %res_ref.1, bf16[128,6144]{1,0:T(8,128)(2,1)} %gate_ref.1), custom_call_target="tpu_custom_call" | custom-call | flops 50331648 | bytes 3932160 | tf_op jit(solution)/shard_map/route_rows/pallas_call | solution.py:381
  17.4 7.8 %inside_blocks.1 = (f32[512,1536]{1,0:T(8,128)S(1)}, bf16[512,1536]{1,0:T(8,128)(2,1)}) custom-call(bf16[512,1536]{1,0:T(8,128)(2,1)} %q_ref.1, bf16[512,1536]{1,0:T(8,128)(2,1)} %k_ref.1, bf16[512,1536]{1,0:T(8,128)(2,1)} %v_ref.1, f32[512,12]{1,0:T(8,128)S(1)} %get-tuple-element.80.cum_ref, f32[12,512]{1,0:T(8,128)} %bitcast.28), custom_call_target="tpu_custom_call" | custom-call | flops 1610612736 | bytes 9437184 | tf_op jit(solution)/shard_map/inside_blocks/pallas_call | solution.py:242
  27.8 6.6 %all-to-all-start.1 = ((bf16[32,48,128]{2,1,0:T(8,128)(2,1)}), bf16[32,48,128]{2,1,0:T(8,128)(2,1)S(1)}, u32[]{:S(2)}, u32[]{:S(2)}) async-start(bf16[32,48,128]{2,1,0:T(8,128)(2,1)} %scan_blocks.1), calls=%async_computation.1 | async-start | bytes 786432 | tf_op jit(solution)/shard_map/all_to_all | solution.py:846
  41.1 3.4 %collective-permute-done.1.refs_2_ = bf16[8,6400]{1,0:T(8,128)(2,1)S(1)} collective-permute-done((bf16[8,6400]{1,0:T(8,128)(2,1)}, bf16[8,6400]{1,0:T(8,128)(2,1)S(1)}, u32[]{:S(2)}, u32[]{:S(2)}) %collective-permute-start.1) | collective-permute-done | bytes 102432 | tf_op jit(solution)/shard_map/ppermute | solution.py:851
  45.7 3.5 %place_rows.1 = (f32[64,1536]{1,0:T(8,128)}, bf16[64,1536]{1,0:T(8,128)(2,1)}) custom-call(s32[1]{0:T(128)} %bitcast.me_ref, f32[512,1536]{1,0:T(8,128)S(1)} %get-tuple-element.96.inside_ref, bf16[512,1536]{1,0:T(8,128)(2,1)} %get-tuple-element.97.qs_ref, bf16[8,6400]{1,0:T(8,128)(2,1)} %get-tuple-element.89.refs_0_, bf16[8,6400]{1,0:T(8,128)(2,1)} %copy-done.8, ...), custom_call_target="tpu_custom_call" | custom-call | flops 1000000 | bytes 200000 | tf_op jit(solution)/shard_map/place_rows/pallas_call | solution.py:454
  51.2 4.0 %all-to-all-start.2 = ((bf16[4,16,1536]{2,1,0:T(8,128)(2,1)}), bf16[4,16,1536]{2,1,0:T(8,128)(2,1)}, u32[]{:S(2)}, u32[]{:S(2)}) async-start(bf16[4,16,1536]{2,1,0:T(8,128)(2,1)} %bitcast.24), calls=%async_computation.2 | async-start | bytes 393216 | tf_op jit(solution)/shard_map/all_to_all | solution.py:846
  55.2 4.3 %carried_blocks.1 = (bf16[128,1536]{1,0:T(8,128)(2,1)}, bf16[128,1536]{1,0:T(8,128)(2,1)}, bf16[128,1536]{1,0:T(8,128)(2,1)}, bf16[128,1536]{1,0:T(8,128)(2,1)}) custom-call(s32[1]{0:T(128)} %bitcast.me_ref, f32[512,1536]{1,0:T(8,128)S(1)} %get-tuple-element.96.inside_ref, bf16[512,1536]{1,0:T(8,128)(2,1)} %get-tuple-element.97.qs_ref, ...), custom_call_target="tpu_custom_call" | custom-call | flops 402653184 | bytes 6291456 | tf_op jit(solution)/shard_map/carried_blocks/pallas_call | solution.py:310
  65.4 4.4 %all-to-all-start.3 = ((bf16[4,16,3072]{2,1,0:T(8,128)(2,1)}), bf16[4,16,3072]{2,1,0:T(8,128)(2,1)S(1)}, u32[]{:S(2)}, u32[]{:S(2)}) async-start(bf16[4,16,3072]{2,1,0:T(8,128)(2,1)} %get-tuple-element.106), calls=%async_computation.3 | async-start | bytes 786432 | tf_op jit(solution)/shard_map/all_to_all | solution.py:846
  81.1 4.9 %all-to-all-start.4 = ((bf16[4,4,16,3072]{3,2,1,0:T(8,128)(2,1)}), bf16[4,4,16,3072]{3,2,1,0:T(8,128)(2,1)S(1)}, u32[]{:S(2)}, u32[]{:S(2)}) async-start(bf16[4,4,16,3072]{3,2,1,0:T(8,128)(2,1)} %repeat.1), calls=%async_computation.4 | async-start | bytes 3145728 | tf_op jit(solution)/shard_map/all_to_all | solution.py:846
  91.3 7.9 %collective-permute-done.7.refs_1_ = bf16[4,16,3072]{2,1,0:T(8,128)(2,1)S(1)} collective-permute-done((bf16[4,16,3072]{2,1,0:T(8,128)(2,1)S(1)}, bf16[4,16,3072]{2,1,0:T(8,128)(2,1)S(1)}, u32[]{:S(2)}, u32[]{:S(2)}) %collective-permute-start.7) | collective-permute-done | bytes 393248 | tf_op jit(solution)/shard_map/ppermute | solution.py:851
  100.0 3.8 %collective-permute-done.8.refs_2_ = bf16[4,16,3072]{2,1,0:T(8,128)(2,1)S(1)} collective-permute-done((bf16[4,16,3072]{2,1,0:T(8,128)(2,1)S(1)}, bf16[4,16,3072]{2,1,0:T(8,128)(2,1)S(1)}, u32[]{:S(2)}, u32[]{:S(2)}) %collective-permute-start.8) | collective-permute-done | bytes 393248 | tf_op jit(solution)/shard_map/ppermute | solution.py:851
  110.7 4.2 %first_act.1 = (bf16[256,288]{1,0:T(8,128)(2,1)S(1)}, bf16[2,288,6144]{2,1,0:T(8,128)(2,1)S(1)}) custom-call(bf16[288,6144]{1,0:T(8,128)(2,1)} %bitcast.22, bf16[288,6144]{1,0:T(8,128)(2,1)} %bitcast.23, bf16[4,4,16,3072]{3,2,1,0:T(8,128)(2,1)S(1)} %all-to-all-done.4.one_ref, bf16[4,16,3072]{2,1,0:T(8,128)(2,1)S(1)} %all-to-all-done.3.refs_0_, ...), custom_call_target="tpu_custom_call" | custom-call | flops 1811939328 | bytes 10223616 | tf_op jit(solution)/shard_map/first_act/pallas_call | solution.py:623
  123.4 3.3 %collective-permute-done.17.refs_0_ = bf16[4,4,16,3584]{3,2,1,0:T(8,128)(2,1)S(1)} collective-permute-done((bf16[4,4,16,3584]{3,2,1,0:T(8,128)(2,1)S(1)}, bf16[4,4,16,3584]{3,2,1,0:T(8,128)(2,1)S(1)}, u32[]{:S(2)}, u32[]{:S(2)}) %collective-permute-start.17) | collective-permute-done | bytes 1835040 | tf_op jit(solution)/shard_map/ppermute | solution.py:851
  126.6 3.6 %expert_down.6 = bf16[4,4,16,3584]{3,2,1,0:T(8,128)(2,1)} custom-call(bf16[256,288]{1,0:T(8,128)(2,1)S(1)} %get-tuple-element.141.act_ref, bf16[288,6144]{1,0:T(8,128)(2,1)} %bitcast.20, bf16[4,4,16,3584]{3,2,1,0:T(8,128)(2,1)S(1)} %collective-permute-done.17.refs_0_), custom_call_target="tpu_custom_call" | custom-call | flops 528482304 | bytes 3899392 | tf_op jit(solution)/shard_map/expert_down/pallas_call | solution.py:733
  130.3 4.5 %all-to-all-start.5 = ((bf16[4,4,16,3584]{3,2,1,0:T(8,128)(2,1)}), bf16[4,4,16,3584]{3,2,1,0:T(8,128)(2,1)S(1)}, u32[]{:S(2)}, u32[]{:S(2)}) async-start(bf16[4,4,16,3584]{3,2,1,0:T(8,128)(2,1)} %expert_down.6), calls=%async_computation.5 | async-start | bytes 3670016 | tf_op jit(solution)/shard_map/all_to_all | solution.py:846
  134.8 3.2 %expert_down.7 = (bf16[4,16,2560]{2,1,0:T(8,128)(2,1)}, bf16[4,16,2560]{2,1,0:T(8,128)(2,1)}, bf16[4,16,2560]{2,1,0:T(8,128)(2,1)}, bf16[4,16,2560]{2,1,0:T(8,128)(2,1)}) custom-call(bf16[256,288]{1,0:T(8,128)(2,1)S(1)} %get-tuple-element.141.act_ref, bf16[288,6144]{1,0:T(8,128)(2,1)} %bitcast.21, bf16[4,4,16,2560]{3,2,1,0:T(8,128)(2,1)S(1)} %collective-permute-done.18.refs_0_), custom_call_target="tpu_custom_call" | custom-call | flops 377487360 | bytes 2785280 | tf_op jit(solution)/shard_map/expert_down/pallas_call | solution.py:733
  141.8 13.3 %collective-permute-done.19.refs_1_ = bf16[4,16,2560]{2,1,0:T(8,128)(2,1)S(1)} collective-permute-done((bf16[4,16,2560]{2,1,0:T(8,128)(2,1)}, bf16[4,16,2560]{2,1,0:T(8,128)(2,1)S(1)}, u32[]{:S(2)}, u32[]{:S(2)}) %collective-permute-start.19) | collective-permute-done | bytes 327712 | tf_op jit(solution)/shard_map/ppermute | solution.py:851
  155.1 3.6 %collective-permute-done.21.refs_3_ = bf16[4,16,2560]{2,1,0:T(8,128)(2,1)S(1)} collective-permute-done((bf16[4,16,2560]{2,1,0:T(8,128)(2,1)}, bf16[4,16,2560]{2,1,0:T(8,128)(2,1)S(1)}, u32[]{:S(2)}, u32[]{:S(2)}) %collective-permute-start.21) | collective-permute-done | bytes 327712 | tf_op jit(solution)/shard_map/ppermute | solution.py:851
  160.4 4.5 %all-to-all-start.6 = ((bf16[4,16,2560]{2,1,0:T(8,128)(2,1)}), bf16[4,16,2560]{2,1,0:T(8,128)(2,1)S(1)}, u32[]{:S(2)}, u32[]{:S(2)}) async-start(bf16[4,16,2560]{2,1,0:T(8,128)(2,1)} %stack_sum.1), calls=%async_computation.6 | async-start | bytes 655360 | tf_op jit(solution)/shard_map/all_to_all | solution.py:846
  168.7 3.6 %collective-permute-done.22.refs_1_ = bf16[16,3584]{1,0:T(8,128)(2,1)S(1)} collective-permute-done((bf16[16,3584]{1,0:T(8,128)(2,1)}, bf16[16,3584]{1,0:T(8,128)(2,1)S(1)}, u32[]{:S(2)}, u32[]{:S(2)}) %collective-permute-start.22) | collective-permute-done | bytes 114720 | tf_op jit(solution)/shard_map/ppermute | solution.py:851
  177.4 3.4 %all-to-all-start.7 = ((bf16[4,4,6144]{2,1,0:T(4,128)(2,1)}), bf16[4,4,6144]{2,1,0:T(4,128)(2,1)S(1)}, u32[]{:S(2)}, u32[]{:S(2)}) async-start(bf16[4,4,6144]{2,1,0:T(4,128)(2,1)} %row_sum.1), calls=%async_computation.7 | async-start | bytes 393216 | tf_op jit(solution)/shard_map/all_to_all | solution.py:846
  181.1 5.0 %hidden_rows.1 = bf16[128,6144]{1,0:T(8,128)(2,1)} custom-call(s32[1]{0:T(128)} %bitcast.me_ref, bf16[128,6144]{1,0:T(8,128)(2,1)} %res_ref.1, bf16[128,6144]{1,0:T(8,128)(2,1)} %gate_ref.1, f32[1,6144]{1,0:T(1,128)} %bitcast.26, bf16[128,1536]{1,0:T(8,128)(2,1)S(1)} %copy-done, bf16[128,1536]{1,0:T(8,128)(2,1)S(1)} %copy-done.4, ...), custom_call_target="tpu_custom_call" | custom-call | flops 15728640 | bytes 6291456 | tf_op jit(solution)/shard_map/hidden_rows/pallas_call | solution.py:524
  (90 shorter events, 68.4 us)
Async XLA Ops:
  5.8 20.1 %all-to-all-start = ((bf16[32,64,128]{2,1,0:T(8,128)(2,1)}), bf16[32,64,128]{2,1,0:T(8,128)(2,1)}, u32[]{:S(2)}, u32[]{:S(2)}) async-start(bf16[32,64,128]{2,1,0:T(8,128)(2,1)} %get-tuple-element.79), calls=%async_computation | async-start | bytes 1048576 | tf_op jit(solution)/shard_map/all_to_all | solution.py:846
  27.8 21.4 %all-to-all-start.1 = ((bf16[32,48,128]{2,1,0:T(8,128)(2,1)}), bf16[32,48,128]{2,1,0:T(8,128)(2,1)S(1)}, u32[]{:S(2)}, u32[]{:S(2)}) async-start(bf16[32,48,128]{2,1,0:T(8,128)(2,1)} %scan_blocks.1), calls=%async_computation.1 | async-start | bytes 786432 | tf_op jit(solution)/shard_map/all_to_all | solution.py:846
  36.1 8.3 %collective-permute-start.1 = (bf16[8,6400]{1,0:T(8,128)(2,1)}, bf16[8,6400]{1,0:T(8,128)(2,1)S(1)}, u32[]{:S(2)}, u32[]{:S(2)}) collective-permute-start(bf16[8,6400]{1,0:T(8,128)(2,1)} %get-tuple-element.91), channel_id=1, source_target_pairs={{0,2},{1,3},{2,0},{3,1},{4,6},{5,7},{6,4},{7,5},{8,10},{9,11},{10,... | collective-permute-start | bytes 307208 | tf_op jit(solution)/shard_map/ppermute | solution.py:851
  51.2 10.4 %all-to-all-start.2 = ((bf16[4,16,1536]{2,1,0:T(8,128)(2,1)}), bf16[4,16,1536]{2,1,0:T(8,128)(2,1)}, u32[]{:S(2)}, u32[]{:S(2)}) async-start(bf16[4,16,1536]{2,1,0:T(8,128)(2,1)} %bitcast.24), calls=%async_computation.2 | async-start | bytes 393216 | tf_op jit(solution)/shard_map/all_to_all | solution.py:846
  61.5 17.3 %collective-permute-start.6 = (bf16[128,1536]{1,0:T(8,128)(2,1)}, bf16[128,1536]{1,0:T(8,128)(2,1)S(1)}, u32[]{:S(2)}, u32[]{:S(2)}) collective-permute-start(bf16[128,1536]{1,0:T(8,128)(2,1)} %get-tuple-element.107), channel_id=1, source_target_pairs={{0,2},{1,3},{2,0},{3,1},{4,6},{5,7},{6,4},{7,5},{8,10},{9,11},{10,... | collective-permute-start | bytes 1179656 | tf_op jit(solution)/shard_map/ppermute | solution.py:851
  65.4 13.4 %all-to-all-start.3 = ((bf16[4,16,3072]{2,1,0:T(8,128)(2,1)}), bf16[4,16,3072]{2,1,0:T(8,128)(2,1)S(1)}, u32[]{:S(2)}, u32[]{:S(2)}) async-start(bf16[4,16,3072]{2,1,0:T(8,128)(2,1)} %get-tuple-element.106), calls=%async_computation.3 | async-start | bytes 786432 | tf_op jit(solution)/shard_map/all_to_all | solution.py:846
  81.1 23.0 %all-to-all-start.4 = ((bf16[4,4,16,3072]{3,2,1,0:T(8,128)(2,1)}), bf16[4,4,16,3072]{3,2,1,0:T(8,128)(2,1)S(1)}, u32[]{:S(2)}, u32[]{:S(2)}) async-start(bf16[4,4,16,3072]{3,2,1,0:T(8,128)(2,1)} %repeat.1), calls=%async_computation.4 | async-start | bytes 3145728 | tf_op jit(solution)/shard_map/all_to_all | solution.py:846
  86.0 13.2 %collective-permute-start.7 = (bf16[4,16,3072]{2,1,0:T(8,128)(2,1)S(1)}, bf16[4,16,3072]{2,1,0:T(8,128)(2,1)S(1)}, u32[]{:S(2)}, u32[]{:S(2)}) collective-permute-start(bf16[4,16,3072]{2,1,0:T(8,128)(2,1)S(1)} %all-to-all-done.3.refs_0_), channel_id=1, source_target_pairs={{0,8},{8,16},{16,24},{24,0},{1,9},{9,17},{17,25},{25,1},{2,10},{10... | collective-permute-start | bytes 1179656 | tf_op jit(solution)/shard_map/ppermute | solution.py:851
  87.0 12.2 %collective-permute-start.10 = (bf16[128,1536]{1,0:T(8,128)(2,1)S(1)}, bf16[128,1536]{1,0:T(8,128)(2,1)S(1)}, u32[]{:S(2)}, u32[]{:S(2)}) collective-permute-start(bf16[128,1536]{1,0:T(8,128)(2,1)S(1)} %copy-done.12), channel_id=1, source_target_pairs={{0,1},{1,2},{2,3},{3,0},{4,5},{5,6},{6,7},{7,4},{8,9},{9,10},{10,1... | collective-permute-start | bytes 1179656 | tf_op jit(solution)/shard_map/ppermute | solution.py:851
  87.7 16.1 %collective-permute-start.8 = (bf16[4,16,3072]{2,1,0:T(8,128)(2,1)S(1)}, bf16[4,16,3072]{2,1,0:T(8,128)(2,1)S(1)}, u32[]{:S(2)}, u32[]{:S(2)}) collective-permute-start(bf16[4,16,3072]{2,1,0:T(8,128)(2,1)S(1)} %all-to-all-done.3.refs_0_), channel_id=1, source_target_pairs={{0,16},{8,24},{16,0},{24,8},{1,17},{9,25},{17,1},{25,9},{2,18},{10... | collective-permute-start | bytes 1179656 | tf_op jit(solution)/shard_map/ppermute | solution.py:851
  90.8 13.3 %collective-permute-start.9 = (bf16[4,16,3072]{2,1,0:T(8,128)(2,1)S(1)}, bf16[4,16,3072]{2,1,0:T(8,128)(2,1)S(1)}, u32[]{:S(2)}, u32[]{:S(2)}) collective-permute-start(bf16[4,16,3072]{2,1,0:T(8,128)(2,1)S(1)} %all-to-all-done.3.refs_0_), channel_id=1, source_target_pairs={{0,24},{8,0},{16,8},{24,16},{1,25},{9,1},{17,9},{25,17},{2,26},{10... | collective-permute-start | bytes 1179656 | tf_op jit(solution)/shard_map/ppermute | solution.py:851
  104.1 10.9 %collective-permute-start.11 = (bf16[4,4,16,3072]{3,2,1,0:T(8,128)(2,1)S(1)}, bf16[4,4,16,3072]{3,2,1,0:T(8,128)(2,1)S(1)}, u32[]{:S(2)}, u32[]{:S(2)}) collective-permute-start(bf16[4,4,16,3072]{3,2,1,0:T(8,128)(2,1)S(1)} %all-to-all-done.4.one_ref), channel_id=1, source_target_pairs={{0,4},{4,0},{1,5},{5,1},{2,6},{6,2},{3,7},{7,3},{8,12},{12,8},{9,1... | collective-permute-start | bytes 4718600 | tf_op jit(solution)/shard_map/ppermute | solution.py:851
  104.6 10.4 %collective-permute-start.13 = (bf16[4,16,3072]{2,1,0:T(8,128)(2,1)S(1)}, bf16[4,16,3072]{2,1,0:T(8,128)(2,1)S(1)}, u32[]{:S(2)}, u32[]{:S(2)}) collective-permute-start(bf16[4,16,3072]{2,1,0:T(8,128)(2,1)S(1)} %collective-permute-done.7.refs_1_), channel_id=1, source_target_pairs={{0,4},{4,0},{1,5},{5,1},{2,6},{6,2},{3,7},{7,3},{8,12},{12,8},{9,1... | collective-permute-start | bytes 1179656 | tf_op jit(solution)/shard_map/ppermute | solution.py:851
  104.7 10.3 %collective-permute-start.14 = (bf16[4,16,3072]{2,1,0:T(8,128)(2,1)S(1)}, bf16[4,16,3072]{2,1,0:T(8,128)(2,1)S(1)}, u32[]{:S(2)}, u32[]{:S(2)}) collective-permute-start(bf16[4,16,3072]{2,1,0:T(8,128)(2,1)S(1)} %collective-permute-done.8.refs_2_), channel_id=1, source_target_pairs={{0,4},{4,0},{1,5},{5,1},{2,6},{6,2},{3,7},{7,3},{8,12},{12,8},{9,1... | collective-permute-start | bytes 1179656 | tf_op jit(solution)/shard_map/ppermute | solution.py:851
  105.1 9.9 %collective-permute-start.15 = (bf16[4,16,3072]{2,1,0:T(8,128)(2,1)S(1)}, bf16[4,16,3072]{2,1,0:T(8,128)(2,1)S(1)}, u32[]{:S(2)}, u32[]{:S(2)}) collective-permute-start(bf16[4,16,3072]{2,1,0:T(8,128)(2,1)S(1)} %collective-permute-done.9.refs_3_), channel_id=1, source_target_pairs={{0,4},{4,0},{1,5},{5,1},{2,6},{6,2},{3,7},{7,3},{8,12},{12,8},{9,1... | collective-permute-start | bytes 1179656 | tf_op jit(solution)/shard_map/ppermute | solution.py:851
  108.1 14.0 %collective-permute-start.16 = (bf16[128,1536]{1,0:T(8,128)(2,1)}, bf16[128,1536]{1,0:T(8,128)(2,1)S(1)}, u32[]{:S(2)}, u32[]{:S(2)}) collective-permute-start(bf16[128,1536]{1,0:T(8,128)(2,1)} %get-tuple-element.134), channel_id=1, source_target_pairs={{0,3},{1,0},{2,1},{3,2},{4,7},{5,4},{6,5},{7,6},{8,11},{9,8},{10,9... | collective-permute-start | bytes 1179656 | tf_op jit(solution)/shard_map/ppermute | solution.py:851
  122.8 7.4 %collective-permute-start.18 = (bf16[4,4,16,2560]{3,2,1,0:T(8,128)(2,1)S(1)}, bf16[4,4,16,2560]{3,2,1,0:T(8,128)(2,1)S(1)}, u32[]{:S(2)}, u32[]{:S(2)}) collective-permute-start(bf16[4,4,16,2560]{3,2,1,0:T(8,128)(2,1)S(1)} %expert_down.5), channel_id=1, source_target_pairs={{0,4},{4,0},{1,5},{5,1},{2,6},{6,2},{3,7},{7,3},{8,12},{12,8},{9,1... | collective-permute-start | bytes 3932168 | tf_op jit(solution)/shard_map/ppermute | solution.py:851
  130.3 28.4 %all-to-all-start.5 = ((bf16[4,4,16,3584]{3,2,1,0:T(8,128)(2,1)}), bf16[4,4,16,3584]{3,2,1,0:T(8,128)(2,1)S(1)}, u32[]{:S(2)}, u32[]{:S(2)}) async-start(bf16[4,4,16,3584]{3,2,1,0:T(8,128)(2,1)} %expert_down.6), calls=%async_computation.5 | async-start | bytes 3670016 | tf_op jit(solution)/shard_map/all_to_all | solution.py:846
  138.0 17.0 %collective-permute-start.19 = (bf16[4,16,2560]{2,1,0:T(8,128)(2,1)}, bf16[4,16,2560]{2,1,0:T(8,128)(2,1)S(1)}, u32[]{:S(2)}, u32[]{:S(2)}) collective-permute-start(bf16[4,16,2560]{2,1,0:T(8,128)(2,1)} %get-tuple-element.144), channel_id=1, source_target_pairs={{0,24},{8,0},{16,8},{24,16},{1,25},{9,1},{17,9},{25,17},{2,26},{10... | collective-permute-start | bytes 983048 | tf_op jit(solution)/shard_map/ppermute | solution.py:851
  140.7 14.4 %collective-permute-start.20 = (bf16[4,16,2560]{2,1,0:T(8,128)(2,1)}, bf16[4,16,2560]{2,1,0:T(8,128)(2,1)S(1)}, u32[]{:S(2)}, u32[]{:S(2)}) collective-permute-start(bf16[4,16,2560]{2,1,0:T(8,128)(2,1)} %get-tuple-element.145), channel_id=1, source_target_pairs={{0,16},{8,24},{16,0},{24,8},{1,17},{9,25},{17,1},{25,9},{2,18},{10... | collective-permute-start | bytes 983048 | tf_op jit(solution)/shard_map/ppermute | solution.py:851
  141.8 16.9 %collective-permute-start.21 = (bf16[4,16,2560]{2,1,0:T(8,128)(2,1)}, bf16[4,16,2560]{2,1,0:T(8,128)(2,1)S(1)}, u32[]{:S(2)}, u32[]{:S(2)}) collective-permute-start(bf16[4,16,2560]{2,1,0:T(8,128)(2,1)} %get-tuple-element.146), channel_id=1, source_target_pairs={{0,8},{8,16},{16,24},{24,0},{1,9},{9,17},{17,25},{25,1},{2,10},{10... | collective-permute-start | bytes 983048 | tf_op jit(solution)/shard_map/ppermute | solution.py:851
  160.4 15.3 %all-to-all-start.6 = ((bf16[4,16,2560]{2,1,0:T(8,128)(2,1)}), bf16[4,16,2560]{2,1,0:T(8,128)(2,1)S(1)}, u32[]{:S(2)}, u32[]{:S(2)}) async-start(bf16[4,16,2560]{2,1,0:T(8,128)(2,1)} %stack_sum.1), calls=%async_computation.6 | async-start | bytes 655360 | tf_op jit(solution)/shard_map/all_to_all | solution.py:846
  167.6 7.1 %collective-permute-start.23 = (bf16[16,3584]{1,0:T(8,128)(2,1)}, bf16[16,3584]{1,0:T(8,128)(2,1)S(1)}, u32[]{:S(2)}, u32[]{:S(2)}) collective-permute-start(bf16[16,3584]{1,0:T(8,128)(2,1)} %get-tuple-element.154), channel_id=1, source_target_pairs={{0,16},{8,24},{16,0},{24,8},{1,17},{9,25},{17,1},{25,9},{2,18},{10... | collective-permute-start | bytes 344072 | tf_op jit(solution)/shard_map/ppermute | solution.py:851
  177.4 9.7 %all-to-all-start.7 = ((bf16[4,4,6144]{2,1,0:T(4,128)(2,1)}), bf16[4,4,6144]{2,1,0:T(4,128)(2,1)S(1)}, u32[]{:S(2)}, u32[]{:S(2)}) async-start(bf16[4,4,6144]{2,1,0:T(4,128)(2,1)} %row_sum.1), calls=%async_computation.7 | async-start | bytes 393216 | tf_op jit(solution)/shard_map/all_to_all | solution.py:846
  (22 other events, 158.2 us)
